TPU v7x, 128 devices: a whole 4x4x4 slice. The times are simulated.
128 devices in a mesh: gx: 32 (over y, z, core), gy: 4 (over x).
Axes of the slice: x: 4, y: 4, z: 4, core: 2. Of those that a mesh axis runs over, the one named last changes fastest.
Arguments:
- point_feats: bfloat16 [32, 4194304], P(None, ('gx', 'gy')), may hold values from -0.5 to 0.5
- point_targets: bfloat16 [4194304], P(('gx', 'gy')), may hold values from -6 to 6
- point_lists: int32 [524288, 8], P(('gx', 'gy')), may hold values from -1 to 32767, as said below
- brick_adjacency: int32 [4096, 4], P(('gx', 'gy')), may hold values from -1 to 4095, as said below
- voxel_feats: float32 [4096, 32, 512], P(('gx', 'gy')), may hold values from -0.25 to 0.25
- voxel_reg: float32 [4096, 512], P(('gx', 'gy')), may hold values from 0.25 to 2
Outputs:
- solution: float32 [4096, 512], P(('gx', 'gy'))
- residual: float32 [4096, 512], P(('gx', 'gy'))
Inputs may be any that keep to these rules, and one draw needn't show every extreme that they name: `point_lists`: row s * 4096 + b lists, in its first slots, distinct indices of the points of source device s in brick b, all within that device's rows b * 8 to b * 8 + 7, then -1 in the remaining slots. Point rows named by no list are unused. `brick_adjacency`: entry k of brick b is the lattice neighbour of b in direction k (minus along the road, plus along the road, minus across, plus across) or -1; the relation is symmetric and -1 wherever the neighbour lies outside the lattice.
All inputs are finite; a program needn't handle non-finite values.
Results may differ from a plain program's by a relative error of at most 0.0003.
Values may be sent and summed in bfloat16 or wider, within the bound.
No kernel may reach another device: no remote copies, remote signals or barrier semaphores. Data moves between devices by JAX's collectives and lax.ppermute only.
A program may use at most 64 MiB of HBM per device.

v0:
```python
import functools

import jax
import jax.numpy as jnp
from jax import lax
from jax.sharding import Mesh
from jax.sharding import PartitionSpec as P

BX = 8
BY = 4
ITERS = 3
GX_GY = ("gx_0", "gx_1", "gx_2", "gy")
GX = ("gx_0", "gx_1", "gx_2")


coupling_weight = 1.0


def with_halo(x, sides, width):
    edges = {}
    for axis, dim in sides:
        devices, length = (lax.axis_size(axis), x.shape[dim])
        up = [(i, (i + 1) % devices) for i in range(devices - 1)]
        last = lax.slice_in_dim(x, length - width, length, axis=dim)
        leading = lax.slice_in_dim(x, 0, width, axis=dim)
        edges[dim] = (
            lax.ppermute(last, axis, up),
            lax.ppermute(leading, axis, [(b, a) for a, b in up]),
        )
    done = []
    for _, dim in sides:
        low, high = edges[dim]
        around = [(width, width) if d in done else (0, 0) for d in range(x.ndim)]
        x = jnp.concatenate([jnp.pad(low, around), x, jnp.pad(high, around)], axis=dim)
        done.append(dim)
    return x


def by_axis(x, axes):
    return functools.reduce(lax.psum, axes, x)


def neighbour_sum(padded, mask):
    total = mask[..., 0:1] * padded[:-2, 1:-1] + mask[..., 1:2] * padded[2:, 1:-1]
    return total + mask[..., 2:3] * padded[1:-1, :-2] + mask[..., 3:4] * padded[1:-1, 2:]


def shards(point_feats, point_targets, point_lists, brick_adjacency, voxel_feats, voxel_reg):
    feat_count = point_feats.shape[0]
    brick_total, slots = point_lists.shape
    local_bricks = voxel_feats.shape[0]
    devices = brick_total // local_bricks
    live = point_lists >= 0
    offset = point_lists - jnp.arange(brick_total, dtype=jnp.int32)[:, None] * slots
    choose = (offset[:, :, None] == jnp.arange(slots, dtype=jnp.int32)[None, None, :]) & live[
        :, :, None
    ]
    choose = choose.astype(jnp.bfloat16)
    blocks = point_feats.reshape(feat_count, brick_total, slots)
    picked = jnp.einsum("ibd,bcd->ibc", blocks, choose, preferred_element_type=jnp.float32).astype(
        jnp.bfloat16
    )
    target_blocks = point_targets.reshape(brick_total, slots)
    targets = jnp.einsum(
        "bd,bcd->bc", target_blocks, choose, preferred_element_type=jnp.float32
    ).astype(jnp.bfloat16)
    sending = picked.reshape(feat_count, devices, local_bricks * slots)
    target_rows = targets.reshape(1, devices, local_bricks * slots)
    got_feats, got_targets = (
        lax.all_to_all(sending, GX_GY, split_axis=1, concat_axis=1, tiled=True),
        lax.all_to_all(target_rows, GX_GY, split_axis=1, concat_axis=1, tiled=True),
    )
    got_feats = got_feats.reshape(feat_count, devices, local_bricks, slots)
    got_targets = got_targets.reshape(devices, local_bricks, slots)
    moments = jnp.einsum("isbc,jsbc->bij", got_feats, got_feats, preferred_element_type=jnp.float32)
    gathered = jnp.einsum(
        "sbc,isbc->bi", got_targets, got_feats, preferred_element_type=jnp.float32
    )
    mask = (brick_adjacency >= 0).astype(jnp.float32).reshape(BX, BY, 4)
    degree = jnp.sum(mask, axis=-1, keepdims=True)

    def operate(vector):
        projected = jnp.einsum("bik,bk->bi", voxel_feats, vector, precision=lax.Precision.HIGHEST)
        lattice = projected.reshape(BX, BY, feat_count)
        padded = with_halo(lattice, ((GX, 0), ("gy", 1)), 1)
        coupled = (degree * lattice - neighbour_sum(padded, mask)).reshape(local_bricks, feat_count)
        middle = jnp.einsum("bij,bj->bi", moments, projected, precision=lax.Precision.HIGHEST)
        middle = middle + coupling_weight * coupled
        back = jnp.einsum("bik,bi->bk", voxel_feats, middle, precision=lax.Precision.HIGHEST)
        return back + voxel_reg * vector

    def two_products(values, image):
        return (by_axis(jnp.sum(values * values), GX_GY), by_axis(jnp.sum(values * image), GX_GY))

    rhs = jnp.einsum("bik,bi->bk", voxel_feats, gathered, precision=lax.Precision.HIGHEST)
    solution = jnp.zeros_like(rhs)
    residual = rhs
    image = operate(residual)
    norm_now, product = two_products(residual, image)
    alpha = norm_now / product
    direction, carried = (residual, image)
    for iteration in range(ITERS):
        solution = solution + alpha * direction
        residual = residual - alpha * carried
        if iteration + 1 < ITERS:
            image = operate(residual)
            norm_next, product = two_products(residual, image)
            ratio = norm_next / norm_now
            alpha = norm_next / (product - ratio * norm_next / alpha)
            direction = residual + ratio * direction
            carried = image + ratio * carried
            norm_now = norm_next
    return (solution, residual)


def solution(mesh):
    torus = Mesh(mesh.devices.reshape(4, 4, 2, mesh.shape["gy"]), ("gx_0", "gx_1", "gx_2", "gy"))
    return jax.shard_map(
        shards,
        mesh=torus,
        in_specs=(
            P(None, GX_GY),
            P(GX_GY),
            P(GX_GY, None),
            P(GX_GY, None),
            P(GX_GY, None, None),
            P(GX_GY, None),
        ),
        out_specs=(P(GX_GY, None), P(GX_GY, None)),
        check_vma=False,
    )
```

profile of v0, /device:TPU:1, one launch (start us, length us, event | category | flops | bytes accessed | tf_op | source)
XLA Modules:
  0.0 293.8 jit_solution(6174218351555194109)
XLA Ops:
  0.7 1.1 broadcast_compare_fusion
  1.8 0.9 broadcast_subtract_fusion
  2.7 2.0 copy.33
  4.6 0.8 copy.34
  5.5 4.5 %reshape.98 = bf16[4096,8,1]{1,2,0:T(2,128)(2,1)} reshape(bf16[32768]{0:T(1024)(128)(2,1)S(1)} %copy-done.5) | data formatting | bytes 131072 | tf_op jit(solution)/shard_map/reshape | solution.py:63
  10.0 23.9 %fusion.3 = f32[4096,1,8]{2,1,0:T(1,128)S(1)} fusion(bf16[4096,8,1]{1,2,0:T(2,128)(2,1)} %reshape.98, s32[4096,8]{1,0:T(8,128)} %copy.33, pred[4096,8]{1,0:T(8,128)(4,1)S(1)} %copy.34), kind=kOutput, calls=%fused_computation.3 | convolution fusion | flops 1048576 | bytes 360448 | tf_op jit(solution)/shard_map/bd,bcd->bc/dot_general | solution.py:64
  34.0 1.1 reshape.99
  35.1 0.5 broadcast.80
  35.7 1.0 reduce.1
  36.7 0.7 reshape.100
  37.3 11.5 %all-to-all-start = ((bf16[128,2,128]{2,1,0:T(2,128)(2,1)}), bf16[128,2,128]{2,1,0:T(2,128)(2,1)S(1)}, u32[]{:S(2)}, u32[]{:S(2)}) async-start(bf16[128,2,128]{2,1,0:T(2,128)(2,1)} %reshape.100), calls=%async_computation | async-start | bytes 131072 | tf_op jit(solution)/shard_map/all_to_all | solution.py:71
  48.8 7.4 %copy.37 = bf16[32,32768]{0,1:T(8,128)(2,1)} copy(bf16[32,32768]{1,0:T(8,128)(2,1)} %param.6) | data formatting | bytes 4194304 | tf_op args[0]
  56.3 25.1 %fusion.10 = bf16[4096,8,32]{2,1,0:T(8,128)(2,1)} fusion(bf16[32,32768]{0,1:T(8,128)(2,1)} %copy.37, s32[4096,8]{1,0:T(8,128)} %copy.33, pred[4096,8]{1,0:T(8,128)(4,1)S(1)} %copy-done.4), kind=kOutput, calls=%fused_computation.9 | convolution fusion | flops 18350080 | bytes 4358144 | tf_op jit(solution)/shard_map/ibd,bcd->ibc/dot_general | solution.py:60
  81.3 7.9 %copy.38 = bf16[32,128,256]{2,0,1:T(8,128)(2,1)} copy(bf16[32,128,256]{0,2,1:T(8,128)(2,1)} %bitcast.160) | data formatting | bytes 4194304 | tf_op jit(solution)/shard_map/reshape | solution.py:67
  89.2 10.2 %all-to-all-start.1 = ((bf16[32,128,256]{2,0,1:T(8,128)(2,1)}), bf16[32,128,256]{2,0,1:T(8,128)(2,1)}, u32[]{:S(2)}, u32[]{:S(2)}) async-start(bf16[32,128,256]{2,0,1:T(8,128)(2,1)} %copy.38), calls=%async_computation.1 | async-start | bytes 4194304 | tf_op jit(solution)/shard_map/all_to_all | solution.py:70
  99.7 0.1 copy.36
  99.8 30.3 %all-to-all-done.1 = bf16[32,128,256]{2,0,1:T(8,128)(2,1)} async-done(((bf16[32,128,256]{2,0,1:T(8,128)(2,1)}), bf16[32,128,256]{2,0,1:T(8,128)(2,1)}, u32[]{:S(2)}, u32[]{:S(2)}) %all-to-all-start.1) | async-done | bytes 2097184 | tf_op jit(solution)/shard_map/all_to_all | solution.py:70
  130.1 5.2 %copy.39 = bf16[32,128,256]{1,0,2:T(8,128)(2,1)} copy(bf16[32,128,256]{2,0,1:T(8,128)(2,1)} %all-to-all-done.1) | data formatting | bytes 4194304 | tf_op jit(solution)/shard_map/all_to_all | solution.py:70
  135.2 3.0 %convolution_bitcast_fusion = f32[32,32,32]{2,1,0:T(8,128)S(1)} fusion(bf16[32,128,32,8]{1,0,3,2:T(8,128)(2,1)} %bitcast.158), kind=kOutput, calls=%fused_computation.10 | convolution fusion | flops 67108864 | bytes 2228224 | tf_op jit(solution)/shard_map/isbc,jsbc->bij/dot_general | solution.py:75
  138.3 0.7 convolution_bitcast_fusion.1
  139.0 1.1 fusion.67
  140.1 1.8 fusion.25
  142.0 2.2 collective-permute-start.2
  144.2 1.3 collective-permute-start.3
  145.5 2.9 collective-permute-start
  148.4 2.1 collective-permute-start.1
  150.5 0.9 fusion.61
  151.4 1.9 collective-permute-done.1
  153.3 0.1 fusion.50
  153.4 1.1 fusion.68
  154.5 0.6 fusion.18
  155.2 7.4 %all-reduce.14 = (f32[]{:T(128)}, f32[]{:T(128)}) all-reduce(f32[]{:T(128)} %get-tuple-element.7, f32[]{:T(128)} %get-tuple-element.6), channel_id=1, replica_groups=mesh['gx_0'=4,'gx_1'=4,'gx_2'=2,'gy'=4] {'gx_0'}, use_global_device_ids=true, to_apply=%region_1.2 | all-reduce | flops 2 | bytes 16 | tf_op jit(solution)/shard_map/psum | solution.py:40
  162.6 10.1 %all-reduce.11 = (f32[]{:T(128)}, f32[]{:T(128)}) all-reduce(f32[]{:T(128)} %get-tuple-element.24, f32[]{:T(128)} %get-tuple-element.25), channel_id=1, replica_groups=mesh['gx_0'=4,'gx_1'=4,'gx_2'=2,'gy'=4] {'gx_1'}, use_global_device_ids=true, to_apply=%region_2.3 | all-reduce | flops 2 | bytes 16 | tf_op jit(solution)/shard_map/psum | solution.py:40
  172.7 4.7 %all-reduce.17 = (f32[]{:T(128)}, f32[]{:T(128)}) all-reduce(f32[]{:T(128)} %get-tuple-element.18, f32[]{:T(128)} %get-tuple-element.19), channel_id=1, replica_groups=mesh['gx_0'=4,'gx_1'=4,'gx_2'=2,'gy'=4] {'gx_2'}, use_global_device_ids=true, to_apply=%region_3.4 | all-reduce | flops 2 | bytes 16 | tf_op jit(solution)/shard_map/psum | solution.py:40
  177.5 9.9 %all-reduce.8 = (f32[]{:T(128)}, f32[]{:T(128)}) all-reduce(f32[]{:T(128)} %get-tuple-element.30, f32[]{:T(128)} %get-tuple-element.31), channel_id=1, replica_groups=mesh['gx_0'=4,'gx_1'=4,'gx_2'=2,'gy'=4] {'gy'}, use_global_device_ids=true, to_apply=%region_4.5 | all-reduce | flops 2 | bytes 16 | tf_op jit(solution)/shard_map/psum | solution.py:40
  188.8 1.8 fusion.23
  190.6 1.3 collective-permute-start.6
  191.9 1.3 collective-permute-start.7
  193.2 5.9 %collective-permute-start.4 = (f32[1,4,32]{2,1,0:T(4,128)S(1)}, f32[1,4,32]{2,1,0:T(4,128)S(1)}, u32[]{:S(2)}, u32[]{:S(2)}) collective-permute-start(f32[1,4,32]{2,1,0:T(4,128)S(1)} %get-tuple-element.41), channel_id=1, source_target_pairs={{0,4},{4,8},{8,12},{12,16},{16,20},{20,24},{24,28},{28,32},{32,36}... | collective-permute-start | bytes 1544 | tf_op jit(solution)/shard_map/ppermute | solution.py:27
  199.1 1.9 collective-permute-start.5
  201.0 0.9 fusion.59
  201.9 2.0 collective-permute-done.5
  204.0 0.1 fusion.40
  204.1 1.1 fusion.69
  205.3 0.7 multiply_reduce_fusion.2
  205.9 6.7 %all-reduce.13 = (f32[]{:T(128)}, f32[]{:T(128)}) all-reduce(f32[]{:T(128)} %get-tuple-element.5, f32[]{:T(128)} %get-tuple-element.4), channel_id=1, replica_groups=mesh['gx_0'=4,'gx_1'=4,'gx_2'=2,'gy'=4] {'gx_0'}, use_global_device_ids=true, to_apply=%region_12.13 | all-reduce | flops 2 | bytes 16 | tf_op jit(solution)/shard_map/psum | solution.py:40
  212.6 9.7 %all-reduce.10 = (f32[]{:T(128)}, f32[]{:T(128)}) all-reduce(f32[]{:T(128)} %get-tuple-element.22, f32[]{:T(128)} %get-tuple-element.23), channel_id=1, replica_groups=mesh['gx_0'=4,'gx_1'=4,'gx_2'=2,'gy'=4] {'gx_1'}, use_global_device_ids=true, to_apply=%region_13.14 | all-reduce | flops 2 | bytes 16 | tf_op jit(solution)/shard_map/psum | solution.py:40
  222.3 3.7 %all-reduce.16 = (f32[]{:T(128)}, f32[]{:T(128)}) all-reduce(f32[]{:T(128)} %get-tuple-element.16, f32[]{:T(128)} %get-tuple-element.17), channel_id=1, replica_groups=mesh['gx_0'=4,'gx_1'=4,'gx_2'=2,'gy'=4] {'gx_2'}, use_global_device_ids=true, to_apply=%region_14.15 | all-reduce | flops 2 | bytes 16 | tf_op jit(solution)/shard_map/psum | solution.py:40
  226.0 9.4 %all-reduce.7 = (f32[]{:T(128)}, f32[]{:T(128)}) all-reduce(f32[]{:T(128)} %get-tuple-element.28, f32[]{:T(128)} %get-tuple-element.29), channel_id=1, replica_groups=mesh['gx_0'=4,'gx_1'=4,'gx_2'=2,'gy'=4] {'gy'}, use_global_device_ids=true, to_apply=%region_15.16 | all-reduce | flops 2 | bytes 16 | tf_op jit(solution)/shard_map/psum | solution.py:40
  240.0 1.8 fusion.21
  241.8 2.1 collective-permute-start.10
  243.9 1.3 collective-permute-start.11
  245.3 6.2 %collective-permute-start.8 = (f32[1,4,32]{2,1,0:T(4,128)S(1)}, f32[1,4,32]{2,1,0:T(4,128)S(1)}, u32[]{:S(2)}, u32[]{:S(2)}) collective-permute-start(f32[1,4,32]{2,1,0:T(4,128)S(1)} %get-tuple-element.37), channel_id=1, source_target_pairs={{0,4},{4,8},{8,12},{12,16},{16,20},{20,24},{24,28},{28,32},{32,36}... | collective-permute-start | bytes 1544 | tf_op jit(solution)/shard_map/ppermute | solution.py:27
  251.4 1.9 collective-permute-start.9
  253.4 0.9 fusion.57
  254.3 2.0 collective-permute-done.9
  256.3 0.1 fusion.30
  256.5 1.1 fusion.70
  257.6 0.6 multiply_reduce_fusion
  258.2 6.6 %all-reduce.12 = (f32[]{:T(128)}, f32[]{:T(128)}) all-reduce(f32[]{:T(128)} %get-tuple-element.3, f32[]{:T(128)} %get-tuple-element.2), channel_id=1, replica_groups=mesh['gx_0'=4,'gx_1'=4,'gx_2'=2,'gy'=4] {'gx_0'}, use_global_device_ids=true, to_apply=%region_22.23 | all-reduce | flops 2 | bytes 16 | tf_op jit(solution)/shard_map/psum | solution.py:40
  264.8 11.4 %all-reduce.9 = (f32[]{:T(128)}, f32[]{:T(128)}) all-reduce(f32[]{:T(128)} %get-tuple-element.20, f32[]{:T(128)} %get-tuple-element.21), channel_id=1, replica_groups=mesh['gx_0'=4,'gx_1'=4,'gx_2'=2,'gy'=4] {'gx_1'}, use_global_device_ids=true, to_apply=%region_23.24 | all-reduce | flops 2 | bytes 16 | tf_op jit(solution)/shard_map/psum | solution.py:40
  276.2 4.0 %all-reduce.15 = (f32[]{:T(128)}, f32[]{:T(128)}) all-reduce(f32[]{:T(128)} %get-tuple-element.14, f32[]{:T(128)} %get-tuple-element.15), channel_id=1, replica_groups=mesh['gx_0'=4,'gx_1'=4,'gx_2'=2,'gy'=4] {'gx_2'}, use_global_device_ids=true, to_apply=%region_24.25 | all-reduce | flops 2 | bytes 16 | tf_op jit(solution)/shard_map/psum | solution.py:40
  280.2 9.0 %all-reduce.6 = (f32[]{:T(128)}, f32[]{:T(128)}) all-reduce(f32[]{:T(128)} %get-tuple-element.26, f32[]{:T(128)} %get-tuple-element.27), channel_id=1, replica_groups=mesh['gx_0'=4,'gx_1'=4,'gx_2'=2,'gy'=4] {'gy'}, use_global_device_ids=true, to_apply=%region_25.26 | all-reduce | flops 2 | bytes 16 | tf_op jit(solution)/shard_map/psum | solution.py:40
  293.1 0.7 multiply_subtract_fusion
  (44 shorter events, 0.5 us)
Async XLA Ops:
  0.6 138.3 %copy-start = (f32[32,32,512]{2,1,0:T(8,128)S(1)}, f32[32,32,512]{2,1,0:T(8,128)}, u32[]{:S(2)}) copy-start(f32[32,32,512]{2,1,0:T(8,128)} %param.10) | copy-start | bytes 6291460
  0.6 4.8 %copy-start.5 = (bf16[32768]{0:T(1024)(128)(2,1)S(1)}, bf16[32768]{0:T(1024)(128)(2,1)}, u32[]{:S(2)}) copy-start(bf16[32768]{0:T(1024)(128)(2,1)} %param.7) | copy-start | bytes 196612
  5.5 28.4 %copy-start.3 = (pred[4096,8]{1,0:T(8,128)(4,1)}, pred[4096,8]{1,0:T(8,128)(4,1)S(1)}, u32[]{:S(2)}) copy-start(pred[4096,8]{1,0:T(8,128)(4,1)S(1)} %copy.34) | copy-start | bytes 98308
  37.3 51.9 %all-to-all-start = ((bf16[128,2,128]{2,1,0:T(2,128)(2,1)}), bf16[128,2,128]{2,1,0:T(2,128)(2,1)S(1)}, u32[]{:S(2)}, u32[]{:S(2)}) async-start(bf16[128,2,128]{2,1,0:T(2,128)(2,1)} %reshape.100), calls=%async_computation | async-start | bytes 131072 | tf_op jit(solution)/shard_map/all_to_all | solution.py:71
  48.8 7.4 %copy-start.4 = (pred[4096,8]{1,0:T(8,128)(4,1)S(1)}, pred[4096,8]{1,0:T(8,128)(4,1)}, u32[]{:S(2)}) copy-start(pred[4096,8]{1,0:T(8,128)(4,1)} %copy-done.3) | copy-start | bytes 98308
  89.2 10.2 %copy-start.6 = (s32[32,4]{0,1:T(4,128)S(1)}, s32[32,4]{0,1:T(4,128)}, u32[]{:S(2)}) copy-start(s32[32,4]{0,1:T(4,128)} %param.9) | copy-start | bytes 1540
  89.2 40.9 %all-to-all-start.1 = ((bf16[32,128,256]{2,0,1:T(8,128)(2,1)}), bf16[32,128,256]{2,0,1:T(8,128)(2,1)}, u32[]{:S(2)}, u32[]{:S(2)}) async-start(bf16[32,128,256]{2,0,1:T(8,128)(2,1)} %copy.38), calls=%async_computation.1 | async-start | bytes 4194304 | tf_op jit(solution)/shard_map/all_to_all | solution.py:70
  135.2 3.0 %copy-start.1 = (bf16[32,128,256]{1,0,2:T(8,128)(2,1)S(1)}, bf16[32,128,256]{1,0,2:T(8,128)(2,1)}, u32[]{:S(2)}) copy-start(bf16[32,128,256]{1,0,2:T(8,128)(2,1)} %copy.39) | copy-start | bytes 6291460
  140.1 14.4 %copy-start.2 = (f32[32,512]{1,0:T(8,128)S(1)}, f32[32,512]{1,0:T(8,128)}, u32[]{:S(2)}) copy-start(f32[32,512]{1,0:T(8,128)} %param.11) | copy-start | bytes 196612
  142.0 11.3 %collective-permute-start.2 = (f32[8,1,32]{2,1,0:T(1,128)S(1)}, f32[8,1,32]{2,1,0:T(1,128)S(1)}, u32[]{:S(2)}, u32[]{:S(2)}) collective-permute-start(f32[8,1,32]{2,1,0:T(1,128)S(1)} %get-tuple-element.47), channel_id=1, source_target_pairs={{0,1},{1,2},{2,3},{4,5},{5,6},{6,7},{8,9},{9,10},{10,11},{12,13},{... | collective-permute-start | bytes 3080 | tf_op jit(solution)/shard_map/ppermute | solution.py:27
  144.2 9.1 %collective-permute-start.3 = (f32[8,1,32]{2,1,0:T(1,128)S(1)}, f32[8,1,32]{2,1,0:T(1,128)S(1)}, u32[]{:S(2)}, u32[]{:S(2)}) collective-permute-start(f32[8,1,32]{2,1,0:T(1,128)S(1)} %get-tuple-element.48), channel_id=1, source_target_pairs={{1,0},{2,1},{3,2},{5,4},{6,5},{7,6},{9,8},{10,9},{11,10},{13,12},{... | collective-permute-start | bytes 3080 | tf_op jit(solution)/shard_map/ppermute | solution.py:28
  145.5 5.9 %collective-permute-start = (f32[1,4,32]{2,1,0:T(4,128)S(1)}, f32[1,4,32]{2,1,0:T(4,128)S(1)}, u32[]{:S(2)}, u32[]{:S(2)}) collective-permute-start(f32[1,4,32]{2,1,0:T(4,128)S(1)} %get-tuple-element.49), channel_id=1, source_target_pairs={{0,4},{4,8},{8,12},{12,16},{16,20},{20,24},{24,28},{28,32},{32,36}... | collective-permute-start | bytes 1544 | tf_op jit(solution)/shard_map/ppermute | solution.py:27
  148.4 4.9 %collective-permute-start.1 = (f32[1,4,32]{2,1,0:T(4,128)S(1)}, f32[1,4,32]{2,1,0:T(4,128)S(1)}, u32[]{:S(2)}, u32[]{:S(2)}) collective-permute-start(f32[1,4,32]{2,1,0:T(4,128)S(1)} %get-tuple-element.50), channel_id=1, source_target_pairs={{4,0},{8,4},{12,8},{16,12},{20,16},{24,20},{28,24},{32,28},{36,32}... | collective-permute-start | bytes 1544 | tf_op jit(solution)/shard_map/ppermute | solution.py:28
  190.6 13.4 %collective-permute-start.6 = (f32[8,1,32]{2,1,0:T(1,128)S(1)}, f32[8,1,32]{2,1,0:T(1,128)S(1)}, u32[]{:S(2)}, u32[]{:S(2)}) collective-permute-start(f32[8,1,32]{2,1,0:T(1,128)S(1)} %get-tuple-element.39), channel_id=1, source_target_pairs={{0,1},{1,2},{2,3},{4,5},{5,6},{6,7},{8,9},{9,10},{10,11},{12,13},{... | collective-permute-start | bytes 3080 | tf_op jit(solution)/shard_map/ppermute | solution.py:27
  191.9 12.1 %collective-permute-start.7 = (f32[8,1,32]{2,1,0:T(1,128)S(1)}, f32[8,1,32]{2,1,0:T(1,128)S(1)}, u32[]{:S(2)}, u32[]{:S(2)}) collective-permute-start(f32[8,1,32]{2,1,0:T(1,128)S(1)} %get-tuple-element.40), channel_id=1, source_target_pairs={{1,0},{2,1},{3,2},{5,4},{6,5},{7,6},{9,8},{10,9},{11,10},{13,12},{... | collective-permute-start | bytes 3080 | tf_op jit(solution)/shard_map/ppermute | solution.py:28
  193.2 8.7 %collective-permute-start.4 = (f32[1,4,32]{2,1,0:T(4,128)S(1)}, f32[1,4,32]{2,1,0:T(4,128)S(1)}, u32[]{:S(2)}, u32[]{:S(2)}) collective-permute-start(f32[1,4,32]{2,1,0:T(4,128)S(1)} %get-tuple-element.41), channel_id=1, source_target_pairs={{0,4},{4,8},{8,12},{12,16},{16,20},{20,24},{24,28},{28,32},{32,36}... | collective-permute-start | bytes 1544 | tf_op jit(solution)/shard_map/ppermute | solution.py:27
  199.1 4.9 %collective-permute-start.5 = (f32[1,4,32]{2,1,0:T(4,128)S(1)}, f32[1,4,32]{2,1,0:T(4,128)S(1)}, u32[]{:S(2)}, u32[]{:S(2)}) collective-permute-start(f32[1,4,32]{2,1,0:T(4,128)S(1)} %get-tuple-element.42), channel_id=1, source_target_pairs={{4,0},{8,4},{12,8},{16,12},{20,16},{24,20},{28,24},{32,28},{36,32}... | collective-permute-start | bytes 1544 | tf_op jit(solution)/shard_map/ppermute | solution.py:28
  241.8 14.5 %collective-permute-start.10 = (f32[8,1,32]{2,1,0:T(1,128)S(1)}, f32[8,1,32]{2,1,0:T(1,128)S(1)}, u32[]{:S(2)}, u32[]{:S(2)}) collective-permute-start(f32[8,1,32]{2,1,0:T(1,128)S(1)} %get-tuple-element.35), channel_id=1, source_target_pairs={{0,1},{1,2},{2,3},{4,5},{5,6},{6,7},{8,9},{9,10},{10,11},{12,13},{... | collective-permute-start | bytes 3080 | tf_op jit(solution)/shard_map/ppermute | solution.py:27
  243.9 12.4 %collective-permute-start.11 = (f32[8,1,32]{2,1,0:T(1,128)S(1)}, f32[8,1,32]{2,1,0:T(1,128)S(1)}, u32[]{:S(2)}, u32[]{:S(2)}) collective-permute-start(f32[8,1,32]{2,1,0:T(1,128)S(1)} %get-tuple-element.36), channel_id=1, source_target_pairs={{1,0},{2,1},{3,2},{5,4},{6,5},{7,6},{9,8},{10,9},{11,10},{13,12},{... | collective-permute-start | bytes 3080 | tf_op jit(solution)/shard_map/ppermute | solution.py:28
  245.3 9.0 %collective-permute-start.8 = (f32[1,4,32]{2,1,0:T(4,128)S(1)}, f32[1,4,32]{2,1,0:T(4,128)S(1)}, u32[]{:S(2)}, u32[]{:S(2)}) collective-permute-start(f32[1,4,32]{2,1,0:T(4,128)S(1)} %get-tuple-element.37), channel_id=1, source_target_pairs={{0,4},{4,8},{8,12},{12,16},{16,20},{20,24},{24,28},{28,32},{32,36}... | collective-permute-start | bytes 1544 | tf_op jit(solution)/shard_map/ppermute | solution.py:27
  251.4 4.9 %collective-permute-start.9 = (f32[1,4,32]{2,1,0:T(4,128)S(1)}, f32[1,4,32]{2,1,0:T(4,128)S(1)}, u32[]{:S(2)}, u32[]{:S(2)}) collective-permute-start(f32[1,4,32]{2,1,0:T(4,128)S(1)} %get-tuple-element.38), channel_id=1, source_target_pairs={{4,0},{8,4},{12,8},{16,12},{20,16},{24,20},{28,24},{32,28},{36,32}... | collective-permute-start | bytes 1544 | tf_op jit(solution)/shard_map/ppermute | solution.py:28
where the time goes:
time: 296 us; the launch traced here: 294 us
  blocking collectives  92.7 us (31%)
  matrix products  65.4 us (22%)
  starting transfers between devices  52 us (18%)
  waiting for transfers between devices  36.2 us (12%)
  local copies, waits for them, and re-layouts  30.5 us (10%)
  between operations  10.9 us (4%)
  other arithmetic  6.18 us (2%)
    psum x12, blocking collectives, by_axis(): return functools.reduce(lax.psum, axes, x)  92.7 us
    all_to_all x1, waiting for transfers between devices, shards(): lax.all_to_all(sending, GX_GY, split_axis=1, concat_axis=1, tiled=True)  30.3 us
    dot_general x1, matrix products, shards(): jnp.einsum('ibd,bcd->ibc', blocks, choose, preferred_element_type=jnp.flo...  25.1 us
    dot_general x1, matrix products, shards(): jnp.einsum('bd,bcd->bc', target_blocks, choose, preferred_element_type=jn...  23.9 us
    ppermute x6, starting transfers between devices, with_halo(): lax.ppermute(last, axis, up)  20.5 us
    all_to_all x1, starting transfers between devices, shards(): lax.all_to_all(target_rows, GX_GY, split_axis=1, concat_axis=1, tiled=True)  11.5 us
    all_to_all x1, starting transfers between devices, shards(): lax.all_to_all(sending, GX_GY, split_axis=1, concat_axis=1, tiled=True)  10.2 us
    ppermute x6, starting transfers between devices, with_halo(): lax.ppermute(leading, axis, [(b, a) for a, b in up])  9.82 us
  transfers between devices with their start and end apart: 14, of which 4 were waited for; matrix products, arithmetic and copies ran while one was open for 15% of the time, Pallas kernels for 0%

commit v1 on v0

v1 whole, which is shorter than its diff:
```python
import functools

import jax
import jax.numpy as jnp
from jax import lax
from jax.experimental import pallas as pl
from jax.experimental.pallas import tpu as pltpu
from jax.sharding import Mesh
from jax.sharding import PartitionSpec as P

BX = 8
BY = 4
ITERS = 3
SLOTS = 8
LANES = 128
GX_GY = ("gx_0", "gx_1", "gx_2", "gy")
GX = ("gx_0", "gx_1", "gx_2")
HIGHEST = lax.Precision.HIGHEST


coupling_weight = 1.0


def pack_kernel(lists_ref, feats_ref, targets_ref, out_ref, mask_ref):
    rows = mask_ref.shape[0]
    width = LANES * SLOTS

    @pl.when(pl.program_id(0) == 0)
    def _():
        lane = lax.broadcasted_iota(jnp.int32, (SLOTS, LANES), 1)
        codes = []
        for block in range(rows):
            chosen = lists_ref[:, block * LANES : (block + 1) * LANES]
            offset = chosen - (lane + block * LANES) * SLOTS
            bits = jnp.where(chosen >= 0, lax.shift_left(1, jnp.clip(offset, 0, SLOTS - 1)), 0)
            codes.append(jnp.sum(bits, axis=0, keepdims=True))
        code = jnp.concatenate(codes, axis=0).astype(jnp.float32).astype(jnp.bfloat16)
        brick = lax.broadcasted_iota(jnp.int32, (LANES, width), 0)
        point = lax.broadcasted_iota(jnp.int32, (LANES, width), 1)
        spread = (lax.shift_right_logical(point, 3) == brick).astype(jnp.float32).astype(jnp.bfloat16)
        wide = jnp.dot(code, spread, preferred_element_type=jnp.float32).astype(jnp.int32)
        slot = lax.broadcasted_iota(jnp.int32, (rows, width), 1) & (SLOTS - 1)
        mask_ref[...] = (lax.shift_right_logical(wide, slot) & 1).astype(jnp.float32)

    step = pl.program_id(0)
    dests = out_ref.shape[0]
    feat_count = feats_ref.shape[0]
    for part in range(dests * 256 // width):
        row = mask_ref[pl.ds(step * (dests * 256 // width) + part, 1), :].astype(jnp.bfloat16)
        masked = feats_ref[:, part * width : (part + 1) * width] * row
        for piece in range(width // LANES):
            dest = (part * width + piece * LANES) // 256
            half = piece % 2
            out_ref[dest, half * feat_count : (half + 1) * feat_count, :] = masked[
                :, piece * LANES : (piece + 1) * LANES
            ]
    for dest in range(dests):
        out_ref[dest, 2 * feat_count : 2 * feat_count + 2, :] = targets_ref[2 * dest : 2 * dest + 2, :]


def pack(point_feats, point_targets, point_lists, devices):
    feat_count, points = point_feats.shape
    bricks = point_lists.shape[0]
    steps = 8
    dests = devices // steps
    return pl.pallas_call(
        pack_kernel,
        grid=(steps,),
        in_specs=[
            pl.BlockSpec((SLOTS, bricks), lambda i: (0, 0)),
            pl.BlockSpec((feat_count, points // steps), lambda i: (0, i)),
            pl.BlockSpec((points // steps // LANES, LANES), lambda i: (i, 0)),
        ],
        out_specs=pl.BlockSpec((dests, 2 * feat_count + 2, LANES), lambda i: (i, 0, 0)),
        out_shape=jax.ShapeDtypeStruct((devices, 2 * feat_count + 2, LANES), jnp.bfloat16),
        scratch_shapes=[pltpu.VMEM((bricks // LANES, LANES * SLOTS), jnp.float32)],
        name="pack",
    )(point_lists.T, point_feats, point_targets.reshape(points // LANES, LANES))


def with_halo(x, sides, width):
    edges = {}
    for axis, dim in sides:
        devices, length = (lax.axis_size(axis), x.shape[dim])
        up = [(i, (i + 1) % devices) for i in range(devices - 1)]
        last = lax.slice_in_dim(x, length - width, length, axis=dim)
        leading = lax.slice_in_dim(x, 0, width, axis=dim)
        edges[dim] = (
            lax.ppermute(last, axis, up),
            lax.ppermute(leading, axis, [(b, a) for a, b in up]),
        )
    done = []
    for _, dim in sides:
        low, high = edges[dim]
        around = [(width, width) if d in done else (0, 0) for d in range(x.ndim)]
        x = jnp.concatenate([jnp.pad(low, around), x, jnp.pad(high, around)], axis=dim)
        done.append(dim)
    return x


def neighbour_sum(padded, mask):
    total = mask[..., 0:1] * padded[:-2, 1:-1] + mask[..., 1:2] * padded[2:, 1:-1]
    return total + mask[..., 2:3] * padded[1:-1, :-2] + mask[..., 3:4] * padded[1:-1, 2:]


def everyone(values, devices):
    spread = jnp.broadcast_to(values[None, :], (devices, values.shape[0]))
    return lax.all_to_all(spread, GX_GY, split_axis=0, concat_axis=0, tiled=True)


def krylov_coefficients(basis, devices):
    peaks = [jnp.max(jnp.abs(v)) for v in basis]
    inverse = [jnp.where(p > 1e-37, 1.0 / p, 0.0) for p in peaks]
    scaled = [v * s for v, s in zip(basis, inverse)]
    pairs = [(a, b) for a in range(4) for b in range(a, 4)]
    local = jnp.stack([jnp.sum(scaled[a] * scaled[b]) for a, b in pairs] + peaks)
    shared = everyone(local, devices)
    peak = jnp.max(shared[:, 10:14], axis=0)
    weight = shared[:, 10:14] / peak[None, :]
    gram = [[None] * 4 for _ in range(4)]
    for column, (a, b) in enumerate(pairs):
        value = jnp.sum(shared[:, column] * weight[:, a] * weight[:, b])
        gram[a][b] = gram[b][a] = value
    growth = [peak[k + 1] / peak[k] for k in range(3)]

    def product(left, right):
        total = 0.0
        for a in range(4):
            for b in range(4):
                if left[a] is not None and right[b] is not None:
                    total = total + left[a] * right[b] * gram[a][b]
        return total

    def plus(left, scale, right):
        out = []
        for a, b in zip(left, right):
            out.append(a if b is None else scale * b if a is None else a + scale * b)
        return out

    def image(vector):
        return [None] + [None if vector[k] is None else vector[k] * growth[k] for k in range(3)]

    one = jnp.float32(1.0)
    solution = [None] * 4
    residual = [one, None, None, None]
    direction = list(residual)
    norm_now = product(residual, residual)
    for iteration in range(ITERS):
        carried = image(direction)
        alpha = norm_now / product(direction, carried)
        solution = plus(solution, alpha, direction)
        residual = plus(residual, -alpha, carried)
        if iteration + 1 < ITERS:
            norm_next = product(residual, residual)
            direction = plus(residual, norm_next / norm_now, direction)
            norm_now = norm_next
    zero = jnp.float32(0.0)
    back = [peak[0] / peak[k] for k in range(4)]
    return [[zero if c is None else c * back[k] for k, c in enumerate(cs)] for cs in (solution, residual)]


def shards(point_feats, point_targets, point_lists, brick_adjacency, voxel_feats, voxel_reg):
    feat_count = point_feats.shape[0]
    brick_total, slots = point_lists.shape
    local_bricks = voxel_feats.shape[0]
    devices = brick_total // local_bricks
    sending = pack(point_feats, point_targets, point_lists, devices)
    got = lax.all_to_all(sending, GX_GY, split_axis=0, concat_axis=0, tiled=True)
    got_feats = got[:, : 2 * feat_count].reshape(devices, 2, feat_count, local_bricks // 2, slots)
    got_targets = got[:, 2 * feat_count :].reshape(devices, 2, local_bricks // 2, slots)
    moments = jnp.einsum(
        "shibc,shjbc->hbij", got_feats, got_feats, preferred_element_type=jnp.float32
    ).reshape(local_bricks, feat_count, feat_count)
    gathered = jnp.einsum(
        "shbc,shibc->hbi", got_targets, got_feats, preferred_element_type=jnp.float32
    ).reshape(local_bricks, feat_count)
    mask = (brick_adjacency >= 0).astype(jnp.float32).reshape(BX, BY, 4)
    degree = jnp.sum(mask, axis=-1, keepdims=True)

    weighted = voxel_feats
    grams = []
    for power in range(ITERS):
        grams.append(jnp.einsum("bik,bjk->bij", weighted, voxel_feats, precision=HIGHEST))
        weighted = weighted * voxel_reg[:, None, :]

    def apply(matrix, vector):
        return jnp.sum(matrix * vector[:, None, :], axis=-1)

    chain = [gathered]
    for step in range(ITERS):
        projected = sum(apply(grams[a], chain[step - a]) for a in range(step + 1))
        lattice = projected.reshape(BX, BY, feat_count)
        padded = with_halo(lattice, ((GX, 0), ("gy", 1)), 1)
        coupled = (degree * lattice - neighbour_sum(padded, mask)).reshape(local_bricks, feat_count)
        chain.append(apply(moments, projected) + coupling_weight * coupled)
    basis = []
    for step, values in enumerate(chain):
        vector = jnp.sum(voxel_feats * values[:, :, None], axis=1)
        if step:
            vector = vector + voxel_reg * basis[-1]
        basis.append(vector)
    in_solution, in_residual = krylov_coefficients(basis, devices)
    return (
        sum(c * v for c, v in zip(in_solution, basis)),
        sum(c * v for c, v in zip(in_residual, basis)),
    )


def solution(mesh):
    torus = Mesh(mesh.devices.reshape(4, 4, 2, mesh.shape["gy"]), ("gx_0", "gx_1", "gx_2", "gy"))
    return jax.shard_map(
        shards,
        mesh=torus,
        in_specs=(
            P(None, GX_GY),
            P(GX_GY),
            P(GX_GY, None),
            P(GX_GY, None),
            P(GX_GY, None, None),
            P(GX_GY, None),
        ),
        out_specs=(P(GX_GY, None), P(GX_GY, None)),
        check_vma=False,
    )
```

time: 296 us -> 176 us (0.59)
  blocking collectives: 92.7 us -> 22.5 us
  matrix products: 65.4 us -> 11.2 us
  between operations: 10.9 us -> 30.8 us
  local copies, waits for them, and re-layouts: 30.5 us -> 17.9 us
  starting transfers between devices: 52 us -> 40.1 us
  Pallas kernels: 0 us -> 6.22 us
  waiting for transfers between devices: 36.2 us -> 40.2 us
    psum x12 -> x0, blocking collectives: 92.7 us -> none  [by_axis(): return functools.reduce(lax.psum, axes, x)]
    dot_general x14 -> x5, matrix products: 65.4 us -> 11.2 us  [the longest x3 6.39 us: shards(): jnp.einsum('bik,bjk->bij', weighted, voxel_feats, precision=HIGHEST)]
    all_to_all x0 -> x1, blocking collectives: none -> 22.5 us  [everyone(): lax.all_to_all(spread, GX_GY, split_axis=0, concat_axis=0, tiled=True)]
    reshape x3 -> x0, local copies, waits for them, and re-layouts: 13.5 us -> none  [the longest x1 7.87 us: shards(): sending = picked.reshape(feat_count, devices, local_bricks * slots)]
    all_to_all x2 -> x1, starting transfers between devices: 21.7 us -> 11.5 us  [shards(): lax.all_to_all(sending, GX_GY, split_axis=0, concat_axis=0, tiled=True)]
    another operation x0 -> x1, local copies, waits for them, and re-layouts: none -> 8.85 us  [krylov_coefficients(): jnp.stack([jnp.sum(scaled[a] * scaled[b]) for a, b in pairs] + peaks)]
    slice x0 -> x7, local copies, waits for them, and re-layouts: none -> 8.57 us  [the longest x2 6.01 us: shards(): got[:, :2 * feat_count]]
    unnamed x18 -> x10, local copies, waits for them, and re-layouts: 8.65 us -> 0.21 us
  transfers between devices with their start and end apart: 14 -> 13, of which waited for: 4 -> 4; matrix products, arithmetic and copies ran while one was open for 15% -> 2% of each run, Pallas kernels for 0% -> 0%
where the time goes in v1:
time: 176 us; the launch traced here: 175 us
  waiting for transfers between devices  40.2 us (23%)
  starting transfers between devices  40.1 us (23%)
  between operations  30.8 us (18%)
  blocking collectives  22.5 us (13%)
  local copies, waits for them, and re-layouts  17.9 us (10%)
  matrix products  11.2 us (6%)
  other arithmetic  6.25 us (4%)
  Pallas kernels  6.22 us (4%)
    all_to_all x1, waiting for transfers between devices, shards(): lax.all_to_all(sending, GX_GY, split_axis=0, concat_axis=0, tiled=True)  33.6 us
    all_to_all x1, blocking collectives, everyone(): lax.all_to_all(spread, GX_GY, split_axis=0, concat_axis=0, tiled=True)  22.5 us
    ppermute x6, starting transfers between devices, with_halo(): lax.ppermute(last, axis, up)  19 us
    all_to_all x1, starting transfers between devices, shards(): lax.all_to_all(sending, GX_GY, split_axis=0, concat_axis=0, tiled=True)  11.5 us
    ppermute x6, starting transfers between devices, with_halo(): lax.ppermute(leading, axis, [(b, a) for a, b in up])  9.64 us
    another operation x1, local copies, waits for them, and re-layouts, krylov_coefficients(): jnp.stack([jnp.sum(scaled[a] * scaled[b]) for a, b in pairs] + peaks)  8.85 us
    ppermute x6, waiting for transfers between devices, with_halo(): lax.ppermute(leading, axis, [(b, a) for a, b in up])  6.6 us
    dot_general x3, matrix products, shards(): jnp.einsum('bik,bjk->bij', weighted, voxel_feats, precision=HIGHEST)  6.39 us
  transfers between devices with their start and end apart: 13, of which 4 were waited for; matrix products, arithmetic and copies ran while one was open for 2% of the time, Pallas kernels for 0%

profile of v1, /device:TPU:1, one launch (start us, length us, event | category | flops | bytes accessed | tf_op | source)
XLA Modules:
  0.0 175.2 jit_solution(2725749405907373259)
XLA Ops:
  0.6 6.2 %pack.1 = bf16[128,66,128]{2,1,0:T(8,128)(2,1)} custom-call(s32[8,4096]{1,0:T(8,128)} %bitcast.92, bf16[32,32768]{1,0:T(8,128)(2,1)} %feats_ref.1, bf16[256,128]{1,0:T(8,128)(2,1)} %bitcast.96), custom_call_target="tpu_custom_call" | custom-call | tf_op jit(solution)/shard_map/pack/pallas_call | solution.py:66
  6.8 0.0 copy-start.4
  6.9 11.5 %all-to-all-start = ((bf16[128,66,128]{2,1,0:T(8,128)(2,1)}), bf16[128,66,128]{2,1,0:T(8,128)(2,1)S(1)}, u32[]{:S(2)}, u32[]{:S(2)}) async-start(bf16[128,66,128]{2,1,0:T(8,128)(2,1)} %pack.1), calls=%async_computation | async-start | bytes 4718592 | tf_op jit(solution)/shard_map/all_to_all | solution.py:168
  18.4 0.0 copy-done.4
  18.4 0.1 mul.596
  18.5 0.1 reshape.150
  18.6 33.6 %all-to-all-done = bf16[128,66,128]{2,1,0:T(8,128)(2,1)S(1)} async-done(((bf16[128,66,128]{2,1,0:T(8,128)(2,1)}), bf16[128,66,128]{2,1,0:T(8,128)(2,1)S(1)}, u32[]{:S(2)}, u32[]{:S(2)}) %all-to-all-start) | async-done | bytes 2162720 | tf_op jit(solution)/shard_map/all_to_all | solution.py:168
  52.2 1.8 %slice.262 = bf16[128,64,128]{2,1,0:T(8,128)(2,1)} slice(bf16[128,66,128]{2,1,0:T(8,128)(2,1)S(1)} %all-to-all-done), slice={[0:128], [0:64], [0:128]} | slice | bytes 4194304 | tf_op jit(solution)/shard_map/slice | solution.py:169
  54.0 0.2 copy-done.1
  54.2 4.2 %copy.43 = bf16[128,64,128]{0,2,1:T(8,128)(2,1)} copy(bf16[128,64,128]{2,1,0:T(8,128)(2,1)} %slice.262) | data formatting | bytes 4194304 | tf_op jit(solution)/shard_map/slice | solution.py:169
  58.4 1.1 slice.261
  59.5 0.1 copy.42
  59.6 3.0 %fusion.3 = f32[2,16,1,32,1]{3,2,4,1,0:T(1,128)S(1)} fusion(bf16[128,2,32,16,8]{0,4,3,2,1:T(8,128)(2,1)} %bitcast.80, bf16[128,2,16,8,1]{0,3,2,1,4:T(8,128)(2,1)S(1)} %bitcast.97), kind=kOutput, calls=%fused_computation.8 | convolution fusion | flops 2097152 | bytes 2166784 | tf_op jit(solution)/shard_map/shbc,shibc->hbi/dot_general | solution.py:174
  62.7 0.0 copy-done
  62.7 1.9 %multiply_reduce_fusion.11 = (f32[32,32]{1,0:T(8,128)S(1)}, f32[32,32,32]{1,2,0:T(8,128)S(1)}) fusion(f32[32,32]{1,0:T(8,128)S(1)} %bitcast.82, f32[32,32,512]{2,1,0:T(8,128)S(1)} %copy-done), kind=kOutput, calls=%fused_computation.24 | convolution fusion | flops 201391104 | bytes 2236416 | tf_op jit(solution)/shard_map/bik,bjk->bij/dot_general | solution.py:183
  64.6 0.0 copy-done.2
  64.7 0.0 copy-start.3
  64.7 1.8 %multiply_reduce_fusion.10 = (f32[2,16,32]{2,1,0:T(8,128)S(1)}, f32[2,16,32,32]{2,3,1,0:T(8,128)S(1)}) fusion(f32[2,16,32]{2,1,0:T(8,128)S(1)} %bitcast.93, bf16[128,2,32,16,8]{0,4,3,2,1:T(8,128)(2,1)S(1)} %bitcast.81), kind=kOutput, calls=%fused_computation.23 | convolution fusion | flops 67173376 | bytes 2236416 | tf_op jit(solution)/shard_map/shibc,shjbc->hbij/dot_general | solution.py:171
  66.4 2.6 %collective-permute-start = (f32[1,4,32]{2,1,0:T(4,128)S(1)}, f32[1,4,32]{2,1,0:T(4,128)S(1)}, u32[]{:S(2)}, u32[]{:S(2)}) collective-permute-start(f32[1,4,32]{2,1,0:T(4,128)S(1)} %get-tuple-element.63), channel_id=1, source_target_pairs={{0,4},{4,8},{8,12},{12,16},{16,20},{20,24},{24,28},{28,32},{32,36}... | collective-permute-start | bytes 1544 | tf_op jit(solution)/shard_map/ppermute | solution.py:89
  69.0 1.9 %collective-permute-start.1 = (f32[1,4,32]{2,1,0:T(4,128)S(1)}, f32[1,4,32]{2,1,0:T(4,128)S(1)}, u32[]{:S(2)}, u32[]{:S(2)}) collective-permute-start(f32[1,4,32]{2,1,0:T(4,128)S(1)} %get-tuple-element.64), channel_id=1, source_target_pairs={{4,0},{8,4},{12,8},{16,12},{20,16},{24,20},{28,24},{32,28},{36,32}... | collective-permute-start | bytes 1544 | tf_op jit(solution)/shard_map/ppermute | solution.py:90
  71.0 2.2 %collective-permute-start.2 = (f32[8,1,32]{2,1,0:T(1,128)S(1)}, f32[8,1,32]{2,1,0:T(1,128)S(1)}, u32[]{:S(2)}, u32[]{:S(2)}) collective-permute-start(f32[8,1,32]{2,1,0:T(1,128)S(1)} %get-tuple-element.61), channel_id=1, source_target_pairs={{0,1},{1,2},{2,3},{4,5},{5,6},{6,7},{8,9},{9,10},{10,11},{12,13},{... | collective-permute-start | bytes 3080 | tf_op jit(solution)/shard_map/ppermute | solution.py:89
  73.2 1.3 collective-permute-start.3
  74.5 0.0 copy-done.3
  74.5 2.2 %fusion.11 = f32[32,32]{1,0:T(8,128)S(1)} fusion(f32[32,32,512]{2,1,0:T(8,128)S(1)} %copy-done, f32[32,512]{1,0:T(8,128)S(1)} %copy-done.3, f32[32,32]{1,0:T(8,128)S(1)} %bitcast.83), kind=kOutput, calls=%fused_computation.14 | convolution fusion | flops 202439680 | bytes 2170880 | tf_op jit(solution)/shard_map/bik,bjk->bij/dot_general | solution.py:183
  76.7 0.0 collective-permute-done
  76.7 0.0 collective-permute-done.1
  76.8 0.0 collective-permute-done.2
  76.8 1.0 collective-permute-done.3
  77.8 0.1 fusion.38
  77.9 2.2 %multiply_reduce_fusion.5 = (f32[32,32]{1,0:T(8,128)S(1)}, f32[32,32]{1,0:T(8,128)S(1)}, f32[32,32]{1,0:T(8,128)S(1)}) fusion(f32[32,32]{1,0:T(8,128)S(1)} %bitcast_add_fusion.2, f32[32,32]{1,0:T(8,128)S(1)} %bitcast.84, f32[32,32,32]{1,2,0:T(8,128)S(1)} %get-tuple-element.70, f32[32,32,512]{2,1,0:T(8,128)S(1)} %copy-done, f32[32,512]{1,0:T(8,128)S(1)} %copy-done.3), kind=kOutput, calls=%fused_computation.18 | convolution fusion | flops 202044416 | bytes 2314240 | tf_op jit(solution)/shard_map/bik,bjk->bij/dot_general | solution.py:183
  80.1 4.8 %collective-permute-start.4 = (f32[1,4,32]{2,1,0:T(4,128)S(1)}, f32[1,4,32]{2,1,0:T(4,128)S(1)}, u32[]{:S(2)}, u32[]{:S(2)}) collective-permute-start(f32[1,4,32]{2,1,0:T(4,128)S(1)} %get-tuple-element.55), channel_id=1, source_target_pairs={{0,4},{4,8},{8,12},{12,16},{16,20},{20,24},{24,28},{28,32},{32,36}... | collective-permute-start | bytes 1544 | tf_op jit(solution)/shard_map/ppermute | solution.py:89
  85.0 1.9 %collective-permute-start.5 = (f32[1,4,32]{2,1,0:T(4,128)S(1)}, f32[1,4,32]{2,1,0:T(4,128)S(1)}, u32[]{:S(2)}, u32[]{:S(2)}) collective-permute-start(f32[1,4,32]{2,1,0:T(4,128)S(1)} %get-tuple-element.56), channel_id=1, source_target_pairs={{4,0},{8,4},{12,8},{16,12},{20,16},{24,20},{28,24},{32,28},{36,32}... | collective-permute-start | bytes 1544 | tf_op jit(solution)/shard_map/ppermute | solution.py:90
  86.9 2.5 %collective-permute-start.6 = (f32[8,1,32]{2,1,0:T(1,128)S(1)}, f32[8,1,32]{2,1,0:T(1,128)S(1)}, u32[]{:S(2)}, u32[]{:S(2)}) collective-permute-start(f32[8,1,32]{2,1,0:T(1,128)S(1)} %get-tuple-element.53), channel_id=1, source_target_pairs={{0,1},{1,2},{2,3},{4,5},{5,6},{6,7},{8,9},{9,10},{10,11},{12,13},{... | collective-permute-start | bytes 3080 | tf_op jit(solution)/shard_map/ppermute | solution.py:89
  89.5 1.3 collective-permute-start.7
  90.8 0.2 multiply_reduce_fusion.7
  91.0 0.0 collective-permute-done.4
  91.0 0.0 collective-permute-done.5
  91.0 0.0 collective-permute-done.6
  91.0 2.8 %collective-permute-done.7 = f32[8,1,32]{2,1,0:T(1,128)S(1)} collective-permute-done((f32[8,1,32]{2,1,0:T(1,128)S(1)}, f32[8,1,32]{2,1,0:T(1,128)S(1)}, u32[]{:S(2)}, u32[]{:S(2)}) %collective-permute-start.7) | collective-permute-done | bytes 1056 | tf_op jit(solution)/shard_map/ppermute | solution.py:90
  93.8 0.1 fusion.28
  93.9 0.2 multiply_reduce_fusion.6
  94.2 5.1 %collective-permute-start.8 = (f32[1,4,32]{2,1,0:T(4,128)S(1)}, f32[1,4,32]{2,1,0:T(4,128)S(1)}, u32[]{:S(2)}, u32[]{:S(2)}) collective-permute-start(f32[1,4,32]{2,1,0:T(4,128)S(1)} %get-tuple-element.51), channel_id=1, source_target_pairs={{0,4},{4,8},{8,12},{12,16},{16,20},{20,24},{24,28},{28,32},{32,36}... | collective-permute-start | bytes 1544 | tf_op jit(solution)/shard_map/ppermute | solution.py:89
  99.3 1.9 %collective-permute-start.9 = (f32[1,4,32]{2,1,0:T(4,128)S(1)}, f32[1,4,32]{2,1,0:T(4,128)S(1)}, u32[]{:S(2)}, u32[]{:S(2)}) collective-permute-start(f32[1,4,32]{2,1,0:T(4,128)S(1)} %get-tuple-element.52), channel_id=1, source_target_pairs={{4,0},{8,4},{12,8},{16,12},{20,16},{24,20},{28,24},{32,28},{36,32}... | collective-permute-start | bytes 1544 | tf_op jit(solution)/shard_map/ppermute | solution.py:90
  101.2 1.7 collective-permute-start.10
  103.0 1.3 collective-permute-start.11
  104.3 0.2 multiply_reduce_fusion.4
  104.5 0.0 collective-permute-done.8
  104.5 0.0 collective-permute-done.9
  104.5 0.0 collective-permute-done.10
  104.5 2.8 %collective-permute-done.11 = f32[8,1,32]{2,1,0:T(1,128)S(1)} collective-permute-done((f32[8,1,32]{2,1,0:T(1,128)S(1)}, f32[8,1,32]{2,1,0:T(1,128)S(1)}, u32[]{:S(2)}, u32[]{:S(2)}) %collective-permute-start.11) | collective-permute-done | bytes 1056 | tf_op jit(solution)/shard_map/ppermute | solution.py:90
  107.3 0.1 fusion.18
  107.5 1.6 multiply_reduce_fusion.3
  109.0 0.6 abs_reduce_fusion.1
  112.3 0.7 abs_reduce_fusion
  115.6 0.7 multiply_reduce_fusion.12
  116.4 8.9 %stack.59 = f32[14]{0:T(128)S(1)} concatenate(f32[1]{0:T(128)} %bitcast.8, f32[1]{0:T(128)} %bitcast.23, f32[1]{0:T(128)} %bitcast.30, f32[1]{0:T(128)} %bitcast.37, f32[1]{0:T(128)} %bitcast.38, f32[1]{0:T(128)} %bitcast.39, f32[1]{0:T(128)} %bitcast.40, f32[1]{0:T(128)} %bitcast.41, f32[1]{0:T(128)} %bitcast.42, f32[1]{0:T(128)} %bitcast.43, f32[1]{0:T(128)} %bitcast.44, ...), dimensions={0} | concatenate | bytes 112 | tf_op jit(solution)/shard_map/stack | solution.py:116
  125.3 22.5 %all_to_all.14 = f32[128,1,14]{2,1,0:T(1,128)S(1)} all-to-all(f32[128,1,14]{2,1,0:T(1,128)S(1)} %broadcast_in_dim.2), channel_id=1, replica_groups=mesh['gx_0'=4,'gx_1'=4,'gx_2'=2,'gy'=4] {'gx_0','gx_1','gx_2','gy'}, dimensions={0} | all-to-all | bytes 14336 | tf_op jit(solution)/shard_map/all_to_all | solution.py:108
  147.8 0.1 slice_reduce_fusion.13
  147.9 0.7 fusion.52
  157.3 0.4 slice_reduce_fusion
  157.8 0.1 slice_divide_fusion
  157.9 0.2 slice_reduce_fusion.2
  158.1 0.7 multiply_reduce_fusion.22
  174.5 0.7 multiply_add_fusion
  (18 shorter events, 0.1 us)
Async XLA Ops:
  6.8 11.5 %copy-start.4 = (s32[32,4]{0,1:T(4,128)S(1)}, s32[32,4]{0,1:T(4,128)}, u32[]{:S(2)}) copy-start(s32[32,4]{0,1:T(4,128)} %param.9) | copy-start | bytes 1540
  6.9 45.3 %all-to-all-start = ((bf16[128,66,128]{2,1,0:T(8,128)(2,1)}), bf16[128,66,128]{2,1,0:T(8,128)(2,1)S(1)}, u32[]{:S(2)}, u32[]{:S(2)}) async-start(bf16[128,66,128]{2,1,0:T(8,128)(2,1)} %pack.1), calls=%async_computation | async-start | bytes 4718592 | tf_op jit(solution)/shard_map/all_to_all | solution.py:168
  52.2 2.0 %copy-start.1 = (bf16[128,66,128]{2,1,0:T(8,128)(2,1)}, bf16[128,66,128]{2,1,0:T(8,128)(2,1)S(1)}, u32[]{:S(2)}) copy-start(bf16[128,66,128]{2,1,0:T(8,128)(2,1)S(1)} %all-to-all-done) | copy-start | bytes 6488068
  58.4 4.3 %copy-start = (f32[32,32,512]{2,1,0:T(8,128)S(1)}, f32[32,32,512]{2,1,0:T(8,128)}, u32[]{:S(2)}) copy-start(f32[32,32,512]{2,1,0:T(8,128)} %param.10) | copy-start | bytes 6291460
  62.7 2.0 %copy-start.2 = (bf16[128,64,128]{0,2,1:T(8,128)(2,1)S(1)}, bf16[128,64,128]{0,2,1:T(8,128)(2,1)}, u32[]{:S(2)}) copy-start(bf16[128,64,128]{0,2,1:T(8,128)(2,1)} %copy.43) | copy-start | bytes 6291460
  64.7 9.8 %copy-start.3 = (f32[32,512]{1,0:T(8,128)S(1)}, f32[32,512]{1,0:T(8,128)}, u32[]{:S(2)}) copy-start(f32[32,512]{1,0:T(8,128)} %param.11) | copy-start | bytes 196612
  66.4 10.3 %collective-permute-start = (f32[1,4,32]{2,1,0:T(4,128)S(1)}, f32[1,4,32]{2,1,0:T(4,128)S(1)}, u32[]{:S(2)}, u32[]{:S(2)}) collective-permute-start(f32[1,4,32]{2,1,0:T(4,128)S(1)} %get-tuple-element.63), channel_id=1, source_target_pairs={{0,4},{4,8},{8,12},{12,16},{16,20},{20,24},{24,28},{28,32},{32,36}... | collective-permute-start | bytes 1544 | tf_op jit(solution)/shard_map/ppermute | solution.py:89
  69.0 7.7 %collective-permute-start.1 = (f32[1,4,32]{2,1,0:T(4,128)S(1)}, f32[1,4,32]{2,1,0:T(4,128)S(1)}, u32[]{:S(2)}, u32[]{:S(2)}) collective-permute-start(f32[1,4,32]{2,1,0:T(4,128)S(1)} %get-tuple-element.64), channel_id=1, source_target_pairs={{4,0},{8,4},{12,8},{16,12},{20,16},{24,20},{28,24},{32,28},{36,32}... | collective-permute-start | bytes 1544 | tf_op jit(solution)/shard_map/ppermute | solution.py:90
  71.0 5.8 %collective-permute-start.2 = (f32[8,1,32]{2,1,0:T(1,128)S(1)}, f32[8,1,32]{2,1,0:T(1,128)S(1)}, u32[]{:S(2)}, u32[]{:S(2)}) collective-permute-start(f32[8,1,32]{2,1,0:T(1,128)S(1)} %get-tuple-element.61), channel_id=1, source_target_pairs={{0,1},{1,2},{2,3},{4,5},{5,6},{6,7},{8,9},{9,10},{10,11},{12,13},{... | collective-permute-start | bytes 3080 | tf_op jit(solution)/shard_map/ppermute | solution.py:89
  73.2 4.6 %collective-permute-start.3 = (f32[8,1,32]{2,1,0:T(1,128)S(1)}, f32[8,1,32]{2,1,0:T(1,128)S(1)}, u32[]{:S(2)}, u32[]{:S(2)}) collective-permute-start(f32[8,1,32]{2,1,0:T(1,128)S(1)} %get-tuple-element.62), channel_id=1, source_target_pairs={{1,0},{2,1},{3,2},{5,4},{6,5},{7,6},{9,8},{10,9},{11,10},{13,12},{... | collective-permute-start | bytes 3080 | tf_op jit(solution)/shard_map/ppermute | solution.py:90
  80.1 10.9 %collective-permute-start.4 = (f32[1,4,32]{2,1,0:T(4,128)S(1)}, f32[1,4,32]{2,1,0:T(4,128)S(1)}, u32[]{:S(2)}, u32[]{:S(2)}) collective-permute-start(f32[1,4,32]{2,1,0:T(4,128)S(1)} %get-tuple-element.55), channel_id=1, source_target_pairs={{0,4},{4,8},{8,12},{12,16},{16,20},{20,24},{24,28},{28,32},{32,36}... | collective-permute-start | bytes 1544 | tf_op jit(solution)/shard_map/ppermute | solution.py:89
  85.0 6.0 %collective-permute-start.5 = (f32[1,4,32]{2,1,0:T(4,128)S(1)}, f32[1,4,32]{2,1,0:T(4,128)S(1)}, u32[]{:S(2)}, u32[]{:S(2)}) collective-permute-start(f32[1,4,32]{2,1,0:T(4,128)S(1)} %get-tuple-element.56), channel_id=1, source_target_pairs={{4,0},{8,4},{12,8},{16,12},{20,16},{24,20},{28,24},{32,28},{36,32}... | collective-permute-start | bytes 1544 | tf_op jit(solution)/shard_map/ppermute | solution.py:90
  86.9 4.1 %collective-permute-start.6 = (f32[8,1,32]{2,1,0:T(1,128)S(1)}, f32[8,1,32]{2,1,0:T(1,128)S(1)}, u32[]{:S(2)}, u32[]{:S(2)}) collective-permute-start(f32[8,1,32]{2,1,0:T(1,128)S(1)} %get-tuple-element.53), channel_id=1, source_target_pairs={{0,1},{1,2},{2,3},{4,5},{5,6},{6,7},{8,9},{9,10},{10,11},{12,13},{... | collective-permute-start | bytes 3080 | tf_op jit(solution)/shard_map/ppermute | solution.py:89
  89.5 4.4 %collective-permute-start.7 = (f32[8,1,32]{2,1,0:T(1,128)S(1)}, f32[8,1,32]{2,1,0:T(1,128)S(1)}, u32[]{:S(2)}, u32[]{:S(2)}) collective-permute-start(f32[8,1,32]{2,1,0:T(1,128)S(1)} %get-tuple-element.54), channel_id=1, source_target_pairs={{1,0},{2,1},{3,2},{5,4},{6,5},{7,6},{9,8},{10,9},{11,10},{13,12},{... | collective-permute-start | bytes 3080 | tf_op jit(solution)/shard_map/ppermute | solution.py:90
  94.2 10.3 %collective-permute-start.8 = (f32[1,4,32]{2,1,0:T(4,128)S(1)}, f32[1,4,32]{2,1,0:T(4,128)S(1)}, u32[]{:S(2)}, u32[]{:S(2)}) collective-permute-start(f32[1,4,32]{2,1,0:T(4,128)S(1)} %get-tuple-element.51), channel_id=1, source_target_pairs={{0,4},{4,8},{8,12},{12,16},{16,20},{20,24},{24,28},{28,32},{32,36}... | collective-permute-start | bytes 1544 | tf_op jit(solution)/shard_map/ppermute | solution.py:89
  99.3 5.2 %collective-permute-start.9 = (f32[1,4,32]{2,1,0:T(4,128)S(1)}, f32[1,4,32]{2,1,0:T(4,128)S(1)}, u32[]{:S(2)}, u32[]{:S(2)}) collective-permute-start(f32[1,4,32]{2,1,0:T(4,128)S(1)} %get-tuple-element.52), channel_id=1, source_target_pairs={{4,0},{8,4},{12,8},{16,12},{20,16},{24,20},{28,24},{32,28},{36,32}... | collective-permute-start | bytes 1544 | tf_op jit(solution)/shard_map/ppermute | solution.py:90
  101.2 3.3 %collective-permute-start.10 = (f32[8,1,32]{2,1,0:T(1,128)S(1)}, f32[8,1,32]{2,1,0:T(1,128)S(1)}, u32[]{:S(2)}, u32[]{:S(2)}) collective-permute-start(f32[8,1,32]{2,1,0:T(1,128)S(1)} %get-tuple-element.49), channel_id=1, source_target_pairs={{0,1},{1,2},{2,3},{4,5},{5,6},{6,7},{8,9},{9,10},{10,11},{12,13},{... | collective-permute-start | bytes 3080 | tf_op jit(solution)/shard_map/ppermute | solution.py:89
  103.0 4.4 %collective-permute-start.11 = (f32[8,1,32]{2,1,0:T(1,128)S(1)}, f32[8,1,32]{2,1,0:T(1,128)S(1)}, u32[]{:S(2)}, u32[]{:S(2)}) collective-permute-start(f32[8,1,32]{2,1,0:T(1,128)S(1)} %get-tuple-element.50), channel_id=1, source_target_pairs={{1,0},{2,1},{3,2},{5,4},{6,5},{7,6},{9,8},{10,9},{11,10},{13,12},{... | collective-permute-start | bytes 3080 | tf_op jit(solution)/shard_map/ppermute | solution.py:90

commit v2 on v1

v2 whole, which is shorter than its diff:
```python
import functools

import jax
import jax.numpy as jnp
from jax import lax
from jax.experimental import pallas as pl
from jax.experimental.pallas import tpu as pltpu
from jax.sharding import Mesh
from jax.sharding import PartitionSpec as P

BX = 8
BY = 4
ITERS = 3
SLOTS = 8
LANES = 128
FEAT = 32
PITCH = 16
SPAN = 256
REACH = 3
GX_GY = ("gx_0", "gx_1", "gx_2", "gy")
GX = ("gx_0", "gx_1", "gx_2")
HIGHEST = lax.Precision.HIGHEST
PAIRS = tuple((a, b) for a in range(4) for b in range(a, 4))


coupling_weight = 1.0

EARLY = ((8, 2), (8, 1), (1, 2))
LATE = ((8, 2), (1, 3))


def padded(rows):
    return (rows + 7) // 8 * 8


def along_rows(section):
    return padded(section[0] * section[1] * BY)


def across_rows(section):
    rows, depth = section
    return padded(rows * sum(BX + 2 * (depth - k) for k in range(1, depth + 1)))


def message_rows(sections, size):
    return sum(size(section) for section in sections)


def piece(ref, start, rows, index):
    if rows == 8 and len(ref.shape) == 3:
        return ref[index]
    return ref[start + rows * index : start + rows * (index + 1), :]


def brick_at(own, low, high, start, section, a, e):
    rows, depth = section
    if a < 0:
        return piece(low, start, rows, (a + depth) * BY + e)
    if a >= BX:
        return piece(high, start, rows, (a - BX) * BY + e)
    return piece(own, 0, rows, a * BY + e)


def fill_across(sections, owns, low, high, to_low, to_high):
    source = target = 0
    for section, own in zip(sections, owns):
        rows, depth = section
        index = 0
        for away in range(1, depth + 1):
            extra = depth - away
            for a in range(-extra, BX + extra):
                place = slice(target + rows * index, target + rows * (index + 1))
                to_low[place, :] = brick_at(own, low, high, source, section, a, away - 1)
                to_high[place, :] = brick_at(own, low, high, source, section, a, BY - away)
                index += 1
        used, whole = rows * index, across_rows(section)
        if used < whole:
            blank = jnp.zeros((whole - used, LANES), jnp.float32)
            to_low[target + used : target + whole, :] = blank
            to_high[target + used : target + whole, :] = blank
        source += along_rows(section)
        target += whole


def place_bricks(put, sections, which, own, along_low, along_high, across_low, across_high):
    section = sections[which]
    rows, depth = section
    start = message_rows(sections[:which], along_rows)
    for a in range(-depth, BX + depth):
        for e in range(BY):
            put(a, e, brick_at(own, along_low, along_high, start, section, a, e))
    start = message_rows(sections[:which], across_rows)
    index = 0
    for away in range(1, depth + 1):
        extra = depth - away
        for a in range(-extra, BX + extra):
            put(a, -away, piece(across_low, start, rows, index))
            put(a, BY - 1 + away, piece(across_high, start, rows, index))
            index += 1


def lane_of(a, e):
    return (a + REACH) * PITCH + e + REACH


def to_lanes(records, lanes_ref):
    for t in range(8):
        lanes_ref[t * LANES : (t + 1) * LANES, :] = records[:, t, :].T


def times(matrix_ref, vector):
    total = None
    for t in range(8):
        for q in range(4):
            i = 8 * q + t
            row = t * LANES + q * FEAT
            term = matrix_ref[row : row + FEAT, :] * vector[i : i + 1, :]
            total = term if total is None else total + term
    return total


def pack_kernel(lists_ref, feats_ref, targets_ref, out_ref, mask_ref):
    rows = mask_ref.shape[0]
    width = LANES * SLOTS

    @pl.when(pl.program_id(0) == 0)
    def _():
        lane = lax.broadcasted_iota(jnp.int32, (SLOTS, LANES), 1)
        codes = []
        for block in range(rows):
            chosen = lists_ref[:, block * LANES : (block + 1) * LANES]
            offset = chosen - (lane + block * LANES) * SLOTS
            bits = jnp.where(chosen >= 0, lax.shift_left(1, jnp.clip(offset, 0, SLOTS - 1)), 0)
            codes.append(jnp.sum(bits, axis=0, keepdims=True))
        code = jnp.concatenate(codes, axis=0).astype(jnp.float32).astype(jnp.bfloat16)
        brick = lax.broadcasted_iota(jnp.int32, (LANES, width), 0)
        point = lax.broadcasted_iota(jnp.int32, (LANES, width), 1)
        spread = (lax.shift_right_logical(point, 3) == brick).astype(jnp.float32).astype(jnp.bfloat16)
        wide = jnp.dot(code, spread, preferred_element_type=jnp.float32).astype(jnp.int32)
        slot = lax.broadcasted_iota(jnp.int32, (rows, width), 1) & (SLOTS - 1)
        mask_ref[...] = (lax.shift_right_logical(wide, slot) & 1).astype(jnp.float32)

    step = pl.program_id(0)
    dests = out_ref.shape[0]
    feat_count = feats_ref.shape[0]
    for part in range(dests * 256 // width):
        row = mask_ref[pl.ds(step * (dests * 256 // width) + part, 1), :].astype(jnp.bfloat16)
        masked = feats_ref[:, part * width : (part + 1) * width] * row
        for half_block in range(width // LANES):
            dest = (part * width + half_block * LANES) // 256
            half = half_block % 2
            out_ref[dest, half * feat_count : (half + 1) * feat_count, :] = masked[
                :, half_block * LANES : (half_block + 1) * LANES
            ]
    for dest in range(dests):
        out_ref[dest, 2 * feat_count : 2 * feat_count + 2, :] = targets_ref[2 * dest : 2 * dest + 2, :]


def pack(point_feats, point_targets, point_lists, devices):
    feat_count, points = point_feats.shape
    bricks = point_lists.shape[0]
    steps = 8
    dests = devices // steps
    return pl.pallas_call(
        pack_kernel,
        grid=(steps,),
        in_specs=[
            pl.BlockSpec((SLOTS, bricks), lambda i: (0, 0)),
            pl.BlockSpec((feat_count, points // steps), lambda i: (0, i)),
            pl.BlockSpec((points // steps // LANES, LANES), lambda i: (i, 0)),
        ],
        out_specs=pl.BlockSpec((dests, 2 * feat_count + 2, LANES), lambda i: (i, 0, 0)),
        out_shape=jax.ShapeDtypeStruct((devices, 2 * feat_count + 2, LANES), jnp.bfloat16),
        scratch_shapes=[pltpu.VMEM((bricks // LANES, LANES * SLOTS), jnp.float32)],
        name="pack",
    )(point_lists.T, point_feats, point_targets.reshape(points // LANES, LANES))


def prepare_kernel(feats_ref, reg_ref, first_ref, second_ref, third_ref, lanes_ref):
    records = (first_ref, second_ref, third_ref)

    def one(b, carry):
        feats = feats_ref[b]
        reg = reg_ref[pl.ds(b, 1), :]
        once = feats * reg
        left = jnp.concatenate([feats, once, once * reg], axis=0)
        product = lax.dot_general(
            left,
            feats,
            (((1,), (1,)), ((), ())),
            precision=HIGHEST,
            preferred_element_type=jnp.float32,
        )
        for power, record in enumerate(records):
            rows = [product[power * FEAT + 8 * q : power * FEAT + 8 * q + 8, :] for q in range(4)]
            record[b] = jnp.concatenate(rows, axis=1)
        return carry

    lax.fori_loop(0, feats_ref.shape[0], one, 0)
    for power, record in enumerate(records):
        for t in range(8):
            block = jnp.concatenate([record[:, t, :], jnp.zeros((96, LANES), jnp.float32)], axis=0)
            lanes_ref[power, t * LANES : (t + 1) * LANES, :] = block.T


def prepare(voxel_feats, voxel_reg):
    bricks = voxel_feats.shape[0]
    record = jax.ShapeDtypeStruct((bricks, 8, LANES), jnp.float32)
    return pl.pallas_call(
        prepare_kernel,
        out_shape=(record, record, record, jax.ShapeDtypeStruct((3, 8 * LANES, LANES), jnp.float32)),
        compiler_params=pltpu.CompilerParams(vmem_limit_bytes=24 << 20),
        cost_estimate=pl.CostEstimate(flops=600_000_000, bytes_accessed=5_000_000, transcendentals=0),
        name="prepare",
    )(voxel_feats, voxel_reg)


def gather_early_kernel(
    first_ref, second_ref, mask_ref, low_ref, high_ref, below_ref, above_ref,
    first_lanes, second_lanes, mask_lanes, first_store, second_store, mask_store,
):
    for store in (first_store, second_store, mask_store):
        store[...] = jnp.zeros_like(store)

    def put(store):
        def write(a, e, value):
            if len(store.shape) == 3:
                store[lane_of(a, e)] = value
            else:
                store[lane_of(a, e) : lane_of(a, e) + 1, :] = value

        return write

    edges = (low_ref, high_ref, below_ref, above_ref)
    place_bricks(put(first_store), EARLY, 0, first_ref, *edges)
    place_bricks(put(second_store), EARLY, 1, second_ref, *edges)
    place_bricks(put(mask_store), EARLY, 2, mask_ref, *edges)
    to_lanes(first_store, first_lanes)
    to_lanes(second_store, second_lanes)
    mask_lanes[...] = mask_store[...].T[:8, :]


def gather_early(first, second, mask, edges):
    lanes = jax.ShapeDtypeStruct((8 * LANES, SPAN), jnp.float32)
    return pl.pallas_call(
        gather_early_kernel,
        out_shape=(lanes, lanes, jax.ShapeDtypeStruct((8, SPAN), jnp.float32)),
        scratch_shapes=[
            pltpu.VMEM((SPAN, 8, LANES), jnp.float32),
            pltpu.VMEM((SPAN, 8, LANES), jnp.float32),
            pltpu.VMEM((SPAN, LANES), jnp.float32),
        ],
        compiler_params=pltpu.CompilerParams(vmem_limit_bytes=24 << 20),
        cost_estimate=pl.CostEstimate(flops=2_000_000, bytes_accessed=3_000_000, transcendentals=0),
        name="gather_early",
    )(first, second, mask, *edges)


def relay_kernel(sections, count, *refs):
    owns, low, high, to_low, to_high = refs[:count], *refs[count:]
    fill_across(sections, owns, low, high, to_low, to_high)


def relay(sections, owns, low, high, name):
    out = jax.ShapeDtypeStruct((message_rows(sections, across_rows), LANES), jnp.float32)
    return pl.pallas_call(
        functools.partial(relay_kernel, sections, len(owns)),
        out_shape=(out, out),
        name=name,
    )(*owns, low, high)


def along_messages(sections, owns):
    to_low, to_high = [], []
    for (rows, depth), own in zip(sections, owns):
        flat = own.reshape(-1, LANES)
        used = rows * depth * BY
        blank = ((0, padded(used) - used), (0, 0))
        to_low.append(jnp.pad(flat[:used], blank))
        to_high.append(jnp.pad(flat[flat.shape[0] - used :], blank))
    return jnp.concatenate(to_low), jnp.concatenate(to_high)


def swap(to_low, to_high, axis):
    count = lax.axis_size(axis)
    up = [(i, i + 1) for i in range(count - 1)]
    down = [(b, a) for a, b in up]
    return lax.ppermute(to_high, axis, up), lax.ppermute(to_low, axis, down)


def begin_kernel(moments_ref, gathered_ref, lanes_ref, vectors_ref, low_ref, high_ref):
    values = jnp.concatenate(
        [gathered_ref[...], jnp.zeros((LANES - gathered_ref.shape[0], FEAT), jnp.float32)], axis=0
    )
    values = jnp.concatenate([values, jnp.zeros((LANES, LANES - FEAT), jnp.float32)], axis=1).T[:FEAT, :]
    applied = [times(lanes_ref.at[power], values) for power in range(3)]
    vectors = jnp.concatenate([*applied, values], axis=0).T
    vectors_ref[...] = vectors[: vectors_ref.shape[0], :]
    depth = LATE[0][1] * BY
    for k in range(depth):
        low_ref[8 * k : 8 * k + 8, :] = moments_ref[k]
        high_ref[8 * k : 8 * k + 8, :] = moments_ref[BX * BY - depth + k]
    deep = LATE[1][1] * BY
    blank = jnp.zeros((padded(deep) - deep, LANES), jnp.float32)
    low_ref[8 * depth :, :] = jnp.concatenate([vectors[:deep], blank], axis=0)
    high_ref[8 * depth :, :] = jnp.concatenate([vectors[BX * BY - deep : BX * BY], blank], axis=0)


def begin(moments, gathered, lanes):
    message = jax.ShapeDtypeStruct((message_rows(LATE, along_rows), LANES), jnp.float32)
    return pl.pallas_call(
        begin_kernel,
        out_shape=(jax.ShapeDtypeStruct((gathered.shape[0], LANES), jnp.float32), message, message),
        name="begin",
    )(moments, gathered, lanes)


def power_of_two(value):
    scale = jnp.ones_like(value)
    inverse = jnp.ones_like(value)
    for k in (64, 32, 16, 8, 4, 2, 1):
        up, down = 2.0**k, 2.0**-k
        large = value * down >= 1.0
        small = value * up <= 1.0
        value = jnp.where(large, value * down, jnp.where(small, value * up, value))
        scale = jnp.where(large, scale * up, jnp.where(small, scale * down, scale))
        inverse = jnp.where(large, inverse * down, jnp.where(small, inverse * up, inverse))
    return scale, inverse


def krylov_kernel(
    moments_ref, vectors_ref, low_ref, high_ref, below_ref, above_ref, first_ref, second_ref, mask_ref,
    feats_ref, reg_ref, basis_ref, message_ref, moment_store, vector_store, moment_lanes,
):
    moment_store[...] = jnp.zeros_like(moment_store)
    vector_store[...] = jnp.zeros_like(vector_store)

    def put_moment(a, e, value):
        moment_store[lane_of(a, e)] = value

    def put_vector(a, e, value):
        vector_store[lane_of(a, e) : lane_of(a, e) + 1, :] = value

    edges = (low_ref, high_ref, below_ref, above_ref)
    place_bricks(put_moment, LATE, 0, moments_ref, *edges)
    place_bricks(put_vector, LATE, 1, vectors_ref, *edges)
    to_lanes(moment_store, moment_lanes)
    vectors = vector_store[...].T
    masks = mask_ref[...]

    def system(z):
        near = masks[0:1] * pltpu.roll(z, PITCH, 1) + masks[1:2] * pltpu.roll(z, SPAN - PITCH, 1)
        near = near + masks[2:3] * pltpu.roll(z, 1, 1) + masks[3:4] * pltpu.roll(z, SPAN - 1, 1)
        return times(moment_lanes, z) + coupling_weight * (masks[4:5] * z - near)

    one = system(vectors[0:FEAT])
    two = system(times(first_ref, one) + vectors[FEAT : 2 * FEAT])
    three = system(times(first_ref, two) + times(second_ref, one) + vectors[2 * FEAT : 3 * FEAT])
    chain = (vectors[3 * FEAT :], one, two, three)
    for b in range(BX * BY):
        lane = lane_of(b // BY, b % BY)
        feats = feats_ref[b]
        for step, values in enumerate(chain):
            basis_ref[step, b : b + 1, :] = jnp.sum(feats * values[:, lane : lane + 1], axis=0, keepdims=True)
    reg = reg_ref[...]
    basis = [basis_ref[0]]
    for step in range(1, 4):
        basis.append(basis_ref[step] + reg * basis[-1])
        basis_ref[step] = basis[-1]

    def folded(x, combine):
        rows = [x[8 * k : 8 * k + 8, :] for k in range(x.shape[0] // 8)]
        parts = [r[:, LANES * k : LANES * (k + 1)] for r in rows for k in range(x.shape[1] // LANES)]
        while len(parts) > 1:
            parts = [combine(parts[k], parts[k + 1]) for k in range(0, len(parts), 2)]
        return parts[0]

    peaks = [jnp.max(folded(jnp.abs(v), jnp.maximum), axis=0, keepdims=True) for v in basis]
    peaks = jnp.max(jnp.concatenate(peaks + peaks, axis=0), axis=1, keepdims=True)
    scale, inverse = power_of_two(jnp.broadcast_to(peaks, (8, LANES)))
    scaled = [v * inverse[k : k + 1, 0:1] for k, v in enumerate(basis)]
    sums = [jnp.sum(folded(scaled[a] * scaled[b], jnp.add), axis=0, keepdims=True) for a, b in PAIRS]
    sums = jnp.concatenate(sums + [jnp.zeros((16 - len(PAIRS), LANES), jnp.float32)], axis=0)
    sums = jnp.sum(sums, axis=1, keepdims=True)
    lane = lax.broadcasted_iota(jnp.int32, (1, LANES), 1)
    row = jnp.zeros((1, LANES), jnp.float32)
    for k in range(len(PAIRS)):
        row = jnp.where(lane == k, sums[k : k + 1, :], row)
    for k in range(4):
        row = jnp.where(lane == 10 + k, scale[k : k + 1, :], row)
        row = jnp.where(lane == 14 + k, inverse[k : k + 1, :], row)
    message_ref[...] = jnp.broadcast_to(row, message_ref.shape)


def krylov(moments, vectors, edges, first, second, masks, voxel_feats, voxel_reg, devices):
    bricks, _, voxels = voxel_feats.shape
    return pl.pallas_call(
        krylov_kernel,
        out_shape=(
            jax.ShapeDtypeStruct((4, bricks, voxels), jnp.float32),
            jax.ShapeDtypeStruct((devices, LANES), jnp.float32),
        ),
        scratch_shapes=[
            pltpu.VMEM((SPAN, 8, LANES), jnp.float32),
            pltpu.VMEM((SPAN, LANES), jnp.float32),
            pltpu.VMEM((8 * LANES, SPAN), jnp.float32),
        ],
        compiler_params=pltpu.CompilerParams(vmem_limit_bytes=32 << 20),
        name="krylov",
    )(moments, vectors, *edges, first, second, masks, voxel_feats, voxel_reg)


def finish_kernel(shared_ref, basis_ref, solution_ref, residual_ref):
    shared = shared_ref[...]
    lane = lax.broadcasted_iota(jnp.int32, (1, LANES), 1)

    def pick(row, k):
        return jnp.sum(jnp.where(lane == k, row, 0.0), axis=1, keepdims=True)

    largest = jnp.max(shared, axis=0, keepdims=True)
    smallest = jnp.min(shared, axis=0, keepdims=True)
    scale = [pick(largest, 10 + k) for k in range(4)]
    inverse = [pick(smallest, 14 + k) for k in range(4)]
    weight = [shared[:, 10 + k : 11 + k] * inverse[k] for k in range(4)]
    left = jnp.zeros_like(shared)
    right = jnp.zeros_like(shared)
    for k, (a, b) in enumerate(PAIRS):
        left = jnp.where(lane == k, weight[a], left)
        right = jnp.where(lane == k, weight[b], right)
    total = jnp.sum(shared * left * right, axis=0, keepdims=True)
    gram = [[None] * 4 for _ in range(4)]
    for k, (a, b) in enumerate(PAIRS):
        gram[a][b] = gram[b][a] = pick(total, k)
    growth = [scale[k + 1] * inverse[k] for k in range(3)]

    def product(left, right):
        terms = [
            left[a] * right[b] * gram[a][b]
            for a in range(4)
            for b in range(4)
            if left[a] is not None and right[b] is not None
        ]
        return functools.reduce(jnp.add, terms)

    def plus(left, factor, right):
        out = []
        for a, b in zip(left, right):
            out.append(a if b is None else factor * b if a is None else a + factor * b)
        return out

    def image(vector):
        return [None] + [None if vector[k] is None else vector[k] * growth[k] for k in range(3)]

    solution = [None] * 4
    residual = [jnp.ones((1, 1), jnp.float32), None, None, None]
    direction = list(residual)
    norm_now = product(residual, residual)
    for iteration in range(ITERS):
        carried = image(direction)
        alpha = norm_now / product(direction, carried)
        solution = plus(solution, alpha, direction)
        residual = plus(residual, -alpha, carried)
        if iteration + 1 < ITERS:
            norm_next = product(residual, residual)
            direction = plus(residual, norm_next / norm_now, direction)
            norm_now = norm_next
    back = [scale[0] * inverse[k] for k in range(4)]
    for out_ref, coefficients in ((solution_ref, solution), (residual_ref, residual)):
        total = None
        for k, c in enumerate(coefficients):
            if c is not None:
                term = (c * back[k]) * basis_ref[k]
                total = term if total is None else total + term
        out_ref[...] = total


def finish(shared, basis):
    _, bricks, voxels = basis.shape
    out = jax.ShapeDtypeStruct((bricks, voxels), jnp.float32)
    return pl.pallas_call(finish_kernel, out_shape=(out, out), name="finish")(shared, basis)


def shards(point_feats, point_targets, point_lists, brick_adjacency, voxel_feats, voxel_reg):
    feat_count = point_feats.shape[0]
    brick_total, slots = point_lists.shape
    local_bricks = voxel_feats.shape[0]
    devices = brick_total // local_bricks
    sending = pack(point_feats, point_targets, point_lists, devices)
    got = lax.all_to_all(sending, GX_GY, split_axis=0, concat_axis=0, tiled=True)

    first, second, third, lanes = prepare(voxel_feats, voxel_reg)
    mask = (brick_adjacency >= 0).astype(jnp.float32)
    mask = jnp.concatenate([mask, jnp.sum(mask, axis=1, keepdims=True)], axis=1)
    mask = jnp.pad(mask, ((0, 0), (0, LANES - 5)))
    early = (first, second, mask)
    low, high = swap(*along_messages(EARLY, early), GX)
    below, above = swap(*relay(EARLY, early, low, high, "relay_early"), "gy")
    first_lanes, second_lanes, mask_lanes = gather_early(first, second, mask, (low, high, below, above))

    got_feats = got[:, : 2 * feat_count].reshape(devices, 2, feat_count, local_bricks // 2, slots)
    got_targets = got[:, 2 * feat_count :].reshape(devices, 2, local_bricks // 2, slots)
    moments = jnp.einsum("shibc,shjbc->hbij", got_feats, got_feats, preferred_element_type=jnp.float32)
    moments = moments.reshape(local_bricks, 4, 8, feat_count).transpose(0, 2, 1, 3)
    moments = moments.reshape(local_bricks, 8, 4 * feat_count)
    gathered = jnp.einsum(
        "shbc,shibc->hbi", got_targets, got_feats, preferred_element_type=jnp.float32
    ).reshape(local_bricks, feat_count)

    vectors, to_low, to_high = begin(moments, gathered, lanes)
    low, high = swap(to_low, to_high, GX)
    below, above = swap(*relay(LATE, (moments, vectors), low, high, "relay_late"), "gy")
    basis, message = krylov(
        moments, vectors, (low, high, below, above), first_lanes, second_lanes, mask_lanes,
        voxel_feats, voxel_reg, devices,
    )
    shared = lax.all_to_all(message, GX_GY, split_axis=0, concat_axis=0, tiled=True)
    return finish(shared, basis)


def solution(mesh):
    torus = Mesh(mesh.devices.reshape(4, 4, 2, mesh.shape["gy"]), ("gx_0", "gx_1", "gx_2", "gy"))
    return jax.shard_map(
        shards,
        mesh=torus,
        in_specs=(
            P(None, GX_GY),
            P(GX_GY),
            P(GX_GY, None),
            P(GX_GY, None),
            P(GX_GY, None, None),
            P(GX_GY, None),
        ),
        out_specs=(P(GX_GY, None), P(GX_GY, None)),
        check_vma=False,
    )
```

time: 176 us -> 125 us (0.71)
  between operations: 30.8 us -> 0.91 us
  waiting for transfers between devices: 40.2 us -> 15.3 us
  Pallas kernels: 6.22 us -> 30.7 us
  starting transfers between devices: 40.1 us -> 30.7 us
  other arithmetic: 6.25 us -> 0.05 us
  blocking collectives: 22.5 us -> 18.5 us
  matrix products: 11.2 us -> 9.02 us
    pallas_call x0 -> x7, Pallas kernels: none -> 24.5 us  [the longest x1 12.5 us: prepare(): pl.pallas_call(prepare_kernel, out_shape=(record, record, record, jax.Sha...]
    all_to_all x1, waiting for transfers between devices: 33.6 us -> 13.9 us  [shards(): lax.all_to_all(sending, GX_GY, split_axis=0, concat_axis=0, tiled=True)]
    ppermute x12 -> x8, starting transfers between devices: 28.6 us -> 18.8 us  [swap(): return (lax.ppermute(to_high, axis, up), lax.ppermute(to_low, axis, down))]
    another operation x1 -> x0, local copies, waits for them, and re-layouts: 8.85 us -> none  [krylov_coefficients(): jnp.stack([jnp.sum(scaled[a] * scaled[b]) for a, b in pairs] + peaks)]
    unnamed x10 -> x42, local copies, waits for them, and re-layouts: 0.21 us -> 8.37 us
    dot_general x3 -> x0, matrix products: 6.39 us -> none  [shards(): jnp.einsum('bik,bjk->bij', weighted, voxel_feats, precision=HIGHEST)]
    ppermute x12 -> x8, waiting for transfers between devices: 6.62 us -> 1.31 us  [swap(): return (lax.ppermute(to_high, axis, up), lax.ppermute(to_low, axis, down))]
    all_to_all x1, blocking collectives: 22.5 us -> 18.5 us  [shards(): lax.all_to_all(message, GX_GY, split_axis=0, concat_axis=0, tiled=True)]
  transfers between devices with their start and end apart: 13 -> 9, of which waited for: 4 -> 2; matrix products, arithmetic and copies ran while one was open for 2% -> 16% of each run, Pallas kernels for 0% -> 16%
where the time goes in v2:
time: 125 us; the launch traced here: 124 us
  Pallas kernels  30.7 us (25%)
  starting transfers between devices  30.7 us (25%)
  local copies, waits for them, and re-layouts  18.5 us (15%)
  blocking collectives  18.5 us (15%)
  waiting for transfers between devices  15.3 us (12%)
  matrix products  9.02 us (7%)
    ppermute x8, starting transfers between devices, swap(): return (lax.ppermute(to_high, axis, up), lax.ppermute(to_low, axis, down))  18.8 us
    all_to_all x1, blocking collectives, shards(): lax.all_to_all(message, GX_GY, split_axis=0, concat_axis=0, tiled=True)  18.5 us
    all_to_all x1, waiting for transfers between devices, shards(): lax.all_to_all(sending, GX_GY, split_axis=0, concat_axis=0, tiled=True)  13.9 us
    pallas_call x1, Pallas kernels, prepare(): pl.pallas_call(prepare_kernel, out_shape=(record, record, record, jax.Sha...  12.5 us
    all_to_all x1, starting transfers between devices, shards(): lax.all_to_all(sending, GX_GY, split_axis=0, concat_axis=0, tiled=True)  11.9 us
    unnamed x42, local copies, waits for them, and re-layouts  8.37 us
    slice x2, local copies, waits for them, and re-layouts, shards(): got[:, :2 * feat_count]  7.3 us
    pallas_call x1, Pallas kernels, pack(): pl.pallas_call(pack_kernel, grid=(steps,), in_specs=[pl.BlockSpec((SLOTS,...  6.21 us
  transfers between devices with their start and end apart: 9, of which 2 were waited for; matrix products, arithmetic and copies ran while one was open for 16% of the time, Pallas kernels for 16%

profile of v2, /device:TPU:1, one launch (start us, length us, event | category | flops | bytes accessed | tf_op | source)
XLA Modules:
  0.0 123.7 jit_solution(93985705399924734)
XLA Ops:
  0.6 6.2 %pack.1 = bf16[128,66,128]{2,1,0:T(8,128)(2,1)} custom-call(s32[8,4096]{1,0:T(8,128)} %bitcast.37, bf16[32,32768]{1,0:T(8,128)(2,1)} %feats_ref.3, bf16[256,128]{1,0:T(8,128)(2,1)} %bitcast.38), custom_call_target="tpu_custom_call" | custom-call | tf_op jit(solution)/shard_map/pack/pallas_call | solution.py:164
  6.8 0.0 copy-start.20
  6.9 11.9 %all-to-all-start = ((bf16[128,66,128]{2,1,0:T(8,128)(2,1)}), bf16[128,66,128]{2,1,0:T(8,128)(2,1)}, u32[]{:S(2)}, u32[]{:S(2)}) async-start(bf16[128,66,128]{2,1,0:T(8,128)(2,1)} %pack.1), calls=%async_computation | async-start | bytes 4718592 | tf_op jit(solution)/shard_map/all_to_all | solution.py:489
  18.8 0.0 copy-done.20
  18.8 0.1 copy.27
  18.9 0.0 copy-done
  18.9 0.0 copy-done.17
  18.9 12.5 %prepare.1 = (f32[32,8,128]{2,1,0:T(8,128)S(1)}, f32[32,8,128]{2,1,0:T(8,128)S(1)}, f32[32,8,128]{2,1,0:T(8,128)}, f32[3,1024,128]{2,1,0:T(8,128)S(1)}) custom-call(f32[32,32,512]{2,1,0:T(8,128)S(1)} %copy-done, f32[32,512]{1,0:T(8,128)S(1)} %copy-done.17), custom_call_target="tpu_custom_call" | custom-call | flops 600000000 | bytes 5000000 | tf_op jit(solution)/shard_map/prepare/pallas_call | solution.py:209
  31.4 1.2 copy-done.2
  32.7 3.7 %collective-permute-start.4 = (f32[104,128]{1,0:T(8,128)S(1)}, f32[104,128]{1,0:T(8,128)S(1)}, u32[]{:S(2)}, u32[]{:S(2)}) collective-permute-start(f32[104,128]{1,0:T(8,128)S(1)} %pad_maximum_fusion), channel_id=1, source_target_pairs={{0,4},{4,8},{8,12},{12,16},{16,20},{20,24},{24,28},{28,32},{32,36}... | collective-permute-start | bytes 159752 | tf_op jit(solution)/shard_map/ppermute | solution.py:288
  36.4 1.9 %collective-permute-start.5 = (f32[104,128]{1,0:T(8,128)S(1)}, f32[104,128]{1,0:T(8,128)S(1)}, u32[]{:S(2)}, u32[]{:S(2)}) collective-permute-start(f32[104,128]{1,0:T(8,128)S(1)} %pad_maximum_fusion.1), channel_id=1, source_target_pairs={{4,0},{8,4},{12,8},{16,12},{20,16},{24,20},{28,24},{32,28},{36,32}... | collective-permute-start | bytes 159752 | tf_op jit(solution)/shard_map/ppermute | solution.py:288
  38.3 13.9 %all-to-all-done = bf16[128,66,128]{2,1,0:T(8,128)(2,1)} async-done(((bf16[128,66,128]{2,1,0:T(8,128)(2,1)}), bf16[128,66,128]{2,1,0:T(8,128)(2,1)}, u32[]{:S(2)}, u32[]{:S(2)}) %all-to-all-start) | async-done | bytes 2162720 | tf_op jit(solution)/shard_map/all_to_all | solution.py:489
  52.3 3.1 %slice.48 = bf16[128,64,128]{2,1,0:T(8,128)(2,1)} slice(bf16[128,66,128]{2,1,0:T(8,128)(2,1)} %all-to-all-done), slice={[0:128], [0:64], [0:128]} | slice | bytes 4194304 | tf_op jit(solution)/shard_map/slice | solution.py:500
  55.4 0.0 copy-done.3
  55.4 0.0 copy-done.5
  55.4 4.2 %copy.22 = bf16[128,64,128]{0,2,1:T(8,128)(2,1)} copy(bf16[128,64,128]{2,1,0:T(8,128)(2,1)} %slice.48) | data formatting | bytes 4194304 | tf_op jit(solution)/shard_map/slice | solution.py:500
  59.6 5.3 %fusion.2 = f32[2,16,32,32,1]{3,2,4,1,0:T(8,128)} fusion(bf16[128,2,32,16,8]{0,4,3,2,1:T(8,128)(2,1)} %bitcast.33), kind=kOutput, calls=%fused_computation.2 | convolution fusion | flops 67108864 | bytes 2228224 | tf_op jit(solution)/shard_map/shibc,shjbc->hbij/dot_general | solution.py:502
  64.9 1.0 slice.49
  65.9 0.1 copy.26
  66.0 0.0 copy-start.19
  66.0 3.7 %fusion = f32[2,16,1,32,1]{3,2,4,1,0:T(1,128)} fusion(bf16[128,2,32,16,8]{0,4,3,2,1:T(8,128)(2,1)} %bitcast.34, bf16[128,2,16,8,1]{0,3,2,1,4:T(8,128)(2,1)S(1)} %bitcast.39), kind=kOutput, calls=%fused_computation | convolution fusion | flops 2097152 | bytes 2166784 | tf_op jit(solution)/shard_map/shbc,shibc->hbi/dot_general | solution.py:505
  69.7 0.0 copy-done.19
  69.7 0.1 copy.39
  69.9 0.9 reshape.33.moments_ref.refs_0_
  70.8 2.4 %begin.1 = (f32[32,128]{1,0:T(8,128)}, f32[80,128]{1,0:T(8,128)}, f32[80,128]{1,0:T(8,128)}) custom-call(f32[32,8,128]{2,1,0:T(8,128)} %reshape.33.moments_ref.refs_0_, f32[32,32]{1,0:T(8,128)} %bitcast.40, f32[3,1024,128]{2,1,0:T(8,128)} %copy-done.2), custom_call_target="tpu_custom_call" | custom-call | tf_op jit(solution)/shard_map/begin/pallas_call | solution.py:311
  73.2 2.6 %collective-permute-start = (f32[80,128]{1,0:T(8,128)}, f32[80,128]{1,0:T(8,128)S(1)}, u32[]{:S(2)}, u32[]{:S(2)}) collective-permute-start(f32[80,128]{1,0:T(8,128)} %get-tuple-element.19), channel_id=1, source_target_pairs={{0,4},{4,8},{8,12},{12,16},{16,20},{20,24},{24,28},{28,32},{32,36}... | collective-permute-start | bytes 122888 | tf_op jit(solution)/shard_map/ppermute | solution.py:288
  75.8 1.9 %collective-permute-start.1 = (f32[80,128]{1,0:T(8,128)}, f32[80,128]{1,0:T(8,128)S(1)}, u32[]{:S(2)}, u32[]{:S(2)}) collective-permute-start(f32[80,128]{1,0:T(8,128)} %get-tuple-element.20), channel_id=1, source_target_pairs={{4,0},{8,4},{12,8},{16,12},{20,16},{24,20},{28,24},{32,28},{36,32}... | collective-permute-start | bytes 122888 | tf_op jit(solution)/shard_map/ppermute | solution.py:288
  77.7 0.6 pad.4.refs_2_.mask_ref
  78.3 0.0 collective-permute-done.4.refs_3_.low_ref
  78.3 0.0 collective-permute-done.5.refs_4_.high_ref
  78.3 0.6 copy-done.8
  78.9 0.6 copy-done.10
  79.5 1.7 %relay_early.1 = (f32[232,128]{1,0:T(8,128)}, f32[232,128]{1,0:T(8,128)}) custom-call(f32[32,8,128]{2,1,0:T(8,128)} %copy-done.3, f32[32,8,128]{2,1,0:T(8,128)} %copy-done.5, f32[32,128]{1,0:T(8,128)} %pad.4.refs_2_.mask_ref, f32[104,128]{1,0:T(8,128)} %copy-done.8, f32[104,128]{1,0:T(8,128)} %copy-done.10), custom_call_target="tpu_custom_call" | custom-call | tf_op jit(solution)/shard_map/relay_early/pallas_call | solution.py:266
  81.3 2.2 %collective-permute-start.6 = (f32[232,128]{1,0:T(8,128)}, f32[232,128]{1,0:T(8,128)S(1)}, u32[]{:S(2)}, u32[]{:S(2)}) collective-permute-start(f32[232,128]{1,0:T(8,128)} %get-tuple-element.25), channel_id=1, source_target_pairs={{0,1},{1,2},{2,3},{4,5},{5,6},{6,7},{8,9},{9,10},{10,11},{12,13},{... | collective-permute-start | bytes 356360 | tf_op jit(solution)/shard_map/ppermute | solution.py:288
  83.5 1.3 %collective-permute-start.7 = (f32[232,128]{1,0:T(8,128)}, f32[232,128]{1,0:T(8,128)S(1)}, u32[]{:S(2)}, u32[]{:S(2)}) collective-permute-start(f32[232,128]{1,0:T(8,128)} %get-tuple-element.26), channel_id=1, source_target_pairs={{1,0},{2,1},{3,2},{5,4},{6,5},{7,6},{9,8},{10,9},{11,10},{13,12},{... | collective-permute-start | bytes 356360 | tf_op jit(solution)/shard_map/ppermute | solution.py:288
  84.8 0.0 collective-permute-done.refs_2_.low_ref
  84.8 0.0 copy-start.12
  84.8 0.0 collective-permute-done.1.refs_3_.high_ref
  84.8 0.0 copy-start.14
  84.8 0.6 copy-done.12
  85.4 0.0 copy-done.14
  85.4 1.6 %relay_late.1 = (f32[176,128]{1,0:T(8,128)}, f32[176,128]{1,0:T(8,128)}) custom-call(f32[32,8,128]{2,1,0:T(8,128)} %reshape.33.moments_ref.refs_0_, f32[32,128]{1,0:T(8,128)} %get-tuple-element.18.refs_1_.vectors_ref, f32[80,128]{1,0:T(8,128)} %copy-done.12, f32[80,128]{1,0:T(8,128)} %copy-done.14), custom_call_target="tpu_custom_call" | custom-call | tf_op jit(solution)/shard_map/relay_late/pallas_call | solution.py:266
  87.0 4.0 %collective-permute-start.2 = (f32[176,128]{1,0:T(8,128)}, f32[176,128]{1,0:T(8,128)S(1)}, u32[]{:S(2)}, u32[]{:S(2)}) collective-permute-start(f32[176,128]{1,0:T(8,128)} %get-tuple-element.21), channel_id=1, source_target_pairs={{0,1},{1,2},{2,3},{4,5},{5,6},{6,7},{8,9},{9,10},{10,11},{12,13},{... | collective-permute-start | bytes 270344 | tf_op jit(solution)/shard_map/ppermute | solution.py:288
  91.0 1.3 %collective-permute-start.3 = (f32[176,128]{1,0:T(8,128)}, f32[176,128]{1,0:T(8,128)S(1)}, u32[]{:S(2)}, u32[]{:S(2)}) collective-permute-start(f32[176,128]{1,0:T(8,128)} %get-tuple-element.22), channel_id=1, source_target_pairs={{1,0},{2,1},{3,2},{5,4},{6,5},{7,6},{9,8},{10,9},{11,10},{13,12},{... | collective-permute-start | bytes 270344 | tf_op jit(solution)/shard_map/ppermute | solution.py:288
  92.3 0.0 collective-permute-done.6.below_ref
  92.3 0.0 collective-permute-done.7.above_ref
  92.4 0.0 copy-done.4
  92.4 0.0 copy-done.6
  92.4 0.0 copy-start.9
  92.4 0.8 copy-done.9
  93.2 0.8 copy-done.11
  94.0 0.7 copy-done.16
  94.7 1.3 %gather_early.1 = (f32[1024,256]{1,0:T(8,128)S(1)}, f32[1024,256]{1,0:T(8,128)S(1)}, f32[8,256]{1,0:T(8,128)S(1)}) custom-call(f32[32,8,128]{2,1,0:T(8,128)S(1)} %copy-done.4, f32[32,8,128]{2,1,0:T(8,128)S(1)} %copy-done.6, f32[32,128]{1,0:T(8,128)S(1)} %copy-done.16, f32[104,128]{1,0:T(8,128)S(1)} %copy-done.9, f32[104,128]{1,0:T(8,128)S(1)} %copy-done.11, ...), custom_call_target="tpu_custom_call" | custom-call | flops 2000000 | bytes 3000000 | tf_op jit(solution)/shard_map/gather_early/pallas_call | solution.py:245
  96.0 0.0 collective-permute-done.2.below_ref
  96.0 1.3 %collective-permute-done.3.above_ref = f32[176,128]{1,0:T(8,128)S(1)} collective-permute-done((f32[176,128]{1,0:T(8,128)}, f32[176,128]{1,0:T(8,128)S(1)}, u32[]{:S(2)}, u32[]{:S(2)}) %collective-permute-start.3) | collective-permute-done | bytes 90144 | tf_op jit(solution)/shard_map/ppermute | solution.py:288
  97.3 0.0 copy-done.1
  97.3 0.8 copy-done.13
  98.1 0.8 copy-done.15
  98.9 0.7 copy-done.18
  99.6 2.8 %krylov.1 = (f32[4,32,512]{2,1,0:T(8,128)S(1)}, f32[128,128]{1,0:T(8,128)S(1)}) custom-call(f32[32,8,128]{2,1,0:T(8,128)S(1)} %copy-done.1, f32[32,128]{1,0:T(8,128)S(1)} %copy-done.18, f32[80,128]{1,0:T(8,128)S(1)} %copy-done.13, f32[80,128]{1,0:T(8,128)S(1)} %copy-done.15, f32[176,128]{1,0:T(8,128)S(1)} %collective-permute-done.2.below_ref, ...), custom_call_target="tpu_custom_call" | custom-call | tf_op jit(solution)/shard_map/krylov/pallas_call | solution.py:397
  102.4 0.0 copy-start.7
  102.4 0.7 copy-done.7
  103.1 18.5 %all_to_all.16 = f32[128,1,128]{2,1,0:T(1,128)} all-to-all(f32[128,1,128]{2,1,0:T(1,128)S(1)} %bitcast.31), channel_id=1, replica_groups=mesh['gx_0'=4,'gx_1'=4,'gx_2'=2,'gy'=4] {'gx_0','gx_1','gx_2','gy'}, dimensions={0} | all-to-all | bytes 131072 | tf_op jit(solution)/shard_map/all_to_all | solution.py:516
  121.6 2.1 %finish.1 = (f32[32,512]{1,0:T(8,128)}, f32[32,512]{1,0:T(8,128)}) custom-call(f32[128,128]{1,0:T(8,128)} %bitcast.36, f32[4,32,512]{2,1,0:T(8,128)} %copy-done.7), custom_call_target="tpu_custom_call" | custom-call | tf_op jit(solution)/shard_map/finish/pallas_call | solution.py:480
  (23 shorter events, 0.1 us)
Async XLA Ops:
  6.8 11.9 %copy-start.20 = (s32[32,4]{0,1:T(4,128)S(1)}, s32[32,4]{0,1:T(4,128)}, u32[]{:S(2)}) copy-start(s32[32,4]{0,1:T(4,128)} %param.9) | copy-start | bytes 1540
  6.8 12.1 %copy-start = (f32[32,32,512]{2,1,0:T(8,128)S(1)}, f32[32,32,512]{2,1,0:T(8,128)}, u32[]{:S(2)}) copy-start(f32[32,32,512]{2,1,0:T(8,128)} %feats_ref.5) | copy-start | bytes 6291460
  6.8 12.1 %copy-start.17 = (f32[32,512]{1,0:T(8,128)S(1)}, f32[32,512]{1,0:T(8,128)}, u32[]{:S(2)}) copy-start(f32[32,512]{1,0:T(8,128)} %reg_ref.3) | copy-start | bytes 196612
  6.9 45.4 %all-to-all-start = ((bf16[128,66,128]{2,1,0:T(8,128)(2,1)}), bf16[128,66,128]{2,1,0:T(8,128)(2,1)}, u32[]{:S(2)}, u32[]{:S(2)}) async-start(bf16[128,66,128]{2,1,0:T(8,128)(2,1)} %pack.1), calls=%async_computation | async-start | bytes 4718592 | tf_op jit(solution)/shard_map/all_to_all | solution.py:489
  31.4 1.2 copy-start.2
  32.7 22.7 %copy-start.3 = (f32[32,8,128]{2,1,0:T(8,128)}, f32[32,8,128]{2,1,0:T(8,128)S(1)}, u32[]{:S(2)}) copy-start(f32[32,8,128]{2,1,0:T(8,128)S(1)} %get-tuple-element.23.refs_0_.first_ref) | copy-start | bytes 393220
  32.7 22.7 %copy-start.5 = (f32[32,8,128]{2,1,0:T(8,128)}, f32[32,8,128]{2,1,0:T(8,128)S(1)}, u32[]{:S(2)}) copy-start(f32[32,8,128]{2,1,0:T(8,128)S(1)} %get-tuple-element.24.refs_1_.second_ref) | copy-start | bytes 393220
  32.7 45.6 %collective-permute-start.4 = (f32[104,128]{1,0:T(8,128)S(1)}, f32[104,128]{1,0:T(8,128)S(1)}, u32[]{:S(2)}, u32[]{:S(2)}) collective-permute-start(f32[104,128]{1,0:T(8,128)S(1)} %pad_maximum_fusion), channel_id=1, source_target_pairs={{0,4},{4,8},{8,12},{12,16},{16,20},{20,24},{24,28},{28,32},{32,36}... | collective-permute-start | bytes 159752 | tf_op jit(solution)/shard_map/ppermute | solution.py:288
  36.4 41.9 %collective-permute-start.5 = (f32[104,128]{1,0:T(8,128)S(1)}, f32[104,128]{1,0:T(8,128)S(1)}, u32[]{:S(2)}, u32[]{:S(2)}) collective-permute-start(f32[104,128]{1,0:T(8,128)S(1)} %pad_maximum_fusion.1), channel_id=1, source_target_pairs={{4,0},{8,4},{12,8},{16,12},{20,16},{24,20},{28,24},{32,28},{36,32}... | collective-permute-start | bytes 159752 | tf_op jit(solution)/shard_map/ppermute | solution.py:288
  66.0 3.7 %copy-start.19 = (f32[2,16,32,32,1]{3,2,4,1,0:T(8,128)S(1)}, f32[2,16,32,32,1]{3,2,4,1,0:T(8,128)}, u32[]{:S(2)}) copy-start(f32[2,16,32,32,1]{3,2,4,1,0:T(8,128)} %fusion.2) | copy-start | bytes 393220
  69.7 22.6 %copy-start.4 = (f32[32,8,128]{2,1,0:T(8,128)S(1)}, f32[32,8,128]{2,1,0:T(8,128)}, u32[]{:S(2)}) copy-start(f32[32,8,128]{2,1,0:T(8,128)} %copy-done.3) | copy-start | bytes 393220
  69.7 22.6 %copy-start.6 = (f32[32,8,128]{2,1,0:T(8,128)S(1)}, f32[32,8,128]{2,1,0:T(8,128)}, u32[]{:S(2)}) copy-start(f32[32,8,128]{2,1,0:T(8,128)} %copy-done.5) | copy-start | bytes 393220
  70.8 26.6 %copy-start.1 = (f32[32,8,128]{2,1,0:T(8,128)S(1)}, f32[32,8,128]{2,1,0:T(8,128)}, u32[]{:S(2)}) copy-start(f32[32,8,128]{2,1,0:T(8,128)} %reshape.33.moments_ref.refs_0_) | copy-start | bytes 393220
  73.2 11.6 %collective-permute-start = (f32[80,128]{1,0:T(8,128)}, f32[80,128]{1,0:T(8,128)S(1)}, u32[]{:S(2)}, u32[]{:S(2)}) collective-permute-start(f32[80,128]{1,0:T(8,128)} %get-tuple-element.19), channel_id=1, source_target_pairs={{0,4},{4,8},{8,12},{12,16},{16,20},{20,24},{24,28},{28,32},{32,36}... | collective-permute-start | bytes 122888 | tf_op jit(solution)/shard_map/ppermute | solution.py:288
  75.8 9.0 %collective-permute-start.1 = (f32[80,128]{1,0:T(8,128)}, f32[80,128]{1,0:T(8,128)S(1)}, u32[]{:S(2)}, u32[]{:S(2)}) collective-permute-start(f32[80,128]{1,0:T(8,128)} %get-tuple-element.20), channel_id=1, source_target_pairs={{4,0},{8,4},{12,8},{16,12},{20,16},{24,20},{28,24},{32,28},{36,32}... | collective-permute-start | bytes 122888 | tf_op jit(solution)/shard_map/ppermute | solution.py:288
  78.3 0.6 copy-start.8
  78.9 0.6 copy-start.10
  81.3 11.1 %collective-permute-start.6 = (f32[232,128]{1,0:T(8,128)}, f32[232,128]{1,0:T(8,128)S(1)}, u32[]{:S(2)}, u32[]{:S(2)}) collective-permute-start(f32[232,128]{1,0:T(8,128)} %get-tuple-element.25), channel_id=1, source_target_pairs={{0,1},{1,2},{2,3},{4,5},{5,6},{6,7},{8,9},{9,10},{10,11},{12,13},{... | collective-permute-start | bytes 356360 | tf_op jit(solution)/shard_map/ppermute | solution.py:288
  83.5 8.9 %collective-permute-start.7 = (f32[232,128]{1,0:T(8,128)}, f32[232,128]{1,0:T(8,128)S(1)}, u32[]{:S(2)}, u32[]{:S(2)}) collective-permute-start(f32[232,128]{1,0:T(8,128)} %get-tuple-element.26), channel_id=1, source_target_pairs={{1,0},{2,1},{3,2},{5,4},{6,5},{7,6},{9,8},{10,9},{11,10},{13,12},{... | collective-permute-start | bytes 356360 | tf_op jit(solution)/shard_map/ppermute | solution.py:288
  84.8 0.6 copy-start.12
  84.8 0.6 copy-start.14
  87.0 9.0 %collective-permute-start.2 = (f32[176,128]{1,0:T(8,128)}, f32[176,128]{1,0:T(8,128)S(1)}, u32[]{:S(2)}, u32[]{:S(2)}) collective-permute-start(f32[176,128]{1,0:T(8,128)} %get-tuple-element.21), channel_id=1, source_target_pairs={{0,1},{1,2},{2,3},{4,5},{5,6},{6,7},{8,9},{9,10},{10,11},{12,13},{... | collective-permute-start | bytes 270344 | tf_op jit(solution)/shard_map/ppermute | solution.py:288
  91.0 6.3 %collective-permute-start.3 = (f32[176,128]{1,0:T(8,128)}, f32[176,128]{1,0:T(8,128)S(1)}, u32[]{:S(2)}, u32[]{:S(2)}) collective-permute-start(f32[176,128]{1,0:T(8,128)} %get-tuple-element.22), channel_id=1, source_target_pairs={{1,0},{2,1},{3,2},{5,4},{6,5},{7,6},{9,8},{10,9},{11,10},{13,12},{... | collective-permute-start | bytes 270344 | tf_op jit(solution)/shard_map/ppermute | solution.py:288
  92.4 0.8 copy-start.9
  93.2 0.8 copy-start.11
  94.0 0.7 copy-start.16
  97.3 0.8 copy-start.13
  98.1 0.8 copy-start.15
  98.9 0.7 copy-start.18
  102.4 0.7 copy-start.7

commit v3 on v2

--- a/solution.py
+++ b/solution.py
@@ -496,6 +496,9 @@
     low, high = swap(*along_messages(EARLY, early), GX)
     below, above = swap(*relay(EARLY, early, low, high, "relay_early"), "gy")
     first_lanes, second_lanes, mask_lanes = gather_early(first, second, mask, (low, high, below, above))
+    got, first_lanes, second_lanes, mask_lanes = lax.optimization_barrier(
+        (got, first_lanes, second_lanes, mask_lanes)
+    )
 
     got_feats = got[:, : 2 * feat_count].reshape(devices, 2, feat_count, local_bricks // 2, slots)
     got_targets = got[:, 2 * feat_count :].reshape(devices, 2, local_bricks // 2, slots)

time: 125 us -> 138 us (1.10)
  local copies, waits for them, and re-layouts: 18.5 us -> 24.7 us
  waiting for transfers between devices: 15.3 us -> 19.5 us
  blocking collectives: 18.5 us -> 21.3 us
  starting transfers between devices: 30.7 us -> 33.4 us
  matrix products: 9.02 us -> 6.75 us
    ppermute x8, waiting for transfers between devices: 1.31 us -> 19.5 us  [swap(): return (lax.ppermute(to_high, axis, up), lax.ppermute(to_low, axis, down))]
    all_to_all x1, waiting for transfers between devices: 13.9 us -> 0.01 us  [shards(): lax.all_to_all(sending, GX_GY, split_axis=0, concat_axis=0, tiled=True)]
    unnamed x42 -> x48, local copies, waits for them, and re-layouts: 8.37 us -> 12.7 us
    all_to_all x1, blocking collectives: 18.5 us -> 21.3 us  [shards(): lax.all_to_all(message, GX_GY, split_axis=0, concat_axis=0, tiled=True)]
    ppermute x8, starting transfers between devices: 18.8 us -> 21.5 us  [swap(): return (lax.ppermute(to_high, axis, up), lax.ppermute(to_low, axis, down))]
    dot_general x1, matrix products: 3.71 us -> 2.08 us  [shards(): jnp.einsum('shbc,shibc->hbi', got_targets, got_feats, preferred_element_t...]
  transfers between devices with their start and end apart: 9 -> 9, of which waited for: 2 -> 7; matrix products, arithmetic and copies ran while one was open for 16% -> 1% of each run, Pallas kernels for 16% -> 11%
where the time goes in v3:
time: 138 us; the launch traced here: 137 us
  starting transfers between devices  33.4 us (24%)
  Pallas kernels  30.6 us (22%)
  local copies, waits for them, and re-layouts  24.7 us (18%)
  blocking collectives  21.3 us (15%)
  waiting for transfers between devices  19.5 us (14%)
  matrix products  6.75 us (5%)
    ppermute x8, starting transfers between devices, swap(): return (lax.ppermute(to_high, axis, up), lax.ppermute(to_low, axis, down))  21.5 us
    all_to_all x1, blocking collectives, shards(): lax.all_to_all(message, GX_GY, split_axis=0, concat_axis=0, tiled=True)  21.3 us
    ppermute x8, waiting for transfers between devices, swap(): return (lax.ppermute(to_high, axis, up), lax.ppermute(to_low, axis, down))  19.5 us
    unnamed x48, local copies, waits for them, and re-layouts  12.7 us
    pallas_call x1, Pallas kernels, prepare(): pl.pallas_call(prepare_kernel, out_shape=(record, record, record, jax.Sha...  12.5 us
    all_to_all x1, starting transfers between devices, shards(): lax.all_to_all(sending, GX_GY, split_axis=0, concat_axis=0, tiled=True)  11.9 us
    slice x2, local copies, waits for them, and re-layouts, shards(): got[:, :2 * feat_count]  7.31 us
    pallas_call x1, Pallas kernels, pack(): pl.pallas_call(pack_kernel, grid=(steps,), in_specs=[pl.BlockSpec((SLOTS,...  6.18 us
  transfers between devices with their start and end apart: 9, of which 7 were waited for; matrix products, arithmetic and copies ran while one was open for 1% of the time, Pallas kernels for 11%

profile of v3, /device:TPU:1, one launch (start us, length us, event | category | flops | bytes accessed | tf_op | source)
XLA Modules:
  0.0 137.2 jit_solution(7524738358206007719)
XLA Ops:
  0.6 6.2 %pack.1 = bf16[128,66,128]{2,1,0:T(8,128)(2,1)} custom-call(s32[8,4096]{1,0:T(8,128)} %bitcast.37, bf16[32,32768]{1,0:T(8,128)(2,1)} %feats_ref.3, bf16[256,128]{1,0:T(8,128)(2,1)} %bitcast.38), custom_call_target="tpu_custom_call" | custom-call | tf_op jit(solution)/shard_map/pack/pallas_call | solution.py:164
  6.8 11.9 %all-to-all-start = ((bf16[128,66,128]{2,1,0:T(8,128)(2,1)}), bf16[128,66,128]{2,1,0:T(8,128)(2,1)}, u32[]{:S(2)}, u32[]{:S(2)}) async-start(bf16[128,66,128]{2,1,0:T(8,128)(2,1)} %pack.1), calls=%async_computation | async-start | bytes 4718592 | tf_op jit(solution)/shard_map/all_to_all | solution.py:489
  18.7 0.0 copy-done.23
  18.8 0.1 copy.22
  18.9 0.0 copy-done
  18.9 0.0 copy-done.19
  18.9 12.5 %prepare.1 = (f32[32,8,128]{2,1,0:T(8,128)S(1)}, f32[32,8,128]{2,1,0:T(8,128)S(1)}, f32[32,8,128]{2,1,0:T(8,128)}, f32[3,1024,128]{2,1,0:T(8,128)S(1)}) custom-call(f32[32,32,512]{2,1,0:T(8,128)S(1)} %copy-done, f32[32,512]{1,0:T(8,128)S(1)} %copy-done.19), custom_call_target="tpu_custom_call" | custom-call | flops 600000000 | bytes 5000000 | tf_op jit(solution)/shard_map/prepare/pallas_call | solution.py:209
  31.4 1.2 copy-done.2
  32.7 3.7 %collective-permute-start = (f32[104,128]{1,0:T(8,128)S(1)}, f32[104,128]{1,0:T(8,128)S(1)}, u32[]{:S(2)}, u32[]{:S(2)}) collective-permute-start(f32[104,128]{1,0:T(8,128)S(1)} %pad_maximum_fusion), channel_id=1, source_target_pairs={{0,4},{4,8},{8,12},{12,16},{16,20},{20,24},{24,28},{28,32},{32,36}... | collective-permute-start | bytes 159752 | tf_op jit(solution)/shard_map/ppermute | solution.py:288
  36.4 1.9 %collective-permute-start.1 = (f32[104,128]{1,0:T(8,128)S(1)}, f32[104,128]{1,0:T(8,128)S(1)}, u32[]{:S(2)}, u32[]{:S(2)}) collective-permute-start(f32[104,128]{1,0:T(8,128)S(1)} %pad_maximum_fusion.1), channel_id=1, source_target_pairs={{4,0},{8,4},{12,8},{16,12},{20,16},{24,20},{28,24},{32,28},{36,32}... | collective-permute-start | bytes 159752 | tf_op jit(solution)/shard_map/ppermute | solution.py:288
  38.3 0.6 pad.4.refs_2_.mask_ref
  38.9 4.9 %collective-permute-done.refs_3_.low_ref = f32[104,128]{1,0:T(8,128)S(1)} collective-permute-done((f32[104,128]{1,0:T(8,128)S(1)}, f32[104,128]{1,0:T(8,128)S(1)}, u32[]{:S(2)}, u32[]{:S(2)}) %collective-permute-start) | collective-permute-done | bytes 53280 | tf_op jit(solution)/shard_map/ppermute | solution.py:288
  43.8 2.3 %collective-permute-done.1.refs_4_.high_ref = f32[104,128]{1,0:T(8,128)S(1)} collective-permute-done((f32[104,128]{1,0:T(8,128)S(1)}, f32[104,128]{1,0:T(8,128)S(1)}, u32[]{:S(2)}, u32[]{:S(2)}) %collective-permute-start.1) | collective-permute-done | bytes 53280 | tf_op jit(solution)/shard_map/ppermute | solution.py:288
  46.2 0.0 copy-done.5
  46.2 0.0 copy-done.7
  46.2 0.0 copy-done.10
  46.2 0.0 copy-start.12
  46.2 0.6 copy-done.12
  46.8 1.7 %relay_early.1 = (f32[232,128]{1,0:T(8,128)}, f32[232,128]{1,0:T(8,128)}) custom-call(f32[32,8,128]{2,1,0:T(8,128)} %copy-done.5, f32[32,8,128]{2,1,0:T(8,128)} %copy-done.7, f32[32,128]{1,0:T(8,128)} %pad.4.refs_2_.mask_ref, f32[104,128]{1,0:T(8,128)} %copy-done.10, f32[104,128]{1,0:T(8,128)} %copy-done.12), custom_call_target="tpu_custom_call" | custom-call | tf_op jit(solution)/shard_map/relay_early/pallas_call | solution.py:266
  48.5 3.5 %collective-permute-start.2 = (f32[232,128]{1,0:T(8,128)}, f32[232,128]{1,0:T(8,128)S(1)}, u32[]{:S(2)}, u32[]{:S(2)}) collective-permute-start(f32[232,128]{1,0:T(8,128)} %get-tuple-element.23), channel_id=1, source_target_pairs={{0,1},{1,2},{2,3},{4,5},{5,6},{6,7},{8,9},{9,10},{10,11},{12,13},{... | collective-permute-start | bytes 356360 | tf_op jit(solution)/shard_map/ppermute | solution.py:288
  52.0 1.3 collective-permute-start.3
  53.3 0.8 collective-permute-done.2.below_ref
  54.1 3.7 %collective-permute-done.3.above_ref = f32[232,128]{1,0:T(8,128)S(1)} collective-permute-done((f32[232,128]{1,0:T(8,128)}, f32[232,128]{1,0:T(8,128)S(1)}, u32[]{:S(2)}, u32[]{:S(2)}) %collective-permute-start.3) | collective-permute-done | bytes 118816 | tf_op jit(solution)/shard_map/ppermute | solution.py:288
  57.8 0.9 copy-done.6
  58.7 0.9 copy-done.8
  59.6 0.8 copy-done.11
  60.4 0.8 copy-done.13
  61.2 0.7 copy-done.18
  62.0 1.3 gather_early.1
  63.3 0.0 copy-start.3
  63.3 1.0 copy-done.3
  64.3 0.0 all-to-all-done
  64.3 1.0 slice.47
  65.3 3.1 %slice.46 = bf16[128,64,128]{2,1,0:T(8,128)(2,1)} slice(bf16[128,66,128]{2,1,0:T(8,128)(2,1)} %all-to-all-done), slice={[0:128], [0:64], [0:128]} | slice | bytes 4194304 | tf_op jit(solution)/shard_map/slice | solution.py:503
  68.4 4.2 %copy.23 = bf16[128,64,128]{0,2,1:T(8,128)(2,1)} copy(bf16[128,64,128]{2,1,0:T(8,128)(2,1)} %slice.46) | data formatting | bytes 4194304 | tf_op jit(solution)/shard_map/slice | solution.py:503
  72.6 0.1 copy.27
  72.7 0.0 copy-start.22
  72.7 4.7 %fusion.2 = f32[2,16,32,32,1]{3,2,4,1,0:T(8,128)S(1)} fusion(bf16[128,2,32,16,8]{0,4,3,2,1:T(8,128)(2,1)} %bitcast.33), kind=kOutput, calls=%fused_computation.2 | convolution fusion | flops 67108864 | bytes 2228224 | tf_op jit(solution)/shard_map/shibc,shjbc->hbij/dot_general | solution.py:505
  77.4 0.0 copy-done.22
  77.4 2.1 %fusion = f32[2,16,1,32,1]{3,2,4,1,0:T(1,128)} fusion(bf16[128,2,32,16,8]{0,4,3,2,1:T(8,128)(2,1)S(1)} %bitcast.34, bf16[128,2,16,8,1]{0,3,2,1,4:T(8,128)(2,1)S(1)} %bitcast.39), kind=kOutput, calls=%fused_computation | convolution fusion | flops 2097152 | bytes 2166784 | tf_op jit(solution)/shard_map/shbc,shibc->hbi/dot_general | solution.py:508
  79.5 0.9 copy.39
  80.4 2.0 %reshape.33.moments_ref.refs_0_ = f32[32,8,128]{2,1,0:T(8,128)} reshape(f32[32,8,4,32]{3,2,1,0:T(4,128)} %bitcast.32) | data formatting | bytes 262144 | tf_op jit(solution)/shard_map/reshape | solution.py:507
  82.4 2.4 %begin.1 = (f32[32,128]{1,0:T(8,128)}, f32[80,128]{1,0:T(8,128)}, f32[80,128]{1,0:T(8,128)}) custom-call(f32[32,8,128]{2,1,0:T(8,128)} %reshape.33.moments_ref.refs_0_, f32[32,32]{1,0:T(8,128)} %bitcast.40, f32[3,1024,128]{2,1,0:T(8,128)} %copy-done.2), custom_call_target="tpu_custom_call" | custom-call | tf_op jit(solution)/shard_map/begin/pallas_call | solution.py:311
  84.7 6.7 %collective-permute-start.4 = (f32[80,128]{1,0:T(8,128)}, f32[80,128]{1,0:T(8,128)S(1)}, u32[]{:S(2)}, u32[]{:S(2)}) collective-permute-start(f32[80,128]{1,0:T(8,128)} %get-tuple-element.31), channel_id=1, source_target_pairs={{0,4},{4,8},{8,12},{12,16},{16,20},{20,24},{24,28},{28,32},{32,36}... | collective-permute-start | bytes 122888 | tf_op jit(solution)/shard_map/ppermute | solution.py:288
  91.4 1.9 %collective-permute-start.5 = (f32[80,128]{1,0:T(8,128)}, f32[80,128]{1,0:T(8,128)S(1)}, u32[]{:S(2)}, u32[]{:S(2)}) collective-permute-start(f32[80,128]{1,0:T(8,128)} %get-tuple-element.32), channel_id=1, source_target_pairs={{4,0},{8,4},{12,8},{16,12},{20,16},{24,20},{28,24},{32,28},{36,32}... | collective-permute-start | bytes 122888 | tf_op jit(solution)/shard_map/ppermute | solution.py:288
  93.3 0.0 collective-permute-done.4.refs_2_.low_ref
  93.3 0.0 copy-start.14
  93.3 3.6 %collective-permute-done.5.refs_3_.high_ref = f32[80,128]{1,0:T(8,128)S(1)} collective-permute-done((f32[80,128]{1,0:T(8,128)}, f32[80,128]{1,0:T(8,128)S(1)}, u32[]{:S(2)}, u32[]{:S(2)}) %collective-permute-start.5) | collective-permute-done | bytes 40992 | tf_op jit(solution)/shard_map/ppermute | solution.py:288
  96.9 0.0 copy-done.14
  96.9 0.6 copy-done.16
  97.5 1.6 %relay_late.1 = (f32[176,128]{1,0:T(8,128)}, f32[176,128]{1,0:T(8,128)}) custom-call(f32[32,8,128]{2,1,0:T(8,128)} %reshape.33.moments_ref.refs_0_, f32[32,128]{1,0:T(8,128)} %get-tuple-element.30.refs_1_.vectors_ref, f32[80,128]{1,0:T(8,128)} %copy-done.14, f32[80,128]{1,0:T(8,128)} %copy-done.16), custom_call_target="tpu_custom_call" | custom-call | tf_op jit(solution)/shard_map/relay_late/pallas_call | solution.py:266
  99.2 1.3 collective-permute-start.6
  100.5 1.3 collective-permute-start.7
  101.8 0.6 collective-permute-done.6.below_ref
  102.3 3.6 %collective-permute-done.7.above_ref = f32[176,128]{1,0:T(8,128)S(1)} collective-permute-done((f32[176,128]{1,0:T(8,128)}, f32[176,128]{1,0:T(8,128)S(1)}, u32[]{:S(2)}, u32[]{:S(2)}) %collective-permute-start.7) | collective-permute-done | bytes 90144 | tf_op jit(solution)/shard_map/ppermute | solution.py:288
  105.9 0.9 copy-done.1
  106.8 1.2 copy-done.4
  108.1 0.8 copy-done.15
  108.9 0.8 copy-done.17
  109.6 0.7 copy-done.21
  110.3 2.7 %krylov.1 = (f32[4,32,512]{2,1,0:T(8,128)S(1)}, f32[128,128]{1,0:T(8,128)S(1)}) custom-call(f32[32,8,128]{2,1,0:T(8,128)S(1)} %copy-done.1, f32[32,128]{1,0:T(8,128)S(1)} %copy-done.21, f32[80,128]{1,0:T(8,128)S(1)} %copy-done.15, f32[80,128]{1,0:T(8,128)S(1)} %copy-done.17, f32[176,128]{1,0:T(8,128)S(1)} %collective-permute-done.6.below_ref, ...), custom_call_target="tpu_custom_call" | custom-call | tf_op jit(solution)/shard_map/krylov/pallas_call | solution.py:397
  113.1 0.7 copy-done.9
  113.8 21.3 %all_to_all.16 = f32[128,1,128]{2,1,0:T(1,128)} all-to-all(f32[128,1,128]{2,1,0:T(1,128)S(1)} %bitcast.31), channel_id=1, replica_groups=mesh['gx_0'=4,'gx_1'=4,'gx_2'=2,'gy'=4] {'gx_0','gx_1','gx_2','gy'}, dimensions={0} | all-to-all | bytes 131072 | tf_op jit(solution)/shard_map/all_to_all | solution.py:519
  135.1 2.1 %finish.1 = (f32[32,512]{1,0:T(8,128)}, f32[32,512]{1,0:T(8,128)}) custom-call(f32[128,128]{1,0:T(8,128)} %bitcast.36, f32[4,32,512]{2,1,0:T(8,128)} %copy-done.9), custom_call_target="tpu_custom_call" | custom-call | tf_op jit(solution)/shard_map/finish/pallas_call | solution.py:480
  (29 shorter events, 0.1 us)
Async XLA Ops:
  6.8 11.9 %copy-start.23 = (s32[32,4]{0,1:T(4,128)S(1)}, s32[32,4]{0,1:T(4,128)}, u32[]{:S(2)}) copy-start(s32[32,4]{0,1:T(4,128)} %param.9) | copy-start | bytes 1540
  6.8 12.1 %copy-start = (f32[32,32,512]{2,1,0:T(8,128)S(1)}, f32[32,32,512]{2,1,0:T(8,128)}, u32[]{:S(2)}) copy-start(f32[32,32,512]{2,1,0:T(8,128)} %feats_ref.5) | copy-start | bytes 6291460
  6.8 12.1 %copy-start.19 = (f32[32,512]{1,0:T(8,128)S(1)}, f32[32,512]{1,0:T(8,128)}, u32[]{:S(2)}) copy-start(f32[32,512]{1,0:T(8,128)} %reg_ref.3) | copy-start | bytes 196612
  6.8 57.4 %all-to-all-start = ((bf16[128,66,128]{2,1,0:T(8,128)(2,1)}), bf16[128,66,128]{2,1,0:T(8,128)(2,1)}, u32[]{:S(2)}, u32[]{:S(2)}) async-start(bf16[128,66,128]{2,1,0:T(8,128)(2,1)} %pack.1), calls=%async_computation | async-start | bytes 4718592 | tf_op jit(solution)/shard_map/all_to_all | solution.py:489
  31.4 1.2 copy-start.2
  32.7 13.5 %copy-start.5 = (f32[32,8,128]{2,1,0:T(8,128)}, f32[32,8,128]{2,1,0:T(8,128)S(1)}, u32[]{:S(2)}) copy-start(f32[32,8,128]{2,1,0:T(8,128)S(1)} %get-tuple-element.21.refs_0_.first_ref) | copy-start | bytes 393220
  32.7 13.5 %copy-start.7 = (f32[32,8,128]{2,1,0:T(8,128)}, f32[32,8,128]{2,1,0:T(8,128)S(1)}, u32[]{:S(2)}) copy-start(f32[32,8,128]{2,1,0:T(8,128)S(1)} %get-tuple-element.22.refs_1_.second_ref) | copy-start | bytes 393220
  32.7 11.1 %collective-permute-start = (f32[104,128]{1,0:T(8,128)S(1)}, f32[104,128]{1,0:T(8,128)S(1)}, u32[]{:S(2)}, u32[]{:S(2)}) collective-permute-start(f32[104,128]{1,0:T(8,128)S(1)} %pad_maximum_fusion), channel_id=1, source_target_pairs={{0,4},{4,8},{8,12},{12,16},{16,20},{20,24},{24,28},{28,32},{32,36}... | collective-permute-start | bytes 159752 | tf_op jit(solution)/shard_map/ppermute | solution.py:288
  36.4 9.8 %collective-permute-start.1 = (f32[104,128]{1,0:T(8,128)S(1)}, f32[104,128]{1,0:T(8,128)S(1)}, u32[]{:S(2)}, u32[]{:S(2)}) collective-permute-start(f32[104,128]{1,0:T(8,128)S(1)} %pad_maximum_fusion.1), channel_id=1, source_target_pairs={{4,0},{8,4},{12,8},{16,12},{20,16},{24,20},{28,24},{32,28},{36,32}... | collective-permute-start | bytes 159752 | tf_op jit(solution)/shard_map/ppermute | solution.py:288
  43.8 2.3 %copy-start.10 = (f32[104,128]{1,0:T(8,128)}, f32[104,128]{1,0:T(8,128)S(1)}, u32[]{:S(2)}) copy-start(f32[104,128]{1,0:T(8,128)S(1)} %collective-permute-done.refs_3_.low_ref) | copy-start | bytes 159748
  46.2 0.6 copy-start.12
  48.5 5.6 %collective-permute-start.2 = (f32[232,128]{1,0:T(8,128)}, f32[232,128]{1,0:T(8,128)S(1)}, u32[]{:S(2)}, u32[]{:S(2)}) collective-permute-start(f32[232,128]{1,0:T(8,128)} %get-tuple-element.23), channel_id=1, source_target_pairs={{0,1},{1,2},{2,3},{4,5},{5,6},{6,7},{8,9},{9,10},{10,11},{12,13},{... | collective-permute-start | bytes 356360 | tf_op jit(solution)/shard_map/ppermute | solution.py:288
  52.0 5.8 %collective-permute-start.3 = (f32[232,128]{1,0:T(8,128)}, f32[232,128]{1,0:T(8,128)S(1)}, u32[]{:S(2)}, u32[]{:S(2)}) collective-permute-start(f32[232,128]{1,0:T(8,128)} %get-tuple-element.24), channel_id=1, source_target_pairs={{1,0},{2,1},{3,2},{5,4},{6,5},{7,6},{9,8},{10,9},{11,10},{13,12},{... | collective-permute-start | bytes 356360 | tf_op jit(solution)/shard_map/ppermute | solution.py:288
  57.8 0.9 copy-start.6
  58.7 0.9 copy-start.8
  59.6 0.8 copy-start.11
  60.4 0.8 copy-start.13
  61.2 0.7 copy-start.18
  63.3 1.0 copy-start.3
  72.7 4.7 %copy-start.22 = (bf16[128,64,128]{0,2,1:T(8,128)(2,1)S(1)}, bf16[128,64,128]{0,2,1:T(8,128)(2,1)}, u32[]{:S(2)}) copy-start(bf16[128,64,128]{0,2,1:T(8,128)(2,1)} %copy.23) | copy-start | bytes 6291460
  79.5 26.5 %copy-start.20 = (f32[32,512]{1,0:T(8,128)S(1)}, f32[32,512]{1,0:T(8,128)}, u32[]{:S(2)}) copy-start(f32[32,512]{1,0:T(8,128)} %reg_ref.3) | copy-start | bytes 196612
  84.7 8.6 %collective-permute-start.4 = (f32[80,128]{1,0:T(8,128)}, f32[80,128]{1,0:T(8,128)S(1)}, u32[]{:S(2)}, u32[]{:S(2)}) collective-permute-start(f32[80,128]{1,0:T(8,128)} %get-tuple-element.31), channel_id=1, source_target_pairs={{0,4},{4,8},{8,12},{12,16},{16,20},{20,24},{24,28},{28,32},{32,36}... | collective-permute-start | bytes 122888 | tf_op jit(solution)/shard_map/ppermute | solution.py:288
  91.4 5.5 %collective-permute-start.5 = (f32[80,128]{1,0:T(8,128)}, f32[80,128]{1,0:T(8,128)S(1)}, u32[]{:S(2)}, u32[]{:S(2)}) collective-permute-start(f32[80,128]{1,0:T(8,128)} %get-tuple-element.32), channel_id=1, source_target_pairs={{4,0},{8,4},{12,8},{16,12},{20,16},{24,20},{28,24},{32,28},{36,32}... | collective-permute-start | bytes 122888 | tf_op jit(solution)/shard_map/ppermute | solution.py:288
  93.3 3.6 %copy-start.14 = (f32[80,128]{1,0:T(8,128)}, f32[80,128]{1,0:T(8,128)S(1)}, u32[]{:S(2)}) copy-start(f32[80,128]{1,0:T(8,128)S(1)} %collective-permute-done.4.refs_2_.low_ref) | copy-start | bytes 122884
  96.9 0.6 copy-start.16
  99.2 3.1 %collective-permute-start.6 = (f32[176,128]{1,0:T(8,128)}, f32[176,128]{1,0:T(8,128)S(1)}, u32[]{:S(2)}, u32[]{:S(2)}) collective-permute-start(f32[176,128]{1,0:T(8,128)} %get-tuple-element.33), channel_id=1, source_target_pairs={{0,1},{1,2},{2,3},{4,5},{5,6},{6,7},{8,9},{9,10},{10,11},{12,13},{... | collective-permute-start | bytes 270344 | tf_op jit(solution)/shard_map/ppermute | solution.py:288
  100.5 5.5 %collective-permute-start.7 = (f32[176,128]{1,0:T(8,128)}, f32[176,128]{1,0:T(8,128)S(1)}, u32[]{:S(2)}, u32[]{:S(2)}) collective-permute-start(f32[176,128]{1,0:T(8,128)} %get-tuple-element.34), channel_id=1, source_target_pairs={{1,0},{2,1},{3,2},{5,4},{6,5},{7,6},{9,8},{10,9},{11,10},{13,12},{... | collective-permute-start | bytes 270344 | tf_op jit(solution)/shard_map/ppermute | solution.py:288
  105.9 0.9 copy-start.1
  106.8 1.2 copy-start.4
  108.1 0.8 copy-start.15
  108.9 0.8 copy-start.17
  109.6 0.7 copy-start.21
  113.1 0.7 copy-start.9

commit v4 on v2

--- a/solution.py
+++ b/solution.py
@@ -288,31 +288,107 @@
     return lax.ppermute(to_high, axis, up), lax.ppermute(to_low, axis, down)
 
 
-def begin_kernel(moments_ref, gathered_ref, lanes_ref, vectors_ref, low_ref, high_ref):
-    values = jnp.concatenate(
-        [gathered_ref[...], jnp.zeros((LANES - gathered_ref.shape[0], FEAT), jnp.float32)], axis=0
-    )
-    values = jnp.concatenate([values, jnp.zeros((LANES, LANES - FEAT), jnp.float32)], axis=1).T[:FEAT, :]
-    applied = [times(lanes_ref.at[power], values) for power in range(3)]
-    vectors = jnp.concatenate([*applied, values], axis=0).T
-    vectors_ref[...] = vectors[: vectors_ref.shape[0], :]
-    depth = LATE[0][1] * BY
-    for k in range(depth):
-        low_ref[8 * k : 8 * k + 8, :] = moments_ref[k]
-        high_ref[8 * k : 8 * k + 8, :] = moments_ref[BX * BY - depth + k]
-    deep = LATE[1][1] * BY
-    blank = jnp.zeros((padded(deep) - deep, LANES), jnp.float32)
-    low_ref[8 * depth :, :] = jnp.concatenate([vectors[:deep], blank], axis=0)
-    high_ref[8 * depth :, :] = jnp.concatenate([vectors[BX * BY - deep : BX * BY], blank], axis=0)
-
-
-def begin(moments, gathered, lanes):
-    message = jax.ShapeDtypeStruct((message_rows(LATE, along_rows), LANES), jnp.float32)
+def moments_kernel(got_ref, lanes_ref, moments_ref, vectors_ref, low_ref, high_ref, turned, sums):
+    step = pl.program_id(0)
+    sources = got_ref.shape[0]
+
+    @pl.when(step == 0)
+    def _():
+        sums[...] = jnp.zeros_like(sums)
+
+    for group in range(sources // 4):
+        for half in range(2):
+            block = got_ref[4 * group : 4 * group + 4, half * FEAT : (half + 1) * FEAT, :]
+            turned[half, step * (sources // 4) + group] = block.reshape(LANES, LANES).T
+    for half in range(2):
+        total = sums[half]
+        for source in range(sources):
+            feats = got_ref[source, half * FEAT : (half + 1) * FEAT, :].astype(jnp.float32)
+            target = got_ref[source, 2 * FEAT : 2 * FEAT + 2, :].astype(jnp.float32)
+            total = total + feats * target[half : half + 1, :]
+        sums[half] = total
+
+    @pl.when(step == pl.num_programs(0) - 1)
+    def _():
+        groups = turned.shape[1]
+        row = lax.broadcasted_iota(jnp.int32, (1, 16, LANES), 1)
+        upper = (row < SLOTS).astype(jnp.float32).astype(jnp.bfloat16)
+        lower = (row >= SLOTS).astype(jnp.float32).astype(jnp.bfloat16)
+        lane_group = lax.broadcasted_iota(jnp.int32, (1, LANES), 1) // FEAT
+        for half in range(2):
+            for pair in range(8):
+                points = turned[half, :, 16 * pair : 16 * pair + 16, :]
+                left = points.reshape(groups * 16, LANES)
+                right = jnp.concatenate(
+                    [(points * upper).reshape(groups * 16, LANES), (points * lower).reshape(groups * 16, LANES)],
+                    axis=1,
+                )
+                product = lax.dot_general(
+                    left, right, (((0,), (0,)), ((), ())), preferred_element_type=jnp.float32
+                )
+                for k in range(2):
+                    square = product[:, k * LANES : (k + 1) * LANES]
+                    own = jnp.zeros((FEAT, LANES), jnp.float32)
+                    for q in range(4):
+                        own = own + jnp.where(lane_group == q, square[q * FEAT : (q + 1) * FEAT, :], 0.0)
+                    own = own + pltpu.roll(own, 64, 1)
+                    own = own + pltpu.roll(own, 32, 1)
+                    record = own[0:8, :]
+                    for q in range(1, 4):
+                        record = jnp.where(lane_group == q, own[8 * q : 8 * q + 8, :], record)
+                    moments_ref[half * 16 + 2 * pair + k] = record
+        point = lax.broadcasted_iota(jnp.int32, (LANES, LANES), 0) // SLOTS
+        lane = lax.broadcasted_iota(jnp.int32, (LANES, LANES), 1)
+        values = jnp.zeros((FEAT, LANES), jnp.float32)
+        for half in range(2):
+            spread = (lane == point + half * 16).astype(jnp.float32)
+            values = values + jnp.dot(
+                sums[half], spread, precision=HIGHEST, preferred_element_type=jnp.float32
+            )
+        applied = [times(lanes_ref.at[power], values) for power in range(3)]
+        vectors = jnp.concatenate([*applied, values], axis=0).T
+        vectors_ref[...] = vectors[: BX * BY, :]
+        depth = LATE[0][1] * BY
+        for k in range(depth):
+            low_ref[8 * k : 8 * k + 8, :] = moments_ref[k]
+            high_ref[8 * k : 8 * k + 8, :] = moments_ref[BX * BY - depth + k]
+        deep = LATE[1][1] * BY
+        blank = jnp.zeros((padded(deep) - deep, LANES), jnp.float32)
+        low_ref[8 * depth :, :] = jnp.concatenate([vectors[:deep], blank], axis=0)
+        high_ref[8 * depth :, :] = jnp.concatenate([vectors[BX * BY - deep : BX * BY], blank], axis=0)
+
+
+def find_moments(got, lanes):
+    devices, rows, _ = got.shape
+    steps = 4
+    bricks = BX * BY
+    message = message_rows(LATE, along_rows)
     return pl.pallas_call(
-        begin_kernel,
-        out_shape=(jax.ShapeDtypeStruct((gathered.shape[0], LANES), jnp.float32), message, message),
-        name="begin",
-    )(moments, gathered, lanes)
+        moments_kernel,
+        grid=(steps,),
+        in_specs=[
+            pl.BlockSpec((devices // steps, rows, LANES), lambda i: (i, 0, 0)),
+            pl.BlockSpec(lanes.shape, lambda i: (0, 0, 0)),
+        ],
+        out_specs=(
+            pl.BlockSpec((bricks, 8, LANES), lambda i: (0, 0, 0)),
+            pl.BlockSpec((bricks, LANES), lambda i: (0, 0)),
+            pl.BlockSpec((message, LANES), lambda i: (0, 0)),
+            pl.BlockSpec((message, LANES), lambda i: (0, 0)),
+        ),
+        out_shape=(
+            jax.ShapeDtypeStruct((bricks, 8, LANES), jnp.float32),
+            jax.ShapeDtypeStruct((bricks, LANES), jnp.float32),
+            jax.ShapeDtypeStruct((message, LANES), jnp.float32),
+            jax.ShapeDtypeStruct((message, LANES), jnp.float32),
+        ),
+        scratch_shapes=[
+            pltpu.VMEM((2, devices // 4, LANES, LANES), jnp.bfloat16),
+            pltpu.VMEM((2, FEAT, LANES), jnp.float32),
+        ],
+        compiler_params=pltpu.CompilerParams(vmem_limit_bytes=20 << 20),
+        name="moments",
+    )(got, lanes)
 
 
 def power_of_two(value):
@@ -496,17 +572,7 @@
     low, high = swap(*along_messages(EARLY, early), GX)
     below, above = swap(*relay(EARLY, early, low, high, "relay_early"), "gy")
     first_lanes, second_lanes, mask_lanes = gather_early(first, second, mask, (low, high, below, above))
-
-    got_feats = got[:, : 2 * feat_count].reshape(devices, 2, feat_count, local_bricks // 2, slots)
-    got_targets = got[:, 2 * feat_count :].reshape(devices, 2, local_bricks // 2, slots)
-    moments = jnp.einsum("shibc,shjbc->hbij", got_feats, got_feats, preferred_element_type=jnp.float32)
-    moments = moments.reshape(local_bricks, 4, 8, feat_count).transpose(0, 2, 1, 3)
-    moments = moments.reshape(local_bricks, 8, 4 * feat_count)
-    gathered = jnp.einsum(
-        "shbc,shibc->hbi", got_targets, got_feats, preferred_element_type=jnp.float32
-    ).reshape(local_bricks, feat_count)
-
-    vectors, to_low, to_high = begin(moments, gathered, lanes)
+    moments, vectors, to_low, to_high = find_moments(got, lanes)
     low, high = swap(to_low, to_high, GX)
     below, above = swap(*relay(LATE, (moments, vectors), low, high, "relay_late"), "gy")
     basis, message = krylov(

time: 125 us -> 114 us (0.912)
  matrix products: 9.02 us -> 0 us
  waiting for transfers between devices: 15.3 us -> 12.7 us
  Pallas kernels: 30.7 us -> 32.3 us
  local copies, waits for them, and re-layouts: 18.5 us -> 17 us
  blocking collectives: 18.5 us -> 20 us
    dot_general x2 -> x0, matrix products: 9.02 us -> none  [the longest x1 5.31 us: shards(): jnp.einsum('shibc,shjbc->hbij', got_feats, got_feats, preferred_element_t...]
    slice x4 -> x0, local copies, waits for them, and re-layouts: 8.41 us -> none  [the longest x2 7.3 us: shards(): got[:, :2 * feat_count]]
    unnamed x42 -> x48, local copies, waits for them, and re-layouts: 8.37 us -> 16.3 us
    pallas_call x1, Pallas kernels: 2.42 us -> 4.04 us  [find_moments(): pl.pallas_call(moments_kernel, grid=(steps,), in_specs=[pl.BlockSpec((dev...]
    all_to_all x1, blocking collectives: 18.5 us -> 20 us  [shards(): lax.all_to_all(message, GX_GY, split_axis=0, concat_axis=0, tiled=True)]
    ppermute x8, waiting for transfers between devices: 1.31 us -> 0.02 us  [swap(): return (lax.ppermute(to_high, axis, up), lax.ppermute(to_low, axis, down))]
    all_to_all x1, waiting for transfers between devices: 13.9 us -> 12.7 us  [shards(): lax.all_to_all(sending, GX_GY, split_axis=0, concat_axis=0, tiled=True)]
  transfers between devices with their start and end apart: 9 -> 9, of which waited for: 2 -> 1; matrix products, arithmetic and copies ran while one was open for 16% -> 1% of each run, Pallas kernels for 16% -> 19%
where the time goes in v4:
time: 114 us; the launch traced here: 113 us
  Pallas kernels  32.3 us (28%)
  starting transfers between devices  30.3 us (27%)
  blocking collectives  20 us (18%)
  local copies, waits for them, and re-layouts  17 us (15%)
  waiting for transfers between devices  12.7 us (11%)
    all_to_all x1, blocking collectives, shards(): lax.all_to_all(message, GX_GY, split_axis=0, concat_axis=0, tiled=True)  20 us
    ppermute x8, starting transfers between devices, swap(): return (lax.ppermute(to_high, axis, up), lax.ppermute(to_low, axis, down))  18.8 us
    unnamed x48, local copies, waits for them, and re-layouts  16.3 us
    all_to_all x1, waiting for transfers between devices, shards(): lax.all_to_all(sending, GX_GY, split_axis=0, concat_axis=0, tiled=True)  12.7 us
    pallas_call x1, Pallas kernels, prepare(): pl.pallas_call(prepare_kernel, out_shape=(record, record, record, jax.Sha...  12.6 us
    all_to_all x1, starting transfers between devices, shards(): lax.all_to_all(sending, GX_GY, split_axis=0, concat_axis=0, tiled=True)  11.5 us
    pallas_call x1, Pallas kernels, pack(): pl.pallas_call(pack_kernel, grid=(steps,), in_specs=[pl.BlockSpec((SLOTS,...  6.2 us
    pallas_call x1, Pallas kernels, find_moments(): pl.pallas_call(moments_kernel, grid=(steps,), in_specs=[pl.BlockSpec((dev...  4.04 us
  transfers between devices with their start and end apart: 9, of which 1 were waited for; matrix products, arithmetic and copies ran while one was open for 1% of the time, Pallas kernels for 19%

profile of v4, /device:TPU:1, one launch (start us, length us, event | category | flops | bytes accessed | tf_op | source)
XLA Modules:
  0.0 113.2 jit_solution(4295658672313161915)
XLA Ops:
  0.6 6.2 %pack.1 = bf16[128,66,128]{2,1,0:T(8,128)(2,1)} custom-call(s32[8,4096]{1,0:T(8,128)} %bitcast.17, bf16[32,32768]{1,0:T(8,128)(2,1)} %feats_ref.3, bf16[256,128]{1,0:T(8,128)(2,1)} %bitcast.18), custom_call_target="tpu_custom_call" | custom-call | tf_op jit(solution)/shard_map/pack/pallas_call | solution.py:164
  6.8 0.0 copy-start.23
  6.8 0.0 copy-start.20
  6.8 11.5 %all-to-all-start = ((bf16[128,66,128]{2,1,0:T(8,128)(2,1)}), bf16[128,66,128]{2,1,0:T(8,128)(2,1)S(1)}, u32[]{:S(2)}, u32[]{:S(2)}) async-start(bf16[128,66,128]{2,1,0:T(8,128)(2,1)} %pack.1), calls=%async_computation | async-start | bytes 4718592 | tf_op jit(solution)/shard_map/all_to_all | solution.py:565
  18.3 0.0 copy-done.23
  18.4 0.1 copy.11
  18.5 0.0 copy-done.20
  18.5 0.0 copy-start
  18.5 1.6 %copy-done = f32[32,32,512]{2,1,0:T(8,128)S(1)} copy-done((f32[32,32,512]{2,1,0:T(8,128)S(1)}, f32[32,32,512]{2,1,0:T(8,128)}, u32[]{:S(2)}) %copy-start) | copy-done | bytes 2097176
  20.1 12.6 %prepare.1 = (f32[32,8,128]{2,1,0:T(8,128)S(1)}, f32[32,8,128]{2,1,0:T(8,128)S(1)}, f32[32,8,128]{2,1,0:T(8,128)}, f32[3,1024,128]{2,1,0:T(8,128)S(1)}) custom-call(f32[32,32,512]{2,1,0:T(8,128)S(1)} %copy-done, f32[32,512]{1,0:T(8,128)S(1)} %copy-done.20), custom_call_target="tpu_custom_call" | custom-call | flops 600000000 | bytes 5000000 | tf_op jit(solution)/shard_map/prepare/pallas_call | solution.py:209
  32.6 0.0 copy-start.2
  32.6 1.1 %copy-done.2 = f32[3,1024,128]{2,1,0:T(8,128)} copy-done((f32[3,1024,128]{2,1,0:T(8,128)}, f32[3,1024,128]{2,1,0:T(8,128)S(1)}, u32[]{:S(2)}) %copy-start.2) | copy-done | bytes 1572888
  33.8 0.0 copy-start.4
  33.8 3.7 %collective-permute-start.4 = (f32[104,128]{1,0:T(8,128)S(1)}, f32[104,128]{1,0:T(8,128)S(1)}, u32[]{:S(2)}, u32[]{:S(2)}) collective-permute-start(f32[104,128]{1,0:T(8,128)S(1)} %pad_maximum_fusion), channel_id=1, source_target_pairs={{0,4},{4,8},{8,12},{12,16},{16,20},{20,24},{24,28},{28,32},{32,36}... | collective-permute-start | bytes 159752 | tf_op jit(solution)/shard_map/ppermute | solution.py:288
  37.5 1.9 %collective-permute-start.5 = (f32[104,128]{1,0:T(8,128)S(1)}, f32[104,128]{1,0:T(8,128)S(1)}, u32[]{:S(2)}, u32[]{:S(2)}) collective-permute-start(f32[104,128]{1,0:T(8,128)S(1)} %pad_maximum_fusion.1), channel_id=1, source_target_pairs={{4,0},{8,4},{12,8},{16,12},{20,16},{24,20},{28,24},{32,28},{36,32}... | collective-permute-start | bytes 159752 | tf_op jit(solution)/shard_map/ppermute | solution.py:288
  39.4 12.7 %all-to-all-done.got_ref = bf16[128,66,128]{2,1,0:T(8,128)(2,1)S(1)} async-done(((bf16[128,66,128]{2,1,0:T(8,128)(2,1)}), bf16[128,66,128]{2,1,0:T(8,128)(2,1)S(1)}, u32[]{:S(2)}, u32[]{:S(2)}) %all-to-all-start) | async-done | bytes 2162720 | tf_op jit(solution)/shard_map/all_to_all | solution.py:565
  52.1 1.4 %copy-done.3 = f32[3,1024,128]{2,1,0:T(8,128)S(1)} copy-done((f32[3,1024,128]{2,1,0:T(8,128)S(1)}, f32[3,1024,128]{2,1,0:T(8,128)}, u32[]{:S(2)}) %copy-start.3) | copy-done | bytes 1572888
  53.5 4.0 %moments.1 = (f32[32,8,128]{2,1,0:T(8,128)S(1)}, f32[32,128]{1,0:T(8,128)S(1)}, f32[80,128]{1,0:T(8,128)S(1)}, f32[80,128]{1,0:T(8,128)S(1)}) custom-call(bf16[128,66,128]{2,1,0:T(8,128)(2,1)S(1)} %all-to-all-done.got_ref, f32[3,1024,128]{2,1,0:T(8,128)S(1)} %copy-done.3), custom_call_target="tpu_custom_call" | custom-call | tf_op jit(solution)/shard_map/moments/pallas_call | solution.py:366
  57.6 0.0 copy-done.4
  57.6 0.0 copy-done.6
  57.6 0.0 copy-start.8
  57.6 0.6 copy-done.8
  58.3 2.6 %collective-permute-start = (f32[80,128]{1,0:T(8,128)S(1)}, f32[80,128]{1,0:T(8,128)S(1)}, u32[]{:S(2)}, u32[]{:S(2)}) collective-permute-start(f32[80,128]{1,0:T(8,128)S(1)} %get-tuple-element.21), channel_id=1, source_target_pairs={{0,4},{4,8},{8,12},{12,16},{16,20},{20,24},{24,28},{28,32},{32,36}... | collective-permute-start | bytes 122888 | tf_op jit(solution)/shard_map/ppermute | solution.py:288
  60.8 1.9 %collective-permute-start.1 = (f32[80,128]{1,0:T(8,128)S(1)}, f32[80,128]{1,0:T(8,128)S(1)}, u32[]{:S(2)}, u32[]{:S(2)}) collective-permute-start(f32[80,128]{1,0:T(8,128)S(1)} %get-tuple-element.22), channel_id=1, source_target_pairs={{4,0},{8,4},{12,8},{16,12},{20,16},{24,20},{28,24},{32,28},{36,32}... | collective-permute-start | bytes 122888 | tf_op jit(solution)/shard_map/ppermute | solution.py:288
  62.8 0.6 pad.4.refs_2_.mask_ref
  63.4 0.0 collective-permute-done.4.refs_3_.low_ref
  63.4 0.0 copy-done.21
  63.4 0.0 collective-permute-done.5.refs_4_.high_ref
  63.4 0.6 copy-done.11
  64.0 0.6 copy-done.13
  64.6 1.7 %relay_early.1 = (f32[232,128]{1,0:T(8,128)}, f32[232,128]{1,0:T(8,128)}) custom-call(f32[32,8,128]{2,1,0:T(8,128)} %copy-done.4, f32[32,8,128]{2,1,0:T(8,128)} %copy-done.6, f32[32,128]{1,0:T(8,128)} %pad.4.refs_2_.mask_ref, f32[104,128]{1,0:T(8,128)} %copy-done.11, f32[104,128]{1,0:T(8,128)} %copy-done.13), custom_call_target="tpu_custom_call" | custom-call | tf_op jit(solution)/shard_map/relay_early/pallas_call | solution.py:266
  66.4 2.2 %collective-permute-start.6 = (f32[232,128]{1,0:T(8,128)}, f32[232,128]{1,0:T(8,128)S(1)}, u32[]{:S(2)}, u32[]{:S(2)}) collective-permute-start(f32[232,128]{1,0:T(8,128)} %get-tuple-element.27), channel_id=1, source_target_pairs={{0,1},{1,2},{2,3},{4,5},{5,6},{6,7},{8,9},{9,10},{10,11},{12,13},{... | collective-permute-start | bytes 356360 | tf_op jit(solution)/shard_map/ppermute | solution.py:288
  68.6 1.3 %collective-permute-start.7 = (f32[232,128]{1,0:T(8,128)}, f32[232,128]{1,0:T(8,128)S(1)}, u32[]{:S(2)}, u32[]{:S(2)}) collective-permute-start(f32[232,128]{1,0:T(8,128)} %get-tuple-element.28), channel_id=1, source_target_pairs={{1,0},{2,1},{3,2},{5,4},{6,5},{7,6},{9,8},{10,9},{11,10},{13,12},{... | collective-permute-start | bytes 356360 | tf_op jit(solution)/shard_map/ppermute | solution.py:288
  69.9 0.0 collective-permute-done.refs_2_.low_ref
  69.9 0.0 copy-start.15
  69.9 0.0 collective-permute-done.1.refs_3_.high_ref
  69.9 0.0 copy-start.17
  69.9 0.6 copy-done.15
  70.5 0.0 copy-done.17
  70.5 1.6 %relay_late.1 = (f32[176,128]{1,0:T(8,128)}, f32[176,128]{1,0:T(8,128)}) custom-call(f32[32,8,128]{2,1,0:T(8,128)} %copy-done.8, f32[32,128]{1,0:T(8,128)} %copy-done.21, f32[80,128]{1,0:T(8,128)} %copy-done.15, f32[80,128]{1,0:T(8,128)} %copy-done.17), custom_call_target="tpu_custom_call" | custom-call | tf_op jit(solution)/shard_map/relay_late/pallas_call | solution.py:266
  72.2 4.0 %collective-permute-start.2 = (f32[176,128]{1,0:T(8,128)}, f32[176,128]{1,0:T(8,128)S(1)}, u32[]{:S(2)}, u32[]{:S(2)}) collective-permute-start(f32[176,128]{1,0:T(8,128)} %get-tuple-element.23), channel_id=1, source_target_pairs={{0,1},{1,2},{2,3},{4,5},{5,6},{6,7},{8,9},{9,10},{10,11},{12,13},{... | collective-permute-start | bytes 270344 | tf_op jit(solution)/shard_map/ppermute | solution.py:288
  76.1 1.3 %collective-permute-start.3 = (f32[176,128]{1,0:T(8,128)}, f32[176,128]{1,0:T(8,128)S(1)}, u32[]{:S(2)}, u32[]{:S(2)}) collective-permute-start(f32[176,128]{1,0:T(8,128)} %get-tuple-element.24), channel_id=1, source_target_pairs={{1,0},{2,1},{3,2},{5,4},{6,5},{7,6},{9,8},{10,9},{11,10},{13,12},{... | collective-permute-start | bytes 270344 | tf_op jit(solution)/shard_map/ppermute | solution.py:288
  77.4 0.0 collective-permute-done.6.below_ref
  77.4 0.0 collective-permute-done.7.above_ref
  77.5 0.0 copy-start.5
  77.5 0.9 copy-done.5
  78.4 0.9 copy-done.7
  79.3 0.8 copy-done.12
  80.1 0.8 copy-done.14
  80.9 0.7 copy-done.19
  81.6 1.3 %gather_early.1 = (f32[1024,256]{1,0:T(8,128)S(1)}, f32[1024,256]{1,0:T(8,128)S(1)}, f32[8,256]{1,0:T(8,128)S(1)}) custom-call(f32[32,8,128]{2,1,0:T(8,128)S(1)} %copy-done.5, f32[32,8,128]{2,1,0:T(8,128)S(1)} %copy-done.7, f32[32,128]{1,0:T(8,128)S(1)} %copy-done.19, f32[104,128]{1,0:T(8,128)S(1)} %copy-done.12, f32[104,128]{1,0:T(8,128)S(1)} %copy-done.14, ...), custom_call_target="tpu_custom_call" | custom-call | flops 2000000 | bytes 3000000 | tf_op jit(solution)/shard_map/gather_early/pallas_call | solution.py:245
  82.9 0.0 collective-permute-done.2.below_ref
  82.9 0.0 collective-permute-done.3.above_ref
  83.0 0.0 copy-start.1
  83.0 1.6 %copy-done.1 = f32[32,32,512]{2,1,0:T(8,128)S(1)} copy-done((f32[32,32,512]{2,1,0:T(8,128)S(1)}, f32[32,32,512]{2,1,0:T(8,128)}, u32[]{:S(2)}) %copy-start.1) | copy-done | bytes 2097176
  84.6 0.9 copy-done.9
  85.5 0.8 copy-done.16
  86.2 0.8 copy-done.18
  87.0 0.7 copy-done.22
  87.7 2.7 %krylov.1 = (f32[4,32,512]{2,1,0:T(8,128)S(1)}, f32[128,128]{1,0:T(8,128)S(1)}) custom-call(f32[32,8,128]{2,1,0:T(8,128)S(1)} %copy-done.9, f32[32,128]{1,0:T(8,128)S(1)} %copy-done.22, f32[80,128]{1,0:T(8,128)S(1)} %copy-done.16, f32[80,128]{1,0:T(8,128)S(1)} %copy-done.18, f32[176,128]{1,0:T(8,128)S(1)} %collective-permute-done.2.below_ref, ...), custom_call_target="tpu_custom_call" | custom-call | tf_op jit(solution)/shard_map/krylov/pallas_call | solution.py:473
  90.5 0.0 copy-start.10
  90.5 0.7 copy-done.10
  91.2 20.0 %all_to_all.16 = f32[128,1,128]{2,1,0:T(1,128)} all-to-all(f32[128,1,128]{2,1,0:T(1,128)S(1)} %bitcast.15), channel_id=1, replica_groups=mesh['gx_0'=4,'gx_1'=4,'gx_2'=2,'gy'=4] {'gx_0','gx_1','gx_2','gy'}, dimensions={0} | all-to-all | bytes 131072 | tf_op jit(solution)/shard_map/all_to_all | solution.py:582
  111.1 2.1 %finish.1 = (f32[32,512]{1,0:T(8,128)}, f32[32,512]{1,0:T(8,128)}) custom-call(f32[128,128]{1,0:T(8,128)} %bitcast.16, f32[4,32,512]{2,1,0:T(8,128)} %copy-done.10), custom_call_target="tpu_custom_call" | custom-call | tf_op jit(solution)/shard_map/finish/pallas_call | solution.py:556
  (21 shorter events, 0.1 us)
Async XLA Ops:
  6.8 11.5 %copy-start.23 = (s32[32,4]{0,1:T(4,128)S(1)}, s32[32,4]{0,1:T(4,128)}, u32[]{:S(2)}) copy-start(s32[32,4]{0,1:T(4,128)} %param.9) | copy-start | bytes 1540
  6.8 11.7 %copy-start.20 = (f32[32,512]{1,0:T(8,128)S(1)}, f32[32,512]{1,0:T(8,128)}, u32[]{:S(2)}) copy-start(f32[32,512]{1,0:T(8,128)} %reg_ref.3) | copy-start | bytes 196612
  6.8 45.3 %all-to-all-start = ((bf16[128,66,128]{2,1,0:T(8,128)(2,1)}), bf16[128,66,128]{2,1,0:T(8,128)(2,1)S(1)}, u32[]{:S(2)}, u32[]{:S(2)}) async-start(bf16[128,66,128]{2,1,0:T(8,128)(2,1)} %pack.1), calls=%async_computation | async-start | bytes 4718592 | tf_op jit(solution)/shard_map/all_to_all | solution.py:565
  18.5 1.6 %copy-start = (f32[32,32,512]{2,1,0:T(8,128)S(1)}, f32[32,32,512]{2,1,0:T(8,128)}, u32[]{:S(2)}) copy-start(f32[32,32,512]{2,1,0:T(8,128)} %feats_ref.5) | copy-start | bytes 6291460
  32.6 1.2 %copy-start.2 = (f32[3,1024,128]{2,1,0:T(8,128)}, f32[3,1024,128]{2,1,0:T(8,128)S(1)}, u32[]{:S(2)}) copy-start(f32[3,1024,128]{2,1,0:T(8,128)S(1)} %get-tuple-element.18.lanes_ref) | copy-start | bytes 4718596
  33.8 23.8 %copy-start.4 = (f32[32,8,128]{2,1,0:T(8,128)}, f32[32,8,128]{2,1,0:T(8,128)S(1)}, u32[]{:S(2)}) copy-start(f32[32,8,128]{2,1,0:T(8,128)S(1)} %get-tuple-element.25.refs_0_.first_ref) | copy-start | bytes 393220
  33.8 23.8 %copy-start.6 = (f32[32,8,128]{2,1,0:T(8,128)}, f32[32,8,128]{2,1,0:T(8,128)S(1)}, u32[]{:S(2)}) copy-start(f32[32,8,128]{2,1,0:T(8,128)S(1)} %get-tuple-element.26.refs_1_.second_ref) | copy-start | bytes 393220
  33.8 29.5 %collective-permute-start.4 = (f32[104,128]{1,0:T(8,128)S(1)}, f32[104,128]{1,0:T(8,128)S(1)}, u32[]{:S(2)}, u32[]{:S(2)}) collective-permute-start(f32[104,128]{1,0:T(8,128)S(1)} %pad_maximum_fusion), channel_id=1, source_target_pairs={{0,4},{4,8},{8,12},{12,16},{16,20},{20,24},{24,28},{28,32},{32,36}... | collective-permute-start | bytes 159752 | tf_op jit(solution)/shard_map/ppermute | solution.py:288
  37.5 25.9 %collective-permute-start.5 = (f32[104,128]{1,0:T(8,128)S(1)}, f32[104,128]{1,0:T(8,128)S(1)}, u32[]{:S(2)}, u32[]{:S(2)}) collective-permute-start(f32[104,128]{1,0:T(8,128)S(1)} %pad_maximum_fusion.1), channel_id=1, source_target_pairs={{4,0},{8,4},{12,8},{16,12},{20,16},{24,20},{28,24},{32,28},{36,32}... | collective-permute-start | bytes 159752 | tf_op jit(solution)/shard_map/ppermute | solution.py:288
  52.1 1.4 %copy-start.3 = (f32[3,1024,128]{2,1,0:T(8,128)S(1)}, f32[3,1024,128]{2,1,0:T(8,128)}, u32[]{:S(2)}) copy-start(f32[3,1024,128]{2,1,0:T(8,128)} %copy-done.2) | copy-start | bytes 4718596
  57.6 0.7 copy-start.8
  58.3 5.1 %copy-start.21 = (f32[32,128]{1,0:T(8,128)}, f32[32,128]{1,0:T(8,128)S(1)}, u32[]{:S(2)}) copy-start(f32[32,128]{1,0:T(8,128)S(1)} %get-tuple-element.20.refs_1_.vectors_ref) | copy-start | bytes 49156
  58.3 11.6 %collective-permute-start = (f32[80,128]{1,0:T(8,128)S(1)}, f32[80,128]{1,0:T(8,128)S(1)}, u32[]{:S(2)}, u32[]{:S(2)}) collective-permute-start(f32[80,128]{1,0:T(8,128)S(1)} %get-tuple-element.21), channel_id=1, source_target_pairs={{0,4},{4,8},{8,12},{12,16},{16,20},{20,24},{24,28},{28,32},{32,36}... | collective-permute-start | bytes 122888 | tf_op jit(solution)/shard_map/ppermute | solution.py:288
  60.8 9.0 %collective-permute-start.1 = (f32[80,128]{1,0:T(8,128)S(1)}, f32[80,128]{1,0:T(8,128)S(1)}, u32[]{:S(2)}, u32[]{:S(2)}) collective-permute-start(f32[80,128]{1,0:T(8,128)S(1)} %get-tuple-element.22), channel_id=1, source_target_pairs={{4,0},{8,4},{12,8},{16,12},{20,16},{24,20},{28,24},{32,28},{36,32}... | collective-permute-start | bytes 122888 | tf_op jit(solution)/shard_map/ppermute | solution.py:288
  63.4 0.6 copy-start.11
  64.0 0.6 copy-start.13
  66.4 11.1 %collective-permute-start.6 = (f32[232,128]{1,0:T(8,128)}, f32[232,128]{1,0:T(8,128)S(1)}, u32[]{:S(2)}, u32[]{:S(2)}) collective-permute-start(f32[232,128]{1,0:T(8,128)} %get-tuple-element.27), channel_id=1, source_target_pairs={{0,1},{1,2},{2,3},{4,5},{5,6},{6,7},{8,9},{9,10},{10,11},{12,13},{... | collective-permute-start | bytes 356360 | tf_op jit(solution)/shard_map/ppermute | solution.py:288
  68.6 8.9 %collective-permute-start.7 = (f32[232,128]{1,0:T(8,128)}, f32[232,128]{1,0:T(8,128)S(1)}, u32[]{:S(2)}, u32[]{:S(2)}) collective-permute-start(f32[232,128]{1,0:T(8,128)} %get-tuple-element.28), channel_id=1, source_target_pairs={{1,0},{2,1},{3,2},{5,4},{6,5},{7,6},{9,8},{10,9},{11,10},{13,12},{... | collective-permute-start | bytes 356360 | tf_op jit(solution)/shard_map/ppermute | solution.py:288
  69.9 0.6 copy-start.15
  69.9 0.6 copy-start.17
  72.2 10.8 %collective-permute-start.2 = (f32[176,128]{1,0:T(8,128)}, f32[176,128]{1,0:T(8,128)S(1)}, u32[]{:S(2)}, u32[]{:S(2)}) collective-permute-start(f32[176,128]{1,0:T(8,128)} %get-tuple-element.23), channel_id=1, source_target_pairs={{0,1},{1,2},{2,3},{4,5},{5,6},{6,7},{8,9},{9,10},{10,11},{12,13},{... | collective-permute-start | bytes 270344 | tf_op jit(solution)/shard_map/ppermute | solution.py:288
  76.1 6.8 %collective-permute-start.3 = (f32[176,128]{1,0:T(8,128)}, f32[176,128]{1,0:T(8,128)S(1)}, u32[]{:S(2)}, u32[]{:S(2)}) collective-permute-start(f32[176,128]{1,0:T(8,128)} %get-tuple-element.24), channel_id=1, source_target_pairs={{1,0},{2,1},{3,2},{5,4},{6,5},{7,6},{9,8},{10,9},{11,10},{13,12},{... | collective-permute-start | bytes 270344 | tf_op jit(solution)/shard_map/ppermute | solution.py:288
  77.5 0.9 copy-start.5
  78.4 0.9 copy-start.7
  79.3 0.8 copy-start.12
  80.1 0.8 copy-start.14
  80.9 0.7 copy-start.19
  83.0 1.6 %copy-start.1 = (f32[32,32,512]{2,1,0:T(8,128)S(1)}, f32[32,32,512]{2,1,0:T(8,128)}, u32[]{:S(2)}) copy-start(f32[32,32,512]{2,1,0:T(8,128)} %feats_ref.5) | copy-start | bytes 6291460
  84.5 0.9 copy-start.9
  85.5 0.8 copy-start.16
  86.2 0.8 copy-start.18
  87.0 0.7 copy-start.22
  90.5 0.7 copy-start.10

commit v5 on v4

--- a/solution.py
+++ b/solution.py
@@ -209,7 +209,7 @@
     return pl.pallas_call(
         prepare_kernel,
         out_shape=(record, record, record, jax.ShapeDtypeStruct((3, 8 * LANES, LANES), jnp.float32)),
-        compiler_params=pltpu.CompilerParams(vmem_limit_bytes=24 << 20),
+        compiler_params=pltpu.CompilerParams(vmem_limit_bytes=10 << 20),
         cost_estimate=pl.CostEstimate(flops=600_000_000, bytes_accessed=5_000_000, transcendentals=0),
         name="prepare",
     )(voxel_feats, voxel_reg)
@@ -250,7 +250,7 @@
             pltpu.VMEM((SPAN, 8, LANES), jnp.float32),
             pltpu.VMEM((SPAN, LANES), jnp.float32),
         ],
-        compiler_params=pltpu.CompilerParams(vmem_limit_bytes=24 << 20),
+        compiler_params=pltpu.CompilerParams(vmem_limit_bytes=10 << 20),
         cost_estimate=pl.CostEstimate(flops=2_000_000, bytes_accessed=3_000_000, transcendentals=0),
         name="gather_early",
     )(first, second, mask, *edges)
@@ -266,6 +266,7 @@
     return pl.pallas_call(
         functools.partial(relay_kernel, sections, len(owns)),
         out_shape=(out, out),
+        compiler_params=pltpu.CompilerParams(vmem_limit_bytes=4 << 20),
         name=name,
     )(*owns, low, high)
 
@@ -386,7 +387,7 @@
             pltpu.VMEM((2, devices // 4, LANES, LANES), jnp.bfloat16),
             pltpu.VMEM((2, FEAT, LANES), jnp.float32),
         ],
-        compiler_params=pltpu.CompilerParams(vmem_limit_bytes=20 << 20),
+        compiler_params=pltpu.CompilerParams(vmem_limit_bytes=12 << 20),
         name="moments",
     )(got, lanes)
 
@@ -481,7 +482,7 @@
             pltpu.VMEM((SPAN, LANES), jnp.float32),
             pltpu.VMEM((8 * LANES, SPAN), jnp.float32),
         ],
-        compiler_params=pltpu.CompilerParams(vmem_limit_bytes=32 << 20),
+        compiler_params=pltpu.CompilerParams(vmem_limit_bytes=12 << 20),
         name="krylov",
     )(moments, vectors, *edges, first, second, masks, voxel_feats, voxel_reg)
 
@@ -553,7 +554,12 @@
 def finish(shared, basis):
     _, bricks, voxels = basis.shape
     out = jax.ShapeDtypeStruct((bricks, voxels), jnp.float32)
-    return pl.pallas_call(finish_kernel, out_shape=(out, out), name="finish")(shared, basis)
+    return pl.pallas_call(
+        finish_kernel,
+        out_shape=(out, out),
+        compiler_params=pltpu.CompilerParams(vmem_limit_bytes=4 << 20),
+        name="finish",
+    )(shared, basis)
 
 
 def shards(point_feats, point_targets, point_lists, brick_adjacency, voxel_feats, voxel_reg):

time: 114 us -> 98.4 us (0.86)
  local copies, waits for them, and re-layouts: 17 us -> 4.26 us
  Pallas kernels: 32.3 us -> 28 us
  waiting for transfers between devices: 12.7 us -> 16.2 us
  blocking collectives: 20 us -> 18.2 us
    unnamed x48 -> x12, local copies, waits for them, and re-layouts: 16.3 us -> 4.16 us
    ppermute x8, waiting for transfers between devices: 0.02 us -> 3.47 us  [swap(): return (lax.ppermute(to_high, axis, up), lax.ppermute(to_low, axis, down))]
    pallas_call x2, Pallas kernels: 3.37 us -> 0.06 us  [relay(): pl.pallas_call(functools.partial(relay_kernel, sections, len(owns)), out_...]
    all_to_all x1, blocking collectives: 20 us -> 18.2 us  [shards(): lax.all_to_all(message, GX_GY, split_axis=0, concat_axis=0, tiled=True)]
  transfers between devices with their start and end apart: 9 -> 9, of which waited for: 1 -> 3; matrix products, arithmetic and copies ran while one was open for 1% -> 0% of each run, Pallas kernels for 19% -> 18%
where the time goes in v5:
time: 98.4 us; the launch traced here: 97.8 us
  starting transfers between devices  30.4 us (31%)
  Pallas kernels  28 us (28%)
  blocking collectives  18.2 us (18%)
  waiting for transfers between devices  16.2 us (16%)
  local copies, waits for them, and re-layouts  4.26 us (4%)
    ppermute x8, starting transfers between devices, swap(): return (lax.ppermute(to_high, axis, up), lax.ppermute(to_low, axis, down))  18.9 us
    all_to_all x1, blocking collectives, shards(): lax.all_to_all(message, GX_GY, split_axis=0, concat_axis=0, tiled=True)  18.2 us
    all_to_all x1, waiting for transfers between devices, shards(): lax.all_to_all(sending, GX_GY, split_axis=0, concat_axis=0, tiled=True)  12.7 us
    pallas_call x1, Pallas kernels, prepare(): pl.pallas_call(prepare_kernel, out_shape=(record, record, record, jax.Sha...  12.5 us
    all_to_all x1, starting transfers between devices, shards(): lax.all_to_all(sending, GX_GY, split_axis=0, concat_axis=0, tiled=True)  11.5 us
    pallas_call x1, Pallas kernels, pack(): pl.pallas_call(pack_kernel, grid=(steps,), in_specs=[pl.BlockSpec((SLOTS,...  6.19 us
    unnamed x12, local copies, waits for them, and re-layouts  4.16 us
    pallas_call x1, Pallas kernels, find_moments(): pl.pallas_call(moments_kernel, grid=(steps,), in_specs=[pl.BlockSpec((dev...  4.04 us
  transfers between devices with their start and end apart: 9, of which 3 were waited for; matrix products, arithmetic and copies ran while one was open for 0% of the time, Pallas kernels for 18%

profile of v5, /device:TPU:1, one launch (start us, length us, event | category | flops | bytes accessed | tf_op | source)
XLA Modules:
  0.0 97.8 jit_solution(10196262424678057669)
XLA Ops:
  0.6 6.2 %pack.1 = bf16[128,66,128]{2,1,0:T(8,128)(2,1)} custom-call(s32[8,4096]{1,0:T(8,128)} %bitcast.17, bf16[32,32768]{1,0:T(8,128)(2,1)} %feats_ref.3, bf16[256,128]{1,0:T(8,128)(2,1)} %bitcast.18), custom_call_target="tpu_custom_call" | custom-call | tf_op jit(solution)/shard_map/pack/pallas_call | solution.py:164
  6.8 0.0 copy-start.5
  6.8 0.0 copy-start.4
  6.8 11.5 %all-to-all-start = ((bf16[128,66,128]{2,1,0:T(8,128)(2,1)}), bf16[128,66,128]{2,1,0:T(8,128)(2,1)S(1)}, u32[]{:S(2)}, u32[]{:S(2)}) async-start(bf16[128,66,128]{2,1,0:T(8,128)(2,1)} %pack.1), calls=%async_computation | async-start | bytes 4718592 | tf_op jit(solution)/shard_map/all_to_all | solution.py:571
  18.3 0.0 copy-done.5
  18.4 0.1 copy.11
  18.5 0.0 copy-done.4
  18.5 0.0 copy-start
  18.5 1.6 %copy-done = f32[32,32,512]{2,1,0:T(8,128)S(1)} copy-done((f32[32,32,512]{2,1,0:T(8,128)S(1)}, f32[32,32,512]{2,1,0:T(8,128)}, u32[]{:S(2)}) %copy-start) | copy-done | bytes 2097176
  20.1 12.5 %prepare.1 = (f32[32,8,128]{2,1,0:T(8,128)S(1)}, f32[32,8,128]{2,1,0:T(8,128)S(1)}, f32[32,8,128]{2,1,0:T(8,128)}, f32[3,1024,128]{2,1,0:T(8,128)S(1)}) custom-call(f32[32,32,512]{2,1,0:T(8,128)S(1)} %copy-done, f32[32,512]{1,0:T(8,128)S(1)} %copy-done.4), custom_call_target="tpu_custom_call" | custom-call | flops 600000000 | bytes 5000000 | tf_op jit(solution)/shard_map/prepare/pallas_call | solution.py:209
  32.6 0.0 copy-start.2
  32.6 1.1 %copy-done.2 = f32[3,1024,128]{2,1,0:T(8,128)} copy-done((f32[3,1024,128]{2,1,0:T(8,128)}, f32[3,1024,128]{2,1,0:T(8,128)S(1)}, u32[]{:S(2)}) %copy-start.2) | copy-done | bytes 1572888
  33.8 3.7 %collective-permute-start.4 = (f32[104,128]{1,0:T(8,128)S(1)}, f32[104,128]{1,0:T(8,128)S(1)}, u32[]{:S(2)}, u32[]{:S(2)}) collective-permute-start(f32[104,128]{1,0:T(8,128)S(1)} %pad_maximum_fusion), channel_id=1, source_target_pairs={{0,4},{4,8},{8,12},{12,16},{16,20},{20,24},{24,28},{28,32},{32,36}... | collective-permute-start | bytes 159752 | tf_op jit(solution)/shard_map/ppermute | solution.py:289
  37.5 1.9 %collective-permute-start.5 = (f32[104,128]{1,0:T(8,128)S(1)}, f32[104,128]{1,0:T(8,128)S(1)}, u32[]{:S(2)}, u32[]{:S(2)}) collective-permute-start(f32[104,128]{1,0:T(8,128)S(1)} %pad_maximum_fusion.1), channel_id=1, source_target_pairs={{4,0},{8,4},{12,8},{16,12},{20,16},{24,20},{28,24},{32,28},{36,32}... | collective-permute-start | bytes 159752 | tf_op jit(solution)/shard_map/ppermute | solution.py:289
  39.4 12.7 %all-to-all-done.got_ref = bf16[128,66,128]{2,1,0:T(8,128)(2,1)S(1)} async-done(((bf16[128,66,128]{2,1,0:T(8,128)(2,1)}), bf16[128,66,128]{2,1,0:T(8,128)(2,1)S(1)}, u32[]{:S(2)}, u32[]{:S(2)}) %all-to-all-start) | async-done | bytes 2162720 | tf_op jit(solution)/shard_map/all_to_all | solution.py:571
  52.1 0.0 copy-start.3
  52.1 1.4 %copy-done.3 = f32[3,1024,128]{2,1,0:T(8,128)S(1)} copy-done((f32[3,1024,128]{2,1,0:T(8,128)S(1)}, f32[3,1024,128]{2,1,0:T(8,128)}, u32[]{:S(2)}) %copy-start.3) | copy-done | bytes 1572888
  53.5 0.0 copy-start.1
  53.5 4.0 %moments.1 = (f32[32,8,128]{2,1,0:T(8,128)S(1)}, f32[32,128]{1,0:T(8,128)S(1)}, f32[80,128]{1,0:T(8,128)S(1)}, f32[80,128]{1,0:T(8,128)S(1)}) custom-call(bf16[128,66,128]{2,1,0:T(8,128)(2,1)S(1)} %all-to-all-done.got_ref, f32[3,1024,128]{2,1,0:T(8,128)S(1)} %copy-done.3), custom_call_target="tpu_custom_call" | custom-call | tf_op jit(solution)/shard_map/moments/pallas_call | solution.py:367
  57.6 2.6 %collective-permute-start = (f32[80,128]{1,0:T(8,128)S(1)}, f32[80,128]{1,0:T(8,128)S(1)}, u32[]{:S(2)}, u32[]{:S(2)}) collective-permute-start(f32[80,128]{1,0:T(8,128)S(1)} %get-tuple-element.21), channel_id=1, source_target_pairs={{0,4},{4,8},{8,12},{12,16},{16,20},{20,24},{24,28},{28,32},{32,36}... | collective-permute-start | bytes 122888 | tf_op jit(solution)/shard_map/ppermute | solution.py:289
  60.2 1.9 %collective-permute-start.1 = (f32[80,128]{1,0:T(8,128)S(1)}, f32[80,128]{1,0:T(8,128)S(1)}, u32[]{:S(2)}, u32[]{:S(2)}) collective-permute-start(f32[80,128]{1,0:T(8,128)S(1)} %get-tuple-element.22), channel_id=1, source_target_pairs={{4,0},{8,4},{12,8},{16,12},{20,16},{24,20},{28,24},{32,28},{36,32}... | collective-permute-start | bytes 122888 | tf_op jit(solution)/shard_map/ppermute | solution.py:289
  62.1 0.0 collective-permute-done.4.refs_3_.low_ref
  62.1 0.0 collective-permute-done.5.refs_4_.high_ref
  62.2 2.2 %collective-permute-start.6 = (f32[232,128]{1,0:T(8,128)S(1)}, f32[232,128]{1,0:T(8,128)S(1)}, u32[]{:S(2)}, u32[]{:S(2)}) collective-permute-start(f32[232,128]{1,0:T(8,128)S(1)} %get-tuple-element.27), channel_id=1, source_target_pairs={{0,1},{1,2},{2,3},{4,5},{5,6},{6,7},{8,9},{9,10},{10,11},{12,13},{... | collective-permute-start | bytes 356360 | tf_op jit(solution)/shard_map/ppermute | solution.py:289
  64.4 1.3 %collective-permute-start.7 = (f32[232,128]{1,0:T(8,128)S(1)}, f32[232,128]{1,0:T(8,128)S(1)}, u32[]{:S(2)}, u32[]{:S(2)}) collective-permute-start(f32[232,128]{1,0:T(8,128)S(1)} %get-tuple-element.28), channel_id=1, source_target_pairs={{1,0},{2,1},{3,2},{5,4},{6,5},{7,6},{9,8},{10,9},{11,10},{13,12},{... | collective-permute-start | bytes 356360 | tf_op jit(solution)/shard_map/ppermute | solution.py:289
  65.7 0.0 collective-permute-done.refs_2_.low_ref
  65.7 0.0 collective-permute-done.1.refs_3_.high_ref
  65.8 4.0 %collective-permute-start.2 = (f32[176,128]{1,0:T(8,128)S(1)}, f32[176,128]{1,0:T(8,128)S(1)}, u32[]{:S(2)}, u32[]{:S(2)}) collective-permute-start(f32[176,128]{1,0:T(8,128)S(1)} %get-tuple-element.23), channel_id=1, source_target_pairs={{0,1},{1,2},{2,3},{4,5},{5,6},{6,7},{8,9},{9,10},{10,11},{12,13},{... | collective-permute-start | bytes 270344 | tf_op jit(solution)/shard_map/ppermute | solution.py:289
  69.8 1.3 %collective-permute-start.3 = (f32[176,128]{1,0:T(8,128)S(1)}, f32[176,128]{1,0:T(8,128)S(1)}, u32[]{:S(2)}, u32[]{:S(2)}) collective-permute-start(f32[176,128]{1,0:T(8,128)S(1)} %get-tuple-element.24), channel_id=1, source_target_pairs={{1,0},{2,1},{3,2},{5,4},{6,5},{7,6},{9,8},{10,9},{11,10},{13,12},{... | collective-permute-start | bytes 270344 | tf_op jit(solution)/shard_map/ppermute | solution.py:289
  71.1 0.0 collective-permute-done.6.below_ref
  71.1 0.4 collective-permute-done.7.above_ref
  71.4 1.3 %gather_early.1 = (f32[1024,256]{1,0:T(8,128)S(1)}, f32[1024,256]{1,0:T(8,128)S(1)}, f32[8,256]{1,0:T(8,128)S(1)}) custom-call(f32[32,8,128]{2,1,0:T(8,128)S(1)} %get-tuple-element.25.refs_0_.first_ref, f32[32,8,128]{2,1,0:T(8,128)S(1)} %get-tuple-element.26.refs_1_.second_ref, f32[32,128]{1,0:T(8,128)S(1)} %pad.4.refs_2_.mask_ref, ...), custom_call_target="tpu_custom_call" | custom-call | flops 2000000 | bytes 3000000 | tf_op jit(solution)/shard_map/gather_early/pallas_call | solution.py:245
  72.8 0.0 collective-permute-done.2.below_ref
  72.8 3.1 %collective-permute-done.3.above_ref = f32[176,128]{1,0:T(8,128)S(1)} collective-permute-done((f32[176,128]{1,0:T(8,128)S(1)}, f32[176,128]{1,0:T(8,128)S(1)}, u32[]{:S(2)}, u32[]{:S(2)}) %collective-permute-start.3) | collective-permute-done | bytes 90144 | tf_op jit(solution)/shard_map/ppermute | solution.py:289
  75.9 0.0 copy-done.1
  75.9 2.7 %krylov.1 = (f32[4,32,512]{2,1,0:T(8,128)S(1)}, f32[128,128]{1,0:T(8,128)S(1)}) custom-call(f32[32,8,128]{2,1,0:T(8,128)S(1)} %get-tuple-element.19.refs_0_.moments_ref, f32[32,128]{1,0:T(8,128)S(1)} %get-tuple-element.20.refs_1_.vectors_ref, f32[80,128]{1,0:T(8,128)S(1)} %collective-permute-done.refs_2_.low_ref, ...), custom_call_target="tpu_custom_call" | custom-call | tf_op jit(solution)/shard_map/krylov/pallas_call | solution.py:474
  78.6 18.2 %all_to_all.16 = f32[128,1,128]{2,1,0:T(1,128)S(1)} all-to-all(f32[128,1,128]{2,1,0:T(1,128)S(1)} %bitcast.16), channel_id=1, replica_groups=mesh['gx_0'=4,'gx_1'=4,'gx_2'=2,'gy'=4] {'gx_0','gx_1','gx_2','gy'}, dimensions={0} | all-to-all | bytes 131072 | tf_op jit(solution)/shard_map/all_to_all | solution.py:588
  96.7 1.1 %finish.1 = (f32[32,512]{1,0:T(8,128)}, f32[32,512]{1,0:T(8,128)}) custom-call(f32[128,128]{1,0:T(8,128)S(1)} %bitcast.15, f32[4,32,512]{2,1,0:T(8,128)S(1)} %get-tuple-element.33.basis_ref), custom_call_target="tpu_custom_call" | custom-call | tf_op jit(solution)/shard_map/finish/pallas_call | solution.py:557
  (11 shorter events, 0.1 us)
Async XLA Ops:
  6.8 11.5 %copy-start.5 = (s32[32,4]{0,1:T(4,128)S(1)}, s32[32,4]{0,1:T(4,128)}, u32[]{:S(2)}) copy-start(s32[32,4]{0,1:T(4,128)} %param.9) | copy-start | bytes 1540
  6.8 11.7 %copy-start.4 = (f32[32,512]{1,0:T(8,128)S(1)}, f32[32,512]{1,0:T(8,128)}, u32[]{:S(2)}) copy-start(f32[32,512]{1,0:T(8,128)} %reg_ref.3) | copy-start | bytes 196612
  6.8 45.3 %all-to-all-start = ((bf16[128,66,128]{2,1,0:T(8,128)(2,1)}), bf16[128,66,128]{2,1,0:T(8,128)(2,1)S(1)}, u32[]{:S(2)}, u32[]{:S(2)}) async-start(bf16[128,66,128]{2,1,0:T(8,128)(2,1)} %pack.1), calls=%async_computation | async-start | bytes 4718592 | tf_op jit(solution)/shard_map/all_to_all | solution.py:571
  18.5 1.6 %copy-start = (f32[32,32,512]{2,1,0:T(8,128)S(1)}, f32[32,32,512]{2,1,0:T(8,128)}, u32[]{:S(2)}) copy-start(f32[32,32,512]{2,1,0:T(8,128)} %feats_ref.5) | copy-start | bytes 6291460
  32.6 1.1 %copy-start.2 = (f32[3,1024,128]{2,1,0:T(8,128)}, f32[3,1024,128]{2,1,0:T(8,128)S(1)}, u32[]{:S(2)}) copy-start(f32[3,1024,128]{2,1,0:T(8,128)S(1)} %get-tuple-element.18.lanes_ref) | copy-start | bytes 4718596
  33.8 28.3 %collective-permute-start.4 = (f32[104,128]{1,0:T(8,128)S(1)}, f32[104,128]{1,0:T(8,128)S(1)}, u32[]{:S(2)}, u32[]{:S(2)}) collective-permute-start(f32[104,128]{1,0:T(8,128)S(1)} %pad_maximum_fusion), channel_id=1, source_target_pairs={{0,4},{4,8},{8,12},{12,16},{16,20},{20,24},{24,28},{28,32},{32,36}... | collective-permute-start | bytes 159752 | tf_op jit(solution)/shard_map/ppermute | solution.py:289
  37.5 24.7 %collective-permute-start.5 = (f32[104,128]{1,0:T(8,128)S(1)}, f32[104,128]{1,0:T(8,128)S(1)}, u32[]{:S(2)}, u32[]{:S(2)}) collective-permute-start(f32[104,128]{1,0:T(8,128)S(1)} %pad_maximum_fusion.1), channel_id=1, source_target_pairs={{4,0},{8,4},{12,8},{16,12},{20,16},{24,20},{28,24},{32,28},{36,32}... | collective-permute-start | bytes 159752 | tf_op jit(solution)/shard_map/ppermute | solution.py:289
  52.1 1.4 %copy-start.3 = (f32[3,1024,128]{2,1,0:T(8,128)S(1)}, f32[3,1024,128]{2,1,0:T(8,128)}, u32[]{:S(2)}) copy-start(f32[3,1024,128]{2,1,0:T(8,128)} %copy-done.2) | copy-start | bytes 4718596
  53.5 22.3 %copy-start.1 = (f32[32,32,512]{2,1,0:T(8,128)S(1)}, f32[32,32,512]{2,1,0:T(8,128)}, u32[]{:S(2)}) copy-start(f32[32,32,512]{2,1,0:T(8,128)} %feats_ref.5) | copy-start | bytes 6291460
  57.6 8.1 %collective-permute-start = (f32[80,128]{1,0:T(8,128)S(1)}, f32[80,128]{1,0:T(8,128)S(1)}, u32[]{:S(2)}, u32[]{:S(2)}) collective-permute-start(f32[80,128]{1,0:T(8,128)S(1)} %get-tuple-element.21), channel_id=1, source_target_pairs={{0,4},{4,8},{8,12},{12,16},{16,20},{20,24},{24,28},{28,32},{32,36}... | collective-permute-start | bytes 122888 | tf_op jit(solution)/shard_map/ppermute | solution.py:289
  60.2 5.5 %collective-permute-start.1 = (f32[80,128]{1,0:T(8,128)S(1)}, f32[80,128]{1,0:T(8,128)S(1)}, u32[]{:S(2)}, u32[]{:S(2)}) collective-permute-start(f32[80,128]{1,0:T(8,128)S(1)} %get-tuple-element.22), channel_id=1, source_target_pairs={{4,0},{8,4},{12,8},{16,12},{20,16},{24,20},{28,24},{32,28},{36,32}... | collective-permute-start | bytes 122888 | tf_op jit(solution)/shard_map/ppermute | solution.py:289
  62.2 8.9 %collective-permute-start.6 = (f32[232,128]{1,0:T(8,128)S(1)}, f32[232,128]{1,0:T(8,128)S(1)}, u32[]{:S(2)}, u32[]{:S(2)}) collective-permute-start(f32[232,128]{1,0:T(8,128)S(1)} %get-tuple-element.27), channel_id=1, source_target_pairs={{0,1},{1,2},{2,3},{4,5},{5,6},{6,7},{8,9},{9,10},{10,11},{12,13},{... | collective-permute-start | bytes 356360 | tf_op jit(solution)/shard_map/ppermute | solution.py:289
  64.4 7.0 %collective-permute-start.7 = (f32[232,128]{1,0:T(8,128)S(1)}, f32[232,128]{1,0:T(8,128)S(1)}, u32[]{:S(2)}, u32[]{:S(2)}) collective-permute-start(f32[232,128]{1,0:T(8,128)S(1)} %get-tuple-element.28), channel_id=1, source_target_pairs={{1,0},{2,1},{3,2},{5,4},{6,5},{7,6},{9,8},{10,9},{11,10},{13,12},{... | collective-permute-start | bytes 356360 | tf_op jit(solution)/shard_map/ppermute | solution.py:289
  65.8 7.0 %collective-permute-start.2 = (f32[176,128]{1,0:T(8,128)S(1)}, f32[176,128]{1,0:T(8,128)S(1)}, u32[]{:S(2)}, u32[]{:S(2)}) collective-permute-start(f32[176,128]{1,0:T(8,128)S(1)} %get-tuple-element.23), channel_id=1, source_target_pairs={{0,1},{1,2},{2,3},{4,5},{5,6},{6,7},{8,9},{9,10},{10,11},{12,13},{... | collective-permute-start | bytes 270344 | tf_op jit(solution)/shard_map/ppermute | solution.py:289
  69.8 6.1 %collective-permute-start.3 = (f32[176,128]{1,0:T(8,128)S(1)}, f32[176,128]{1,0:T(8,128)S(1)}, u32[]{:S(2)}, u32[]{:S(2)}) collective-permute-start(f32[176,128]{1,0:T(8,128)S(1)} %get-tuple-element.24), channel_id=1, source_target_pairs={{1,0},{2,1},{3,2},{5,4},{6,5},{7,6},{9,8},{10,9},{11,10},{13,12},{... | collective-permute-start | bytes 270344 | tf_op jit(solution)/shard_map/ppermute | solution.py:289

commit v6 on v2

--- a/solution.py
+++ b/solution.py
@@ -119,88 +119,127 @@
     return total
 
 
-def pack_kernel(lists_ref, feats_ref, targets_ref, out_ref, mask_ref):
-    rows = mask_ref.shape[0]
+def pack_kernel(lists_ref, feats_ref, targets_ref, out_ref, feats, packed, arrived, left):
+    steps = arrived.shape[0]
+    devices = out_ref.shape[0]
+    bricks = lists_ref.shape[1]
+    dests = devices // steps
     width = LANES * SLOTS
-
-    @pl.when(pl.program_id(0) == 0)
-    def _():
-        lane = lax.broadcasted_iota(jnp.int32, (SLOTS, LANES), 1)
-        codes = []
-        for block in range(rows):
-            chosen = lists_ref[:, block * LANES : (block + 1) * LANES]
-            offset = chosen - (lane + block * LANES) * SLOTS
-            bits = jnp.where(chosen >= 0, lax.shift_left(1, jnp.clip(offset, 0, SLOTS - 1)), 0)
-            codes.append(jnp.sum(bits, axis=0, keepdims=True))
-        code = jnp.concatenate(codes, axis=0).astype(jnp.float32).astype(jnp.bfloat16)
-        brick = lax.broadcasted_iota(jnp.int32, (LANES, width), 0)
-        point = lax.broadcasted_iota(jnp.int32, (LANES, width), 1)
-        spread = (lax.shift_right_logical(point, 3) == brick).astype(jnp.float32).astype(jnp.bfloat16)
-        wide = jnp.dot(code, spread, preferred_element_type=jnp.float32).astype(jnp.int32)
-        slot = lax.broadcasted_iota(jnp.int32, (rows, width), 1) & (SLOTS - 1)
-        mask_ref[...] = (lax.shift_right_logical(wide, slot) & 1).astype(jnp.float32)
-
-    step = pl.program_id(0)
-    dests = out_ref.shape[0]
-    feat_count = feats_ref.shape[0]
-    for part in range(dests * 256 // width):
-        row = mask_ref[pl.ds(step * (dests * 256 // width) + part, 1), :].astype(jnp.bfloat16)
-        masked = feats_ref[:, part * width : (part + 1) * width] * row
-        for half_block in range(width // LANES):
-            dest = (part * width + half_block * LANES) // 256
-            half = half_block % 2
-            out_ref[dest, half * feat_count : (half + 1) * feat_count, :] = masked[
-                :, half_block * LANES : (half_block + 1) * LANES
-            ]
-    for dest in range(dests):
-        out_ref[dest, 2 * feat_count : 2 * feat_count + 2, :] = targets_ref[2 * dest : 2 * dest + 2, :]
+    points = bricks * SLOTS // steps
+    arriving = [
+        pltpu.make_async_copy(
+            feats_ref.at[:, k * points : (k + 1) * points], feats.at[:, k * points : (k + 1) * points], arrived.at[k]
+        )
+        for k in range(steps)
+    ]
+    leaving = [
+        pltpu.make_async_copy(
+            packed.at[k * dests : (k + 1) * dests], out_ref.at[k * dests : (k + 1) * dests], left.at[k]
+        )
+        for k in range(steps)
+    ]
+    for copy in arriving:
+        copy.start()
+    rows = bricks // LANES
+    lane = lax.broadcasted_iota(jnp.int32, (SLOTS, LANES), 1)
+    codes = []
+    for block in range(rows):
+        chosen = lists_ref[:, block * LANES : (block + 1) * LANES]
+        offset = chosen - (lane + block * LANES) * SLOTS
+        bits = jnp.where(chosen >= 0, lax.shift_left(1, jnp.clip(offset, 0, SLOTS - 1)), 0)
+        codes.append(jnp.sum(bits, axis=0, keepdims=True))
+    code = jnp.concatenate(codes, axis=0).astype(jnp.float32).astype(jnp.bfloat16)
+    brick = lax.broadcasted_iota(jnp.int32, (LANES, width), 0)
+    point = lax.broadcasted_iota(jnp.int32, (LANES, width), 1)
+    spread = (lax.shift_right_logical(point, 3) == brick).astype(jnp.float32).astype(jnp.bfloat16)
+    wide = jnp.dot(code, spread, preferred_element_type=jnp.float32).astype(jnp.int32)
+    slot = lax.broadcasted_iota(jnp.int32, (rows, width), 1) & (SLOTS - 1)
+    mask = (lax.shift_right_logical(wide, slot) & 1).astype(jnp.float32)
+    for k in range(steps):
+        arriving[k].wait()
+        for part in range(points // width):
+            first = k * points + part * width
+            row = mask[first // width : first // width + 1, :].astype(jnp.bfloat16)
+            masked = feats[:, first : first + width] * row
+            for piece_index in range(width // LANES):
+                dest = (first + piece_index * LANES) // (2 * LANES)
+                half = piece_index % 2
+                packed[dest, half * FEAT : (half + 1) * FEAT, :] = masked[
+                    :, piece_index * LANES : (piece_index + 1) * LANES
+                ]
+        for dest in range(k * dests, (k + 1) * dests):
+            packed[dest, 2 * FEAT : 2 * FEAT + 2, :] = targets_ref[2 * dest : 2 * dest + 2, :]
+        leaving[k].start()
+    for copy in leaving:
+        copy.wait()
 
 
 def pack(point_feats, point_targets, point_lists, devices):
-    feat_count, points = point_feats.shape
-    bricks = point_lists.shape[0]
+    points = point_feats.shape[1]
     steps = 8
-    dests = devices // steps
+    rows = 2 * FEAT + 2
     return pl.pallas_call(
         pack_kernel,
-        grid=(steps,),
         in_specs=[
-            pl.BlockSpec((SLOTS, bricks), lambda i: (0, 0)),
-            pl.BlockSpec((feat_count, points // steps), lambda i: (0, i)),
-            pl.BlockSpec((points // steps // LANES, LANES), lambda i: (i, 0)),
+            pl.BlockSpec(memory_space=pltpu.VMEM),
+            pl.BlockSpec(memory_space=pl.ANY),
+            pl.BlockSpec(memory_space=pltpu.VMEM),
         ],
-        out_specs=pl.BlockSpec((dests, 2 * feat_count + 2, LANES), lambda i: (i, 0, 0)),
-        out_shape=jax.ShapeDtypeStruct((devices, 2 * feat_count + 2, LANES), jnp.bfloat16),
-        scratch_shapes=[pltpu.VMEM((bricks // LANES, LANES * SLOTS), jnp.float32)],
+        out_specs=pl.BlockSpec(memory_space=pl.ANY),
+        out_shape=jax.ShapeDtypeStruct((devices, rows, LANES), jnp.bfloat16),
+        scratch_shapes=[
+            pltpu.VMEM((FEAT, points), jnp.bfloat16),
+            pltpu.VMEM((devices, rows, LANES), jnp.bfloat16),
+            pltpu.SemaphoreType.DMA((steps,)),
+            pltpu.SemaphoreType.DMA((steps,)),
+        ],
         name="pack",
     )(point_lists.T, point_feats, point_targets.reshape(points // LANES, LANES))
 
 
-def prepare_kernel(feats_ref, reg_ref, first_ref, second_ref, third_ref, lanes_ref):
-    records = (first_ref, second_ref, third_ref)
-
-    def one(b, carry):
-        feats = feats_ref[b]
-        reg = reg_ref[pl.ds(b, 1), :]
-        once = feats * reg
-        left = jnp.concatenate([feats, once, once * reg], axis=0)
-        product = lax.dot_general(
-            left,
-            feats,
-            (((1,), (1,)), ((), ())),
-            precision=HIGHEST,
-            preferred_element_type=jnp.float32,
-        )
-        for power, record in enumerate(records):
-            rows = [product[power * FEAT + 8 * q : power * FEAT + 8 * q + 8, :] for q in range(4)]
-            record[b] = jnp.concatenate(rows, axis=1)
+def spread_rows(square, lane_group):
+    square = square + pltpu.roll(square, 64, 1)
+    square = square + pltpu.roll(square, 32, 1)
+    record = square[0:8, :]
+    for q in range(1, 4):
+        record = jnp.where(lane_group == q, square[8 * q : 8 * q + 8, :], record)
+    return record
+
+
+def three_parts(x):
+    high = x.astype(jnp.bfloat16)
+    rest = x - high.astype(jnp.float32)
+    middle = rest.astype(jnp.bfloat16)
+    return high, middle, (rest - middle.astype(jnp.float32)).astype(jnp.bfloat16)
+
+
+def prepare_kernel(feats_ref, reg_ref, *records):
+
+    lane_group = lax.broadcasted_iota(jnp.int32, (1, LANES), 1) // FEAT
+    together = 4
+
+    def some(step, carry):
+        for k in range(together):
+            b = step * together + k
+            feats = feats_ref[b]
+            reg = reg_ref[pl.ds(b, 1), :]
+            once = feats * reg
+            parts = three_parts(jnp.concatenate([feats, once, once * reg], axis=0))
+            left = jnp.concatenate(parts, axis=0)
+            right = [part[:FEAT, :] for part in parts]
+            right = jnp.concatenate([*right, jnp.zeros_like(right[0])], axis=0)
+            product = lax.dot_general(
+                left, right, (((1,), (1,)), ((), ())), preferred_element_type=jnp.float32
+            )
+            size = 3 * FEAT
+            total = jnp.where(lane_group < 1, product[2 * size :, :], 0.0)
+            total = total + jnp.where(lane_group < 2, product[size : 2 * size, :], 0.0)
+            total = total + product[:size, :]
+            for power, record in enumerate(records):
+                record[b] = spread_rows(total[power * FEAT : (power + 1) * FEAT, :], lane_group)
         return carry
 
-    lax.fori_loop(0, feats_ref.shape[0], one, 0)
-    for power, record in enumerate(records):
-        for t in range(8):
-            block = jnp.concatenate([record[:, t, :], jnp.zeros((96, LANES), jnp.float32)], axis=0)
-            lanes_ref[power, t * LANES : (t + 1) * LANES, :] = block.T
+    lax.fori_loop(0, feats_ref.shape[0] // together, some, 0)
 
 
 def prepare(voxel_feats, voxel_reg):
@@ -208,8 +247,8 @@
     record = jax.ShapeDtypeStruct((bricks, 8, LANES), jnp.float32)
     return pl.pallas_call(
         prepare_kernel,
-        out_shape=(record, record, record, jax.ShapeDtypeStruct((3, 8 * LANES, LANES), jnp.float32)),
-        compiler_params=pltpu.CompilerParams(vmem_limit_bytes=24 << 20),
+        out_shape=(record, record, record),
+        compiler_params=pltpu.CompilerParams(vmem_limit_bytes=10 << 20),
         cost_estimate=pl.CostEstimate(flops=600_000_000, bytes_accessed=5_000_000, transcendentals=0),
         name="prepare",
     )(voxel_feats, voxel_reg)
@@ -250,7 +289,7 @@
             pltpu.VMEM((SPAN, 8, LANES), jnp.float32),
             pltpu.VMEM((SPAN, LANES), jnp.float32),
         ],
-        compiler_params=pltpu.CompilerParams(vmem_limit_bytes=24 << 20),
+        compiler_params=pltpu.CompilerParams(vmem_limit_bytes=10 << 20),
         cost_estimate=pl.CostEstimate(flops=2_000_000, bytes_accessed=3_000_000, transcendentals=0),
         name="gather_early",
     )(first, second, mask, *edges)
@@ -266,6 +305,7 @@
     return pl.pallas_call(
         functools.partial(relay_kernel, sections, len(owns)),
         out_shape=(out, out),
+        compiler_params=pltpu.CompilerParams(vmem_limit_bytes=4 << 20),
         name=name,
     )(*owns, low, high)
 
@@ -288,14 +328,60 @@
     return lax.ppermute(to_high, axis, up), lax.ppermute(to_low, axis, down)
 
 
-def begin_kernel(moments_ref, gathered_ref, lanes_ref, vectors_ref, low_ref, high_ref):
-    values = jnp.concatenate(
-        [gathered_ref[...], jnp.zeros((LANES - gathered_ref.shape[0], FEAT), jnp.float32)], axis=0
-    )
-    values = jnp.concatenate([values, jnp.zeros((LANES, LANES - FEAT), jnp.float32)], axis=1).T[:FEAT, :]
+def moments_kernel(
+    got_ref, first_ref, second_ref, third_ref, moments_ref, vectors_ref, low_ref, high_ref, turned, lanes_ref
+):
+    for power, record in enumerate((first_ref, second_ref, third_ref)):
+        for t in range(8):
+            block = jnp.concatenate([record[:, t, :], jnp.zeros((LANES - BX * BY, LANES), jnp.float32)], axis=0)
+            lanes_ref[power, t * LANES : (t + 1) * LANES, :] = block.T
+    sources = got_ref.shape[0]
+    for group in range(sources // 4):
+        for half in range(2):
+            block = got_ref[4 * group : 4 * group + 4, half * FEAT : (half + 1) * FEAT, :]
+            turned[half, group] = block.reshape(LANES, LANES).T
+    sums = []
+    for half in range(2):
+        total = jnp.zeros((FEAT, LANES), jnp.float32)
+        for source in range(sources):
+            feats = got_ref[source, half * FEAT : (half + 1) * FEAT, :].astype(jnp.float32)
+            target = got_ref[source, 2 * FEAT : 2 * FEAT + 2, :].astype(jnp.float32)
+            total = total + feats * target[half : half + 1, :]
+        sums.append(total)
+
+    groups = turned.shape[1]
+    row = lax.broadcasted_iota(jnp.int32, (1, 16, LANES), 1)
+    upper = (row < SLOTS).astype(jnp.float32).astype(jnp.bfloat16)
+    lower = (row >= SLOTS).astype(jnp.float32).astype(jnp.bfloat16)
+    lane_group = lax.broadcasted_iota(jnp.int32, (1, LANES), 1) // FEAT
+    for half in range(2):
+        for pair in range(8):
+            points = turned[half, :, 16 * pair : 16 * pair + 16, :]
+            left = points.reshape(groups * 16, LANES)
+            right = jnp.concatenate(
+                [(points * upper).reshape(groups * 16, LANES), (points * lower).reshape(groups * 16, LANES)],
+                axis=1,
+            )
+            product = lax.dot_general(
+                left, right, (((0,), (0,)), ((), ())), preferred_element_type=jnp.float32
+            )
+            for k in range(2):
+                square = product[:, k * LANES : (k + 1) * LANES]
+                own = jnp.zeros((FEAT, LANES), jnp.float32)
+                for q in range(4):
+                    own = own + jnp.where(lane_group == q, square[q * FEAT : (q + 1) * FEAT, :], 0.0)
+                moments_ref[half * 16 + 2 * pair + k] = spread_rows(own, lane_group)
+    point = lax.broadcasted_iota(jnp.int32, (LANES, LANES), 0) // SLOTS
+    lane = lax.broadcasted_iota(jnp.int32, (LANES, LANES), 1)
+    values = jnp.zeros((FEAT, LANES), jnp.float32)
+    for half in range(2):
+        spread = (lane == point + half * 16).astype(jnp.float32)
+        values = values + jnp.dot(
+            sums[half], spread, precision=HIGHEST, preferred_element_type=jnp.float32
+        )
     applied = [times(lanes_ref.at[power], values) for power in range(3)]
     vectors = jnp.concatenate([*applied, values], axis=0).T
-    vectors_ref[...] = vectors[: vectors_ref.shape[0], :]
+    vectors_ref[...] = vectors[: BX * BY, :]
     depth = LATE[0][1] * BY
     for k in range(depth):
         low_ref[8 * k : 8 * k + 8, :] = moments_ref[k]
@@ -306,13 +392,26 @@
     high_ref[8 * depth :, :] = jnp.concatenate([vectors[BX * BY - deep : BX * BY], blank], axis=0)
 
 
-def begin(moments, gathered, lanes):
+def find_moments(got, records):
+    devices = got.shape[0]
+    bricks = BX * BY
     message = jax.ShapeDtypeStruct((message_rows(LATE, along_rows), LANES), jnp.float32)
     return pl.pallas_call(
-        begin_kernel,
-        out_shape=(jax.ShapeDtypeStruct((gathered.shape[0], LANES), jnp.float32), message, message),
-        name="begin",
-    )(moments, gathered, lanes)
+        moments_kernel,
+        out_shape=(
+            jax.ShapeDtypeStruct((bricks, 8, LANES), jnp.float32),
+            jax.ShapeDtypeStruct((bricks, LANES), jnp.float32),
+            message,
+            message,
+        ),
+        scratch_shapes=[
+            pltpu.VMEM((2, devices // 4, LANES, LANES), jnp.bfloat16),
+            pltpu.VMEM((3, 8 * LANES, LANES), jnp.float32),
+        ],
+        compiler_params=pltpu.CompilerParams(vmem_limit_bytes=12 << 20),
+        cost_estimate=pl.CostEstimate(flops=1_000_000_000, bytes_accessed=12_000_000, transcendentals=0),
+        name="moments",
+    )(got, *records)
 
 
 def power_of_two(value):
@@ -405,7 +504,7 @@
             pltpu.VMEM((SPAN, LANES), jnp.float32),
             pltpu.VMEM((8 * LANES, SPAN), jnp.float32),
         ],
-        compiler_params=pltpu.CompilerParams(vmem_limit_bytes=32 << 20),
+        compiler_params=pltpu.CompilerParams(vmem_limit_bytes=12 << 20),
         name="krylov",
     )(moments, vectors, *edges, first, second, masks, voxel_feats, voxel_reg)
 
@@ -477,7 +576,12 @@
 def finish(shared, basis):
     _, bricks, voxels = basis.shape
     out = jax.ShapeDtypeStruct((bricks, voxels), jnp.float32)
-    return pl.pallas_call(finish_kernel, out_shape=(out, out), name="finish")(shared, basis)
+    return pl.pallas_call(
+        finish_kernel,
+        out_shape=(out, out),
+        compiler_params=pltpu.CompilerParams(vmem_limit_bytes=4 << 20),
+        name="finish",
+    )(shared, basis)
 
 
 def shards(point_feats, point_targets, point_lists, brick_adjacency, voxel_feats, voxel_reg):
@@ -488,25 +592,19 @@
     sending = pack(point_feats, point_targets, point_lists, devices)
     got = lax.all_to_all(sending, GX_GY, split_axis=0, concat_axis=0, tiled=True)
 
-    first, second, third, lanes = prepare(voxel_feats, voxel_reg)
+    first, second, third = prepare(voxel_feats, voxel_reg)
     mask = (brick_adjacency >= 0).astype(jnp.float32)
     mask = jnp.concatenate([mask, jnp.sum(mask, axis=1, keepdims=True)], axis=1)
     mask = jnp.pad(mask, ((0, 0), (0, LANES - 5)))
     early = (first, second, mask)
     low, high = swap(*along_messages(EARLY, early), GX)
-    below, above = swap(*relay(EARLY, early, low, high, "relay_early"), "gy")
+    across = relay(EARLY, early, low, high, "relay_early")
+    got = lax.optimization_barrier((got, *across))[0]
+    below, above = swap(*across, "gy")
+    moments, vectors, to_low, to_high = find_moments(got, (first, second, third))
+    to_low, to_high, below, above = lax.optimization_barrier((to_low, to_high, below, above))
     first_lanes, second_lanes, mask_lanes = gather_early(first, second, mask, (low, high, below, above))
 
-    got_feats = got[:, : 2 * feat_count].reshape(devices, 2, feat_count, local_bricks // 2, slots)
-    got_targets = got[:, 2 * feat_count :].reshape(devices, 2, local_bricks // 2, slots)
-    moments = jnp.einsum("shibc,shjbc->hbij", got_feats, got_feats, preferred_element_type=jnp.float32)
-    moments = moments.reshape(local_bricks, 4, 8, feat_count).transpose(0, 2, 1, 3)
-    moments = moments.reshape(local_bricks, 8, 4 * feat_count)
-    gathered = jnp.einsum(
-        "shbc,shibc->hbi", got_targets, got_feats, preferred_element_type=jnp.float32
-    ).reshape(local_bricks, feat_count)
-
-    vectors, to_low, to_high = begin(moments, gathered, lanes)
     low, high = swap(to_low, to_high, GX)
     below, above = swap(*relay(LATE, (moments, vectors), low, high, "relay_late"), "gy")
     basis, message = krylov(

time: 125 us -> 97.6 us (0.78)
  local copies, waits for them, and re-layouts: 18.5 us -> 1.72 us
  Pallas kernels: 30.7 us -> 18.5 us
  matrix products: 9.02 us -> 0 us
  blocking collectives: 18.5 us -> 23.5 us
  starting transfers between devices: 30.7 us -> 35 us
  waiting for transfers between devices: 15.3 us -> 17.5 us
    ppermute x8, waiting for transfers between devices: 1.31 us -> 16.2 us  [swap(): return (lax.ppermute(to_high, axis, up), lax.ppermute(to_low, axis, down))]
    all_to_all x1, waiting for transfers between devices: 13.9 us -> 1.26 us  [shards(): lax.all_to_all(sending, GX_GY, split_axis=0, concat_axis=0, tiled=True)]
    dot_general x2 -> x0, matrix products: 9.02 us -> none  [the longest x1 5.31 us: shards(): jnp.einsum('shibc,shjbc->hbij', got_feats, got_feats, preferred_element_t...]
    pallas_call x4, Pallas kernels: 23.2 us -> 14.4 us  [the longest x1 4.92 us: prepare(): pl.pallas_call(prepare_kernel, out_shape=(record, record, record), compil...]
    slice x4 -> x0, local copies, waits for them, and re-layouts: 8.41 us -> none  [the longest x2 7.3 us: shards(): got[:, :2 * feat_count]]
    unnamed x42 -> x8, local copies, waits for them, and re-layouts: 8.37 us -> 1.61 us
    all_to_all x1, blocking collectives: 18.5 us -> 23.5 us  [shards(): lax.all_to_all(message, GX_GY, split_axis=0, concat_axis=0, tiled=True)]
    ppermute x8, starting transfers between devices: 18.8 us -> 23.5 us  [swap(): return (lax.ppermute(to_high, axis, up), lax.ppermute(to_low, axis, down))]
  transfers between devices with their start and end apart: 9 -> 9, of which waited for: 2 -> 5; matrix products, arithmetic and copies ran while one was open for 16% -> 0% of each run, Pallas kernels for 16% -> 12%
where the time goes in v6:
time: 97.6 us; the launch traced here: 97.1 us
  starting transfers between devices  35 us (36%)
  blocking collectives  23.5 us (24%)
  Pallas kernels  18.5 us (19%)
  waiting for transfers between devices  17.5 us (18%)
  local copies, waits for them, and re-layouts  1.72 us (2%)
    ppermute x8, starting transfers between devices, swap(): return (lax.ppermute(to_high, axis, up), lax.ppermute(to_low, axis, down))  23.5 us
    all_to_all x1, blocking collectives, shards(): lax.all_to_all(message, GX_GY, split_axis=0, concat_axis=0, tiled=True)  23.5 us
    ppermute x8, waiting for transfers between devices, swap(): return (lax.ppermute(to_high, axis, up), lax.ppermute(to_low, axis, down))  16.2 us
    all_to_all x1, starting transfers between devices, shards(): lax.all_to_all(sending, GX_GY, split_axis=0, concat_axis=0, tiled=True)  11.5 us
    pallas_call x1, Pallas kernels, prepare(): pl.pallas_call(prepare_kernel, out_shape=(record, record, record), compil...  4.92 us
    pallas_call x1, Pallas kernels, find_moments(): pl.pallas_call(moments_kernel, out_shape=(jax.ShapeDtypeStruct((bricks, 8...  4.91 us
    pallas_call x1, Pallas kernels, pack(): pl.pallas_call(pack_kernel, in_specs=[pl.BlockSpec(memory_space=pltpu.VME...  3.46 us
    pallas_call x1, Pallas kernels, krylov(): pl.pallas_call(krylov_kernel, out_shape=(jax.ShapeDtypeStruct((4, bricks,...  2.72 us
  transfers between devices with their start and end apart: 9, of which 5 were waited for; matrix products, arithmetic and copies ran while one was open for 0% of the time, Pallas kernels for 12%

profile of v6, /device:TPU:1, one launch (start us, length us, event | category | flops | bytes accessed | tf_op | source)
XLA Modules:
  0.0 97.1 jit_solution(18042964310937863899)
XLA Ops:
  0.6 3.5 %pack.1 = bf16[128,66,128]{2,1,0:T(8,128)(2,1)} custom-call(s32[8,4096]{1,0:T(8,128)} %bitcast.17, bf16[32,32768]{1,0:T(8,128)(2,1)} %feats_ref.3, bf16[256,128]{1,0:T(8,128)(2,1)} %bitcast.18), custom_call_target="tpu_custom_call" | custom-call | tf_op jit(solution)/shard_map/pack/pallas_call | solution.py:181
  4.1 0.0 copy-start.3
  4.1 0.0 copy-start.2
  4.1 11.5 %all-to-all-start = ((bf16[128,66,128]{2,1,0:T(8,128)(2,1)}), bf16[128,66,128]{2,1,0:T(8,128)(2,1)S(1)}, u32[]{:S(2)}, u32[]{:S(2)}) async-start(bf16[128,66,128]{2,1,0:T(8,128)(2,1)} %pack.1), calls=%async_computation | async-start | bytes 4718592 | tf_op jit(solution)/shard_map/all_to_all | solution.py:593
  15.6 0.0 copy-done.3
  15.7 0.1 copy.11
  15.8 0.0 copy-done.2
  15.8 0.0 copy-start
  15.8 1.6 %copy-done = f32[32,32,512]{2,1,0:T(8,128)S(1)} copy-done((f32[32,32,512]{2,1,0:T(8,128)S(1)}, f32[32,32,512]{2,1,0:T(8,128)}, u32[]{:S(2)}) %copy-start) | copy-done | bytes 2097176
  17.4 4.9 %prepare.1 = (f32[32,8,128]{2,1,0:T(8,128)S(1)}, f32[32,8,128]{2,1,0:T(8,128)S(1)}, f32[32,8,128]{2,1,0:T(8,128)S(1)}) custom-call(f32[32,32,512]{2,1,0:T(8,128)S(1)} %copy-done, f32[32,512]{1,0:T(8,128)S(1)} %copy-done.2), custom_call_target="tpu_custom_call" | custom-call | flops 600000000 | bytes 5000000 | tf_op jit(solution)/shard_map/prepare/pallas_call | solution.py:248
  22.4 3.7 %collective-permute-start = (f32[104,128]{1,0:T(8,128)S(1)}, f32[104,128]{1,0:T(8,128)S(1)}, u32[]{:S(2)}, u32[]{:S(2)}) collective-permute-start(f32[104,128]{1,0:T(8,128)S(1)} %pad_maximum_fusion), channel_id=1, source_target_pairs={{0,4},{4,8},{8,12},{12,16},{16,20},{20,24},{24,28},{28,32},{32,36}... | collective-permute-start | bytes 159752 | tf_op jit(solution)/shard_map/ppermute | solution.py:328
  26.0 1.9 %collective-permute-start.1 = (f32[104,128]{1,0:T(8,128)S(1)}, f32[104,128]{1,0:T(8,128)S(1)}, u32[]{:S(2)}, u32[]{:S(2)}) collective-permute-start(f32[104,128]{1,0:T(8,128)S(1)} %pad_maximum_fusion.1), channel_id=1, source_target_pairs={{4,0},{8,4},{12,8},{16,12},{20,16},{24,20},{28,24},{32,28},{36,32}... | collective-permute-start | bytes 159752 | tf_op jit(solution)/shard_map/ppermute | solution.py:328
  28.0 4.5 %collective-permute-done.refs_3_.low_ref = f32[104,128]{1,0:T(8,128)S(1)} collective-permute-done((f32[104,128]{1,0:T(8,128)S(1)}, f32[104,128]{1,0:T(8,128)S(1)}, u32[]{:S(2)}, u32[]{:S(2)}) %collective-permute-start) | collective-permute-done | bytes 53280 | tf_op jit(solution)/shard_map/ppermute | solution.py:328
  32.5 5.7 %collective-permute-done.1.refs_4_.high_ref = f32[104,128]{1,0:T(8,128)S(1)} collective-permute-done((f32[104,128]{1,0:T(8,128)S(1)}, f32[104,128]{1,0:T(8,128)S(1)}, u32[]{:S(2)}, u32[]{:S(2)}) %collective-permute-start.1) | collective-permute-done | bytes 53280 | tf_op jit(solution)/shard_map/ppermute | solution.py:328
  38.2 8.7 %collective-permute-start.2 = (f32[232,128]{1,0:T(8,128)S(1)}, f32[232,128]{1,0:T(8,128)S(1)}, u32[]{:S(2)}, u32[]{:S(2)}) collective-permute-start(f32[232,128]{1,0:T(8,128)S(1)} %get-tuple-element.26), channel_id=1, source_target_pairs={{0,1},{1,2},{2,3},{4,5},{5,6},{6,7},{8,9},{9,10},{10,11},{12,13},{... | collective-permute-start | bytes 356360 | tf_op jit(solution)/shard_map/ppermute | solution.py:328
  46.9 1.3 %collective-permute-start.3 = (f32[232,128]{1,0:T(8,128)S(1)}, f32[232,128]{1,0:T(8,128)S(1)}, u32[]{:S(2)}, u32[]{:S(2)}) collective-permute-start(f32[232,128]{1,0:T(8,128)S(1)} %get-tuple-element.25), channel_id=1, source_target_pairs={{1,0},{2,1},{3,2},{5,4},{6,5},{7,6},{9,8},{10,9},{11,10},{13,12},{... | collective-permute-start | bytes 356360 | tf_op jit(solution)/shard_map/ppermute | solution.py:328
  48.2 1.3 %all-to-all-done.got_ref = bf16[128,66,128]{2,1,0:T(8,128)(2,1)S(1)} async-done(((bf16[128,66,128]{2,1,0:T(8,128)(2,1)}), bf16[128,66,128]{2,1,0:T(8,128)(2,1)S(1)}, u32[]{:S(2)}, u32[]{:S(2)}) %all-to-all-start) | async-done | bytes 2162720 | tf_op jit(solution)/shard_map/all_to_all | solution.py:593
  49.4 0.0 copy-start.1
  49.4 4.9 %moments.1 = (f32[32,8,128]{2,1,0:T(8,128)S(1)}, f32[32,128]{1,0:T(8,128)S(1)}, f32[80,128]{1,0:T(8,128)S(1)}, f32[80,128]{1,0:T(8,128)S(1)}) custom-call(bf16[128,66,128]{2,1,0:T(8,128)(2,1)S(1)} %all-to-all-done.got_ref, f32[32,8,128]{2,1,0:T(8,128)S(1)} %get-tuple-element.23.refs_0_.first_ref, f32[32,8,128]{2,1,0:T(8,128)S(1)} %get-tuple-element.24.refs_1_.second_ref, ...), custom_call_target="tpu_custom_call" | custom-call | flops 1000000000 | bytes 12000000 | tf_op jit(solution)/shard_map/moments/pallas_call | solution.py:399
  54.3 0.0 collective-permute-done.2.below_ref
  54.4 0.0 collective-permute-done.3.above_ref
  54.4 2.6 %collective-permute-start.4 = (f32[80,128]{1,0:T(8,128)S(1)}, f32[80,128]{1,0:T(8,128)S(1)}, u32[]{:S(2)}, u32[]{:S(2)}) collective-permute-start(f32[80,128]{1,0:T(8,128)S(1)} %get-tuple-element.33), channel_id=1, source_target_pairs={{0,4},{4,8},{8,12},{12,16},{16,20},{20,24},{24,28},{28,32},{32,36}... | collective-permute-start | bytes 122888 | tf_op jit(solution)/shard_map/ppermute | solution.py:328
  57.0 1.9 %collective-permute-start.5 = (f32[80,128]{1,0:T(8,128)S(1)}, f32[80,128]{1,0:T(8,128)S(1)}, u32[]{:S(2)}, u32[]{:S(2)}) collective-permute-start(f32[80,128]{1,0:T(8,128)S(1)} %get-tuple-element.34), channel_id=1, source_target_pairs={{4,0},{8,4},{12,8},{16,12},{20,16},{24,20},{28,24},{32,28},{36,32}... | collective-permute-start | bytes 122888 | tf_op jit(solution)/shard_map/ppermute | solution.py:328
  58.9 0.0 collective-permute-done.4.refs_2_.low_ref
  58.9 3.4 %collective-permute-done.5.refs_3_.high_ref = f32[80,128]{1,0:T(8,128)S(1)} collective-permute-done((f32[80,128]{1,0:T(8,128)S(1)}, f32[80,128]{1,0:T(8,128)S(1)}, u32[]{:S(2)}, u32[]{:S(2)}) %collective-permute-start.5) | collective-permute-done | bytes 40992 | tf_op jit(solution)/shard_map/ppermute | solution.py:328
  62.3 2.2 %collective-permute-start.6 = (f32[176,128]{1,0:T(8,128)S(1)}, f32[176,128]{1,0:T(8,128)S(1)}, u32[]{:S(2)}, u32[]{:S(2)}) collective-permute-start(f32[176,128]{1,0:T(8,128)S(1)} %get-tuple-element.35), channel_id=1, source_target_pairs={{0,1},{1,2},{2,3},{4,5},{5,6},{6,7},{8,9},{9,10},{10,11},{12,13},{... | collective-permute-start | bytes 270344 | tf_op jit(solution)/shard_map/ppermute | solution.py:328
  64.5 1.3 %collective-permute-start.7 = (f32[176,128]{1,0:T(8,128)S(1)}, f32[176,128]{1,0:T(8,128)S(1)}, u32[]{:S(2)}, u32[]{:S(2)}) collective-permute-start(f32[176,128]{1,0:T(8,128)S(1)} %get-tuple-element.36), channel_id=1, source_target_pairs={{1,0},{2,1},{3,2},{5,4},{6,5},{7,6},{9,8},{10,9},{11,10},{13,12},{... | collective-permute-start | bytes 270344 | tf_op jit(solution)/shard_map/ppermute | solution.py:328
  65.8 1.3 %gather_early.1 = (f32[1024,256]{1,0:T(8,128)S(1)}, f32[1024,256]{1,0:T(8,128)S(1)}, f32[8,256]{1,0:T(8,128)S(1)}) custom-call(f32[32,8,128]{2,1,0:T(8,128)S(1)} %get-tuple-element.23.refs_0_.first_ref, f32[32,8,128]{2,1,0:T(8,128)S(1)} %get-tuple-element.24.refs_1_.second_ref, f32[32,128]{1,0:T(8,128)S(1)} %pad.4.refs_2_.mask_ref, ...), custom_call_target="tpu_custom_call" | custom-call | flops 2000000 | bytes 3000000 | tf_op jit(solution)/shard_map/gather_early/pallas_call | solution.py:284
  67.2 0.0 collective-permute-done.6.below_ref
  67.2 2.6 %collective-permute-done.7.above_ref = f32[176,128]{1,0:T(8,128)S(1)} collective-permute-done((f32[176,128]{1,0:T(8,128)S(1)}, f32[176,128]{1,0:T(8,128)S(1)}, u32[]{:S(2)}, u32[]{:S(2)}) %collective-permute-start.7) | collective-permute-done | bytes 90144 | tf_op jit(solution)/shard_map/ppermute | solution.py:328
  69.8 0.0 copy-done.1
  69.8 2.7 %krylov.1 = (f32[4,32,512]{2,1,0:T(8,128)S(1)}, f32[128,128]{1,0:T(8,128)S(1)}) custom-call(f32[32,8,128]{2,1,0:T(8,128)S(1)} %get-tuple-element.29.refs_0_.moments_ref, f32[32,128]{1,0:T(8,128)S(1)} %get-tuple-element.30.refs_1_.vectors_ref, f32[80,128]{1,0:T(8,128)S(1)} %collective-permute-done.4.refs_2_.low_ref, ...), custom_call_target="tpu_custom_call" | custom-call | tf_op jit(solution)/shard_map/krylov/pallas_call | solution.py:496
  72.5 23.5 %all_to_all.16 = f32[128,1,128]{2,1,0:T(1,128)S(1)} all-to-all(f32[128,1,128]{2,1,0:T(1,128)S(1)} %bitcast.16), channel_id=1, replica_groups=mesh['gx_0'=4,'gx_1'=4,'gx_2'=2,'gy'=4] {'gx_0','gx_1','gx_2','gy'}, dimensions={0} | all-to-all | bytes 131072 | tf_op jit(solution)/shard_map/all_to_all | solution.py:614
  96.0 1.1 %finish.1 = (f32[32,512]{1,0:T(8,128)}, f32[32,512]{1,0:T(8,128)}) custom-call(f32[128,128]{1,0:T(8,128)S(1)} %bitcast.15, f32[4,32,512]{2,1,0:T(8,128)S(1)} %get-tuple-element.43.basis_ref), custom_call_target="tpu_custom_call" | custom-call | tf_op jit(solution)/shard_map/finish/pallas_call | solution.py:579
  (11 shorter events, 0.1 us)
Async XLA Ops:
  4.1 11.5 %copy-start.3 = (s32[32,4]{0,1:T(4,128)S(1)}, s32[32,4]{0,1:T(4,128)}, u32[]{:S(2)}) copy-start(s32[32,4]{0,1:T(4,128)} %param.9) | copy-start | bytes 1540
  4.1 11.7 %copy-start.2 = (f32[32,512]{1,0:T(8,128)S(1)}, f32[32,512]{1,0:T(8,128)}, u32[]{:S(2)}) copy-start(f32[32,512]{1,0:T(8,128)} %reg_ref.3) | copy-start | bytes 196612
  4.1 45.3 %all-to-all-start = ((bf16[128,66,128]{2,1,0:T(8,128)(2,1)}), bf16[128,66,128]{2,1,0:T(8,128)(2,1)S(1)}, u32[]{:S(2)}, u32[]{:S(2)}) async-start(bf16[128,66,128]{2,1,0:T(8,128)(2,1)} %pack.1), calls=%async_computation | async-start | bytes 4718592 | tf_op jit(solution)/shard_map/all_to_all | solution.py:593
  15.8 1.6 %copy-start = (f32[32,32,512]{2,1,0:T(8,128)S(1)}, f32[32,32,512]{2,1,0:T(8,128)}, u32[]{:S(2)}) copy-start(f32[32,32,512]{2,1,0:T(8,128)} %feats_ref.5) | copy-start | bytes 6291460
  22.4 10.2 %collective-permute-start = (f32[104,128]{1,0:T(8,128)S(1)}, f32[104,128]{1,0:T(8,128)S(1)}, u32[]{:S(2)}, u32[]{:S(2)}) collective-permute-start(f32[104,128]{1,0:T(8,128)S(1)} %pad_maximum_fusion), channel_id=1, source_target_pairs={{0,4},{4,8},{8,12},{12,16},{16,20},{20,24},{24,28},{28,32},{32,36}... | collective-permute-start | bytes 159752 | tf_op jit(solution)/shard_map/ppermute | solution.py:328
  26.0 12.1 %collective-permute-start.1 = (f32[104,128]{1,0:T(8,128)S(1)}, f32[104,128]{1,0:T(8,128)S(1)}, u32[]{:S(2)}, u32[]{:S(2)}) collective-permute-start(f32[104,128]{1,0:T(8,128)S(1)} %pad_maximum_fusion.1), channel_id=1, source_target_pairs={{4,0},{8,4},{12,8},{16,12},{20,16},{24,20},{28,24},{32,28},{36,32}... | collective-permute-start | bytes 159752 | tf_op jit(solution)/shard_map/ppermute | solution.py:328
  38.2 16.1 %collective-permute-start.2 = (f32[232,128]{1,0:T(8,128)S(1)}, f32[232,128]{1,0:T(8,128)S(1)}, u32[]{:S(2)}, u32[]{:S(2)}) collective-permute-start(f32[232,128]{1,0:T(8,128)S(1)} %get-tuple-element.26), channel_id=1, source_target_pairs={{0,1},{1,2},{2,3},{4,5},{5,6},{6,7},{8,9},{9,10},{10,11},{12,13},{... | collective-permute-start | bytes 356360 | tf_op jit(solution)/shard_map/ppermute | solution.py:328
  46.9 7.5 %collective-permute-start.3 = (f32[232,128]{1,0:T(8,128)S(1)}, f32[232,128]{1,0:T(8,128)S(1)}, u32[]{:S(2)}, u32[]{:S(2)}) collective-permute-start(f32[232,128]{1,0:T(8,128)S(1)} %get-tuple-element.25), channel_id=1, source_target_pairs={{1,0},{2,1},{3,2},{5,4},{6,5},{7,6},{9,8},{10,9},{11,10},{13,12},{... | collective-permute-start | bytes 356360 | tf_op jit(solution)/shard_map/ppermute | solution.py:328
  49.4 20.4 %copy-start.1 = (f32[32,32,512]{2,1,0:T(8,128)S(1)}, f32[32,32,512]{2,1,0:T(8,128)}, u32[]{:S(2)}) copy-start(f32[32,32,512]{2,1,0:T(8,128)} %feats_ref.5) | copy-start | bytes 6291460
  54.4 4.5 %collective-permute-start.4 = (f32[80,128]{1,0:T(8,128)S(1)}, f32[80,128]{1,0:T(8,128)S(1)}, u32[]{:S(2)}, u32[]{:S(2)}) collective-permute-start(f32[80,128]{1,0:T(8,128)S(1)} %get-tuple-element.33), channel_id=1, source_target_pairs={{0,4},{4,8},{8,12},{12,16},{16,20},{20,24},{24,28},{28,32},{32,36}... | collective-permute-start | bytes 122888 | tf_op jit(solution)/shard_map/ppermute | solution.py:328
  57.0 5.3 %collective-permute-start.5 = (f32[80,128]{1,0:T(8,128)S(1)}, f32[80,128]{1,0:T(8,128)S(1)}, u32[]{:S(2)}, u32[]{:S(2)}) collective-permute-start(f32[80,128]{1,0:T(8,128)S(1)} %get-tuple-element.34), channel_id=1, source_target_pairs={{4,0},{8,4},{12,8},{16,12},{20,16},{24,20},{28,24},{32,28},{36,32}... | collective-permute-start | bytes 122888 | tf_op jit(solution)/shard_map/ppermute | solution.py:328
  62.3 4.8 %collective-permute-start.6 = (f32[176,128]{1,0:T(8,128)S(1)}, f32[176,128]{1,0:T(8,128)S(1)}, u32[]{:S(2)}, u32[]{:S(2)}) collective-permute-start(f32[176,128]{1,0:T(8,128)S(1)} %get-tuple-element.35), channel_id=1, source_target_pairs={{0,1},{1,2},{2,3},{4,5},{5,6},{6,7},{8,9},{9,10},{10,11},{12,13},{... | collective-permute-start | bytes 270344 | tf_op jit(solution)/shard_map/ppermute | solution.py:328
  64.5 5.3 %collective-permute-start.7 = (f32[176,128]{1,0:T(8,128)S(1)}, f32[176,128]{1,0:T(8,128)S(1)}, u32[]{:S(2)}, u32[]{:S(2)}) collective-permute-start(f32[176,128]{1,0:T(8,128)S(1)} %get-tuple-element.36), channel_id=1, source_target_pairs={{1,0},{2,1},{3,2},{5,4},{6,5},{7,6},{9,8},{10,9},{11,10},{13,12},{... | collective-permute-start | bytes 270344 | tf_op jit(solution)/shard_map/ppermute | solution.py:328

commit v7 on v6

--- a/solution.py
+++ b/solution.py
@@ -25,8 +25,9 @@
 
 coupling_weight = 1.0
 
-EARLY = ((8, 2), (8, 1), (1, 2))
-LATE = ((8, 2), (1, 3))
+EARLY = ((8, 2, False), (8, 1, False), (1, 2, False))
+LATE = ((8, 2, True), (1, 3, True))
+CORNER_ROWS = 24
 
 
 def padded(rows):
@@ -37,9 +38,13 @@
     return padded(section[0] * section[1] * BY)
 
 
+def beyond(section, away):
+    return section[1] - away if section[2] else 0
+
+
 def across_rows(section):
-    rows, depth = section
-    return padded(rows * sum(BX + 2 * (depth - k) for k in range(1, depth + 1)))
+    rows, depth, _ = section
+    return padded(rows * sum(BX + 2 * beyond(section, k) for k in range(1, depth + 1)))
 
 
 def message_rows(sections, size):
@@ -53,7 +58,7 @@
 
 
 def brick_at(own, low, high, start, section, a, e):
-    rows, depth = section
+    rows, depth, _ = section
     if a < 0:
         return piece(low, start, rows, (a + depth) * BY + e)
     if a >= BX:
@@ -64,10 +69,10 @@
 def fill_across(sections, owns, low, high, to_low, to_high):
     source = target = 0
     for section, own in zip(sections, owns):
-        rows, depth = section
+        rows, depth, _ = section
         index = 0
         for away in range(1, depth + 1):
-            extra = depth - away
+            extra = beyond(section, away)
             for a in range(-extra, BX + extra):
                 place = slice(target + rows * index, target + rows * (index + 1))
                 to_low[place, :] = brick_at(own, low, high, source, section, a, away - 1)
@@ -84,7 +89,7 @@
 
 def place_bricks(put, sections, which, own, along_low, along_high, across_low, across_high):
     section = sections[which]
-    rows, depth = section
+    rows, depth, _ = section
     start = message_rows(sections[:which], along_rows)
     for a in range(-depth, BX + depth):
         for e in range(BY):
@@ -92,7 +97,7 @@
     start = message_rows(sections[:which], across_rows)
     index = 0
     for away in range(1, depth + 1):
-        extra = depth - away
+        extra = beyond(section, away)
         for a in range(-extra, BX + extra):
             put(a, -away, piece(across_low, start, rows, index))
             put(a, BY - 1 + away, piece(across_high, start, rows, index))
@@ -295,24 +300,46 @@
     )(first, second, mask, *edges)
 
 
-def relay_kernel(sections, count, *refs):
-    owns, low, high, to_low, to_high = refs[:count], *refs[count:]
-    fill_across(sections, owns, low, high, to_low, to_high)
-
-
-def relay(sections, owns, low, high, name):
-    out = jax.ShapeDtypeStruct((message_rows(sections, across_rows), LANES), jnp.float32)
-    return pl.pallas_call(
-        functools.partial(relay_kernel, sections, len(owns)),
+def across_early_kernel(first_ref, second_ref, mask_ref, to_low, to_high):
+    fill_across(EARLY, (first_ref, second_ref, mask_ref), None, None, to_low, to_high)
+
+
+def across_early(owns):
+    out = jax.ShapeDtypeStruct((message_rows(EARLY, across_rows), LANES), jnp.float32)
+    return pl.pallas_call(
+        across_early_kernel,
         out_shape=(out, out),
         compiler_params=pltpu.CompilerParams(vmem_limit_bytes=4 << 20),
-        name=name,
-    )(*owns, low, high)
+        name="across_early",
+    )(*owns)
+
+
+def across_late_kernel(moments_ref, vectors_ref, low, high, early_low, early_high, to_low, to_high):
+    fill_across(LATE, (moments_ref, vectors_ref), low, high, to_low, to_high)
+    start = message_rows(LATE, across_rows)
+    masks = message_rows(EARLY[:2], along_rows)
+    for out, e in ((to_low, 0), (to_high, BY - 1)):
+        rows = []
+        for k, (source, index) in enumerate(((early_low, BY + e), (early_high, e))):
+            out[start + 8 * k : start + 8 * k + 8, :] = source[8 * index : 8 * index + 8, :]
+            rows.append(source[masks + index : masks + index + 1, :])
+        rows.append(jnp.zeros((6, LANES), jnp.float32))
+        out[start + 16 : start + CORNER_ROWS, :] = jnp.concatenate(rows, axis=0)
+
+
+def across_late(moments, vectors, low, high, early_low, early_high):
+    out = jax.ShapeDtypeStruct((message_rows(LATE, across_rows) + CORNER_ROWS, LANES), jnp.float32)
+    return pl.pallas_call(
+        across_late_kernel,
+        out_shape=(out, out),
+        compiler_params=pltpu.CompilerParams(vmem_limit_bytes=4 << 20),
+        name="across_late",
+    )(moments, vectors, low, high, early_low, early_high)
 
 
 def along_messages(sections, owns):
     to_low, to_high = [], []
-    for (rows, depth), own in zip(sections, owns):
+    for (rows, depth, _), own in zip(sections, owns):
         flat = own.reshape(-1, LANES)
         used = rows * depth * BY
         blank = ((0, padded(used) - used), (0, 0))
@@ -321,11 +348,15 @@
     return jnp.concatenate(to_low), jnp.concatenate(to_high)
 
 
-def swap(to_low, to_high, axis):
+def swap(to_low, to_high, axis, even):
     count = lax.axis_size(axis)
-    up = [(i, i + 1) for i in range(count - 1)]
-    down = [(b, a) for a, b in up]
-    return lax.ppermute(to_high, axis, up), lax.ppermute(to_low, axis, down)
+
+    def pairs(start):
+        return [pair for a in range(start, count - 1, 2) for pair in ((a, a + 1), (a + 1, a))]
+
+    first = lax.ppermute(jnp.where(even, to_high, to_low), axis, pairs(0))
+    second = lax.ppermute(jnp.where(even, to_low, to_high), axis, pairs(1))
+    return jnp.where(even, second, first), jnp.where(even, first, second)
 
 
 def moments_kernel(
@@ -430,8 +461,11 @@
 def krylov_kernel(
     moments_ref, vectors_ref, low_ref, high_ref, below_ref, above_ref, first_ref, second_ref, mask_ref,
     feats_ref, reg_ref, basis_ref, message_ref, moment_store, vector_store, moment_lanes,
+    corner_store, corner_masks, corner_lanes,
 ):
     moment_store[...] = jnp.zeros_like(moment_store)
+    corner_store[...] = jnp.zeros_like(corner_store)
+    corner_masks[...] = jnp.zeros_like(corner_masks)
     vector_store[...] = jnp.zeros_like(vector_store)
 
     def put_moment(a, e, value):
@@ -443,9 +477,23 @@
     edges = (low_ref, high_ref, below_ref, above_ref)
     place_bricks(put_moment, LATE, 0, moments_ref, *edges)
     place_bricks(put_vector, LATE, 1, vectors_ref, *edges)
+    start = message_rows(LATE, across_rows)
+    for ref, e in ((below_ref, -1), (above_ref, BY)):
+        for k, a in enumerate((-1, BX)):
+            place = lane_of(a, e) % LANES
+            corner_store[place] = ref[start + 8 * k : start + 8 * k + 8, :]
+            corner_masks[place : place + 1, :] = ref[start + 16 + k : start + 17 + k, :]
     to_lanes(moment_store, moment_lanes)
+    to_lanes(corner_store, corner_lanes)
     vectors = vector_store[...].T
-    masks = mask_ref[...]
+    lane = lax.broadcasted_iota(jnp.int32, (1, LANES), 1)
+    front = (lane == lane_of(-1, -1)) | (lane == lane_of(-1, BY))
+    rear = (lane == lane_of(BX, -1) % LANES) | (lane == lane_of(BX, BY) % LANES)
+
+    def both_tiles(x):
+        return jnp.concatenate([jnp.where(front, x, 0.0), jnp.where(rear, x, 0.0)], axis=1)
+
+    masks = mask_ref[...] + both_tiles(corner_masks[...].T[:8, :])
 
     def system(z):
         near = masks[0:1] * pltpu.roll(z, PITCH, 1) + masks[1:2] * pltpu.roll(z, SPAN - PITCH, 1)
@@ -453,14 +501,15 @@
         return times(moment_lanes, z) + coupling_weight * (masks[4:5] * z - near)
 
     one = system(vectors[0:FEAT])
-    two = system(times(first_ref, one) + vectors[FEAT : 2 * FEAT])
+    corners = times(corner_lanes, jnp.where(front, one[:, :LANES], one[:, LANES:]))
+    two = system(times(first_ref, one) + both_tiles(corners) + vectors[FEAT : 2 * FEAT])
     three = system(times(first_ref, two) + times(second_ref, one) + vectors[2 * FEAT : 3 * FEAT])
     chain = (vectors[3 * FEAT :], one, two, three)
     for b in range(BX * BY):
-        lane = lane_of(b // BY, b % BY)
+        place = lane_of(b // BY, b % BY)
         feats = feats_ref[b]
         for step, values in enumerate(chain):
-            basis_ref[step, b : b + 1, :] = jnp.sum(feats * values[:, lane : lane + 1], axis=0, keepdims=True)
+            basis_ref[step, b : b + 1, :] = jnp.sum(feats * values[:, place : place + 1], axis=0, keepdims=True)
     reg = reg_ref[...]
     basis = [basis_ref[0]]
     for step in range(1, 4):
@@ -481,7 +530,6 @@
     sums = [jnp.sum(folded(scaled[a] * scaled[b], jnp.add), axis=0, keepdims=True) for a, b in PAIRS]
     sums = jnp.concatenate(sums + [jnp.zeros((16 - len(PAIRS), LANES), jnp.float32)], axis=0)
     sums = jnp.sum(sums, axis=1, keepdims=True)
-    lane = lax.broadcasted_iota(jnp.int32, (1, LANES), 1)
     row = jnp.zeros((1, LANES), jnp.float32)
     for k in range(len(PAIRS)):
         row = jnp.where(lane == k, sums[k : k + 1, :], row)
@@ -503,6 +551,9 @@
             pltpu.VMEM((SPAN, 8, LANES), jnp.float32),
             pltpu.VMEM((SPAN, LANES), jnp.float32),
             pltpu.VMEM((8 * LANES, SPAN), jnp.float32),
+            pltpu.VMEM((LANES, 8, LANES), jnp.float32),
+            pltpu.VMEM((LANES, LANES), jnp.float32),
+            pltpu.VMEM((8 * LANES, LANES), jnp.float32),
         ],
         compiler_params=pltpu.CompilerParams(vmem_limit_bytes=12 << 20),
         name="krylov",
@@ -597,16 +648,19 @@
     mask = jnp.concatenate([mask, jnp.sum(mask, axis=1, keepdims=True)], axis=1)
     mask = jnp.pad(mask, ((0, 0), (0, LANES - 5)))
     early = (first, second, mask)
-    low, high = swap(*along_messages(EARLY, early), GX)
-    across = relay(EARLY, early, low, high, "relay_early")
-    got = lax.optimization_barrier((got, *across))[0]
-    below, above = swap(*across, "gy")
+    along_even = lax.axis_index("gx_2") == 0
+    across_even = lax.axis_index("gy") % 2 == 0
+    early_low, early_high = swap(*along_messages(EARLY, early), GX, along_even)
+    early_below, early_above = swap(*across_early(early), "gy", across_even)
+
     moments, vectors, to_low, to_high = find_moments(got, (first, second, third))
-    to_low, to_high, below, above = lax.optimization_barrier((to_low, to_high, below, above))
-    first_lanes, second_lanes, mask_lanes = gather_early(first, second, mask, (low, high, below, above))
-
-    low, high = swap(to_low, to_high, GX)
-    below, above = swap(*relay(LATE, (moments, vectors), low, high, "relay_late"), "gy")
+    low, high = swap(to_low, to_high, GX, along_even)
+    first_lanes, second_lanes, mask_lanes = gather_early(
+        first, second, mask, (early_low, early_high, early_below, early_above)
+    )
+    below, above = swap(
+        *across_late(moments, vectors, low, high, early_low, early_high), "gy", across_even
+    )
     basis, message = krylov(
         moments, vectors, (low, high, below, above), first_lanes, second_lanes, mask_lanes,
         voxel_feats, voxel_reg, devices,

time: 97.6 us -> 88.1 us (0.903)
  starting transfers between devices: 35 us -> 20.6 us
  waiting for transfers between devices: 17.5 us -> 26.2 us
  blocking collectives: 23.5 us -> 19.3 us
    all_to_all x1, waiting for transfers between devices: 1.26 us -> 21.6 us  [shards(): lax.all_to_all(sending, GX_GY, split_axis=0, concat_axis=0, tiled=True)]
    ppermute x8, starting transfers between devices: 23.5 us -> 9.06 us  [the longest x4 6.16 us: swap(): second = lax.ppermute(jnp.where(even, to_low, to_high), axis, pairs(1))]
    ppermute x8, waiting for transfers between devices: 16.2 us -> 4.63 us  [the longest x4 3.46 us: swap(): second = lax.ppermute(jnp.where(even, to_low, to_high), axis, pairs(1))]
    all_to_all x1, blocking collectives: 23.5 us -> 19.3 us  [shards(): lax.all_to_all(message, GX_GY, split_axis=0, concat_axis=0, tiled=True)]
  transfers between devices with their start and end apart: 9 -> 9, of which waited for: 5 -> 3; matrix products, arithmetic and copies ran while one was open for 0% -> 0% of each run, Pallas kernels for 12% -> 13%
where the time goes in v7:
time: 88.1 us; the launch traced here: 87.7 us
  waiting for transfers between devices  26.2 us (30%)
  starting transfers between devices  20.6 us (23%)
  blocking collectives  19.3 us (22%)
  Pallas kernels  18.9 us (21%)
  local copies, waits for them, and re-layouts  1.72 us (2%)
  between operations  0.91 us (1%)
    all_to_all x1, waiting for transfers between devices, shards(): lax.all_to_all(sending, GX_GY, split_axis=0, concat_axis=0, tiled=True)  21.6 us
    all_to_all x1, blocking collectives, shards(): lax.all_to_all(message, GX_GY, split_axis=0, concat_axis=0, tiled=True)  19.3 us
    all_to_all x1, starting transfers between devices, shards(): lax.all_to_all(sending, GX_GY, split_axis=0, concat_axis=0, tiled=True)  11.5 us
    ppermute x4, starting transfers between devices, swap(): second = lax.ppermute(jnp.where(even, to_low, to_high), axis, pairs(1))  6.16 us
    pallas_call x1, Pallas kernels, prepare(): pl.pallas_call(prepare_kernel, out_shape=(record, record, record), compil...  4.92 us
    pallas_call x1, Pallas kernels, find_moments(): pl.pallas_call(moments_kernel, out_shape=(jax.ShapeDtypeStruct((bricks, 8...  4.91 us
    pallas_call x1, Pallas kernels, pack(): pl.pallas_call(pack_kernel, in_specs=[pl.BlockSpec(memory_space=pltpu.VME...  3.48 us
    ppermute x4, waiting for transfers between devices, swap(): second = lax.ppermute(jnp.where(even, to_low, to_high), axis, pairs(1))  3.46 us
  transfers between devices with their start and end apart: 9, of which 3 were waited for; matrix products, arithmetic and copies ran while one was open for 0% of the time, Pallas kernels for 13%

profile of v7, /device:TPU:1, one launch (start us, length us, event | category | flops | bytes accessed | tf_op | source)
XLA Modules:
  0.0 87.7 jit_solution(18292832696362875920)
XLA Ops:
  0.6 3.5 %pack.1 = bf16[128,66,128]{2,1,0:T(8,128)(2,1)} custom-call(s32[8,4096]{1,0:T(8,128)} %bitcast.17, bf16[32,32768]{1,0:T(8,128)(2,1)} %feats_ref.3, bf16[256,128]{1,0:T(8,128)(2,1)} %bitcast.18), custom_call_target="tpu_custom_call" | custom-call | tf_op jit(solution)/shard_map/pack/pallas_call | solution.py:186
  4.1 0.0 copy-start.3
  4.1 0.0 copy-start.2
  4.1 11.5 %all-to-all-start = ((bf16[128,66,128]{2,1,0:T(8,128)(2,1)}), bf16[128,66,128]{2,1,0:T(8,128)(2,1)S(1)}, u32[]{:S(2)}, u32[]{:S(2)}) async-start(bf16[128,66,128]{2,1,0:T(8,128)(2,1)} %pack.1), calls=%async_computation | async-start | bytes 4718592 | tf_op jit(solution)/shard_map/all_to_all | solution.py:644
  15.7 0.0 copy-done.3
  15.7 0.1 copy.11
  15.8 0.0 copy-done.2
  15.8 0.0 copy-start
  15.8 1.6 %copy-done = f32[32,32,512]{2,1,0:T(8,128)S(1)} copy-done((f32[32,32,512]{2,1,0:T(8,128)S(1)}, f32[32,32,512]{2,1,0:T(8,128)}, u32[]{:S(2)}) %copy-start) | copy-done | bytes 2097176
  17.4 4.9 %prepare.1 = (f32[32,8,128]{2,1,0:T(8,128)S(1)}, f32[32,8,128]{2,1,0:T(8,128)S(1)}, f32[32,8,128]{2,1,0:T(8,128)S(1)}) custom-call(f32[32,32,512]{2,1,0:T(8,128)S(1)} %copy-done, f32[32,512]{1,0:T(8,128)S(1)} %copy-done.2), custom_call_target="tpu_custom_call" | custom-call | flops 600000000 | bytes 5000000 | tf_op jit(solution)/shard_map/prepare/pallas_call | solution.py:253
  22.4 1.1 %collective-permute-start.3 = (f32[104,128]{1,0:T(8,128)S(1)}, f32[104,128]{1,0:T(8,128)S(1)}, u32[]{:S(2)}, u32[]{:S(2)}) collective-permute-start(f32[104,128]{1,0:T(8,128)S(1)} %get-tuple-element.48), channel_id=1, source_target_pairs={{0,4},{4,0},{8,12},{12,8},{16,20},{20,16},{24,28},{28,24},{32,36},... | collective-permute-start | bytes 159752 | tf_op jit(solution)/shard_map/ppermute | solution.py:357
  23.5 2.7 %collective-permute-start.2 = (f32[104,128]{1,0:T(8,128)S(1)}, f32[104,128]{1,0:T(8,128)S(1)}, u32[]{:S(2)}, u32[]{:S(2)}) collective-permute-start(f32[104,128]{1,0:T(8,128)S(1)} %get-tuple-element.49), channel_id=1, source_target_pairs={{4,8},{8,4},{12,16},{16,12},{20,24},{24,20},{28,32},{32,28},{36,40... | collective-permute-start | bytes 159752 | tf_op jit(solution)/shard_map/ppermute | solution.py:358
  26.4 1.3 %collective-permute-start.7 = (f32[208,128]{1,0:T(8,128)S(1)}, f32[208,128]{1,0:T(8,128)S(1)}, u32[]{:S(2)}, u32[]{:S(2)}) collective-permute-start(f32[208,128]{1,0:T(8,128)S(1)} %get-tuple-element.36), channel_id=1, source_target_pairs={{0,1},{1,0},{2,3},{3,2},{4,5},{5,4},{6,7},{7,6},{8,9},{9,8},{10,11... | collective-permute-start | bytes 319496 | tf_op jit(solution)/shard_map/ppermute | solution.py:357
  27.6 0.7 collective-permute-start.6
  28.3 21.6 %all-to-all-done.got_ref = bf16[128,66,128]{2,1,0:T(8,128)(2,1)S(1)} async-done(((bf16[128,66,128]{2,1,0:T(8,128)(2,1)}), bf16[128,66,128]{2,1,0:T(8,128)(2,1)S(1)}, u32[]{:S(2)}, u32[]{:S(2)}) %all-to-all-start) | async-done | bytes 2162720 | tf_op jit(solution)/shard_map/all_to_all | solution.py:644
  49.9 0.0 copy-start.1
  49.9 4.9 %moments.1 = (f32[32,8,128]{2,1,0:T(8,128)S(1)}, f32[32,128]{1,0:T(8,128)S(1)}, f32[80,128]{1,0:T(8,128)S(1)}, f32[80,128]{1,0:T(8,128)S(1)}) custom-call(bf16[128,66,128]{2,1,0:T(8,128)(2,1)S(1)} %all-to-all-done.got_ref, f32[32,8,128]{2,1,0:T(8,128)S(1)} %get-tuple-element.18.first_ref, f32[32,8,128]{2,1,0:T(8,128)S(1)} %get-tuple-element.19.second_ref, ...), custom_call_target="tpu_custom_call" | custom-call | flops 1000000000 | bytes 12000000 | tf_op jit(solution)/shard_map/moments/pallas_call | solution.py:430
  54.9 0.1 collective-permute-start.1
  55.0 0.0 collective-permute-done.3
  55.0 2.1 %collective-permute-start = (f32[80,128]{1,0:T(8,128)S(1)}, f32[80,128]{1,0:T(8,128)S(1)}, u32[]{:S(2)}, u32[]{:S(2)}) collective-permute-start(f32[80,128]{1,0:T(8,128)S(1)} %get-tuple-element.53), channel_id=1, source_target_pairs={{4,8},{8,4},{12,16},{16,12},{20,24},{24,20},{28,32},{32,28},{36,40... | collective-permute-start | bytes 122888 | tf_op jit(solution)/shard_map/ppermute | solution.py:358
  57.1 0.0 collective-permute-done.2
  57.1 0.0 collective-permute-done.1
  57.1 3.5 %collective-permute-done = f32[80,128]{1,0:T(8,128)S(1)} collective-permute-done((f32[80,128]{1,0:T(8,128)S(1)}, f32[80,128]{1,0:T(8,128)S(1)}, u32[]{:S(2)}, u32[]{:S(2)}) %collective-permute-start) | collective-permute-done | bytes 40992 | tf_op jit(solution)/shard_map/ppermute | solution.py:358
  60.7 0.4 collective-permute-start.5
  61.0 0.7 collective-permute-start.4
  61.7 0.0 collective-permute-done.7
  61.7 0.0 collective-permute-done.6
  61.8 1.3 %gather_early.1 = (f32[1024,256]{1,0:T(8,128)S(1)}, f32[1024,256]{1,0:T(8,128)S(1)}, f32[8,256]{1,0:T(8,128)S(1)}) custom-call(f32[32,8,128]{2,1,0:T(8,128)S(1)} %get-tuple-element.18.first_ref, f32[32,8,128]{2,1,0:T(8,128)S(1)} %get-tuple-element.19.second_ref, f32[32,128]{1,0:T(8,128)S(1)} %pad.4.mask_ref, ...), custom_call_target="tpu_custom_call" | custom-call | flops 2000000 | bytes 3000000 | tf_op jit(solution)/shard_map/gather_early/pallas_call | solution.py:289
  63.1 1.2 %collective-permute-done.5 = f32[200,128]{1,0:T(8,128)S(1)} collective-permute-done((f32[200,128]{1,0:T(8,128)S(1)}, f32[200,128]{1,0:T(8,128)S(1)}, u32[]{:S(2)}, u32[]{:S(2)}) %collective-permute-start.5) | collective-permute-done | bytes 102432 | tf_op jit(solution)/shard_map/ppermute | solution.py:357
  64.3 0.0 collective-permute-done.4
  64.3 0.0 copy-done.1
  64.3 3.1 %krylov.1 = (f32[4,32,512]{2,1,0:T(8,128)S(1)}, f32[128,128]{1,0:T(8,128)S(1)}) custom-call(f32[32,8,128]{2,1,0:T(8,128)S(1)} %get-tuple-element.21.moments_ref, f32[32,128]{1,0:T(8,128)S(1)} %get-tuple-element.22.vectors_ref, f32[80,128]{1,0:T(8,128)S(1)} %get-tuple-element.51.low.low_ref, f32[80,128]{1,0:T(8,128)S(1)} %get-tuple-element.50.high.high_ref, ...), custom_call_target="tpu_custom_call" | custom-call | tf_op jit(solution)/shard_map/krylov/pallas_call | solution.py:544
  67.4 19.3 %all_to_all.16 = f32[128,1,128]{2,1,0:T(1,128)S(1)} all-to-all(f32[128,1,128]{2,1,0:T(1,128)S(1)} %bitcast.16), channel_id=1, replica_groups=mesh['gx_0'=4,'gx_1'=4,'gx_2'=2,'gy'=4] {'gx_0','gx_1','gx_2','gy'}, dimensions={0} | all-to-all | bytes 131072 | tf_op jit(solution)/shard_map/all_to_all | solution.py:668
  86.7 1.1 %finish.1 = (f32[32,512]{1,0:T(8,128)}, f32[32,512]{1,0:T(8,128)}) custom-call(f32[128,128]{1,0:T(8,128)S(1)} %bitcast.15, f32[4,32,512]{2,1,0:T(8,128)S(1)} %get-tuple-element.33.basis_ref), custom_call_target="tpu_custom_call" | custom-call | tf_op jit(solution)/shard_map/finish/pallas_call | solution.py:630
  (17 shorter events, 0.2 us)
Async XLA Ops:
  4.1 11.5 %copy-start.3 = (s32[32,4]{0,1:T(4,128)S(1)}, s32[32,4]{0,1:T(4,128)}, u32[]{:S(2)}) copy-start(s32[32,4]{0,1:T(4,128)} %param.9) | copy-start | bytes 1540
  4.1 11.7 %copy-start.2 = (f32[32,512]{1,0:T(8,128)S(1)}, f32[32,512]{1,0:T(8,128)}, u32[]{:S(2)}) copy-start(f32[32,512]{1,0:T(8,128)} %reg_ref.3) | copy-start | bytes 196612
  4.1 45.8 %all-to-all-start = ((bf16[128,66,128]{2,1,0:T(8,128)(2,1)}), bf16[128,66,128]{2,1,0:T(8,128)(2,1)S(1)}, u32[]{:S(2)}, u32[]{:S(2)}) async-start(bf16[128,66,128]{2,1,0:T(8,128)(2,1)} %pack.1), calls=%async_computation | async-start | bytes 4718592 | tf_op jit(solution)/shard_map/all_to_all | solution.py:644
  15.8 1.6 %copy-start = (f32[32,32,512]{2,1,0:T(8,128)S(1)}, f32[32,32,512]{2,1,0:T(8,128)}, u32[]{:S(2)}) copy-start(f32[32,32,512]{2,1,0:T(8,128)} %feats_ref.5) | copy-start | bytes 6291460
  22.4 32.6 %collective-permute-start.3 = (f32[104,128]{1,0:T(8,128)S(1)}, f32[104,128]{1,0:T(8,128)S(1)}, u32[]{:S(2)}, u32[]{:S(2)}) collective-permute-start(f32[104,128]{1,0:T(8,128)S(1)} %get-tuple-element.48), channel_id=1, source_target_pairs={{0,4},{4,0},{8,12},{12,8},{16,20},{20,16},{24,28},{28,24},{32,36},... | collective-permute-start | bytes 159752 | tf_op jit(solution)/shard_map/ppermute | solution.py:357
  23.5 33.6 %collective-permute-start.2 = (f32[104,128]{1,0:T(8,128)S(1)}, f32[104,128]{1,0:T(8,128)S(1)}, u32[]{:S(2)}, u32[]{:S(2)}) collective-permute-start(f32[104,128]{1,0:T(8,128)S(1)} %get-tuple-element.49), channel_id=1, source_target_pairs={{4,8},{8,4},{12,16},{16,12},{20,24},{24,20},{28,32},{32,28},{36,40... | collective-permute-start | bytes 159752 | tf_op jit(solution)/shard_map/ppermute | solution.py:358
  26.4 35.4 %collective-permute-start.7 = (f32[208,128]{1,0:T(8,128)S(1)}, f32[208,128]{1,0:T(8,128)S(1)}, u32[]{:S(2)}, u32[]{:S(2)}) collective-permute-start(f32[208,128]{1,0:T(8,128)S(1)} %get-tuple-element.36), channel_id=1, source_target_pairs={{0,1},{1,0},{2,3},{3,2},{4,5},{5,4},{6,7},{7,6},{8,9},{9,8},{10,11... | collective-permute-start | bytes 319496 | tf_op jit(solution)/shard_map/ppermute | solution.py:357
  27.6 34.1 %collective-permute-start.6 = (f32[208,128]{1,0:T(8,128)S(1)}, f32[208,128]{1,0:T(8,128)S(1)}, u32[]{:S(2)}, u32[]{:S(2)}) collective-permute-start(f32[208,128]{1,0:T(8,128)S(1)} %get-tuple-element.37), channel_id=1, source_target_pairs={{1,2},{2,1},{5,6},{6,5},{9,10},{10,9},{13,14},{14,13},{17,18},{18,... | collective-permute-start | bytes 319496 | tf_op jit(solution)/shard_map/ppermute | solution.py:358
  49.9 14.4 %copy-start.1 = (f32[32,32,512]{2,1,0:T(8,128)S(1)}, f32[32,32,512]{2,1,0:T(8,128)}, u32[]{:S(2)}) copy-start(f32[32,32,512]{2,1,0:T(8,128)} %feats_ref.5) | copy-start | bytes 6291460
  54.9 2.3 %collective-permute-start.1 = (f32[80,128]{1,0:T(8,128)S(1)}, f32[80,128]{1,0:T(8,128)S(1)}, u32[]{:S(2)}, u32[]{:S(2)}) collective-permute-start(f32[80,128]{1,0:T(8,128)S(1)} %get-tuple-element.52), channel_id=1, source_target_pairs={{0,4},{4,0},{8,12},{12,8},{16,20},{20,16},{24,28},{28,24},{32,36},... | collective-permute-start | bytes 122888 | tf_op jit(solution)/shard_map/ppermute | solution.py:357
  55.0 5.6 %collective-permute-start = (f32[80,128]{1,0:T(8,128)S(1)}, f32[80,128]{1,0:T(8,128)S(1)}, u32[]{:S(2)}, u32[]{:S(2)}) collective-permute-start(f32[80,128]{1,0:T(8,128)S(1)} %get-tuple-element.53), channel_id=1, source_target_pairs={{4,8},{8,4},{12,16},{16,12},{20,24},{24,20},{28,32},{32,28},{36,40... | collective-permute-start | bytes 122888 | tf_op jit(solution)/shard_map/ppermute | solution.py:358
  60.7 3.6 %collective-permute-start.5 = (f32[200,128]{1,0:T(8,128)S(1)}, f32[200,128]{1,0:T(8,128)S(1)}, u32[]{:S(2)}, u32[]{:S(2)}) collective-permute-start(f32[200,128]{1,0:T(8,128)S(1)} %get-tuple-element.40), channel_id=1, source_target_pairs={{0,1},{1,0},{2,3},{3,2},{4,5},{5,4},{6,7},{7,6},{8,9},{9,8},{10,11... | collective-permute-start | bytes 307208 | tf_op jit(solution)/shard_map/ppermute | solution.py:357
  61.0 3.2 %collective-permute-start.4 = (f32[200,128]{1,0:T(8,128)S(1)}, f32[200,128]{1,0:T(8,128)S(1)}, u32[]{:S(2)}, u32[]{:S(2)}) collective-permute-start(f32[200,128]{1,0:T(8,128)S(1)} %get-tuple-element.41), channel_id=1, source_target_pairs={{1,2},{2,1},{5,6},{6,5},{9,10},{10,9},{13,14},{14,13},{17,18},{18,... | collective-permute-start | bytes 307208 | tf_op jit(solution)/shard_map/ppermute | solution.py:358

commit v8 on v7

--- a/solution.py
+++ b/solution.py
@@ -124,8 +124,14 @@
     return total
 
 
-def pack_kernel(lists_ref, feats_ref, targets_ref, out_ref, feats, packed, arrived, left):
+def pack_kernel(
+    lists_hbm, feats_ref, targets_hbm, out_ref, lists_ref, feats, targets_ref, packed, arrived, left, small
+):
     steps = arrived.shape[0]
+    lists_copy = pltpu.make_async_copy(lists_hbm, lists_ref, small.at[0])
+    targets_copy = pltpu.make_async_copy(targets_hbm, targets_ref, small.at[1])
+    lists_copy.start()
+    targets_copy.start()
     devices = out_ref.shape[0]
     bricks = lists_ref.shape[1]
     dests = devices // steps
@@ -145,6 +151,7 @@
     ]
     for copy in arriving:
         copy.start()
+    lists_copy.wait()
     rows = bricks // LANES
     lane = lax.broadcasted_iota(jnp.int32, (SLOTS, LANES), 1)
     codes = []
@@ -160,6 +167,7 @@
     wide = jnp.dot(code, spread, preferred_element_type=jnp.float32).astype(jnp.int32)
     slot = lax.broadcasted_iota(jnp.int32, (rows, width), 1) & (SLOTS - 1)
     mask = (lax.shift_right_logical(wide, slot) & 1).astype(jnp.float32)
+    targets_copy.wait()
     for k in range(steps):
         arriving[k].wait()
         for part in range(points // width):
@@ -186,17 +194,20 @@
     return pl.pallas_call(
         pack_kernel,
         in_specs=[
-            pl.BlockSpec(memory_space=pltpu.VMEM),
             pl.BlockSpec(memory_space=pl.ANY),
-            pl.BlockSpec(memory_space=pltpu.VMEM),
+            pl.BlockSpec(memory_space=pl.ANY),
+            pl.BlockSpec(memory_space=pl.ANY),
         ],
         out_specs=pl.BlockSpec(memory_space=pl.ANY),
         out_shape=jax.ShapeDtypeStruct((devices, rows, LANES), jnp.bfloat16),
         scratch_shapes=[
+            pltpu.VMEM(point_lists.shape[::-1], jnp.int32),
             pltpu.VMEM((FEAT, points), jnp.bfloat16),
+            pltpu.VMEM((points // LANES, LANES), jnp.bfloat16),
             pltpu.VMEM((devices, rows, LANES), jnp.bfloat16),
             pltpu.SemaphoreType.DMA((steps,)),
             pltpu.SemaphoreType.DMA((steps,)),
+            pltpu.SemaphoreType.DMA((2,)),
         ],
         name="pack",
     )(point_lists.T, point_feats, point_targets.reshape(points // LANES, LANES))
@@ -362,15 +373,15 @@
 def moments_kernel(
     got_ref, first_ref, second_ref, third_ref, moments_ref, vectors_ref, low_ref, high_ref, turned, lanes_ref
 ):
-    for power, record in enumerate((first_ref, second_ref, third_ref)):
-        for t in range(8):
-            block = jnp.concatenate([record[:, t, :], jnp.zeros((LANES - BX * BY, LANES), jnp.float32)], axis=0)
-            lanes_ref[power, t * LANES : (t + 1) * LANES, :] = block.T
+    for t in range(8):
+        block = [record[:, t, :] for record in (first_ref, second_ref, third_ref)]
+        block = jnp.concatenate([*block, jnp.zeros((BX * BY, LANES), jnp.float32)], axis=0)
+        lanes_ref[t * LANES : (t + 1) * LANES, :] = block.T
     sources = got_ref.shape[0]
     for group in range(sources // 4):
         for half in range(2):
             block = got_ref[4 * group : 4 * group + 4, half * FEAT : (half + 1) * FEAT, :]
-            turned[half, group] = block.reshape(LANES, LANES).T
+            turned[half, group] = block.astype(jnp.float32).reshape(LANES, LANES).T
     sums = []
     for half in range(2):
         total = jnp.zeros((FEAT, LANES), jnp.float32)
@@ -381,38 +392,35 @@
         sums.append(total)
 
     groups = turned.shape[1]
-    row = lax.broadcasted_iota(jnp.int32, (1, 16, LANES), 1)
-    upper = (row < SLOTS).astype(jnp.float32).astype(jnp.bfloat16)
-    lower = (row >= SLOTS).astype(jnp.float32).astype(jnp.bfloat16)
     lane_group = lax.broadcasted_iota(jnp.int32, (1, LANES), 1) // FEAT
     for half in range(2):
         for pair in range(8):
-            points = turned[half, :, 16 * pair : 16 * pair + 16, :]
-            left = points.reshape(groups * 16, LANES)
-            right = jnp.concatenate(
-                [(points * upper).reshape(groups * 16, LANES), (points * lower).reshape(groups * 16, LANES)],
-                axis=1,
-            )
-            product = lax.dot_general(
-                left, right, (((0,), (0,)), ((), ())), preferred_element_type=jnp.float32
-            )
             for k in range(2):
-                square = product[:, k * LANES : (k + 1) * LANES]
+                b = 2 * pair + k
+                points = turned[half, :, 8 * b : 8 * b + 8, :].reshape(groups * 8, LANES)
+                square = lax.dot_general(
+                    points.T.astype(jnp.bfloat16),
+                    points.astype(jnp.bfloat16),
+                    (((1,), (0,)), ((), ())),
+                    preferred_element_type=jnp.float32,
+                )
                 own = jnp.zeros((FEAT, LANES), jnp.float32)
                 for q in range(4):
                     own = own + jnp.where(lane_group == q, square[q * FEAT : (q + 1) * FEAT, :], 0.0)
-                moments_ref[half * 16 + 2 * pair + k] = spread_rows(own, lane_group)
+                moments_ref[half * 16 + b] = spread_rows(own, lane_group)
     point = lax.broadcasted_iota(jnp.int32, (LANES, LANES), 0) // SLOTS
     lane = lax.broadcasted_iota(jnp.int32, (LANES, LANES), 1)
     values = jnp.zeros((FEAT, LANES), jnp.float32)
     for half in range(2):
-        spread = (lane == point + half * 16).astype(jnp.float32)
+        spread = (lane % (BX * BY) == point + half * 16).astype(jnp.float32)
         values = values + jnp.dot(
             sums[half], spread, precision=HIGHEST, preferred_element_type=jnp.float32
         )
-    applied = [times(lanes_ref.at[power], values) for power in range(3)]
-    vectors = jnp.concatenate([*applied, values], axis=0).T
-    vectors_ref[...] = vectors[: BX * BY, :]
+    values = times(lanes_ref, values) + jnp.where(lane_group == 3, values, 0.0)
+    values = jnp.concatenate([values, jnp.zeros((LANES - FEAT, LANES), jnp.float32)], axis=0).T
+    bricks = BX * BY
+    vectors = jnp.concatenate([values[k * bricks : (k + 1) * bricks, :FEAT] for k in range(4)], axis=1)
+    vectors_ref[...] = vectors
     depth = LATE[0][1] * BY
     for k in range(depth):
         low_ref[8 * k : 8 * k + 8, :] = moments_ref[k]
@@ -436,8 +444,8 @@
             message,
         ),
         scratch_shapes=[
-            pltpu.VMEM((2, devices // 4, LANES, LANES), jnp.bfloat16),
-            pltpu.VMEM((3, 8 * LANES, LANES), jnp.float32),
+            pltpu.VMEM((2, devices // 4, LANES, LANES), jnp.float32),
+            pltpu.VMEM((8 * LANES, LANES), jnp.float32),
         ],
         compiler_params=pltpu.CompilerParams(vmem_limit_bytes=12 << 20),
         cost_estimate=pl.CostEstimate(flops=1_000_000_000, bytes_accessed=12_000_000, transcendentals=0),

time: 88.1 us -> 86.8 us (0.985)
  Pallas kernels: 18.9 us -> 17.6 us
    pallas_call x1, Pallas kernels: 4.91 us -> 3.85 us  [find_moments(): pl.pallas_call(moments_kernel, out_shape=(jax.ShapeDtypeStruct((bricks, 8...]
  transfers between devices with their start and end apart: 9 -> 9, of which waited for: 3 -> 3; matrix products, arithmetic and copies ran while one was open for 0% -> 0% of each run, Pallas kernels for 13% -> 12%
where the time goes in v8:
time: 86.8 us; the launch traced here: 86.4 us
  waiting for transfers between devices  26.3 us (30%)
  starting transfers between devices  20.5 us (24%)
  blocking collectives  19.2 us (22%)
  Pallas kernels  17.6 us (20%)
  local copies, waits for them, and re-layouts  1.72 us (2%)
  between operations  0.92 us (1%)
    all_to_all x1, waiting for transfers between devices, shards(): lax.all_to_all(sending, GX_GY, split_axis=0, concat_axis=0, tiled=True)  21.6 us
    all_to_all x1, blocking collectives, shards(): lax.all_to_all(message, GX_GY, split_axis=0, concat_axis=0, tiled=True)  19.2 us
    all_to_all x1, starting transfers between devices, shards(): lax.all_to_all(sending, GX_GY, split_axis=0, concat_axis=0, tiled=True)  11.5 us
    ppermute x4, starting transfers between devices, swap(): second = lax.ppermute(jnp.where(even, to_low, to_high), axis, pairs(1))  6.16 us
    pallas_call x1, Pallas kernels, prepare(): pl.pallas_call(prepare_kernel, out_shape=(record, record, record), compil...  4.92 us
    pallas_call x1, Pallas kernels, find_moments(): pl.pallas_call(moments_kernel, out_shape=(jax.ShapeDtypeStruct((bricks, 8...  3.85 us
    ppermute x4, waiting for transfers between devices, swap(): second = lax.ppermute(jnp.where(even, to_low, to_high), axis, pairs(1))  3.46 us
    pallas_call x1, Pallas kernels, pack(): pl.pallas_call(pack_kernel, in_specs=[pl.BlockSpec(memory_space=pl.ANY),...  3.23 us
  transfers between devices with their start and end apart: 9, of which 3 were waited for; matrix products, arithmetic and copies ran while one was open for 0% of the time, Pallas kernels for 12%

profile of v8, /device:TPU:1, one launch (start us, length us, event | category | flops | bytes accessed | tf_op | source)
XLA Modules:
  0.0 86.4 jit_solution(3547350993469536707)
XLA Ops:
  0.6 3.2 %pack.1 = bf16[128,66,128]{2,1,0:T(8,128)(2,1)} custom-call(s32[8,4096]{1,0:T(8,128)} %bitcast.17, bf16[32,32768]{1,0:T(8,128)(2,1)} %feats_ref.3, bf16[256,128]{1,0:T(8,128)(2,1)} %bitcast.18), custom_call_target="tpu_custom_call" | custom-call | tf_op jit(solution)/shard_map/pack/pallas_call | solution.py:194
  3.9 0.0 copy-start.3
  3.9 0.0 copy-start.2
  3.9 11.5 %all-to-all-start = ((bf16[128,66,128]{2,1,0:T(8,128)(2,1)}), bf16[128,66,128]{2,1,0:T(8,128)(2,1)S(1)}, u32[]{:S(2)}, u32[]{:S(2)}) async-start(bf16[128,66,128]{2,1,0:T(8,128)(2,1)} %pack.1), calls=%async_computation | async-start | bytes 4718592 | tf_op jit(solution)/shard_map/all_to_all | solution.py:652
  15.4 0.0 copy-done.3
  15.5 0.1 copy.11
  15.6 0.0 copy-done.2
  15.6 0.0 copy-start
  15.6 1.6 %copy-done = f32[32,32,512]{2,1,0:T(8,128)S(1)} copy-done((f32[32,32,512]{2,1,0:T(8,128)S(1)}, f32[32,32,512]{2,1,0:T(8,128)}, u32[]{:S(2)}) %copy-start) | copy-done | bytes 2097176
  17.1 4.9 %prepare.1 = (f32[32,8,128]{2,1,0:T(8,128)S(1)}, f32[32,8,128]{2,1,0:T(8,128)S(1)}, f32[32,8,128]{2,1,0:T(8,128)S(1)}) custom-call(f32[32,32,512]{2,1,0:T(8,128)S(1)} %copy-done, f32[32,512]{1,0:T(8,128)S(1)} %copy-done.2), custom_call_target="tpu_custom_call" | custom-call | flops 600000000 | bytes 5000000 | tf_op jit(solution)/shard_map/prepare/pallas_call | solution.py:264
  22.1 1.1 %collective-permute-start.3 = (f32[104,128]{1,0:T(8,128)S(1)}, f32[104,128]{1,0:T(8,128)S(1)}, u32[]{:S(2)}, u32[]{:S(2)}) collective-permute-start(f32[104,128]{1,0:T(8,128)S(1)} %get-tuple-element.48), channel_id=1, source_target_pairs={{0,4},{4,0},{8,12},{12,8},{16,20},{20,16},{24,28},{28,24},{32,36},... | collective-permute-start | bytes 159752 | tf_op jit(solution)/shard_map/ppermute | solution.py:368
  23.3 2.7 %collective-permute-start.2 = (f32[104,128]{1,0:T(8,128)S(1)}, f32[104,128]{1,0:T(8,128)S(1)}, u32[]{:S(2)}, u32[]{:S(2)}) collective-permute-start(f32[104,128]{1,0:T(8,128)S(1)} %get-tuple-element.49), channel_id=1, source_target_pairs={{4,8},{8,4},{12,16},{16,12},{20,24},{24,20},{28,32},{32,28},{36,40... | collective-permute-start | bytes 159752 | tf_op jit(solution)/shard_map/ppermute | solution.py:369
  26.1 1.3 %collective-permute-start.7 = (f32[208,128]{1,0:T(8,128)S(1)}, f32[208,128]{1,0:T(8,128)S(1)}, u32[]{:S(2)}, u32[]{:S(2)}) collective-permute-start(f32[208,128]{1,0:T(8,128)S(1)} %get-tuple-element.36), channel_id=1, source_target_pairs={{0,1},{1,0},{2,3},{3,2},{4,5},{5,4},{6,7},{7,6},{8,9},{9,8},{10,11... | collective-permute-start | bytes 319496 | tf_op jit(solution)/shard_map/ppermute | solution.py:368
  27.4 0.7 collective-permute-start.6
  28.0 21.6 %all-to-all-done.got_ref = bf16[128,66,128]{2,1,0:T(8,128)(2,1)S(1)} async-done(((bf16[128,66,128]{2,1,0:T(8,128)(2,1)}), bf16[128,66,128]{2,1,0:T(8,128)(2,1)S(1)}, u32[]{:S(2)}, u32[]{:S(2)}) %all-to-all-start) | async-done | bytes 2162720 | tf_op jit(solution)/shard_map/all_to_all | solution.py:652
  49.7 0.0 copy-start.1
  49.7 3.8 %moments.1 = (f32[32,8,128]{2,1,0:T(8,128)S(1)}, f32[32,128]{1,0:T(8,128)S(1)}, f32[80,128]{1,0:T(8,128)S(1)}, f32[80,128]{1,0:T(8,128)S(1)}) custom-call(bf16[128,66,128]{2,1,0:T(8,128)(2,1)S(1)} %all-to-all-done.got_ref, f32[32,8,128]{2,1,0:T(8,128)S(1)} %get-tuple-element.18.first_ref, f32[32,8,128]{2,1,0:T(8,128)S(1)} %get-tuple-element.19.second_ref, ...), custom_call_target="tpu_custom_call" | custom-call | flops 1000000000 | bytes 12000000 | tf_op jit(solution)/shard_map/moments/pallas_call | solution.py:438
  53.5 0.1 collective-permute-start.1
  53.6 0.0 collective-permute-done.3
  53.6 2.1 %collective-permute-start = (f32[80,128]{1,0:T(8,128)S(1)}, f32[80,128]{1,0:T(8,128)S(1)}, u32[]{:S(2)}, u32[]{:S(2)}) collective-permute-start(f32[80,128]{1,0:T(8,128)S(1)} %get-tuple-element.53), channel_id=1, source_target_pairs={{4,8},{8,4},{12,16},{16,12},{20,24},{24,20},{28,32},{32,28},{36,40... | collective-permute-start | bytes 122888 | tf_op jit(solution)/shard_map/ppermute | solution.py:369
  55.8 0.0 collective-permute-done.2
  55.8 0.0 collective-permute-done.1
  55.8 3.5 %collective-permute-done = f32[80,128]{1,0:T(8,128)S(1)} collective-permute-done((f32[80,128]{1,0:T(8,128)S(1)}, f32[80,128]{1,0:T(8,128)S(1)}, u32[]{:S(2)}, u32[]{:S(2)}) %collective-permute-start) | collective-permute-done | bytes 40992 | tf_op jit(solution)/shard_map/ppermute | solution.py:369
  59.3 0.4 collective-permute-start.5
  59.7 0.7 collective-permute-start.4
  60.4 0.0 collective-permute-done.7
  60.4 0.0 collective-permute-done.6
  60.4 1.3 %gather_early.1 = (f32[1024,256]{1,0:T(8,128)S(1)}, f32[1024,256]{1,0:T(8,128)S(1)}, f32[8,256]{1,0:T(8,128)S(1)}) custom-call(f32[32,8,128]{2,1,0:T(8,128)S(1)} %get-tuple-element.18.first_ref, f32[32,8,128]{2,1,0:T(8,128)S(1)} %get-tuple-element.19.second_ref, f32[32,128]{1,0:T(8,128)S(1)} %pad.4.mask_ref, ...), custom_call_target="tpu_custom_call" | custom-call | flops 2000000 | bytes 3000000 | tf_op jit(solution)/shard_map/gather_early/pallas_call | solution.py:300
  61.8 1.2 %collective-permute-done.5 = f32[200,128]{1,0:T(8,128)S(1)} collective-permute-done((f32[200,128]{1,0:T(8,128)S(1)}, f32[200,128]{1,0:T(8,128)S(1)}, u32[]{:S(2)}, u32[]{:S(2)}) %collective-permute-start.5) | collective-permute-done | bytes 102432 | tf_op jit(solution)/shard_map/ppermute | solution.py:368
  62.9 0.0 collective-permute-done.4
  63.0 0.0 copy-done.1
  63.0 3.1 %krylov.1 = (f32[4,32,512]{2,1,0:T(8,128)S(1)}, f32[128,128]{1,0:T(8,128)S(1)}) custom-call(f32[32,8,128]{2,1,0:T(8,128)S(1)} %get-tuple-element.21.moments_ref, f32[32,128]{1,0:T(8,128)S(1)} %get-tuple-element.22.vectors_ref, f32[80,128]{1,0:T(8,128)S(1)} %get-tuple-element.51.low.low_ref, f32[80,128]{1,0:T(8,128)S(1)} %get-tuple-element.50.high.high_ref, ...), custom_call_target="tpu_custom_call" | custom-call | tf_op jit(solution)/shard_map/krylov/pallas_call | solution.py:552
  66.1 19.2 %all_to_all.16 = f32[128,1,128]{2,1,0:T(1,128)S(1)} all-to-all(f32[128,1,128]{2,1,0:T(1,128)S(1)} %bitcast.16), channel_id=1, replica_groups=mesh['gx_0'=4,'gx_1'=4,'gx_2'=2,'gy'=4] {'gx_0','gx_1','gx_2','gy'}, dimensions={0} | all-to-all | bytes 131072 | tf_op jit(solution)/shard_map/all_to_all | solution.py:676
  85.3 1.1 %finish.1 = (f32[32,512]{1,0:T(8,128)}, f32[32,512]{1,0:T(8,128)}) custom-call(f32[128,128]{1,0:T(8,128)S(1)} %bitcast.15, f32[4,32,512]{2,1,0:T(8,128)S(1)} %get-tuple-element.33.basis_ref), custom_call_target="tpu_custom_call" | custom-call | tf_op jit(solution)/shard_map/finish/pallas_call | solution.py:638
  (17 shorter events, 0.2 us)
Async XLA Ops:
  3.9 11.5 %copy-start.3 = (s32[32,4]{0,1:T(4,128)S(1)}, s32[32,4]{0,1:T(4,128)}, u32[]{:S(2)}) copy-start(s32[32,4]{0,1:T(4,128)} %param.9) | copy-start | bytes 1540
  3.9 11.7 %copy-start.2 = (f32[32,512]{1,0:T(8,128)S(1)}, f32[32,512]{1,0:T(8,128)}, u32[]{:S(2)}) copy-start(f32[32,512]{1,0:T(8,128)} %reg_ref.3) | copy-start | bytes 196612
  3.9 45.8 %all-to-all-start = ((bf16[128,66,128]{2,1,0:T(8,128)(2,1)}), bf16[128,66,128]{2,1,0:T(8,128)(2,1)S(1)}, u32[]{:S(2)}, u32[]{:S(2)}) async-start(bf16[128,66,128]{2,1,0:T(8,128)(2,1)} %pack.1), calls=%async_computation | async-start | bytes 4718592 | tf_op jit(solution)/shard_map/all_to_all | solution.py:652
  15.6 1.6 %copy-start = (f32[32,32,512]{2,1,0:T(8,128)S(1)}, f32[32,32,512]{2,1,0:T(8,128)}, u32[]{:S(2)}) copy-start(f32[32,32,512]{2,1,0:T(8,128)} %feats_ref.5) | copy-start | bytes 6291460
  22.1 31.5 %collective-permute-start.3 = (f32[104,128]{1,0:T(8,128)S(1)}, f32[104,128]{1,0:T(8,128)S(1)}, u32[]{:S(2)}, u32[]{:S(2)}) collective-permute-start(f32[104,128]{1,0:T(8,128)S(1)} %get-tuple-element.48), channel_id=1, source_target_pairs={{0,4},{4,0},{8,12},{12,8},{16,20},{20,16},{24,28},{28,24},{32,36},... | collective-permute-start | bytes 159752 | tf_op jit(solution)/shard_map/ppermute | solution.py:368
  23.3 32.5 %collective-permute-start.2 = (f32[104,128]{1,0:T(8,128)S(1)}, f32[104,128]{1,0:T(8,128)S(1)}, u32[]{:S(2)}, u32[]{:S(2)}) collective-permute-start(f32[104,128]{1,0:T(8,128)S(1)} %get-tuple-element.49), channel_id=1, source_target_pairs={{4,8},{8,4},{12,16},{16,12},{20,24},{24,20},{28,32},{32,28},{36,40... | collective-permute-start | bytes 159752 | tf_op jit(solution)/shard_map/ppermute | solution.py:369
  26.1 34.3 %collective-permute-start.7 = (f32[208,128]{1,0:T(8,128)S(1)}, f32[208,128]{1,0:T(8,128)S(1)}, u32[]{:S(2)}, u32[]{:S(2)}) collective-permute-start(f32[208,128]{1,0:T(8,128)S(1)} %get-tuple-element.36), channel_id=1, source_target_pairs={{0,1},{1,0},{2,3},{3,2},{4,5},{5,4},{6,7},{7,6},{8,9},{9,8},{10,11... | collective-permute-start | bytes 319496 | tf_op jit(solution)/shard_map/ppermute | solution.py:368
  27.4 33.0 %collective-permute-start.6 = (f32[208,128]{1,0:T(8,128)S(1)}, f32[208,128]{1,0:T(8,128)S(1)}, u32[]{:S(2)}, u32[]{:S(2)}) collective-permute-start(f32[208,128]{1,0:T(8,128)S(1)} %get-tuple-element.37), channel_id=1, source_target_pairs={{1,2},{2,1},{5,6},{6,5},{9,10},{10,9},{13,14},{14,13},{17,18},{18,... | collective-permute-start | bytes 319496 | tf_op jit(solution)/shard_map/ppermute | solution.py:369
  49.7 13.3 %copy-start.1 = (f32[32,32,512]{2,1,0:T(8,128)S(1)}, f32[32,32,512]{2,1,0:T(8,128)}, u32[]{:S(2)}) copy-start(f32[32,32,512]{2,1,0:T(8,128)} %feats_ref.5) | copy-start | bytes 6291460
  53.5 2.3 %collective-permute-start.1 = (f32[80,128]{1,0:T(8,128)S(1)}, f32[80,128]{1,0:T(8,128)S(1)}, u32[]{:S(2)}, u32[]{:S(2)}) collective-permute-start(f32[80,128]{1,0:T(8,128)S(1)} %get-tuple-element.52), channel_id=1, source_target_pairs={{0,4},{4,0},{8,12},{12,8},{16,20},{20,16},{24,28},{28,24},{32,36},... | collective-permute-start | bytes 122888 | tf_op jit(solution)/shard_map/ppermute | solution.py:368
  53.6 5.6 %collective-permute-start = (f32[80,128]{1,0:T(8,128)S(1)}, f32[80,128]{1,0:T(8,128)S(1)}, u32[]{:S(2)}, u32[]{:S(2)}) collective-permute-start(f32[80,128]{1,0:T(8,128)S(1)} %get-tuple-element.53), channel_id=1, source_target_pairs={{4,8},{8,4},{12,16},{16,12},{20,24},{24,20},{28,32},{32,28},{36,40... | collective-permute-start | bytes 122888 | tf_op jit(solution)/shard_map/ppermute | solution.py:369
  59.3 3.6 %collective-permute-start.5 = (f32[200,128]{1,0:T(8,128)S(1)}, f32[200,128]{1,0:T(8,128)S(1)}, u32[]{:S(2)}, u32[]{:S(2)}) collective-permute-start(f32[200,128]{1,0:T(8,128)S(1)} %get-tuple-element.40), channel_id=1, source_target_pairs={{0,1},{1,0},{2,3},{3,2},{4,5},{5,4},{6,7},{7,6},{8,9},{9,8},{10,11... | collective-permute-start | bytes 307208 | tf_op jit(solution)/shard_map/ppermute | solution.py:368
  59.7 3.2 %collective-permute-start.4 = (f32[200,128]{1,0:T(8,128)S(1)}, f32[200,128]{1,0:T(8,128)S(1)}, u32[]{:S(2)}, u32[]{:S(2)}) collective-permute-start(f32[200,128]{1,0:T(8,128)S(1)} %get-tuple-element.41), channel_id=1, source_target_pairs={{1,2},{2,1},{5,6},{6,5},{9,10},{10,9},{13,14},{14,13},{17,18},{18,... | collective-permute-start | bytes 307208 | tf_op jit(solution)/shard_map/ppermute | solution.py:369

commit v9 on v8

--- a/solution.py
+++ b/solution.py
@@ -26,7 +26,7 @@
 coupling_weight = 1.0
 
 EARLY = ((8, 2, False), (8, 1, False), (1, 2, False))
-LATE = ((8, 2, True), (1, 3, True))
+LATE = ((8, 1, True), (1, 3, True))
 CORNER_ROWS = 24
 
 
@@ -365,13 +365,14 @@
     def pairs(start):
         return [pair for a in range(start, count - 1, 2) for pair in ((a, a + 1), (a + 1, a))]
 
+    second = lax.ppermute(jnp.where(even, to_low, to_high), axis, pairs(1))
     first = lax.ppermute(jnp.where(even, to_high, to_low), axis, pairs(0))
-    second = lax.ppermute(jnp.where(even, to_low, to_high), axis, pairs(1))
     return jnp.where(even, second, first), jnp.where(even, first, second)
 
 
 def moments_kernel(
-    got_ref, first_ref, second_ref, third_ref, moments_ref, vectors_ref, low_ref, high_ref, turned, lanes_ref
+    got_ref, first_ref, second_ref, third_ref, moments_ref, vectors_ref, gathered_ref, low_ref, high_ref,
+    turned, lanes_ref, moment_lanes,
 ):
     for t in range(8):
         block = [record[:, t, :] for record in (first_ref, second_ref, third_ref)]
@@ -416,7 +417,12 @@
         values = values + jnp.dot(
             sums[half], spread, precision=HIGHEST, preferred_element_type=jnp.float32
         )
-    values = times(lanes_ref, values) + jnp.where(lane_group == 3, values, 0.0)
+    gathered_ref[...] = values
+    values = times(lanes_ref, values)
+    for t in range(8):
+        block = [moments_ref[:, t, :], jnp.zeros((LANES - BX * BY, LANES), jnp.float32)]
+        moment_lanes[t * LANES : (t + 1) * LANES, :] = jnp.concatenate(block, axis=0).T
+    values = jnp.where(lane_group == 3, pltpu.roll(times(moment_lanes, values), 96, 1), values)
     values = jnp.concatenate([values, jnp.zeros((LANES - FEAT, LANES), jnp.float32)], axis=0).T
     bricks = BX * BY
     vectors = jnp.concatenate([values[k * bricks : (k + 1) * bricks, :FEAT] for k in range(4)], axis=1)
@@ -440,11 +446,13 @@
         out_shape=(
             jax.ShapeDtypeStruct((bricks, 8, LANES), jnp.float32),
             jax.ShapeDtypeStruct((bricks, LANES), jnp.float32),
+            jax.ShapeDtypeStruct((FEAT, LANES), jnp.float32),
             message,
             message,
         ),
         scratch_shapes=[
             pltpu.VMEM((2, devices // 4, LANES, LANES), jnp.float32),
+            pltpu.VMEM((8 * LANES, LANES), jnp.float32),
             pltpu.VMEM((8 * LANES, LANES), jnp.float32),
         ],
         compiler_params=pltpu.CompilerParams(vmem_limit_bytes=12 << 20),
@@ -467,7 +475,7 @@
 
 
 def krylov_kernel(
-    moments_ref, vectors_ref, low_ref, high_ref, below_ref, above_ref, first_ref, second_ref, mask_ref,
+    moments_ref, vectors_ref, gathered_ref, low_ref, high_ref, below_ref, above_ref, first_ref, second_ref, mask_ref,
     feats_ref, reg_ref, basis_ref, message_ref, moment_store, vector_store, moment_lanes,
     corner_store, corner_masks, corner_lanes,
 ):
@@ -503,21 +511,25 @@
 
     masks = mask_ref[...] + both_tiles(corner_masks[...].T[:8, :])
 
-    def system(z):
+    def coupled(z):
         near = masks[0:1] * pltpu.roll(z, PITCH, 1) + masks[1:2] * pltpu.roll(z, SPAN - PITCH, 1)
         near = near + masks[2:3] * pltpu.roll(z, 1, 1) + masks[3:4] * pltpu.roll(z, SPAN - 1, 1)
-        return times(moment_lanes, z) + coupling_weight * (masks[4:5] * z - near)
-
-    one = system(vectors[0:FEAT])
+        return coupling_weight * (masks[4:5] * z - near)
+
+    def system(z):
+        return times(moment_lanes, z) + coupled(z)
+
+    one = vectors[3 * FEAT :] + coupled(vectors[0:FEAT])
     corners = times(corner_lanes, jnp.where(front, one[:, :LANES], one[:, LANES:]))
     two = system(times(first_ref, one) + both_tiles(corners) + vectors[FEAT : 2 * FEAT])
     three = system(times(first_ref, two) + times(second_ref, one) + vectors[2 * FEAT : 3 * FEAT])
-    chain = (vectors[3 * FEAT :], one, two, three)
+    gathered = gathered_ref[...]
     for b in range(BX * BY):
         place = lane_of(b // BY, b % BY)
         feats = feats_ref[b]
-        for step, values in enumerate(chain):
-            basis_ref[step, b : b + 1, :] = jnp.sum(feats * values[:, place : place + 1], axis=0, keepdims=True)
+        columns = [gathered[:, b : b + 1]] + [values[:, place : place + 1] for values in (one, two, three)]
+        for step, column in enumerate(columns):
+            basis_ref[step, b : b + 1, :] = jnp.sum(feats * column, axis=0, keepdims=True)
     reg = reg_ref[...]
     basis = [basis_ref[0]]
     for step in range(1, 4):
@@ -547,7 +559,7 @@
     message_ref[...] = jnp.broadcast_to(row, message_ref.shape)
 
 
-def krylov(moments, vectors, edges, first, second, masks, voxel_feats, voxel_reg, devices):
+def krylov(moments, vectors, gathered, edges, first, second, masks, voxel_feats, voxel_reg, devices):
     bricks, _, voxels = voxel_feats.shape
     return pl.pallas_call(
         krylov_kernel,
@@ -565,7 +577,7 @@
         ],
         compiler_params=pltpu.CompilerParams(vmem_limit_bytes=12 << 20),
         name="krylov",
-    )(moments, vectors, *edges, first, second, masks, voxel_feats, voxel_reg)
+    )(moments, vectors, gathered, *edges, first, second, masks, voxel_feats, voxel_reg)
 
 
 def finish_kernel(shared_ref, basis_ref, solution_ref, residual_ref):
@@ -661,7 +673,7 @@
     early_low, early_high = swap(*along_messages(EARLY, early), GX, along_even)
     early_below, early_above = swap(*across_early(early), "gy", across_even)
 
-    moments, vectors, to_low, to_high = find_moments(got, (first, second, third))
+    moments, vectors, gathered, to_low, to_high = find_moments(got, (first, second, third))
     low, high = swap(to_low, to_high, GX, along_even)
     first_lanes, second_lanes, mask_lanes = gather_early(
         first, second, mask, (early_low, early_high, early_below, early_above)
@@ -670,7 +682,7 @@
         *across_late(moments, vectors, low, high, early_low, early_high), "gy", across_even
     )
     basis, message = krylov(
-        moments, vectors, (low, high, below, above), first_lanes, second_lanes, mask_lanes,
+        moments, vectors, gathered, (low, high, below, above), first_lanes, second_lanes, mask_lanes,
         voxel_feats, voxel_reg, devices,
     )
     shared = lax.all_to_all(message, GX_GY, split_axis=0, concat_axis=0, tiled=True)

time: 86.8 us -> 86.4 us (level)
  no operation moved by 1% of the time
where the time goes in v9:
time: 86.4 us; the launch traced here: 86 us
  waiting for transfers between devices  25.5 us (30%)
  starting transfers between devices  20.5 us (24%)
  blocking collectives  19.4 us (22%)
  Pallas kernels  17.8 us (21%)
  local copies, waits for them, and re-layouts  1.72 us (2%)
  between operations  0.91 us (1%)
    all_to_all x1, waiting for transfers between devices, shards(): lax.all_to_all(sending, GX_GY, split_axis=0, concat_axis=0, tiled=True)  21.6 us
    all_to_all x1, blocking collectives, shards(): lax.all_to_all(message, GX_GY, split_axis=0, concat_axis=0, tiled=True)  19.4 us
    all_to_all x1, starting transfers between devices, shards(): lax.all_to_all(sending, GX_GY, split_axis=0, concat_axis=0, tiled=True)  11.5 us
    ppermute x4, starting transfers between devices, swap(): second = lax.ppermute(jnp.where(even, to_low, to_high), axis, pairs(1))  6.16 us
    pallas_call x1, Pallas kernels, prepare(): pl.pallas_call(prepare_kernel, out_shape=(record, record, record), compil...  4.92 us
    pallas_call x1, Pallas kernels, find_moments(): pl.pallas_call(moments_kernel, out_shape=(jax.ShapeDtypeStruct((bricks, 8...  4.06 us
    pallas_call x1, Pallas kernels, pack(): pl.pallas_call(pack_kernel, in_specs=[pl.BlockSpec(memory_space=pl.ANY),...  3.23 us
    ppermute x4, waiting for transfers between devices, swap(): second = lax.ppermute(jnp.where(even, to_low, to_high), axis, pairs(1))  3.16 us
  transfers between devices with their start and end apart: 9, of which 3 were waited for; matrix products, arithmetic and copies ran while one was open for 0% of the time, Pallas kernels for 12%

profile of v9, /device:TPU:1, one launch (start us, length us, event | category | flops | bytes accessed | tf_op | source)
XLA Modules:
  0.0 86.0 jit_solution(10014602824097835978)
XLA Ops:
  0.6 3.2 %pack.1 = bf16[128,66,128]{2,1,0:T(8,128)(2,1)} custom-call(s32[8,4096]{1,0:T(8,128)} %bitcast.17, bf16[32,32768]{1,0:T(8,128)(2,1)} %feats_ref.3, bf16[256,128]{1,0:T(8,128)(2,1)} %bitcast.18), custom_call_target="tpu_custom_call" | custom-call | tf_op jit(solution)/shard_map/pack/pallas_call | solution.py:194
  3.9 0.0 copy-start.3
  3.9 0.0 copy-start.2
  3.9 11.5 %all-to-all-start = ((bf16[128,66,128]{2,1,0:T(8,128)(2,1)}), bf16[128,66,128]{2,1,0:T(8,128)(2,1)S(1)}, u32[]{:S(2)}, u32[]{:S(2)}) async-start(bf16[128,66,128]{2,1,0:T(8,128)(2,1)} %pack.1), calls=%async_computation | async-start | bytes 4718592 | tf_op jit(solution)/shard_map/all_to_all | solution.py:664
  15.4 0.0 copy-done.3
  15.5 0.1 copy.11
  15.6 0.0 copy-done.2
  15.6 0.0 copy-start
  15.6 1.6 %copy-done = f32[32,32,512]{2,1,0:T(8,128)S(1)} copy-done((f32[32,32,512]{2,1,0:T(8,128)S(1)}, f32[32,32,512]{2,1,0:T(8,128)}, u32[]{:S(2)}) %copy-start) | copy-done | bytes 2097176
  17.1 4.9 %prepare.1 = (f32[32,8,128]{2,1,0:T(8,128)S(1)}, f32[32,8,128]{2,1,0:T(8,128)S(1)}, f32[32,8,128]{2,1,0:T(8,128)S(1)}) custom-call(f32[32,32,512]{2,1,0:T(8,128)S(1)} %copy-done, f32[32,512]{1,0:T(8,128)S(1)} %copy-done.2), custom_call_target="tpu_custom_call" | custom-call | flops 600000000 | bytes 5000000 | tf_op jit(solution)/shard_map/prepare/pallas_call | solution.py:264
  22.1 1.1 %collective-permute-start.3 = (f32[104,128]{1,0:T(8,128)S(1)}, f32[104,128]{1,0:T(8,128)S(1)}, u32[]{:S(2)}, u32[]{:S(2)}) collective-permute-start(f32[104,128]{1,0:T(8,128)S(1)} %get-tuple-element.50), channel_id=1, source_target_pairs={{0,4},{4,0},{8,12},{12,8},{16,20},{20,16},{24,28},{28,24},{32,36},... | collective-permute-start | bytes 159752 | tf_op jit(solution)/shard_map/ppermute | solution.py:369
  23.3 2.7 %collective-permute-start.2 = (f32[104,128]{1,0:T(8,128)S(1)}, f32[104,128]{1,0:T(8,128)S(1)}, u32[]{:S(2)}, u32[]{:S(2)}) collective-permute-start(f32[104,128]{1,0:T(8,128)S(1)} %get-tuple-element.51), channel_id=1, source_target_pairs={{4,8},{8,4},{12,16},{16,12},{20,24},{24,20},{28,32},{32,28},{36,40... | collective-permute-start | bytes 159752 | tf_op jit(solution)/shard_map/ppermute | solution.py:368
  26.1 1.3 %collective-permute-start.7 = (f32[208,128]{1,0:T(8,128)S(1)}, f32[208,128]{1,0:T(8,128)S(1)}, u32[]{:S(2)}, u32[]{:S(2)}) collective-permute-start(f32[208,128]{1,0:T(8,128)S(1)} %get-tuple-element.38), channel_id=1, source_target_pairs={{0,1},{1,0},{2,3},{3,2},{4,5},{5,4},{6,7},{7,6},{8,9},{9,8},{10,11... | collective-permute-start | bytes 319496 | tf_op jit(solution)/shard_map/ppermute | solution.py:369
  27.4 0.7 collective-permute-start.6
  28.0 21.6 %all-to-all-done.got_ref = bf16[128,66,128]{2,1,0:T(8,128)(2,1)S(1)} async-done(((bf16[128,66,128]{2,1,0:T(8,128)(2,1)}), bf16[128,66,128]{2,1,0:T(8,128)(2,1)S(1)}, u32[]{:S(2)}, u32[]{:S(2)}) %all-to-all-start) | async-done | bytes 2162720 | tf_op jit(solution)/shard_map/all_to_all | solution.py:664
  49.7 0.0 copy-start.1
  49.7 4.1 %moments.1 = (f32[32,8,128]{2,1,0:T(8,128)S(1)}, f32[32,128]{1,0:T(8,128)S(1)}, f32[32,128]{1,0:T(8,128)S(1)}, f32[48,128]{1,0:T(8,128)S(1)}, f32[48,128]{1,0:T(8,128)S(1)}) custom-call(bf16[128,66,128]{2,1,0:T(8,128)(2,1)S(1)} %all-to-all-done.got_ref, f32[32,8,128]{2,1,0:T(8,128)S(1)} %get-tuple-element.19.first_ref, ...), custom_call_target="tpu_custom_call" | custom-call | flops 1000000000 | bytes 12000000 | tf_op jit(solution)/shard_map/moments/pallas_call | solution.py:444
  53.8 0.1 collective-permute-start.1
  53.9 0.0 collective-permute-done.3
  53.9 2.1 %collective-permute-start = (f32[48,128]{1,0:T(8,128)S(1)}, f32[48,128]{1,0:T(8,128)S(1)}, u32[]{:S(2)}, u32[]{:S(2)}) collective-permute-start(f32[48,128]{1,0:T(8,128)S(1)} %get-tuple-element.55), channel_id=1, source_target_pairs={{4,8},{8,4},{12,16},{16,12},{20,24},{24,20},{28,32},{32,28},{36,40... | collective-permute-start | bytes 73736 | tf_op jit(solution)/shard_map/ppermute | solution.py:368
  56.0 0.0 collective-permute-done.2
  56.0 0.0 collective-permute-done.1
  56.0 3.2 %collective-permute-done = f32[48,128]{1,0:T(8,128)S(1)} collective-permute-done((f32[48,128]{1,0:T(8,128)S(1)}, f32[48,128]{1,0:T(8,128)S(1)}, u32[]{:S(2)}, u32[]{:S(2)}) %collective-permute-start) | collective-permute-done | bytes 24608 | tf_op jit(solution)/shard_map/ppermute | solution.py:368
  59.2 0.4 collective-permute-start.5
  59.6 0.7 collective-permute-start.4
  60.3 0.0 collective-permute-done.7
  60.3 0.0 collective-permute-done.6
  60.3 1.3 %gather_early.1 = (f32[1024,256]{1,0:T(8,128)S(1)}, f32[1024,256]{1,0:T(8,128)S(1)}, f32[8,256]{1,0:T(8,128)S(1)}) custom-call(f32[32,8,128]{2,1,0:T(8,128)S(1)} %get-tuple-element.19.first_ref, f32[32,8,128]{2,1,0:T(8,128)S(1)} %get-tuple-element.20.second_ref, f32[32,128]{1,0:T(8,128)S(1)} %pad.4.mask_ref, ...), custom_call_target="tpu_custom_call" | custom-call | flops 2000000 | bytes 3000000 | tf_op jit(solution)/shard_map/gather_early/pallas_call | solution.py:300
  61.7 0.7 collective-permute-done.5
  62.4 0.0 collective-permute-done.4
  62.4 0.0 copy-done.1
  62.4 3.1 %krylov.1 = (f32[4,32,512]{2,1,0:T(8,128)S(1)}, f32[128,128]{1,0:T(8,128)S(1)}) custom-call(f32[32,8,128]{2,1,0:T(8,128)S(1)} %get-tuple-element.22.moments_ref, f32[32,128]{1,0:T(8,128)S(1)} %get-tuple-element.23.vectors_ref, f32[32,128]{1,0:T(8,128)S(1)} %get-tuple-element.24.gathered_ref, f32[48,128]{1,0:T(8,128)S(1)} %get-tuple-element.53.low.low_ref, ...), custom_call_target="tpu_custom_call" | custom-call | tf_op jit(solution)/shard_map/krylov/pallas_call | solution.py:564
  65.5 19.4 %all_to_all.16 = f32[128,1,128]{2,1,0:T(1,128)S(1)} all-to-all(f32[128,1,128]{2,1,0:T(1,128)S(1)} %bitcast.16), channel_id=1, replica_groups=mesh['gx_0'=4,'gx_1'=4,'gx_2'=2,'gy'=4] {'gx_0','gx_1','gx_2','gy'}, dimensions={0} | all-to-all | bytes 131072 | tf_op jit(solution)/shard_map/all_to_all | solution.py:688
  84.9 1.1 %finish.1 = (f32[32,512]{1,0:T(8,128)}, f32[32,512]{1,0:T(8,128)}) custom-call(f32[128,128]{1,0:T(8,128)S(1)} %bitcast.15, f32[4,32,512]{2,1,0:T(8,128)S(1)} %get-tuple-element.35.basis_ref), custom_call_target="tpu_custom_call" | custom-call | tf_op jit(solution)/shard_map/finish/pallas_call | solution.py:650
  (17 shorter events, 0.2 us)
Async XLA Ops:
  3.9 11.5 %copy-start.3 = (s32[32,4]{0,1:T(4,128)S(1)}, s32[32,4]{0,1:T(4,128)}, u32[]{:S(2)}) copy-start(s32[32,4]{0,1:T(4,128)} %param.9) | copy-start | bytes 1540
  3.9 11.7 %copy-start.2 = (f32[32,512]{1,0:T(8,128)S(1)}, f32[32,512]{1,0:T(8,128)}, u32[]{:S(2)}) copy-start(f32[32,512]{1,0:T(8,128)} %reg_ref.3) | copy-start | bytes 196612
  3.9 45.8 %all-to-all-start = ((bf16[128,66,128]{2,1,0:T(8,128)(2,1)}), bf16[128,66,128]{2,1,0:T(8,128)(2,1)S(1)}, u32[]{:S(2)}, u32[]{:S(2)}) async-start(bf16[128,66,128]{2,1,0:T(8,128)(2,1)} %pack.1), calls=%async_computation | async-start | bytes 4718592 | tf_op jit(solution)/shard_map/all_to_all | solution.py:664
  15.6 1.6 %copy-start = (f32[32,32,512]{2,1,0:T(8,128)S(1)}, f32[32,32,512]{2,1,0:T(8,128)}, u32[]{:S(2)}) copy-start(f32[32,32,512]{2,1,0:T(8,128)} %feats_ref.5) | copy-start | bytes 6291460
  22.1 31.7 %collective-permute-start.3 = (f32[104,128]{1,0:T(8,128)S(1)}, f32[104,128]{1,0:T(8,128)S(1)}, u32[]{:S(2)}, u32[]{:S(2)}) collective-permute-start(f32[104,128]{1,0:T(8,128)S(1)} %get-tuple-element.50), channel_id=1, source_target_pairs={{0,4},{4,0},{8,12},{12,8},{16,20},{20,16},{24,28},{28,24},{32,36},... | collective-permute-start | bytes 159752 | tf_op jit(solution)/shard_map/ppermute | solution.py:369
  23.3 32.7 %collective-permute-start.2 = (f32[104,128]{1,0:T(8,128)S(1)}, f32[104,128]{1,0:T(8,128)S(1)}, u32[]{:S(2)}, u32[]{:S(2)}) collective-permute-start(f32[104,128]{1,0:T(8,128)S(1)} %get-tuple-element.51), channel_id=1, source_target_pairs={{4,8},{8,4},{12,16},{16,12},{20,24},{24,20},{28,32},{32,28},{36,40... | collective-permute-start | bytes 159752 | tf_op jit(solution)/shard_map/ppermute | solution.py:368
  26.1 34.2 %collective-permute-start.7 = (f32[208,128]{1,0:T(8,128)S(1)}, f32[208,128]{1,0:T(8,128)S(1)}, u32[]{:S(2)}, u32[]{:S(2)}) collective-permute-start(f32[208,128]{1,0:T(8,128)S(1)} %get-tuple-element.38), channel_id=1, source_target_pairs={{0,1},{1,0},{2,3},{3,2},{4,5},{5,4},{6,7},{7,6},{8,9},{9,8},{10,11... | collective-permute-start | bytes 319496 | tf_op jit(solution)/shard_map/ppermute | solution.py:369
  27.4 32.9 %collective-permute-start.6 = (f32[208,128]{1,0:T(8,128)S(1)}, f32[208,128]{1,0:T(8,128)S(1)}, u32[]{:S(2)}, u32[]{:S(2)}) collective-permute-start(f32[208,128]{1,0:T(8,128)S(1)} %get-tuple-element.39), channel_id=1, source_target_pairs={{1,2},{2,1},{5,6},{6,5},{9,10},{10,9},{13,14},{14,13},{17,18},{18,... | collective-permute-start | bytes 319496 | tf_op jit(solution)/shard_map/ppermute | solution.py:368
  49.7 12.7 %copy-start.1 = (f32[32,32,512]{2,1,0:T(8,128)S(1)}, f32[32,32,512]{2,1,0:T(8,128)}, u32[]{:S(2)}) copy-start(f32[32,32,512]{2,1,0:T(8,128)} %feats_ref.5) | copy-start | bytes 6291460
  53.8 2.3 %collective-permute-start.1 = (f32[48,128]{1,0:T(8,128)S(1)}, f32[48,128]{1,0:T(8,128)S(1)}, u32[]{:S(2)}, u32[]{:S(2)}) collective-permute-start(f32[48,128]{1,0:T(8,128)S(1)} %get-tuple-element.54), channel_id=1, source_target_pairs={{0,4},{4,0},{8,12},{12,8},{16,20},{20,16},{24,28},{28,24},{32,36},... | collective-permute-start | bytes 73736 | tf_op jit(solution)/shard_map/ppermute | solution.py:369
  53.9 5.3 %collective-permute-start = (f32[48,128]{1,0:T(8,128)S(1)}, f32[48,128]{1,0:T(8,128)S(1)}, u32[]{:S(2)}, u32[]{:S(2)}) collective-permute-start(f32[48,128]{1,0:T(8,128)S(1)} %get-tuple-element.55), channel_id=1, source_target_pairs={{4,8},{8,4},{12,16},{16,12},{20,24},{24,20},{28,32},{32,28},{36,40... | collective-permute-start | bytes 73736 | tf_op jit(solution)/shard_map/ppermute | solution.py:368
  59.2 3.2 %collective-permute-start.5 = (f32[120,128]{1,0:T(8,128)S(1)}, f32[120,128]{1,0:T(8,128)S(1)}, u32[]{:S(2)}, u32[]{:S(2)}) collective-permute-start(f32[120,128]{1,0:T(8,128)S(1)} %get-tuple-element.46), channel_id=1, source_target_pairs={{0,1},{1,0},{2,3},{3,2},{4,5},{5,4},{6,7},{7,6},{8,9},{9,8},{10,11... | collective-permute-start | bytes 184328 | tf_op jit(solution)/shard_map/ppermute | solution.py:369
  59.6 2.8 %collective-permute-start.4 = (f32[120,128]{1,0:T(8,128)S(1)}, f32[120,128]{1,0:T(8,128)S(1)}, u32[]{:S(2)}, u32[]{:S(2)}) collective-permute-start(f32[120,128]{1,0:T(8,128)S(1)} %get-tuple-element.47), channel_id=1, source_target_pairs={{1,2},{2,1},{5,6},{6,5},{9,10},{10,9},{13,14},{14,13},{17,18},{18,... | collective-permute-start | bytes 184328 | tf_op jit(solution)/shard_map/ppermute | solution.py:368

commit v10 on v9

--- a/solution.py
+++ b/solution.py
@@ -365,9 +365,10 @@
     def pairs(start):
         return [pair for a in range(start, count - 1, 2) for pair in ((a, a + 1), (a + 1, a))]
 
-    second = lax.ppermute(jnp.where(even, to_low, to_high), axis, pairs(1))
-    first = lax.ppermute(jnp.where(even, to_high, to_low), axis, pairs(0))
-    return jnp.where(even, second, first), jnp.where(even, first, second)
+    odd = jnp.logical_not(even)
+    second = lax.ppermute(jnp.where(odd, to_high, to_low), axis, pairs(1))
+    first = lax.ppermute(jnp.where(odd, to_low, to_high), axis, pairs(0))
+    return jnp.where(odd, first, second), jnp.where(odd, second, first)
 
 
 def moments_kernel(

time: 86.4 us -> 85.4 us (0.988)
  starting transfers between devices: 20.5 us -> 24.1 us
  waiting for transfers between devices: 25.5 us -> 22.4 us
  blocking collectives: 19.4 us -> 17.9 us
    ppermute x8, starting transfers between devices: 9.04 us -> 12.6 us  [the longest x4 7.11 us: swap(): second = lax.ppermute(jnp.where(odd, to_high, to_low), axis, pairs(1))]
    all_to_all x1, waiting for transfers between devices: 21.6 us -> 19.3 us  [shards(): lax.all_to_all(sending, GX_GY, split_axis=0, concat_axis=0, tiled=True)]
    all_to_all x1, blocking collectives: 19.4 us -> 17.9 us  [shards(): lax.all_to_all(message, GX_GY, split_axis=0, concat_axis=0, tiled=True)]
where the time goes in v10:
time: 85.4 us; the launch traced here: 85.1 us
  starting transfers between devices  24.1 us (28%)
  waiting for transfers between devices  22.4 us (26%)
  blocking collectives  17.9 us (21%)
  Pallas kernels  17.8 us (21%)
  local copies, waits for them, and re-layouts  1.72 us (2%)
  between operations  0.91 us (1%)
    all_to_all x1, waiting for transfers between devices, shards(): lax.all_to_all(sending, GX_GY, split_axis=0, concat_axis=0, tiled=True)  19.3 us
    all_to_all x1, blocking collectives, shards(): lax.all_to_all(message, GX_GY, split_axis=0, concat_axis=0, tiled=True)  17.9 us
    all_to_all x1, starting transfers between devices, shards(): lax.all_to_all(sending, GX_GY, split_axis=0, concat_axis=0, tiled=True)  11.5 us
    ppermute x4, starting transfers between devices, swap(): second = lax.ppermute(jnp.where(odd, to_high, to_low), axis, pairs(1))  7.11 us
    ppermute x4, starting transfers between devices, swap(): first = lax.ppermute(jnp.where(odd, to_low, to_high), axis, pairs(0))  5.53 us
    pallas_call x1, Pallas kernels, prepare(): pl.pallas_call(prepare_kernel, out_shape=(record, record, record), compil...  4.92 us
    pallas_call x1, Pallas kernels, find_moments(): pl.pallas_call(moments_kernel, out_shape=(jax.ShapeDtypeStruct((bricks, 8...  4.06 us
    pallas_call x1, Pallas kernels, pack(): pl.pallas_call(pack_kernel, in_specs=[pl.BlockSpec(memory_space=pl.ANY),...  3.23 us
  transfers between devices with their start and end apart: 9, of which 3 were waited for; matrix products, arithmetic and copies ran while one was open for 0% of the time, Pallas kernels for 12%

profile of v10, /device:TPU:1, one launch (start us, length us, event | category | flops | bytes accessed | tf_op | source)
XLA Modules:
  0.0 85.1 jit_solution(18214223620713196231)
XLA Ops:
  0.6 3.2 %pack.1 = bf16[128,66,128]{2,1,0:T(8,128)(2,1)} custom-call(s32[8,4096]{1,0:T(8,128)} %bitcast.17, bf16[32,32768]{1,0:T(8,128)(2,1)} %feats_ref.3, bf16[256,128]{1,0:T(8,128)(2,1)} %bitcast.18), custom_call_target="tpu_custom_call" | custom-call | tf_op jit(solution)/shard_map/pack/pallas_call | solution.py:194
  3.9 0.0 copy-start.3
  3.9 0.0 copy-start.2
  3.9 11.5 %all-to-all-start = ((bf16[128,66,128]{2,1,0:T(8,128)(2,1)}), bf16[128,66,128]{2,1,0:T(8,128)(2,1)S(1)}, u32[]{:S(2)}, u32[]{:S(2)}) async-start(bf16[128,66,128]{2,1,0:T(8,128)(2,1)} %pack.1), calls=%async_computation | async-start | bytes 4718592 | tf_op jit(solution)/shard_map/all_to_all | solution.py:665
  15.4 0.0 copy-done.3
  15.5 0.1 copy.11
  15.6 0.0 copy-done.2
  15.6 0.0 copy-start
  15.6 1.6 %copy-done = f32[32,32,512]{2,1,0:T(8,128)S(1)} copy-done((f32[32,32,512]{2,1,0:T(8,128)S(1)}, f32[32,32,512]{2,1,0:T(8,128)}, u32[]{:S(2)}) %copy-start) | copy-done | bytes 2097176
  17.1 4.9 %prepare.1 = (f32[32,8,128]{2,1,0:T(8,128)S(1)}, f32[32,8,128]{2,1,0:T(8,128)S(1)}, f32[32,8,128]{2,1,0:T(8,128)S(1)}) custom-call(f32[32,32,512]{2,1,0:T(8,128)S(1)} %copy-done, f32[32,512]{1,0:T(8,128)S(1)} %copy-done.2), custom_call_target="tpu_custom_call" | custom-call | flops 600000000 | bytes 5000000 | tf_op jit(solution)/shard_map/prepare/pallas_call | solution.py:264
  22.1 3.7 %collective-permute-start.3 = (f32[104,128]{1,0:T(8,128)S(1)}, f32[104,128]{1,0:T(8,128)S(1)}, u32[]{:S(2)}, u32[]{:S(2)}) collective-permute-start(f32[104,128]{1,0:T(8,128)S(1)} %get-tuple-element.50), channel_id=1, source_target_pairs={{4,8},{8,4},{12,16},{16,12},{20,24},{24,20},{28,32},{32,28},{36,40... | collective-permute-start | bytes 159752 | tf_op jit(solution)/shard_map/ppermute | solution.py:369
  25.8 0.1 collective-permute-start.2
  26.0 0.7 collective-permute-start.7
  26.7 3.7 %collective-permute-start.6 = (f32[208,128]{1,0:T(8,128)S(1)}, f32[208,128]{1,0:T(8,128)S(1)}, u32[]{:S(2)}, u32[]{:S(2)}) collective-permute-start(f32[208,128]{1,0:T(8,128)S(1)} %get-tuple-element.39), channel_id=1, source_target_pairs={{0,1},{1,0},{2,3},{3,2},{4,5},{5,4},{6,7},{7,6},{8,9},{9,8},{10,11... | collective-permute-start | bytes 319496 | tf_op jit(solution)/shard_map/ppermute | solution.py:370
  30.4 19.3 %all-to-all-done.got_ref = bf16[128,66,128]{2,1,0:T(8,128)(2,1)S(1)} async-done(((bf16[128,66,128]{2,1,0:T(8,128)(2,1)}), bf16[128,66,128]{2,1,0:T(8,128)(2,1)S(1)}, u32[]{:S(2)}, u32[]{:S(2)}) %all-to-all-start) | async-done | bytes 2162720 | tf_op jit(solution)/shard_map/all_to_all | solution.py:665
  49.7 0.0 copy-start.1
  49.7 4.1 %moments.1 = (f32[32,8,128]{2,1,0:T(8,128)S(1)}, f32[32,128]{1,0:T(8,128)S(1)}, f32[32,128]{1,0:T(8,128)S(1)}, f32[48,128]{1,0:T(8,128)S(1)}, f32[48,128]{1,0:T(8,128)S(1)}) custom-call(bf16[128,66,128]{2,1,0:T(8,128)(2,1)S(1)} %all-to-all-done.got_ref, f32[32,8,128]{2,1,0:T(8,128)S(1)} %get-tuple-element.19.first_ref, ...), custom_call_target="tpu_custom_call" | custom-call | flops 1000000000 | bytes 12000000 | tf_op jit(solution)/shard_map/moments/pallas_call | solution.py:445
  53.8 2.1 %collective-permute-start.1 = (f32[48,128]{1,0:T(8,128)S(1)}, f32[48,128]{1,0:T(8,128)S(1)}, u32[]{:S(2)}, u32[]{:S(2)}) collective-permute-start(f32[48,128]{1,0:T(8,128)S(1)} %get-tuple-element.54), channel_id=1, source_target_pairs={{4,8},{8,4},{12,16},{16,12},{20,24},{24,20},{28,32},{32,28},{36,40... | collective-permute-start | bytes 73736 | tf_op jit(solution)/shard_map/ppermute | solution.py:369
  55.9 0.0 collective-permute-done.3
  55.9 0.1 collective-permute-start
  56.0 0.0 collective-permute-done.2
  56.0 2.9 %collective-permute-done.1 = f32[48,128]{1,0:T(8,128)S(1)} collective-permute-done((f32[48,128]{1,0:T(8,128)S(1)}, f32[48,128]{1,0:T(8,128)S(1)}, u32[]{:S(2)}, u32[]{:S(2)}) %collective-permute-start.1) | collective-permute-done | bytes 24608 | tf_op jit(solution)/shard_map/ppermute | solution.py:369
  58.9 0.0 collective-permute-done
  59.0 0.7 collective-permute-start.5
  59.6 1.6 %collective-permute-start.4 = (f32[120,128]{1,0:T(8,128)S(1)}, f32[120,128]{1,0:T(8,128)S(1)}, u32[]{:S(2)}, u32[]{:S(2)}) collective-permute-start(f32[120,128]{1,0:T(8,128)S(1)} %get-tuple-element.47), channel_id=1, source_target_pairs={{0,1},{1,0},{2,3},{3,2},{4,5},{5,4},{6,7},{7,6},{8,9},{9,8},{10,11... | collective-permute-start | bytes 184328 | tf_op jit(solution)/shard_map/ppermute | solution.py:370
  61.3 0.0 collective-permute-done.7
  61.3 0.0 collective-permute-done.6
  61.3 1.3 %gather_early.1 = (f32[1024,256]{1,0:T(8,128)S(1)}, f32[1024,256]{1,0:T(8,128)S(1)}, f32[8,256]{1,0:T(8,128)S(1)}) custom-call(f32[32,8,128]{2,1,0:T(8,128)S(1)} %get-tuple-element.19.first_ref, f32[32,8,128]{2,1,0:T(8,128)S(1)} %get-tuple-element.20.second_ref, f32[32,128]{1,0:T(8,128)S(1)} %pad.4.mask_ref, ...), custom_call_target="tpu_custom_call" | custom-call | flops 2000000 | bytes 3000000 | tf_op jit(solution)/shard_map/gather_early/pallas_call | solution.py:300
  62.6 0.0 collective-permute-done.5
  62.7 0.2 collective-permute-done.4
  62.9 0.0 copy-done.1
  62.9 3.1 %krylov.1 = (f32[4,32,512]{2,1,0:T(8,128)S(1)}, f32[128,128]{1,0:T(8,128)S(1)}) custom-call(f32[32,8,128]{2,1,0:T(8,128)S(1)} %get-tuple-element.22.moments_ref, f32[32,128]{1,0:T(8,128)S(1)} %get-tuple-element.23.vectors_ref, f32[32,128]{1,0:T(8,128)S(1)} %get-tuple-element.24.gathered_ref, f32[48,128]{1,0:T(8,128)S(1)} %get-tuple-element.53.low.low_ref, ...), custom_call_target="tpu_custom_call" | custom-call | tf_op jit(solution)/shard_map/krylov/pallas_call | solution.py:565
  66.0 17.9 %all_to_all.16 = f32[128,1,128]{2,1,0:T(1,128)S(1)} all-to-all(f32[128,1,128]{2,1,0:T(1,128)S(1)} %bitcast.16), channel_id=1, replica_groups=mesh['gx_0'=4,'gx_1'=4,'gx_2'=2,'gy'=4] {'gx_0','gx_1','gx_2','gy'}, dimensions={0} | all-to-all | bytes 131072 | tf_op jit(solution)/shard_map/all_to_all | solution.py:689
  84.0 1.1 %finish.1 = (f32[32,512]{1,0:T(8,128)}, f32[32,512]{1,0:T(8,128)}) custom-call(f32[128,128]{1,0:T(8,128)S(1)} %bitcast.15, f32[4,32,512]{2,1,0:T(8,128)S(1)} %get-tuple-element.35.basis_ref), custom_call_target="tpu_custom_call" | custom-call | tf_op jit(solution)/shard_map/finish/pallas_call | solution.py:651
  (17 shorter events, 0.2 us)
Async XLA Ops:
  3.9 11.5 %copy-start.3 = (s32[32,4]{0,1:T(4,128)S(1)}, s32[32,4]{0,1:T(4,128)}, u32[]{:S(2)}) copy-start(s32[32,4]{0,1:T(4,128)} %param.9) | copy-start | bytes 1540
  3.9 11.7 %copy-start.2 = (f32[32,512]{1,0:T(8,128)S(1)}, f32[32,512]{1,0:T(8,128)}, u32[]{:S(2)}) copy-start(f32[32,512]{1,0:T(8,128)} %reg_ref.3) | copy-start | bytes 196612
  3.9 45.8 %all-to-all-start = ((bf16[128,66,128]{2,1,0:T(8,128)(2,1)}), bf16[128,66,128]{2,1,0:T(8,128)(2,1)S(1)}, u32[]{:S(2)}, u32[]{:S(2)}) async-start(bf16[128,66,128]{2,1,0:T(8,128)(2,1)} %pack.1), calls=%async_computation | async-start | bytes 4718592 | tf_op jit(solution)/shard_map/all_to_all | solution.py:665
  15.6 1.6 %copy-start = (f32[32,32,512]{2,1,0:T(8,128)S(1)}, f32[32,32,512]{2,1,0:T(8,128)}, u32[]{:S(2)}) copy-start(f32[32,32,512]{2,1,0:T(8,128)} %feats_ref.5) | copy-start | bytes 6291460
  22.1 33.7 %collective-permute-start.3 = (f32[104,128]{1,0:T(8,128)S(1)}, f32[104,128]{1,0:T(8,128)S(1)}, u32[]{:S(2)}, u32[]{:S(2)}) collective-permute-start(f32[104,128]{1,0:T(8,128)S(1)} %get-tuple-element.50), channel_id=1, source_target_pairs={{4,8},{8,4},{12,16},{16,12},{20,24},{24,20},{28,32},{32,28},{36,40... | collective-permute-start | bytes 159752 | tf_op jit(solution)/shard_map/ppermute | solution.py:369
  25.8 30.2 %collective-permute-start.2 = (f32[104,128]{1,0:T(8,128)S(1)}, f32[104,128]{1,0:T(8,128)S(1)}, u32[]{:S(2)}, u32[]{:S(2)}) collective-permute-start(f32[104,128]{1,0:T(8,128)S(1)} %get-tuple-element.51), channel_id=1, source_target_pairs={{0,4},{4,0},{8,12},{12,8},{16,20},{20,16},{24,28},{28,24},{32,36},... | collective-permute-start | bytes 159752 | tf_op jit(solution)/shard_map/ppermute | solution.py:370
  26.0 35.3 %collective-permute-start.7 = (f32[208,128]{1,0:T(8,128)S(1)}, f32[208,128]{1,0:T(8,128)S(1)}, u32[]{:S(2)}, u32[]{:S(2)}) collective-permute-start(f32[208,128]{1,0:T(8,128)S(1)} %get-tuple-element.38), channel_id=1, source_target_pairs={{1,2},{2,1},{5,6},{6,5},{9,10},{10,9},{13,14},{14,13},{17,18},{18,... | collective-permute-start | bytes 319496 | tf_op jit(solution)/shard_map/ppermute | solution.py:369
  26.7 34.6 %collective-permute-start.6 = (f32[208,128]{1,0:T(8,128)S(1)}, f32[208,128]{1,0:T(8,128)S(1)}, u32[]{:S(2)}, u32[]{:S(2)}) collective-permute-start(f32[208,128]{1,0:T(8,128)S(1)} %get-tuple-element.39), channel_id=1, source_target_pairs={{0,1},{1,0},{2,3},{3,2},{4,5},{5,4},{6,7},{7,6},{8,9},{9,8},{10,11... | collective-permute-start | bytes 319496 | tf_op jit(solution)/shard_map/ppermute | solution.py:370
  49.7 13.2 %copy-start.1 = (f32[32,32,512]{2,1,0:T(8,128)S(1)}, f32[32,32,512]{2,1,0:T(8,128)}, u32[]{:S(2)}) copy-start(f32[32,32,512]{2,1,0:T(8,128)} %feats_ref.5) | copy-start | bytes 6291460
  53.8 5.1 %collective-permute-start.1 = (f32[48,128]{1,0:T(8,128)S(1)}, f32[48,128]{1,0:T(8,128)S(1)}, u32[]{:S(2)}, u32[]{:S(2)}) collective-permute-start(f32[48,128]{1,0:T(8,128)S(1)} %get-tuple-element.54), channel_id=1, source_target_pairs={{4,8},{8,4},{12,16},{16,12},{20,24},{24,20},{28,32},{32,28},{36,40... | collective-permute-start | bytes 73736 | tf_op jit(solution)/shard_map/ppermute | solution.py:369
  55.9 3.0 %collective-permute-start = (f32[48,128]{1,0:T(8,128)S(1)}, f32[48,128]{1,0:T(8,128)S(1)}, u32[]{:S(2)}, u32[]{:S(2)}) collective-permute-start(f32[48,128]{1,0:T(8,128)S(1)} %get-tuple-element.55), channel_id=1, source_target_pairs={{0,4},{4,0},{8,12},{12,8},{16,20},{20,16},{24,28},{28,24},{32,36},... | collective-permute-start | bytes 73736 | tf_op jit(solution)/shard_map/ppermute | solution.py:370
  59.0 3.7 %collective-permute-start.5 = (f32[120,128]{1,0:T(8,128)S(1)}, f32[120,128]{1,0:T(8,128)S(1)}, u32[]{:S(2)}, u32[]{:S(2)}) collective-permute-start(f32[120,128]{1,0:T(8,128)S(1)} %get-tuple-element.46), channel_id=1, source_target_pairs={{1,2},{2,1},{5,6},{6,5},{9,10},{10,9},{13,14},{14,13},{17,18},{18,... | collective-permute-start | bytes 184328 | tf_op jit(solution)/shard_map/ppermute | solution.py:369
  59.6 3.3 %collective-permute-start.4 = (f32[120,128]{1,0:T(8,128)S(1)}, f32[120,128]{1,0:T(8,128)S(1)}, u32[]{:S(2)}, u32[]{:S(2)}) collective-permute-start(f32[120,128]{1,0:T(8,128)S(1)} %get-tuple-element.47), channel_id=1, source_target_pairs={{0,1},{1,0},{2,3},{3,2},{4,5},{5,4},{6,7},{7,6},{8,9},{9,8},{10,11... | collective-permute-start | bytes 184328 | tf_op jit(solution)/shard_map/ppermute | solution.py:370

commit v11 on v10

--- a/solution.py
+++ b/solution.py
@@ -271,11 +271,19 @@
 
 
 def gather_early_kernel(
-    first_ref, second_ref, mask_ref, low_ref, high_ref, below_ref, above_ref,
-    first_lanes, second_lanes, mask_lanes, first_store, second_store, mask_store,
+    first_ref, second_ref, mask_ref, low_ref, high_ref, below_ref, above_ref, moments_ref, late_low, late_high,
+    gathered_ref, feats_ref, first_lanes, second_lanes, mask_lanes, moment_lanes, start_ref,
+    first_store, second_store, mask_store, moment_store,
 ):
-    for store in (first_store, second_store, mask_store):
+    for store in (first_store, second_store, mask_store, moment_store):
         store[...] = jnp.zeros_like(store)
+    for a in range(-1, BX + 1):
+        for e in range(BY):
+            moment_store[lane_of(a, e)] = brick_at(moments_ref, late_low, late_high, 0, LATE[0], a, e)
+    to_lanes(moment_store, moment_lanes)
+    gathered = gathered_ref[...]
+    for b in range(BX * BY):
+        start_ref[b : b + 1, :] = jnp.sum(feats_ref[b] * gathered[:, b : b + 1], axis=0, keepdims=True)
 
     def put(store):
         def write(a, e, value):
@@ -295,20 +303,24 @@
     mask_lanes[...] = mask_store[...].T[:8, :]
 
 
-def gather_early(first, second, mask, edges):
+def gather_early(first, second, mask, edges, moments, late, gathered, voxel_feats):
     lanes = jax.ShapeDtypeStruct((8 * LANES, SPAN), jnp.float32)
+    bricks, _, voxels = voxel_feats.shape
+    store = pltpu.VMEM((SPAN, 8, LANES), jnp.float32)
     return pl.pallas_call(
         gather_early_kernel,
-        out_shape=(lanes, lanes, jax.ShapeDtypeStruct((8, SPAN), jnp.float32)),
-        scratch_shapes=[
-            pltpu.VMEM((SPAN, 8, LANES), jnp.float32),
-            pltpu.VMEM((SPAN, 8, LANES), jnp.float32),
-            pltpu.VMEM((SPAN, LANES), jnp.float32),
-        ],
-        compiler_params=pltpu.CompilerParams(vmem_limit_bytes=10 << 20),
-        cost_estimate=pl.CostEstimate(flops=2_000_000, bytes_accessed=3_000_000, transcendentals=0),
+        out_shape=(
+            lanes,
+            lanes,
+            jax.ShapeDtypeStruct((8, SPAN), jnp.float32),
+            lanes,
+            jax.ShapeDtypeStruct((bricks, voxels), jnp.float32),
+        ),
+        scratch_shapes=[store, store, pltpu.VMEM((SPAN, LANES), jnp.float32), store],
+        compiler_params=pltpu.CompilerParams(vmem_limit_bytes=12 << 20),
+        cost_estimate=pl.CostEstimate(flops=3_000_000, bytes_accessed=5_000_000, transcendentals=0),
         name="gather_early",
-    )(first, second, mask, *edges)
+    )(first, second, mask, *edges, moments, *late, gathered, voxel_feats)
 
 
 def across_early_kernel(first_ref, second_ref, mask_ref, to_low, to_high):
@@ -476,39 +488,43 @@
 
 
 def krylov_kernel(
-    moments_ref, vectors_ref, gathered_ref, low_ref, high_ref, below_ref, above_ref, first_ref, second_ref, mask_ref,
-    feats_ref, reg_ref, basis_ref, message_ref, moment_store, vector_store, moment_lanes,
-    corner_store, corner_masks, corner_lanes,
+    moment_lanes, vectors_ref, start_ref, low_ref, high_ref, below_ref, above_ref, first_ref, second_ref, mask_ref,
+    feats_ref, reg_ref, basis_ref, message_ref, vector_store, corner_store, corner_masks, corner_lanes,
 ):
-    moment_store[...] = jnp.zeros_like(moment_store)
     corner_store[...] = jnp.zeros_like(corner_store)
     corner_masks[...] = jnp.zeros_like(corner_masks)
     vector_store[...] = jnp.zeros_like(vector_store)
 
-    def put_moment(a, e, value):
-        moment_store[lane_of(a, e)] = value
-
     def put_vector(a, e, value):
         vector_store[lane_of(a, e) : lane_of(a, e) + 1, :] = value
 
     edges = (low_ref, high_ref, below_ref, above_ref)
-    place_bricks(put_moment, LATE, 0, moments_ref, *edges)
     place_bricks(put_vector, LATE, 1, vectors_ref, *edges)
     start = message_rows(LATE, across_rows)
     for ref, e in ((below_ref, -1), (above_ref, BY)):
         for k, a in enumerate((-1, BX)):
             place = lane_of(a, e) % LANES
-            corner_store[place] = ref[start + 8 * k : start + 8 * k + 8, :]
+            corner_store[(lane_of(a, e) + 8) % LANES] = ref[start + 8 * k : start + 8 * k + 8, :]
             corner_masks[place : place + 1, :] = ref[start + 16 + k : start + 17 + k, :]
-    to_lanes(moment_store, moment_lanes)
+        for a in range(BX):
+            corner_store[lane_of(a, e) % LANES] = piece(ref, 0, 8, a)
     to_lanes(corner_store, corner_lanes)
     vectors = vector_store[...].T
     lane = lax.broadcasted_iota(jnp.int32, (1, LANES), 1)
     front = (lane == lane_of(-1, -1)) | (lane == lane_of(-1, BY))
     rear = (lane == lane_of(BX, -1) % LANES) | (lane == lane_of(BX, BY) % LANES)
 
+    column = lane % PITCH
+    beside = (column == REACH - 1) | (column == REACH + BY)
+    beside_front = beside & (lane >= lane_of(0, -1))
+    beside_rear = beside & (lane < lane_of(0, -1) - 8)
+
     def both_tiles(x):
         return jnp.concatenate([jnp.where(front, x, 0.0), jnp.where(rear, x, 0.0)], axis=1)
+
+    def beside_times(z):
+        x = times(corner_lanes, jnp.where(beside_front, z[:, :LANES], z[:, LANES:]))
+        return jnp.concatenate([jnp.where(beside_front, x, 0.0), jnp.where(beside_rear, x, 0.0)], axis=1)
 
     masks = mask_ref[...] + both_tiles(corner_masks[...].T[:8, :])
 
@@ -521,16 +537,17 @@
         return times(moment_lanes, z) + coupled(z)
 
     one = vectors[3 * FEAT :] + coupled(vectors[0:FEAT])
-    corners = times(corner_lanes, jnp.where(front, one[:, :LANES], one[:, LANES:]))
-    two = system(times(first_ref, one) + both_tiles(corners) + vectors[FEAT : 2 * FEAT])
+    corners = pltpu.roll(jnp.where(front, one[:, :LANES], one[:, LANES:]), 8, 1)
+    corners = pltpu.roll(times(corner_lanes, corners), LANES - 8, 1)
+    second_z = times(first_ref, one) + both_tiles(corners) + vectors[FEAT : 2 * FEAT]
+    two = system(second_z) + beside_times(second_z)
     three = system(times(first_ref, two) + times(second_ref, one) + vectors[2 * FEAT : 3 * FEAT])
-    gathered = gathered_ref[...]
+    basis_ref[0] = start_ref[...]
     for b in range(BX * BY):
         place = lane_of(b // BY, b % BY)
         feats = feats_ref[b]
-        columns = [gathered[:, b : b + 1]] + [values[:, place : place + 1] for values in (one, two, three)]
-        for step, column in enumerate(columns):
-            basis_ref[step, b : b + 1, :] = jnp.sum(feats * column, axis=0, keepdims=True)
+        for step, values in enumerate((one, two, three)):
+            basis_ref[step + 1, b : b + 1, :] = jnp.sum(feats * values[:, place : place + 1], axis=0, keepdims=True)
     reg = reg_ref[...]
     basis = [basis_ref[0]]
     for step in range(1, 4):
@@ -560,7 +577,7 @@
     message_ref[...] = jnp.broadcast_to(row, message_ref.shape)
 
 
-def krylov(moments, vectors, gathered, edges, first, second, masks, voxel_feats, voxel_reg, devices):
+def krylov(moment_lanes, vectors, start, edges, first, second, masks, voxel_feats, voxel_reg, devices):
     bricks, _, voxels = voxel_feats.shape
     return pl.pallas_call(
         krylov_kernel,
@@ -569,16 +586,14 @@
             jax.ShapeDtypeStruct((devices, LANES), jnp.float32),
         ),
         scratch_shapes=[
-            pltpu.VMEM((SPAN, 8, LANES), jnp.float32),
             pltpu.VMEM((SPAN, LANES), jnp.float32),
-            pltpu.VMEM((8 * LANES, SPAN), jnp.float32),
             pltpu.VMEM((LANES, 8, LANES), jnp.float32),
             pltpu.VMEM((LANES, LANES), jnp.float32),
             pltpu.VMEM((8 * LANES, LANES), jnp.float32),
         ],
         compiler_params=pltpu.CompilerParams(vmem_limit_bytes=12 << 20),
         name="krylov",
-    )(moments, vectors, gathered, *edges, first, second, masks, voxel_feats, voxel_reg)
+    )(moment_lanes, vectors, start, *edges, first, second, masks, voxel_feats, voxel_reg)
 
 
 def finish_kernel(shared_ref, basis_ref, solution_ref, residual_ref):
@@ -676,14 +691,15 @@
 
     moments, vectors, gathered, to_low, to_high = find_moments(got, (first, second, third))
     low, high = swap(to_low, to_high, GX, along_even)
-    first_lanes, second_lanes, mask_lanes = gather_early(
-        first, second, mask, (early_low, early_high, early_below, early_above)
+    first_lanes, second_lanes, mask_lanes, moment_lanes, start = gather_early(
+        first, second, mask, (early_low, early_high, early_below, early_above),
+        moments, (low, high), gathered, voxel_feats,
     )
     below, above = swap(
         *across_late(moments, vectors, low, high, early_low, early_high), "gy", across_even
     )
     basis, message = krylov(
-        moments, vectors, gathered, (low, high, below, above), first_lanes, second_lanes, mask_lanes,
+        moment_lanes, vectors, start, (low, high, below, above), first_lanes, second_lanes, mask_lanes,
         voxel_feats, voxel_reg, devices,
     )
     shared = lax.all_to_all(message, GX_GY, split_axis=0, concat_axis=0, tiled=True)

time: 85.4 us -> 87.3 us (1.022)
  waiting for transfers between devices: 22.4 us -> 26.1 us
  starting transfers between devices: 24.1 us -> 20.9 us
  Pallas kernels: 17.8 us -> 19.6 us
  local copies, waits for them, and re-layouts: 1.72 us -> 0.13 us
  blocking collectives: 17.9 us -> 19.2 us
    all_to_all x1, waiting for transfers between devices: 19.3 us -> 22.9 us  [shards(): lax.all_to_all(sending, GX_GY, split_axis=0, concat_axis=0, tiled=True)]
    ppermute x4, starting transfers between devices: 5.53 us -> 2.95 us  [swap(): first = lax.ppermute(jnp.where(odd, to_low, to_high), axis, pairs(0))]
    pallas_call x1, Pallas kernels: 4.06 us -> 5.73 us  [find_moments(): pl.pallas_call(moments_kernel, out_shape=(jax.ShapeDtypeStruct((bricks, 8...]
    unnamed x8 -> x6, local copies, waits for them, and re-layouts: 1.61 us -> 0.02 us
    all_to_all x1, blocking collectives: 17.9 us -> 19.2 us  [shards(): lax.all_to_all(message, GX_GY, split_axis=0, concat_axis=0, tiled=True)]
    ppermute x4, starting transfers between devices: 7.11 us -> 6.08 us  [swap(): second = lax.ppermute(jnp.where(odd, to_high, to_low), axis, pairs(1))]
    pallas_call x1, Pallas kernels: 1.33 us -> 2.21 us  [gather_early(): pl.pallas_call(gather_early_kernel, out_shape=(lanes, lanes, jax.ShapeDty...]
  transfers between devices with their start and end apart: 9 -> 9, of which waited for: 3 -> 2; matrix products, arithmetic and copies ran while one was open for 0% -> 0% of each run, Pallas kernels for 12% -> 15%
where the time goes in v11:
time: 87.3 us; the launch traced here: 87 us
  waiting for transfers between devices  26.1 us (30%)
  starting transfers between devices  20.9 us (24%)
  Pallas kernels  19.6 us (22%)
  blocking collectives  19.2 us (22%)
  between operations  0.93 us (1%)
    all_to_all x1, waiting for transfers between devices, shards(): lax.all_to_all(sending, GX_GY, split_axis=0, concat_axis=0, tiled=True)  22.9 us
    all_to_all x1, blocking collectives, shards(): lax.all_to_all(message, GX_GY, split_axis=0, concat_axis=0, tiled=True)  19.2 us
    all_to_all x1, starting transfers between devices, shards(): lax.all_to_all(sending, GX_GY, split_axis=0, concat_axis=0, tiled=True)  11.9 us
    ppermute x4, starting transfers between devices, swap(): second = lax.ppermute(jnp.where(odd, to_high, to_low), axis, pairs(1))  6.08 us
    pallas_call x1, Pallas kernels, find_moments(): pl.pallas_call(moments_kernel, out_shape=(jax.ShapeDtypeStruct((bricks, 8...  5.73 us
    pallas_call x1, Pallas kernels, prepare(): pl.pallas_call(prepare_kernel, out_shape=(record, record, record), compil...  4.92 us
    pallas_call x1, Pallas kernels, pack(): pl.pallas_call(pack_kernel, in_specs=[pl.BlockSpec(memory_space=pl.ANY),...  3.23 us
    ppermute x4, waiting for transfers between devices, swap(): second = lax.ppermute(jnp.where(odd, to_high, to_low), axis, pairs(1))  3.17 us
  transfers between devices with their start and end apart: 9, of which 2 were waited for; matrix products, arithmetic and copies ran while one was open for 0% of the time, Pallas kernels for 15%

profile of v11, /device:TPU:1, one launch (start us, length us, event | category | flops | bytes accessed | tf_op | source)
XLA Modules:
  0.0 87.0 jit_solution(1172770679366769800)
XLA Ops:
  0.6 3.2 %pack.1 = bf16[128,66,128]{2,1,0:T(8,128)(2,1)} custom-call(s32[8,4096]{1,0:T(8,128)} %bitcast.17, bf16[32,32768]{1,0:T(8,128)(2,1)} %feats_ref.5, bf16[256,128]{1,0:T(8,128)(2,1)} %bitcast.18), custom_call_target="tpu_custom_call" | custom-call | tf_op jit(solution)/shard_map/pack/pallas_call | solution.py:194
  3.9 0.0 copy-start.2
  3.9 0.0 copy-start
  3.9 0.0 copy-start.1
  3.9 11.9 %all-to-all-start = ((bf16[128,66,128]{2,1,0:T(8,128)(2,1)}), bf16[128,66,128]{2,1,0:T(8,128)(2,1)}, u32[]{:S(2)}, u32[]{:S(2)}) async-start(bf16[128,66,128]{2,1,0:T(8,128)(2,1)} %pack.1), calls=%async_computation | async-start | bytes 4718592 | tf_op jit(solution)/shard_map/all_to_all | solution.py:680
  15.8 0.0 copy-done.2
  15.9 0.1 copy.11
  16.0 0.0 copy-done
  16.0 0.0 copy-done.1
  16.0 4.9 %prepare.1 = (f32[32,8,128]{2,1,0:T(8,128)S(1)}, f32[32,8,128]{2,1,0:T(8,128)S(1)}, f32[32,8,128]{2,1,0:T(8,128)S(1)}) custom-call(f32[32,32,512]{2,1,0:T(8,128)S(1)} %copy-done, f32[32,512]{1,0:T(8,128)S(1)} %copy-done.1), custom_call_target="tpu_custom_call" | custom-call | flops 600000000 | bytes 5000000 | tf_op jit(solution)/shard_map/prepare/pallas_call | solution.py:264
  21.0 1.2 %collective-permute-start = (f32[104,128]{1,0:T(8,128)S(1)}, f32[104,128]{1,0:T(8,128)S(1)}, u32[]{:S(2)}, u32[]{:S(2)}) collective-permute-start(f32[104,128]{1,0:T(8,128)S(1)} %get-tuple-element.55), channel_id=1, source_target_pairs={{0,4},{4,0},{8,12},{12,8},{16,20},{20,16},{24,28},{28,24},{32,36},... | collective-permute-start | bytes 159752 | tf_op jit(solution)/shard_map/ppermute | solution.py:382
  22.2 2.7 %collective-permute-start.1 = (f32[104,128]{1,0:T(8,128)S(1)}, f32[104,128]{1,0:T(8,128)S(1)}, u32[]{:S(2)}, u32[]{:S(2)}) collective-permute-start(f32[104,128]{1,0:T(8,128)S(1)} %get-tuple-element.54), channel_id=1, source_target_pairs={{4,8},{8,4},{12,16},{16,12},{20,24},{24,20},{28,32},{32,28},{36,40... | collective-permute-start | bytes 159752 | tf_op jit(solution)/shard_map/ppermute | solution.py:381
  24.9 1.3 %collective-permute-start.2 = (f32[208,128]{1,0:T(8,128)S(1)}, f32[208,128]{1,0:T(8,128)S(1)}, u32[]{:S(2)}, u32[]{:S(2)}) collective-permute-start(f32[208,128]{1,0:T(8,128)S(1)} %get-tuple-element.43), channel_id=1, source_target_pairs={{0,1},{1,0},{2,3},{3,2},{4,5},{5,4},{6,7},{7,6},{8,9},{9,8},{10,11... | collective-permute-start | bytes 319496 | tf_op jit(solution)/shard_map/ppermute | solution.py:382
  26.2 0.7 collective-permute-start.3
  26.9 22.9 %all-to-all-done.got_ref = bf16[128,66,128]{2,1,0:T(8,128)(2,1)} async-done(((bf16[128,66,128]{2,1,0:T(8,128)(2,1)}), bf16[128,66,128]{2,1,0:T(8,128)(2,1)}, u32[]{:S(2)}, u32[]{:S(2)}) %all-to-all-start) | async-done | bytes 2162720 | tf_op jit(solution)/shard_map/all_to_all | solution.py:680
  49.8 5.7 %moments.1 = (f32[32,8,128]{2,1,0:T(8,128)S(1)}, f32[32,128]{1,0:T(8,128)S(1)}, f32[32,128]{1,0:T(8,128)S(1)}, f32[48,128]{1,0:T(8,128)S(1)}, f32[48,128]{1,0:T(8,128)S(1)}) custom-call(bf16[128,66,128]{2,1,0:T(8,128)(2,1)} %all-to-all-done.got_ref, f32[32,8,128]{2,1,0:T(8,128)S(1)} %get-tuple-element.21.first_ref, ...), custom_call_target="tpu_custom_call" | custom-call | flops 1000000000 | bytes 12000000 | tf_op jit(solution)/shard_map/moments/pallas_call | solution.py:457
  55.5 0.1 collective-permute-start.4
  55.6 0.0 collective-permute-done
  55.6 2.1 %collective-permute-start.5 = (f32[48,128]{1,0:T(8,128)S(1)}, f32[48,128]{1,0:T(8,128)S(1)}, u32[]{:S(2)}, u32[]{:S(2)}) collective-permute-start(f32[48,128]{1,0:T(8,128)S(1)} %get-tuple-element.58), channel_id=1, source_target_pairs={{4,8},{8,4},{12,16},{16,12},{20,24},{24,20},{28,32},{32,28},{36,40... | collective-permute-start | bytes 73736 | tf_op jit(solution)/shard_map/ppermute | solution.py:381
  57.8 0.0 collective-permute-done.1
  57.8 0.0 collective-permute-done.4
  57.8 3.2 %collective-permute-done.5 = f32[48,128]{1,0:T(8,128)S(1)} collective-permute-done((f32[48,128]{1,0:T(8,128)S(1)}, f32[48,128]{1,0:T(8,128)S(1)}, u32[]{:S(2)}, u32[]{:S(2)}) %collective-permute-start.5) | collective-permute-done | bytes 24608 | tf_op jit(solution)/shard_map/ppermute | solution.py:381
  61.0 0.4 collective-permute-start.6
  61.4 0.7 collective-permute-start.7
  62.1 0.0 collective-permute-done.2
  62.1 0.0 collective-permute-done.3
  62.1 2.2 %gather_early.1 = (f32[1024,256]{1,0:T(8,128)S(1)}, f32[1024,256]{1,0:T(8,128)S(1)}, f32[8,256]{1,0:T(8,128)S(1)}, f32[1024,256]{1,0:T(8,128)S(1)}, f32[32,512]{1,0:T(8,128)S(1)}) custom-call(f32[32,8,128]{2,1,0:T(8,128)S(1)} %get-tuple-element.21.first_ref, f32[32,8,128]{2,1,0:T(8,128)S(1)} %get-tuple-element.22.second_ref, f32[32,128]{1,0:T(8,128)S(1)} %pad.4.mask_ref, ...), custom_call_target="tpu_custom_call" | custom-call | flops 3000000 | bytes 5000000 | tf_op jit(solution)/shard_map/gather_early/pallas_call | solution.py:310
  64.3 0.0 collective-permute-done.6
  64.3 0.0 collective-permute-done.7
  64.4 2.3 %krylov.1 = (f32[4,32,512]{2,1,0:T(8,128)S(1)}, f32[128,128]{1,0:T(8,128)S(1)}) custom-call(f32[1024,256]{1,0:T(8,128)S(1)} %get-tuple-element.30.moment_lanes, f32[32,128]{1,0:T(8,128)S(1)} %get-tuple-element.31.vectors_ref, f32[32,512]{1,0:T(8,128)S(1)} %get-tuple-element.32.start_ref, f32[48,128]{1,0:T(8,128)S(1)} %get-tuple-element.57.late_low.low.low_ref, ...), custom_call_target="tpu_custom_call" | custom-call | tf_op jit(solution)/shard_map/krylov/pallas_call | solution.py:582
  66.7 19.2 %all_to_all.16 = f32[128,1,128]{2,1,0:T(1,128)S(1)} all-to-all(f32[128,1,128]{2,1,0:T(1,128)S(1)} %bitcast.16), channel_id=1, replica_groups=mesh['gx_0'=4,'gx_1'=4,'gx_2'=2,'gy'=4] {'gx_0','gx_1','gx_2','gy'}, dimensions={0} | all-to-all | bytes 131072 | tf_op jit(solution)/shard_map/all_to_all | solution.py:705
  85.9 1.1 %finish.1 = (f32[32,512]{1,0:T(8,128)}, f32[32,512]{1,0:T(8,128)}) custom-call(f32[128,128]{1,0:T(8,128)S(1)} %bitcast.15, f32[4,32,512]{2,1,0:T(8,128)S(1)} %get-tuple-element.39.basis_ref), custom_call_target="tpu_custom_call" | custom-call | tf_op jit(solution)/shard_map/finish/pallas_call | solution.py:666
  (17 shorter events, 0.2 us)
Async XLA Ops:
  3.9 12.0 %copy-start.2 = (s32[32,4]{0,1:T(4,128)S(1)}, s32[32,4]{0,1:T(4,128)}, u32[]{:S(2)}) copy-start(s32[32,4]{0,1:T(4,128)} %param.9) | copy-start | bytes 1540
  3.9 12.1 %copy-start = (f32[32,32,512]{2,1,0:T(8,128)S(1)}, f32[32,32,512]{2,1,0:T(8,128)}, u32[]{:S(2)}) copy-start(f32[32,32,512]{2,1,0:T(8,128)} %feats_ref.7) | copy-start | bytes 6291460
  3.9 12.1 %copy-start.1 = (f32[32,512]{1,0:T(8,128)S(1)}, f32[32,512]{1,0:T(8,128)}, u32[]{:S(2)}) copy-start(f32[32,512]{1,0:T(8,128)} %reg_ref.3) | copy-start | bytes 196612
  3.9 45.9 %all-to-all-start = ((bf16[128,66,128]{2,1,0:T(8,128)(2,1)}), bf16[128,66,128]{2,1,0:T(8,128)(2,1)}, u32[]{:S(2)}, u32[]{:S(2)}) async-start(bf16[128,66,128]{2,1,0:T(8,128)(2,1)} %pack.1), calls=%async_computation | async-start | bytes 4718592 | tf_op jit(solution)/shard_map/all_to_all | solution.py:680
  21.0 34.7 %collective-permute-start = (f32[104,128]{1,0:T(8,128)S(1)}, f32[104,128]{1,0:T(8,128)S(1)}, u32[]{:S(2)}, u32[]{:S(2)}) collective-permute-start(f32[104,128]{1,0:T(8,128)S(1)} %get-tuple-element.55), channel_id=1, source_target_pairs={{0,4},{4,0},{8,12},{12,8},{16,20},{20,16},{24,28},{28,24},{32,36},... | collective-permute-start | bytes 159752 | tf_op jit(solution)/shard_map/ppermute | solution.py:382
  22.2 35.6 %collective-permute-start.1 = (f32[104,128]{1,0:T(8,128)S(1)}, f32[104,128]{1,0:T(8,128)S(1)}, u32[]{:S(2)}, u32[]{:S(2)}) collective-permute-start(f32[104,128]{1,0:T(8,128)S(1)} %get-tuple-element.54), channel_id=1, source_target_pairs={{4,8},{8,4},{12,16},{16,12},{20,24},{24,20},{28,32},{32,28},{36,40... | collective-permute-start | bytes 159752 | tf_op jit(solution)/shard_map/ppermute | solution.py:381
  24.9 37.1 %collective-permute-start.2 = (f32[208,128]{1,0:T(8,128)S(1)}, f32[208,128]{1,0:T(8,128)S(1)}, u32[]{:S(2)}, u32[]{:S(2)}) collective-permute-start(f32[208,128]{1,0:T(8,128)S(1)} %get-tuple-element.43), channel_id=1, source_target_pairs={{0,1},{1,0},{2,3},{3,2},{4,5},{5,4},{6,7},{7,6},{8,9},{9,8},{10,11... | collective-permute-start | bytes 319496 | tf_op jit(solution)/shard_map/ppermute | solution.py:382
  26.2 35.9 %collective-permute-start.3 = (f32[208,128]{1,0:T(8,128)S(1)}, f32[208,128]{1,0:T(8,128)S(1)}, u32[]{:S(2)}, u32[]{:S(2)}) collective-permute-start(f32[208,128]{1,0:T(8,128)S(1)} %get-tuple-element.42), channel_id=1, source_target_pairs={{1,2},{2,1},{5,6},{6,5},{9,10},{10,9},{13,14},{14,13},{17,18},{18,... | collective-permute-start | bytes 319496 | tf_op jit(solution)/shard_map/ppermute | solution.py:381
  55.5 2.3 %collective-permute-start.4 = (f32[48,128]{1,0:T(8,128)S(1)}, f32[48,128]{1,0:T(8,128)S(1)}, u32[]{:S(2)}, u32[]{:S(2)}) collective-permute-start(f32[48,128]{1,0:T(8,128)S(1)} %get-tuple-element.59), channel_id=1, source_target_pairs={{0,4},{4,0},{8,12},{12,8},{16,20},{20,16},{24,28},{28,24},{32,36},... | collective-permute-start | bytes 73736 | tf_op jit(solution)/shard_map/ppermute | solution.py:382
  55.6 5.3 %collective-permute-start.5 = (f32[48,128]{1,0:T(8,128)S(1)}, f32[48,128]{1,0:T(8,128)S(1)}, u32[]{:S(2)}, u32[]{:S(2)}) collective-permute-start(f32[48,128]{1,0:T(8,128)S(1)} %get-tuple-element.58), channel_id=1, source_target_pairs={{4,8},{8,4},{12,16},{16,12},{20,24},{24,20},{28,32},{32,28},{36,40... | collective-permute-start | bytes 73736 | tf_op jit(solution)/shard_map/ppermute | solution.py:381
  61.0 3.3 %collective-permute-start.6 = (f32[120,128]{1,0:T(8,128)S(1)}, f32[120,128]{1,0:T(8,128)S(1)}, u32[]{:S(2)}, u32[]{:S(2)}) collective-permute-start(f32[120,128]{1,0:T(8,128)S(1)} %get-tuple-element.51), channel_id=1, source_target_pairs={{0,1},{1,0},{2,3},{3,2},{4,5},{5,4},{6,7},{7,6},{8,9},{9,8},{10,11... | collective-permute-start | bytes 184328 | tf_op jit(solution)/shard_map/ppermute | solution.py:382
  61.4 2.9 %collective-permute-start.7 = (f32[120,128]{1,0:T(8,128)S(1)}, f32[120,128]{1,0:T(8,128)S(1)}, u32[]{:S(2)}, u32[]{:S(2)}) collective-permute-start(f32[120,128]{1,0:T(8,128)S(1)} %get-tuple-element.50), channel_id=1, source_target_pairs={{1,2},{2,1},{5,6},{6,5},{9,10},{10,9},{13,14},{14,13},{17,18},{18,... | collective-permute-start | bytes 184328 | tf_op jit(solution)/shard_map/ppermute | solution.py:381

commit v12 on v11

--- a/solution.py
+++ b/solution.py
@@ -272,7 +272,7 @@
 
 def gather_early_kernel(
     first_ref, second_ref, mask_ref, low_ref, high_ref, below_ref, above_ref, moments_ref, late_low, late_high,
-    gathered_ref, feats_ref, first_lanes, second_lanes, mask_lanes, moment_lanes, start_ref,
+    first_lanes, second_lanes, mask_lanes, moment_lanes,
     first_store, second_store, mask_store, moment_store,
 ):
     for store in (first_store, second_store, mask_store, moment_store):
@@ -281,9 +281,6 @@
         for e in range(BY):
             moment_store[lane_of(a, e)] = brick_at(moments_ref, late_low, late_high, 0, LATE[0], a, e)
     to_lanes(moment_store, moment_lanes)
-    gathered = gathered_ref[...]
-    for b in range(BX * BY):
-        start_ref[b : b + 1, :] = jnp.sum(feats_ref[b] * gathered[:, b : b + 1], axis=0, keepdims=True)
 
     def put(store):
         def write(a, e, value):
@@ -303,9 +300,8 @@
     mask_lanes[...] = mask_store[...].T[:8, :]
 
 
-def gather_early(first, second, mask, edges, moments, late, gathered, voxel_feats):
+def gather_early(first, second, mask, edges, moments, late):
     lanes = jax.ShapeDtypeStruct((8 * LANES, SPAN), jnp.float32)
-    bricks, _, voxels = voxel_feats.shape
     store = pltpu.VMEM((SPAN, 8, LANES), jnp.float32)
     return pl.pallas_call(
         gather_early_kernel,
@@ -314,13 +310,12 @@
             lanes,
             jax.ShapeDtypeStruct((8, SPAN), jnp.float32),
             lanes,
-            jax.ShapeDtypeStruct((bricks, voxels), jnp.float32),
         ),
         scratch_shapes=[store, store, pltpu.VMEM((SPAN, LANES), jnp.float32), store],
-        compiler_params=pltpu.CompilerParams(vmem_limit_bytes=12 << 20),
+        compiler_params=pltpu.CompilerParams(vmem_limit_bytes=8 << 20),
         cost_estimate=pl.CostEstimate(flops=3_000_000, bytes_accessed=5_000_000, transcendentals=0),
         name="gather_early",
-    )(first, second, mask, *edges, moments, *late, gathered, voxel_feats)
+    )(first, second, mask, *edges, moments, *late)
 
 
 def across_early_kernel(first_ref, second_ref, mask_ref, to_low, to_high):
@@ -377,10 +372,9 @@
     def pairs(start):
         return [pair for a in range(start, count - 1, 2) for pair in ((a, a + 1), (a + 1, a))]
 
-    odd = jnp.logical_not(even)
-    second = lax.ppermute(jnp.where(odd, to_high, to_low), axis, pairs(1))
-    first = lax.ppermute(jnp.where(odd, to_low, to_high), axis, pairs(0))
-    return jnp.where(odd, first, second), jnp.where(odd, second, first)
+    second = lax.ppermute(jnp.where(even, to_low, to_high), axis, pairs(1))
+    first = lax.ppermute(jnp.where(even, to_high, to_low), axis, pairs(0))
+    return jnp.where(even, second, first), jnp.where(even, first, second)
 
 
 def moments_kernel(
@@ -488,7 +482,7 @@
 
 
 def krylov_kernel(
-    moment_lanes, vectors_ref, start_ref, low_ref, high_ref, below_ref, above_ref, first_ref, second_ref, mask_ref,
+    moment_lanes, vectors_ref, gathered_ref, low_ref, high_ref, below_ref, above_ref, first_ref, second_ref, mask_ref,
     feats_ref, reg_ref, basis_ref, message_ref, vector_store, corner_store, corner_masks, corner_lanes,
 ):
     corner_store[...] = jnp.zeros_like(corner_store)
@@ -542,12 +536,13 @@
     second_z = times(first_ref, one) + both_tiles(corners) + vectors[FEAT : 2 * FEAT]
     two = system(second_z) + beside_times(second_z)
     three = system(times(first_ref, two) + times(second_ref, one) + vectors[2 * FEAT : 3 * FEAT])
-    basis_ref[0] = start_ref[...]
+    gathered = gathered_ref[...]
     for b in range(BX * BY):
         place = lane_of(b // BY, b % BY)
         feats = feats_ref[b]
-        for step, values in enumerate((one, two, three)):
-            basis_ref[step + 1, b : b + 1, :] = jnp.sum(feats * values[:, place : place + 1], axis=0, keepdims=True)
+        columns = [gathered[:, b : b + 1]] + [values[:, place : place + 1] for values in (one, two, three)]
+        for step, column in enumerate(columns):
+            basis_ref[step, b : b + 1, :] = jnp.sum(feats * column, axis=0, keepdims=True)
     reg = reg_ref[...]
     basis = [basis_ref[0]]
     for step in range(1, 4):
@@ -577,7 +572,7 @@
     message_ref[...] = jnp.broadcast_to(row, message_ref.shape)
 
 
-def krylov(moment_lanes, vectors, start, edges, first, second, masks, voxel_feats, voxel_reg, devices):
+def krylov(moment_lanes, vectors, gathered, edges, first, second, masks, voxel_feats, voxel_reg, devices):
     bricks, _, voxels = voxel_feats.shape
     return pl.pallas_call(
         krylov_kernel,
@@ -591,9 +586,9 @@
             pltpu.VMEM((LANES, LANES), jnp.float32),
             pltpu.VMEM((8 * LANES, LANES), jnp.float32),
         ],
-        compiler_params=pltpu.CompilerParams(vmem_limit_bytes=12 << 20),
+        compiler_params=pltpu.CompilerParams(vmem_limit_bytes=8 << 20),
         name="krylov",
-    )(moment_lanes, vectors, start, *edges, first, second, masks, voxel_feats, voxel_reg)
+    )(moment_lanes, vectors, gathered, *edges, first, second, masks, voxel_feats, voxel_reg)
 
 
 def finish_kernel(shared_ref, basis_ref, solution_ref, residual_ref):
@@ -691,15 +686,15 @@
 
     moments, vectors, gathered, to_low, to_high = find_moments(got, (first, second, third))
     low, high = swap(to_low, to_high, GX, along_even)
-    first_lanes, second_lanes, mask_lanes, moment_lanes, start = gather_early(
+    first_lanes, second_lanes, mask_lanes, moment_lanes = gather_early(
         first, second, mask, (early_low, early_high, early_below, early_above),
-        moments, (low, high), gathered, voxel_feats,
+        moments, (low, high),
     )
     below, above = swap(
         *across_late(moments, vectors, low, high, early_low, early_high), "gy", across_even
     )
     basis, message = krylov(
-        moment_lanes, vectors, start, (low, high, below, above), first_lanes, second_lanes, mask_lanes,
+        moment_lanes, vectors, gathered, (low, high, below, above), first_lanes, second_lanes, mask_lanes,
         voxel_feats, voxel_reg, devices,
     )
     shared = lax.all_to_all(message, GX_GY, split_axis=0, concat_axis=0, tiled=True)

time: 87.3 us -> 84.8 us (0.971)
  waiting for transfers between devices: 26.1 us -> 22.2 us
  starting transfers between devices: 20.9 us -> 24.1 us
  Pallas kernels: 19.6 us -> 17.8 us
  blocking collectives: 19.2 us -> 17.5 us
  local copies, waits for them, and re-layouts: 0.13 us -> 1.72 us
    all_to_all x1, waiting for transfers between devices: 22.9 us -> 19.3 us  [shards(): lax.all_to_all(sending, GX_GY, split_axis=0, concat_axis=0, tiled=True)]
    ppermute x8, starting transfers between devices: 9.03 us -> 12.6 us  [the longest x4 7.1 us: swap(): second = lax.ppermute(jnp.where(even, to_low, to_high), axis, pairs(1))]
    pallas_call x1, Pallas kernels: 5.73 us -> 4.06 us  [find_moments(): pl.pallas_call(moments_kernel, out_shape=(jax.ShapeDtypeStruct((bricks, 8...]
    all_to_all x1, blocking collectives: 19.2 us -> 17.5 us  [shards(): lax.all_to_all(message, GX_GY, split_axis=0, concat_axis=0, tiled=True)]
    unnamed x6 -> x8, local copies, waits for them, and re-layouts: 0.02 us -> 1.61 us
  transfers between devices with their start and end apart: 9 -> 9, of which waited for: 2 -> 2; matrix products, arithmetic and copies ran while one was open for 0% -> 0% of each run, Pallas kernels for 15% -> 13%
where the time goes in v12:
time: 84.8 us; the launch traced here: 84.4 us
  starting transfers between devices  24.1 us (28%)
  waiting for transfers between devices  22.2 us (26%)
  Pallas kernels  17.8 us (21%)
  blocking collectives  17.5 us (21%)
  local copies, waits for them, and re-layouts  1.72 us (2%)
  between operations  0.92 us (1%)
    all_to_all x1, waiting for transfers between devices, shards(): lax.all_to_all(sending, GX_GY, split_axis=0, concat_axis=0, tiled=True)  19.3 us
    all_to_all x1, blocking collectives, shards(): lax.all_to_all(message, GX_GY, split_axis=0, concat_axis=0, tiled=True)  17.5 us
    all_to_all x1, starting transfers between devices, shards(): lax.all_to_all(sending, GX_GY, split_axis=0, concat_axis=0, tiled=True)  11.5 us
    ppermute x4, starting transfers between devices, swap(): second = lax.ppermute(jnp.where(even, to_low, to_high), axis, pairs(1))  7.1 us
    ppermute x4, starting transfers between devices, swap(): first = lax.ppermute(jnp.where(even, to_high, to_low), axis, pairs(0))  5.53 us
    pallas_call x1, Pallas kernels, prepare(): pl.pallas_call(prepare_kernel, out_shape=(record, record, record), compil...  4.92 us
    pallas_call x1, Pallas kernels, find_moments(): pl.pallas_call(moments_kernel, out_shape=(jax.ShapeDtypeStruct((bricks, 8...  4.06 us
    pallas_call x1, Pallas kernels, pack(): pl.pallas_call(pack_kernel, in_specs=[pl.BlockSpec(memory_space=pl.ANY),...  3.23 us
  transfers between devices with their start and end apart: 9, of which 2 were waited for; matrix products, arithmetic and copies ran while one was open for 0% of the time, Pallas kernels for 13%

profile of v12, /device:TPU:1, one launch (start us, length us, event | category | flops | bytes accessed | tf_op | source)
XLA Modules:
  0.0 84.4 jit_solution(1952495985560644744)
XLA Ops:
  0.6 3.2 %pack.1 = bf16[128,66,128]{2,1,0:T(8,128)(2,1)} custom-call(s32[8,4096]{1,0:T(8,128)} %bitcast.17, bf16[32,32768]{1,0:T(8,128)(2,1)} %feats_ref.4, bf16[256,128]{1,0:T(8,128)(2,1)} %bitcast.18), custom_call_target="tpu_custom_call" | custom-call | tf_op jit(solution)/shard_map/pack/pallas_call | solution.py:194
  3.9 0.0 copy-start.3
  3.9 0.0 copy-start.2
  3.9 11.5 %all-to-all-start = ((bf16[128,66,128]{2,1,0:T(8,128)(2,1)}), bf16[128,66,128]{2,1,0:T(8,128)(2,1)S(1)}, u32[]{:S(2)}, u32[]{:S(2)}) async-start(bf16[128,66,128]{2,1,0:T(8,128)(2,1)} %pack.1), calls=%async_computation | async-start | bytes 4718592 | tf_op jit(solution)/shard_map/all_to_all | solution.py:675
  15.4 0.0 copy-done.3
  15.5 0.1 copy.11
  15.6 0.0 copy-done.2
  15.6 0.0 copy-start
  15.6 1.6 %copy-done = f32[32,32,512]{2,1,0:T(8,128)S(1)} copy-done((f32[32,32,512]{2,1,0:T(8,128)S(1)}, f32[32,32,512]{2,1,0:T(8,128)}, u32[]{:S(2)}) %copy-start) | copy-done | bytes 2097176
  17.1 4.9 %prepare.1 = (f32[32,8,128]{2,1,0:T(8,128)S(1)}, f32[32,8,128]{2,1,0:T(8,128)S(1)}, f32[32,8,128]{2,1,0:T(8,128)S(1)}) custom-call(f32[32,32,512]{2,1,0:T(8,128)S(1)} %copy-done, f32[32,512]{1,0:T(8,128)S(1)} %copy-done.2), custom_call_target="tpu_custom_call" | custom-call | flops 600000000 | bytes 5000000 | tf_op jit(solution)/shard_map/prepare/pallas_call | solution.py:264
  22.1 3.7 %collective-permute-start = (f32[104,128]{1,0:T(8,128)S(1)}, f32[104,128]{1,0:T(8,128)S(1)}, u32[]{:S(2)}, u32[]{:S(2)}) collective-permute-start(f32[104,128]{1,0:T(8,128)S(1)} %get-tuple-element.53), channel_id=1, source_target_pairs={{4,8},{8,4},{12,16},{16,12},{20,24},{24,20},{28,32},{32,28},{36,40... | collective-permute-start | bytes 159752 | tf_op jit(solution)/shard_map/ppermute | solution.py:375
  25.8 0.1 collective-permute-start.1
  26.0 0.7 collective-permute-start.2
  26.7 3.7 %collective-permute-start.3 = (f32[208,128]{1,0:T(8,128)S(1)}, f32[208,128]{1,0:T(8,128)S(1)}, u32[]{:S(2)}, u32[]{:S(2)}) collective-permute-start(f32[208,128]{1,0:T(8,128)S(1)} %get-tuple-element.40), channel_id=1, source_target_pairs={{0,1},{1,0},{2,3},{3,2},{4,5},{5,4},{6,7},{7,6},{8,9},{9,8},{10,11... | collective-permute-start | bytes 319496 | tf_op jit(solution)/shard_map/ppermute | solution.py:376
  30.4 19.3 %all-to-all-done.got_ref = bf16[128,66,128]{2,1,0:T(8,128)(2,1)S(1)} async-done(((bf16[128,66,128]{2,1,0:T(8,128)(2,1)}), bf16[128,66,128]{2,1,0:T(8,128)(2,1)S(1)}, u32[]{:S(2)}, u32[]{:S(2)}) %all-to-all-start) | async-done | bytes 2162720 | tf_op jit(solution)/shard_map/all_to_all | solution.py:675
  49.7 0.0 copy-start.1
  49.7 4.1 %moments.1 = (f32[32,8,128]{2,1,0:T(8,128)S(1)}, f32[32,128]{1,0:T(8,128)S(1)}, f32[32,128]{1,0:T(8,128)S(1)}, f32[48,128]{1,0:T(8,128)S(1)}, f32[48,128]{1,0:T(8,128)S(1)}) custom-call(bf16[128,66,128]{2,1,0:T(8,128)(2,1)S(1)} %all-to-all-done.got_ref, f32[32,8,128]{2,1,0:T(8,128)S(1)} %get-tuple-element.20.first_ref, ...), custom_call_target="tpu_custom_call" | custom-call | flops 1000000000 | bytes 12000000 | tf_op jit(solution)/shard_map/moments/pallas_call | solution.py:451
  53.8 2.1 %collective-permute-start.4 = (f32[48,128]{1,0:T(8,128)S(1)}, f32[48,128]{1,0:T(8,128)S(1)}, u32[]{:S(2)}, u32[]{:S(2)}) collective-permute-start(f32[48,128]{1,0:T(8,128)S(1)} %get-tuple-element.57), channel_id=1, source_target_pairs={{4,8},{8,4},{12,16},{16,12},{20,24},{24,20},{28,32},{32,28},{36,40... | collective-permute-start | bytes 73736 | tf_op jit(solution)/shard_map/ppermute | solution.py:375
  55.9 0.0 collective-permute-done
  55.9 0.1 collective-permute-start.5
  56.0 0.0 collective-permute-done.1
  56.0 2.9 %collective-permute-done.4 = f32[48,128]{1,0:T(8,128)S(1)} collective-permute-done((f32[48,128]{1,0:T(8,128)S(1)}, f32[48,128]{1,0:T(8,128)S(1)}, u32[]{:S(2)}, u32[]{:S(2)}) %collective-permute-start.4) | collective-permute-done | bytes 24608 | tf_op jit(solution)/shard_map/ppermute | solution.py:375
  58.9 0.0 collective-permute-done.5
  59.0 0.7 collective-permute-start.6
  59.6 1.6 %collective-permute-start.7 = (f32[120,128]{1,0:T(8,128)S(1)}, f32[120,128]{1,0:T(8,128)S(1)}, u32[]{:S(2)}, u32[]{:S(2)}) collective-permute-start(f32[120,128]{1,0:T(8,128)S(1)} %get-tuple-element.48), channel_id=1, source_target_pairs={{0,1},{1,0},{2,3},{3,2},{4,5},{5,4},{6,7},{7,6},{8,9},{9,8},{10,11... | collective-permute-start | bytes 184328 | tf_op jit(solution)/shard_map/ppermute | solution.py:376
  61.3 0.0 collective-permute-done.2
  61.3 0.0 collective-permute-done.3
  61.3 1.9 %gather_early.1 = (f32[1024,256]{1,0:T(8,128)S(1)}, f32[1024,256]{1,0:T(8,128)S(1)}, f32[8,256]{1,0:T(8,128)S(1)}, f32[1024,256]{1,0:T(8,128)S(1)}) custom-call(f32[32,8,128]{2,1,0:T(8,128)S(1)} %get-tuple-element.20.first_ref, f32[32,8,128]{2,1,0:T(8,128)S(1)} %get-tuple-element.21.second_ref, f32[32,128]{1,0:T(8,128)S(1)} %pad.4.mask_ref, ...), custom_call_target="tpu_custom_call" | custom-call | flops 3000000 | bytes 5000000 | tf_op jit(solution)/shard_map/gather_early/pallas_call | solution.py:306
  63.3 0.0 collective-permute-done.6
  63.3 0.0 collective-permute-done.7
  63.3 0.0 copy-done.1
  63.3 2.5 %krylov.1 = (f32[4,32,512]{2,1,0:T(8,128)S(1)}, f32[128,128]{1,0:T(8,128)S(1)}) custom-call(f32[1024,256]{1,0:T(8,128)S(1)} %get-tuple-element.28.moment_lanes, f32[32,128]{1,0:T(8,128)S(1)} %get-tuple-element.29.vectors_ref, f32[32,128]{1,0:T(8,128)S(1)} %get-tuple-element.30.gathered_ref, f32[48,128]{1,0:T(8,128)S(1)} %get-tuple-element.55.late_low.low.low_ref, ...), custom_call_target="tpu_custom_call" | custom-call | tf_op jit(solution)/shard_map/krylov/pallas_call | solution.py:577
  65.8 17.5 %all_to_all.16 = f32[128,1,128]{2,1,0:T(1,128)S(1)} all-to-all(f32[128,1,128]{2,1,0:T(1,128)S(1)} %bitcast.16), channel_id=1, replica_groups=mesh['gx_0'=4,'gx_1'=4,'gx_2'=2,'gy'=4] {'gx_0','gx_1','gx_2','gy'}, dimensions={0} | all-to-all | bytes 131072 | tf_op jit(solution)/shard_map/all_to_all | solution.py:700
  83.3 1.1 %finish.1 = (f32[32,512]{1,0:T(8,128)}, f32[32,512]{1,0:T(8,128)}) custom-call(f32[128,128]{1,0:T(8,128)S(1)} %bitcast.15, f32[4,32,512]{2,1,0:T(8,128)S(1)} %get-tuple-element.37.basis_ref), custom_call_target="tpu_custom_call" | custom-call | tf_op jit(solution)/shard_map/finish/pallas_call | solution.py:661
  (17 shorter events, 0.2 us)
Async XLA Ops:
  3.9 11.5 %copy-start.3 = (s32[32,4]{0,1:T(4,128)S(1)}, s32[32,4]{0,1:T(4,128)}, u32[]{:S(2)}) copy-start(s32[32,4]{0,1:T(4,128)} %param.9) | copy-start | bytes 1540
  3.9 11.7 %copy-start.2 = (f32[32,512]{1,0:T(8,128)S(1)}, f32[32,512]{1,0:T(8,128)}, u32[]{:S(2)}) copy-start(f32[32,512]{1,0:T(8,128)} %reg_ref.3) | copy-start | bytes 196612
  3.9 45.8 %all-to-all-start = ((bf16[128,66,128]{2,1,0:T(8,128)(2,1)}), bf16[128,66,128]{2,1,0:T(8,128)(2,1)S(1)}, u32[]{:S(2)}, u32[]{:S(2)}) async-start(bf16[128,66,128]{2,1,0:T(8,128)(2,1)} %pack.1), calls=%async_computation | async-start | bytes 4718592 | tf_op jit(solution)/shard_map/all_to_all | solution.py:675
  15.6 1.6 %copy-start = (f32[32,32,512]{2,1,0:T(8,128)S(1)}, f32[32,32,512]{2,1,0:T(8,128)}, u32[]{:S(2)}) copy-start(f32[32,32,512]{2,1,0:T(8,128)} %feats_ref.5) | copy-start | bytes 6291460
  22.1 33.7 %collective-permute-start = (f32[104,128]{1,0:T(8,128)S(1)}, f32[104,128]{1,0:T(8,128)S(1)}, u32[]{:S(2)}, u32[]{:S(2)}) collective-permute-start(f32[104,128]{1,0:T(8,128)S(1)} %get-tuple-element.53), channel_id=1, source_target_pairs={{4,8},{8,4},{12,16},{16,12},{20,24},{24,20},{28,32},{32,28},{36,40... | collective-permute-start | bytes 159752 | tf_op jit(solution)/shard_map/ppermute | solution.py:375
  25.8 30.2 %collective-permute-start.1 = (f32[104,128]{1,0:T(8,128)S(1)}, f32[104,128]{1,0:T(8,128)S(1)}, u32[]{:S(2)}, u32[]{:S(2)}) collective-permute-start(f32[104,128]{1,0:T(8,128)S(1)} %get-tuple-element.52), channel_id=1, source_target_pairs={{0,4},{4,0},{8,12},{12,8},{16,20},{20,16},{24,28},{28,24},{32,36},... | collective-permute-start | bytes 159752 | tf_op jit(solution)/shard_map/ppermute | solution.py:376
  26.0 35.3 %collective-permute-start.2 = (f32[208,128]{1,0:T(8,128)S(1)}, f32[208,128]{1,0:T(8,128)S(1)}, u32[]{:S(2)}, u32[]{:S(2)}) collective-permute-start(f32[208,128]{1,0:T(8,128)S(1)} %get-tuple-element.41), channel_id=1, source_target_pairs={{1,2},{2,1},{5,6},{6,5},{9,10},{10,9},{13,14},{14,13},{17,18},{18,... | collective-permute-start | bytes 319496 | tf_op jit(solution)/shard_map/ppermute | solution.py:375
  26.7 34.6 %collective-permute-start.3 = (f32[208,128]{1,0:T(8,128)S(1)}, f32[208,128]{1,0:T(8,128)S(1)}, u32[]{:S(2)}, u32[]{:S(2)}) collective-permute-start(f32[208,128]{1,0:T(8,128)S(1)} %get-tuple-element.40), channel_id=1, source_target_pairs={{0,1},{1,0},{2,3},{3,2},{4,5},{5,4},{6,7},{7,6},{8,9},{9,8},{10,11... | collective-permute-start | bytes 319496 | tf_op jit(solution)/shard_map/ppermute | solution.py:376
  49.7 13.6 %copy-start.1 = (f32[32,32,512]{2,1,0:T(8,128)S(1)}, f32[32,32,512]{2,1,0:T(8,128)}, u32[]{:S(2)}) copy-start(f32[32,32,512]{2,1,0:T(8,128)} %feats_ref.5) | copy-start | bytes 6291460
  53.8 5.1 %collective-permute-start.4 = (f32[48,128]{1,0:T(8,128)S(1)}, f32[48,128]{1,0:T(8,128)S(1)}, u32[]{:S(2)}, u32[]{:S(2)}) collective-permute-start(f32[48,128]{1,0:T(8,128)S(1)} %get-tuple-element.57), channel_id=1, source_target_pairs={{4,8},{8,4},{12,16},{16,12},{20,24},{24,20},{28,32},{32,28},{36,40... | collective-permute-start | bytes 73736 | tf_op jit(solution)/shard_map/ppermute | solution.py:375
  55.9 3.0 %collective-permute-start.5 = (f32[48,128]{1,0:T(8,128)S(1)}, f32[48,128]{1,0:T(8,128)S(1)}, u32[]{:S(2)}, u32[]{:S(2)}) collective-permute-start(f32[48,128]{1,0:T(8,128)S(1)} %get-tuple-element.56), channel_id=1, source_target_pairs={{0,4},{4,0},{8,12},{12,8},{16,20},{20,16},{24,28},{28,24},{32,36},... | collective-permute-start | bytes 73736 | tf_op jit(solution)/shard_map/ppermute | solution.py:376
  59.0 4.3 %collective-permute-start.6 = (f32[120,128]{1,0:T(8,128)S(1)}, f32[120,128]{1,0:T(8,128)S(1)}, u32[]{:S(2)}, u32[]{:S(2)}) collective-permute-start(f32[120,128]{1,0:T(8,128)S(1)} %get-tuple-element.49), channel_id=1, source_target_pairs={{1,2},{2,1},{5,6},{6,5},{9,10},{10,9},{13,14},{14,13},{17,18},{18,... | collective-permute-start | bytes 184328 | tf_op jit(solution)/shard_map/ppermute | solution.py:375
  59.6 3.6 %collective-permute-start.7 = (f32[120,128]{1,0:T(8,128)S(1)}, f32[120,128]{1,0:T(8,128)S(1)}, u32[]{:S(2)}, u32[]{:S(2)}) collective-permute-start(f32[120,128]{1,0:T(8,128)S(1)} %get-tuple-element.48), channel_id=1, source_target_pairs={{0,1},{1,0},{2,3},{3,2},{4,5},{5,4},{6,7},{7,6},{8,9},{9,8},{10,11... | collective-permute-start | bytes 184328 | tf_op jit(solution)/shard_map/ppermute | solution.py:376

commit v13 on v12

--- a/solution.py
+++ b/solution.py
@@ -372,6 +372,11 @@
     def pairs(start):
         return [pair for a in range(start, count - 1, 2) for pair in ((a, a + 1), (a + 1, a))]
 
+    if axis != GX:
+        odd = jnp.logical_not(even)
+        second = lax.ppermute(jnp.where(odd, to_high, to_low), axis, pairs(1))
+        first = lax.ppermute(jnp.where(odd, to_low, to_high), axis, pairs(0))
+        return jnp.where(odd, first, second), jnp.where(odd, second, first)
     second = lax.ppermute(jnp.where(even, to_low, to_high), axis, pairs(1))
     first = lax.ppermute(jnp.where(even, to_high, to_low), axis, pairs(0))
     return jnp.where(even, second, first), jnp.where(even, first, second)

time: 84.8 us -> 85.7 us (1.011)
  starting transfers between devices: 24.1 us -> 20.4 us
  waiting for transfers between devices: 22.2 us -> 24.8 us
  blocking collectives: 17.5 us -> 19.5 us
    ppermute x4 -> x2, starting transfers between devices: 5.53 us -> 0.17 us  [swap(): first = lax.ppermute(jnp.where(even, to_high, to_low), axis, pairs(0))]
    ppermute x0 -> x4, starting transfers between devices: none -> 2.97 us  [the longest x2 1.66 us: swap(): first = lax.ppermute(jnp.where(odd, to_low, to_high), axis, pairs(0))]
    all_to_all x1, waiting for transfers between devices: 19.3 us -> 21.7 us  [shards(): lax.all_to_all(sending, GX_GY, split_axis=0, concat_axis=0, tiled=True)]
    all_to_all x1, blocking collectives: 17.5 us -> 19.5 us  [shards(): lax.all_to_all(message, GX_GY, split_axis=0, concat_axis=0, tiled=True)]
    ppermute x4 -> x2, starting transfers between devices: 7.1 us -> 5.77 us  [swap(): second = lax.ppermute(jnp.where(even, to_low, to_high), axis, pairs(1))]
    ppermute x4 -> x2, waiting for transfers between devices: 2.9 us -> 2.89 us  [swap(): second = lax.ppermute(jnp.where(even, to_low, to_high), axis, pairs(1))]
  transfers between devices with their start and end apart: 9 -> 9, of which waited for: 2 -> 3; matrix products, arithmetic and copies ran while one was open for 0% -> 0% of each run, Pallas kernels for 13% -> 13%
where the time goes in v13:
time: 85.7 us; the launch traced here: 85.3 us
  waiting for transfers between devices  24.8 us (29%)
  starting transfers between devices  20.4 us (24%)
  blocking collectives  19.5 us (23%)
  Pallas kernels  17.8 us (21%)
  local copies, waits for them, and re-layouts  1.72 us (2%)
  between operations  0.92 us (1%)
    all_to_all x1, waiting for transfers between devices, shards(): lax.all_to_all(sending, GX_GY, split_axis=0, concat_axis=0, tiled=True)  21.7 us
    all_to_all x1, blocking collectives, shards(): lax.all_to_all(message, GX_GY, split_axis=0, concat_axis=0, tiled=True)  19.5 us
    all_to_all x1, starting transfers between devices, shards(): lax.all_to_all(sending, GX_GY, split_axis=0, concat_axis=0, tiled=True)  11.5 us
    ppermute x2, starting transfers between devices, swap(): second = lax.ppermute(jnp.where(even, to_low, to_high), axis, pairs(1))  5.77 us
    pallas_call x1, Pallas kernels, prepare(): pl.pallas_call(prepare_kernel, out_shape=(record, record, record), compil...  4.92 us
    pallas_call x1, Pallas kernels, find_moments(): pl.pallas_call(moments_kernel, out_shape=(jax.ShapeDtypeStruct((bricks, 8...  4.06 us
    pallas_call x1, Pallas kernels, pack(): pl.pallas_call(pack_kernel, in_specs=[pl.BlockSpec(memory_space=pl.ANY),...  3.23 us
    ppermute x2, waiting for transfers between devices, swap(): second = lax.ppermute(jnp.where(even, to_low, to_high), axis, pairs(1))  2.89 us
  transfers between devices with their start and end apart: 9, of which 3 were waited for; matrix products, arithmetic and copies ran while one was open for 0% of the time, Pallas kernels for 13%

profile of v13, /device:TPU:1, one launch (start us, length us, event | category | flops | bytes accessed | tf_op | source)
XLA Modules:
  0.0 85.3 jit_solution(2917086776330584059)
XLA Ops:
  0.6 3.2 %pack.1 = bf16[128,66,128]{2,1,0:T(8,128)(2,1)} custom-call(s32[8,4096]{1,0:T(8,128)} %bitcast.17, bf16[32,32768]{1,0:T(8,128)(2,1)} %feats_ref.4, bf16[256,128]{1,0:T(8,128)(2,1)} %bitcast.18), custom_call_target="tpu_custom_call" | custom-call | tf_op jit(solution)/shard_map/pack/pallas_call | solution.py:194
  3.9 0.0 copy-start.3
  3.9 0.0 copy-start.2
  3.9 11.5 %all-to-all-start = ((bf16[128,66,128]{2,1,0:T(8,128)(2,1)}), bf16[128,66,128]{2,1,0:T(8,128)(2,1)S(1)}, u32[]{:S(2)}, u32[]{:S(2)}) async-start(bf16[128,66,128]{2,1,0:T(8,128)(2,1)} %pack.1), calls=%async_computation | async-start | bytes 4718592 | tf_op jit(solution)/shard_map/all_to_all | solution.py:680
  15.4 0.0 copy-done.3
  15.5 0.1 copy.11
  15.6 0.0 copy-done.2
  15.6 0.0 copy-start
  15.6 1.6 %copy-done = f32[32,32,512]{2,1,0:T(8,128)S(1)} copy-done((f32[32,32,512]{2,1,0:T(8,128)S(1)}, f32[32,32,512]{2,1,0:T(8,128)}, u32[]{:S(2)}) %copy-start) | copy-done | bytes 2097176
  17.1 4.9 %prepare.1 = (f32[32,8,128]{2,1,0:T(8,128)S(1)}, f32[32,8,128]{2,1,0:T(8,128)S(1)}, f32[32,8,128]{2,1,0:T(8,128)S(1)}) custom-call(f32[32,32,512]{2,1,0:T(8,128)S(1)} %copy-done, f32[32,512]{1,0:T(8,128)S(1)} %copy-done.2), custom_call_target="tpu_custom_call" | custom-call | flops 600000000 | bytes 5000000 | tf_op jit(solution)/shard_map/prepare/pallas_call | solution.py:264
  22.1 3.7 %collective-permute-start = (f32[104,128]{1,0:T(8,128)S(1)}, f32[104,128]{1,0:T(8,128)S(1)}, u32[]{:S(2)}, u32[]{:S(2)}) collective-permute-start(f32[104,128]{1,0:T(8,128)S(1)} %get-tuple-element.53), channel_id=1, source_target_pairs={{4,8},{8,4},{12,16},{16,12},{20,24},{24,20},{28,32},{32,28},{36,40... | collective-permute-start | bytes 159752 | tf_op jit(solution)/shard_map/ppermute | solution.py:380
  25.8 0.1 collective-permute-start.1
  26.0 1.3 %collective-permute-start.2 = (f32[208,128]{1,0:T(8,128)S(1)}, f32[208,128]{1,0:T(8,128)S(1)}, u32[]{:S(2)}, u32[]{:S(2)}) collective-permute-start(f32[208,128]{1,0:T(8,128)S(1)} %get-tuple-element.41), channel_id=1, source_target_pairs={{0,1},{1,0},{2,3},{3,2},{4,5},{5,4},{6,7},{7,6},{8,9},{9,8},{10,11... | collective-permute-start | bytes 319496 | tf_op jit(solution)/shard_map/ppermute | solution.py:378
  27.3 0.7 collective-permute-start.3
  27.9 21.7 %all-to-all-done.got_ref = bf16[128,66,128]{2,1,0:T(8,128)(2,1)S(1)} async-done(((bf16[128,66,128]{2,1,0:T(8,128)(2,1)}), bf16[128,66,128]{2,1,0:T(8,128)(2,1)S(1)}, u32[]{:S(2)}, u32[]{:S(2)}) %all-to-all-start) | async-done | bytes 2162720 | tf_op jit(solution)/shard_map/all_to_all | solution.py:680
  49.7 0.0 copy-start.1
  49.7 4.1 %moments.1 = (f32[32,8,128]{2,1,0:T(8,128)S(1)}, f32[32,128]{1,0:T(8,128)S(1)}, f32[32,128]{1,0:T(8,128)S(1)}, f32[48,128]{1,0:T(8,128)S(1)}, f32[48,128]{1,0:T(8,128)S(1)}) custom-call(bf16[128,66,128]{2,1,0:T(8,128)(2,1)S(1)} %all-to-all-done.got_ref, f32[32,8,128]{2,1,0:T(8,128)S(1)} %get-tuple-element.20.first_ref, ...), custom_call_target="tpu_custom_call" | custom-call | flops 1000000000 | bytes 12000000 | tf_op jit(solution)/shard_map/moments/pallas_call | solution.py:456
  53.8 2.1 %collective-permute-start.4 = (f32[48,128]{1,0:T(8,128)S(1)}, f32[48,128]{1,0:T(8,128)S(1)}, u32[]{:S(2)}, u32[]{:S(2)}) collective-permute-start(f32[48,128]{1,0:T(8,128)S(1)} %get-tuple-element.57), channel_id=1, source_target_pairs={{4,8},{8,4},{12,16},{16,12},{20,24},{24,20},{28,32},{32,28},{36,40... | collective-permute-start | bytes 73736 | tf_op jit(solution)/shard_map/ppermute | solution.py:380
  55.9 0.0 collective-permute-done
  55.9 0.1 collective-permute-start.5
  56.0 0.0 collective-permute-done.1
  56.0 2.9 %collective-permute-done.4 = f32[48,128]{1,0:T(8,128)S(1)} collective-permute-done((f32[48,128]{1,0:T(8,128)S(1)}, f32[48,128]{1,0:T(8,128)S(1)}, u32[]{:S(2)}, u32[]{:S(2)}) %collective-permute-start.4) | collective-permute-done | bytes 24608 | tf_op jit(solution)/shard_map/ppermute | solution.py:380
  58.9 0.0 collective-permute-done.5
  59.0 0.4 collective-permute-start.6
  59.4 0.7 collective-permute-start.7
  60.0 0.0 collective-permute-done.2
  60.0 0.0 collective-permute-done.3
  60.1 1.9 %gather_early.1 = (f32[1024,256]{1,0:T(8,128)S(1)}, f32[1024,256]{1,0:T(8,128)S(1)}, f32[8,256]{1,0:T(8,128)S(1)}, f32[1024,256]{1,0:T(8,128)S(1)}) custom-call(f32[32,8,128]{2,1,0:T(8,128)S(1)} %get-tuple-element.20.first_ref, f32[32,8,128]{2,1,0:T(8,128)S(1)} %get-tuple-element.21.second_ref, f32[32,128]{1,0:T(8,128)S(1)} %pad.4.mask_ref, ...), custom_call_target="tpu_custom_call" | custom-call | flops 3000000 | bytes 5000000 | tf_op jit(solution)/shard_map/gather_early/pallas_call | solution.py:306
  62.0 0.1 collective-permute-done.6
  62.1 0.0 collective-permute-done.7
  62.1 0.0 copy-done.1
  62.2 2.5 %krylov.1 = (f32[4,32,512]{2,1,0:T(8,128)S(1)}, f32[128,128]{1,0:T(8,128)S(1)}) custom-call(f32[1024,256]{1,0:T(8,128)S(1)} %get-tuple-element.28.moment_lanes, f32[32,128]{1,0:T(8,128)S(1)} %get-tuple-element.29.vectors_ref, f32[32,128]{1,0:T(8,128)S(1)} %get-tuple-element.30.gathered_ref, f32[48,128]{1,0:T(8,128)S(1)} %get-tuple-element.55.late_low.low.low_ref, ...), custom_call_target="tpu_custom_call" | custom-call | tf_op jit(solution)/shard_map/krylov/pallas_call | solution.py:582
  64.7 19.5 %all_to_all.16 = f32[128,1,128]{2,1,0:T(1,128)S(1)} all-to-all(f32[128,1,128]{2,1,0:T(1,128)S(1)} %bitcast.16), channel_id=1, replica_groups=mesh['gx_0'=4,'gx_1'=4,'gx_2'=2,'gy'=4] {'gx_0','gx_1','gx_2','gy'}, dimensions={0} | all-to-all | bytes 131072 | tf_op jit(solution)/shard_map/all_to_all | solution.py:705
  84.2 1.1 %finish.1 = (f32[32,512]{1,0:T(8,128)}, f32[32,512]{1,0:T(8,128)}) custom-call(f32[128,128]{1,0:T(8,128)S(1)} %bitcast.15, f32[4,32,512]{2,1,0:T(8,128)S(1)} %get-tuple-element.37.basis_ref), custom_call_target="tpu_custom_call" | custom-call | tf_op jit(solution)/shard_map/finish/pallas_call | solution.py:666
  (17 shorter events, 0.2 us)
Async XLA Ops:
  3.9 11.5 %copy-start.3 = (s32[32,4]{0,1:T(4,128)S(1)}, s32[32,4]{0,1:T(4,128)}, u32[]{:S(2)}) copy-start(s32[32,4]{0,1:T(4,128)} %param.9) | copy-start | bytes 1540
  3.9 11.7 %copy-start.2 = (f32[32,512]{1,0:T(8,128)S(1)}, f32[32,512]{1,0:T(8,128)}, u32[]{:S(2)}) copy-start(f32[32,512]{1,0:T(8,128)} %reg_ref.3) | copy-start | bytes 196612
  3.9 45.8 %all-to-all-start = ((bf16[128,66,128]{2,1,0:T(8,128)(2,1)}), bf16[128,66,128]{2,1,0:T(8,128)(2,1)S(1)}, u32[]{:S(2)}, u32[]{:S(2)}) async-start(bf16[128,66,128]{2,1,0:T(8,128)(2,1)} %pack.1), calls=%async_computation | async-start | bytes 4718592 | tf_op jit(solution)/shard_map/all_to_all | solution.py:680
  15.6 1.6 %copy-start = (f32[32,32,512]{2,1,0:T(8,128)S(1)}, f32[32,32,512]{2,1,0:T(8,128)}, u32[]{:S(2)}) copy-start(f32[32,32,512]{2,1,0:T(8,128)} %feats_ref.5) | copy-start | bytes 6291460
  22.1 33.7 %collective-permute-start = (f32[104,128]{1,0:T(8,128)S(1)}, f32[104,128]{1,0:T(8,128)S(1)}, u32[]{:S(2)}, u32[]{:S(2)}) collective-permute-start(f32[104,128]{1,0:T(8,128)S(1)} %get-tuple-element.53), channel_id=1, source_target_pairs={{4,8},{8,4},{12,16},{16,12},{20,24},{24,20},{28,32},{32,28},{36,40... | collective-permute-start | bytes 159752 | tf_op jit(solution)/shard_map/ppermute | solution.py:380
  25.8 30.2 %collective-permute-start.1 = (f32[104,128]{1,0:T(8,128)S(1)}, f32[104,128]{1,0:T(8,128)S(1)}, u32[]{:S(2)}, u32[]{:S(2)}) collective-permute-start(f32[104,128]{1,0:T(8,128)S(1)} %get-tuple-element.52), channel_id=1, source_target_pairs={{0,4},{4,0},{8,12},{12,8},{16,20},{20,16},{24,28},{28,24},{32,36},... | collective-permute-start | bytes 159752 | tf_op jit(solution)/shard_map/ppermute | solution.py:381
  26.0 34.0 %collective-permute-start.2 = (f32[208,128]{1,0:T(8,128)S(1)}, f32[208,128]{1,0:T(8,128)S(1)}, u32[]{:S(2)}, u32[]{:S(2)}) collective-permute-start(f32[208,128]{1,0:T(8,128)S(1)} %get-tuple-element.41), channel_id=1, source_target_pairs={{0,1},{1,0},{2,3},{3,2},{4,5},{5,4},{6,7},{7,6},{8,9},{9,8},{10,11... | collective-permute-start | bytes 319496 | tf_op jit(solution)/shard_map/ppermute | solution.py:378
  27.3 32.8 %collective-permute-start.3 = (f32[208,128]{1,0:T(8,128)S(1)}, f32[208,128]{1,0:T(8,128)S(1)}, u32[]{:S(2)}, u32[]{:S(2)}) collective-permute-start(f32[208,128]{1,0:T(8,128)S(1)} %get-tuple-element.40), channel_id=1, source_target_pairs={{1,2},{2,1},{5,6},{6,5},{9,10},{10,9},{13,14},{14,13},{17,18},{18,... | collective-permute-start | bytes 319496 | tf_op jit(solution)/shard_map/ppermute | solution.py:377
  49.7 12.5 %copy-start.1 = (f32[32,32,512]{2,1,0:T(8,128)S(1)}, f32[32,32,512]{2,1,0:T(8,128)}, u32[]{:S(2)}) copy-start(f32[32,32,512]{2,1,0:T(8,128)} %feats_ref.5) | copy-start | bytes 6291460
  53.8 5.1 %collective-permute-start.4 = (f32[48,128]{1,0:T(8,128)S(1)}, f32[48,128]{1,0:T(8,128)S(1)}, u32[]{:S(2)}, u32[]{:S(2)}) collective-permute-start(f32[48,128]{1,0:T(8,128)S(1)} %get-tuple-element.57), channel_id=1, source_target_pairs={{4,8},{8,4},{12,16},{16,12},{20,24},{24,20},{28,32},{32,28},{36,40... | collective-permute-start | bytes 73736 | tf_op jit(solution)/shard_map/ppermute | solution.py:380
  55.9 3.0 %collective-permute-start.5 = (f32[48,128]{1,0:T(8,128)S(1)}, f32[48,128]{1,0:T(8,128)S(1)}, u32[]{:S(2)}, u32[]{:S(2)}) collective-permute-start(f32[48,128]{1,0:T(8,128)S(1)} %get-tuple-element.56), channel_id=1, source_target_pairs={{0,4},{4,0},{8,12},{12,8},{16,20},{20,16},{24,28},{28,24},{32,36},... | collective-permute-start | bytes 73736 | tf_op jit(solution)/shard_map/ppermute | solution.py:381
  59.0 3.2 %collective-permute-start.6 = (f32[120,128]{1,0:T(8,128)S(1)}, f32[120,128]{1,0:T(8,128)S(1)}, u32[]{:S(2)}, u32[]{:S(2)}) collective-permute-start(f32[120,128]{1,0:T(8,128)S(1)} %get-tuple-element.49), channel_id=1, source_target_pairs={{0,1},{1,0},{2,3},{3,2},{4,5},{5,4},{6,7},{7,6},{8,9},{9,8},{10,11... | collective-permute-start | bytes 184328 | tf_op jit(solution)/shard_map/ppermute | solution.py:378
  59.4 2.8 %collective-permute-start.7 = (f32[120,128]{1,0:T(8,128)S(1)}, f32[120,128]{1,0:T(8,128)S(1)}, u32[]{:S(2)}, u32[]{:S(2)}) collective-permute-start(f32[120,128]{1,0:T(8,128)S(1)} %get-tuple-element.48), channel_id=1, source_target_pairs={{1,2},{2,1},{5,6},{6,5},{9,10},{10,9},{13,14},{14,13},{17,18},{18,... | collective-permute-start | bytes 184328 | tf_op jit(solution)/shard_map/ppermute | solution.py:377

commit v14 on v12

--- a/solution.py
+++ b/solution.py
@@ -416,14 +416,12 @@
                 for q in range(4):
                     own = own + jnp.where(lane_group == q, square[q * FEAT : (q + 1) * FEAT, :], 0.0)
                 moments_ref[half * 16 + b] = spread_rows(own, lane_group)
-    point = lax.broadcasted_iota(jnp.int32, (LANES, LANES), 0) // SLOTS
-    lane = lax.broadcasted_iota(jnp.int32, (LANES, LANES), 1)
-    values = jnp.zeros((FEAT, LANES), jnp.float32)
-    for half in range(2):
-        spread = (lane % (BX * BY) == point + half * 16).astype(jnp.float32)
-        values = values + jnp.dot(
-            sums[half], spread, precision=HIGHEST, preferred_element_type=jnp.float32
-        )
+    point = lax.broadcasted_iota(jnp.int32, (2 * LANES, LANES), 0) // SLOTS
+    lane = lax.broadcasted_iota(jnp.int32, (2 * LANES, LANES), 1)
+    spread = (lane % (BX * BY) == point).astype(jnp.float32)
+    values = jnp.dot(
+        jnp.concatenate(sums, axis=1), spread, precision=HIGHEST, preferred_element_type=jnp.float32
+    )
     gathered_ref[...] = values
     values = times(lanes_ref, values)
     for t in range(8):

time: 84.8 us -> 84.9 us (level)
  no operation moved by 1% of the time
where the time goes in v14:
time: 84.9 us; the launch traced here: 84.5 us
  starting transfers between devices  24.1 us (28%)
  waiting for transfers between devices  22.2 us (26%)
  Pallas kernels  17.9 us (21%)
  blocking collectives  17.5 us (21%)
  local copies, waits for them, and re-layouts  1.72 us (2%)
  between operations  0.92 us (1%)
    all_to_all x1, waiting for transfers between devices, shards(): lax.all_to_all(sending, GX_GY, split_axis=0, concat_axis=0, tiled=True)  19.3 us
    all_to_all x1, blocking collectives, shards(): lax.all_to_all(message, GX_GY, split_axis=0, concat_axis=0, tiled=True)  17.5 us
    all_to_all x1, starting transfers between devices, shards(): lax.all_to_all(sending, GX_GY, split_axis=0, concat_axis=0, tiled=True)  11.5 us
    ppermute x4, starting transfers between devices, swap(): second = lax.ppermute(jnp.where(even, to_low, to_high), axis, pairs(1))  7.1 us
    ppermute x4, starting transfers between devices, swap(): first = lax.ppermute(jnp.where(even, to_high, to_low), axis, pairs(0))  5.53 us
    pallas_call x1, Pallas kernels, prepare(): pl.pallas_call(prepare_kernel, out_shape=(record, record, record), compil...  4.92 us
    pallas_call x1, Pallas kernels, find_moments(): pl.pallas_call(moments_kernel, out_shape=(jax.ShapeDtypeStruct((bricks, 8...  4.13 us
    pallas_call x1, Pallas kernels, pack(): pl.pallas_call(pack_kernel, in_specs=[pl.BlockSpec(memory_space=pl.ANY),...  3.23 us
  transfers between devices with their start and end apart: 9, of which 2 were waited for; matrix products, arithmetic and copies ran while one was open for 0% of the time, Pallas kernels for 13%

profile of v14, /device:TPU:1, one launch (start us, length us, event | category | flops | bytes accessed | tf_op | source)
XLA Modules:
  0.0 84.5 jit_solution(17417924417454248925)
XLA Ops:
  0.6 3.2 %pack.1 = bf16[128,66,128]{2,1,0:T(8,128)(2,1)} custom-call(s32[8,4096]{1,0:T(8,128)} %bitcast.17, bf16[32,32768]{1,0:T(8,128)(2,1)} %feats_ref.4, bf16[256,128]{1,0:T(8,128)(2,1)} %bitcast.18), custom_call_target="tpu_custom_call" | custom-call | tf_op jit(solution)/shard_map/pack/pallas_call | solution.py:194
  3.9 0.0 copy-start.3
  3.9 0.0 copy-start.2
  3.9 11.5 %all-to-all-start = ((bf16[128,66,128]{2,1,0:T(8,128)(2,1)}), bf16[128,66,128]{2,1,0:T(8,128)(2,1)S(1)}, u32[]{:S(2)}, u32[]{:S(2)}) async-start(bf16[128,66,128]{2,1,0:T(8,128)(2,1)} %pack.1), calls=%async_computation | async-start | bytes 4718592 | tf_op jit(solution)/shard_map/all_to_all | solution.py:673
  15.4 0.0 copy-done.3
  15.5 0.1 copy.11
  15.6 0.0 copy-done.2
  15.6 0.0 copy-start
  15.6 1.6 %copy-done = f32[32,32,512]{2,1,0:T(8,128)S(1)} copy-done((f32[32,32,512]{2,1,0:T(8,128)S(1)}, f32[32,32,512]{2,1,0:T(8,128)}, u32[]{:S(2)}) %copy-start) | copy-done | bytes 2097176
  17.1 4.9 %prepare.1 = (f32[32,8,128]{2,1,0:T(8,128)S(1)}, f32[32,8,128]{2,1,0:T(8,128)S(1)}, f32[32,8,128]{2,1,0:T(8,128)S(1)}) custom-call(f32[32,32,512]{2,1,0:T(8,128)S(1)} %copy-done, f32[32,512]{1,0:T(8,128)S(1)} %copy-done.2), custom_call_target="tpu_custom_call" | custom-call | flops 600000000 | bytes 5000000 | tf_op jit(solution)/shard_map/prepare/pallas_call | solution.py:264
  22.1 3.7 %collective-permute-start = (f32[104,128]{1,0:T(8,128)S(1)}, f32[104,128]{1,0:T(8,128)S(1)}, u32[]{:S(2)}, u32[]{:S(2)}) collective-permute-start(f32[104,128]{1,0:T(8,128)S(1)} %get-tuple-element.53), channel_id=1, source_target_pairs={{4,8},{8,4},{12,16},{16,12},{20,24},{24,20},{28,32},{32,28},{36,40... | collective-permute-start | bytes 159752 | tf_op jit(solution)/shard_map/ppermute | solution.py:375
  25.8 0.1 collective-permute-start.1
  26.0 0.7 collective-permute-start.2
  26.7 3.7 %collective-permute-start.3 = (f32[208,128]{1,0:T(8,128)S(1)}, f32[208,128]{1,0:T(8,128)S(1)}, u32[]{:S(2)}, u32[]{:S(2)}) collective-permute-start(f32[208,128]{1,0:T(8,128)S(1)} %get-tuple-element.40), channel_id=1, source_target_pairs={{0,1},{1,0},{2,3},{3,2},{4,5},{5,4},{6,7},{7,6},{8,9},{9,8},{10,11... | collective-permute-start | bytes 319496 | tf_op jit(solution)/shard_map/ppermute | solution.py:376
  30.4 19.3 %all-to-all-done.got_ref = bf16[128,66,128]{2,1,0:T(8,128)(2,1)S(1)} async-done(((bf16[128,66,128]{2,1,0:T(8,128)(2,1)}), bf16[128,66,128]{2,1,0:T(8,128)(2,1)S(1)}, u32[]{:S(2)}, u32[]{:S(2)}) %all-to-all-start) | async-done | bytes 2162720 | tf_op jit(solution)/shard_map/all_to_all | solution.py:673
  49.7 0.0 copy-start.1
  49.7 4.1 %moments.1 = (f32[32,8,128]{2,1,0:T(8,128)S(1)}, f32[32,128]{1,0:T(8,128)S(1)}, f32[32,128]{1,0:T(8,128)S(1)}, f32[48,128]{1,0:T(8,128)S(1)}, f32[48,128]{1,0:T(8,128)S(1)}) custom-call(bf16[128,66,128]{2,1,0:T(8,128)(2,1)S(1)} %all-to-all-done.got_ref, f32[32,8,128]{2,1,0:T(8,128)S(1)} %get-tuple-element.20.first_ref, ...), custom_call_target="tpu_custom_call" | custom-call | flops 1000000000 | bytes 12000000 | tf_op jit(solution)/shard_map/moments/pallas_call | solution.py:449
  53.8 2.1 %collective-permute-start.4 = (f32[48,128]{1,0:T(8,128)S(1)}, f32[48,128]{1,0:T(8,128)S(1)}, u32[]{:S(2)}, u32[]{:S(2)}) collective-permute-start(f32[48,128]{1,0:T(8,128)S(1)} %get-tuple-element.57), channel_id=1, source_target_pairs={{4,8},{8,4},{12,16},{16,12},{20,24},{24,20},{28,32},{32,28},{36,40... | collective-permute-start | bytes 73736 | tf_op jit(solution)/shard_map/ppermute | solution.py:375
  55.9 0.0 collective-permute-done
  56.0 0.1 collective-permute-start.5
  56.1 0.0 collective-permute-done.1
  56.1 2.9 %collective-permute-done.4 = f32[48,128]{1,0:T(8,128)S(1)} collective-permute-done((f32[48,128]{1,0:T(8,128)S(1)}, f32[48,128]{1,0:T(8,128)S(1)}, u32[]{:S(2)}, u32[]{:S(2)}) %collective-permute-start.4) | collective-permute-done | bytes 24608 | tf_op jit(solution)/shard_map/ppermute | solution.py:375
  59.0 0.0 collective-permute-done.5
  59.0 0.7 collective-permute-start.6
  59.7 1.6 %collective-permute-start.7 = (f32[120,128]{1,0:T(8,128)S(1)}, f32[120,128]{1,0:T(8,128)S(1)}, u32[]{:S(2)}, u32[]{:S(2)}) collective-permute-start(f32[120,128]{1,0:T(8,128)S(1)} %get-tuple-element.48), channel_id=1, source_target_pairs={{0,1},{1,0},{2,3},{3,2},{4,5},{5,4},{6,7},{7,6},{8,9},{9,8},{10,11... | collective-permute-start | bytes 184328 | tf_op jit(solution)/shard_map/ppermute | solution.py:376
  61.4 0.0 collective-permute-done.2
  61.4 0.0 collective-permute-done.3
  61.4 1.9 %gather_early.1 = (f32[1024,256]{1,0:T(8,128)S(1)}, f32[1024,256]{1,0:T(8,128)S(1)}, f32[8,256]{1,0:T(8,128)S(1)}, f32[1024,256]{1,0:T(8,128)S(1)}) custom-call(f32[32,8,128]{2,1,0:T(8,128)S(1)} %get-tuple-element.20.first_ref, f32[32,8,128]{2,1,0:T(8,128)S(1)} %get-tuple-element.21.second_ref, f32[32,128]{1,0:T(8,128)S(1)} %pad.4.mask_ref, ...), custom_call_target="tpu_custom_call" | custom-call | flops 3000000 | bytes 5000000 | tf_op jit(solution)/shard_map/gather_early/pallas_call | solution.py:306
  63.3 0.0 collective-permute-done.6
  63.3 0.0 collective-permute-done.7
  63.4 0.0 copy-done.1
  63.4 2.5 %krylov.1 = (f32[4,32,512]{2,1,0:T(8,128)S(1)}, f32[128,128]{1,0:T(8,128)S(1)}) custom-call(f32[1024,256]{1,0:T(8,128)S(1)} %get-tuple-element.28.moment_lanes, f32[32,128]{1,0:T(8,128)S(1)} %get-tuple-element.29.vectors_ref, f32[32,128]{1,0:T(8,128)S(1)} %get-tuple-element.30.gathered_ref, f32[48,128]{1,0:T(8,128)S(1)} %get-tuple-element.55.late_low.low.low_ref, ...), custom_call_target="tpu_custom_call" | custom-call | tf_op jit(solution)/shard_map/krylov/pallas_call | solution.py:575
  65.9 17.5 %all_to_all.16 = f32[128,1,128]{2,1,0:T(1,128)S(1)} all-to-all(f32[128,1,128]{2,1,0:T(1,128)S(1)} %bitcast.16), channel_id=1, replica_groups=mesh['gx_0'=4,'gx_1'=4,'gx_2'=2,'gy'=4] {'gx_0','gx_1','gx_2','gy'}, dimensions={0} | all-to-all | bytes 131072 | tf_op jit(solution)/shard_map/all_to_all | solution.py:698
  83.4 1.1 %finish.1 = (f32[32,512]{1,0:T(8,128)}, f32[32,512]{1,0:T(8,128)}) custom-call(f32[128,128]{1,0:T(8,128)S(1)} %bitcast.15, f32[4,32,512]{2,1,0:T(8,128)S(1)} %get-tuple-element.37.basis_ref), custom_call_target="tpu_custom_call" | custom-call | tf_op jit(solution)/shard_map/finish/pallas_call | solution.py:659
  (17 shorter events, 0.2 us)
Async XLA Ops:
  3.9 11.5 %copy-start.3 = (s32[32,4]{0,1:T(4,128)S(1)}, s32[32,4]{0,1:T(4,128)}, u32[]{:S(2)}) copy-start(s32[32,4]{0,1:T(4,128)} %param.9) | copy-start | bytes 1540
  3.9 11.7 %copy-start.2 = (f32[32,512]{1,0:T(8,128)S(1)}, f32[32,512]{1,0:T(8,128)}, u32[]{:S(2)}) copy-start(f32[32,512]{1,0:T(8,128)} %reg_ref.3) | copy-start | bytes 196612
  3.9 45.8 %all-to-all-start = ((bf16[128,66,128]{2,1,0:T(8,128)(2,1)}), bf16[128,66,128]{2,1,0:T(8,128)(2,1)S(1)}, u32[]{:S(2)}, u32[]{:S(2)}) async-start(bf16[128,66,128]{2,1,0:T(8,128)(2,1)} %pack.1), calls=%async_computation | async-start | bytes 4718592 | tf_op jit(solution)/shard_map/all_to_all | solution.py:673
  15.6 1.6 %copy-start = (f32[32,32,512]{2,1,0:T(8,128)S(1)}, f32[32,32,512]{2,1,0:T(8,128)}, u32[]{:S(2)}) copy-start(f32[32,32,512]{2,1,0:T(8,128)} %feats_ref.5) | copy-start | bytes 6291460
  22.1 33.8 %collective-permute-start = (f32[104,128]{1,0:T(8,128)S(1)}, f32[104,128]{1,0:T(8,128)S(1)}, u32[]{:S(2)}, u32[]{:S(2)}) collective-permute-start(f32[104,128]{1,0:T(8,128)S(1)} %get-tuple-element.53), channel_id=1, source_target_pairs={{4,8},{8,4},{12,16},{16,12},{20,24},{24,20},{28,32},{32,28},{36,40... | collective-permute-start | bytes 159752 | tf_op jit(solution)/shard_map/ppermute | solution.py:375
  25.8 30.3 %collective-permute-start.1 = (f32[104,128]{1,0:T(8,128)S(1)}, f32[104,128]{1,0:T(8,128)S(1)}, u32[]{:S(2)}, u32[]{:S(2)}) collective-permute-start(f32[104,128]{1,0:T(8,128)S(1)} %get-tuple-element.52), channel_id=1, source_target_pairs={{0,4},{4,0},{8,12},{12,8},{16,20},{20,16},{24,28},{28,24},{32,36},... | collective-permute-start | bytes 159752 | tf_op jit(solution)/shard_map/ppermute | solution.py:376
  26.0 35.4 %collective-permute-start.2 = (f32[208,128]{1,0:T(8,128)S(1)}, f32[208,128]{1,0:T(8,128)S(1)}, u32[]{:S(2)}, u32[]{:S(2)}) collective-permute-start(f32[208,128]{1,0:T(8,128)S(1)} %get-tuple-element.41), channel_id=1, source_target_pairs={{1,2},{2,1},{5,6},{6,5},{9,10},{10,9},{13,14},{14,13},{17,18},{18,... | collective-permute-start | bytes 319496 | tf_op jit(solution)/shard_map/ppermute | solution.py:375
  26.7 34.7 %collective-permute-start.3 = (f32[208,128]{1,0:T(8,128)S(1)}, f32[208,128]{1,0:T(8,128)S(1)}, u32[]{:S(2)}, u32[]{:S(2)}) collective-permute-start(f32[208,128]{1,0:T(8,128)S(1)} %get-tuple-element.40), channel_id=1, source_target_pairs={{0,1},{1,0},{2,3},{3,2},{4,5},{5,4},{6,7},{7,6},{8,9},{9,8},{10,11... | collective-permute-start | bytes 319496 | tf_op jit(solution)/shard_map/ppermute | solution.py:376
  49.7 13.7 %copy-start.1 = (f32[32,32,512]{2,1,0:T(8,128)S(1)}, f32[32,32,512]{2,1,0:T(8,128)}, u32[]{:S(2)}) copy-start(f32[32,32,512]{2,1,0:T(8,128)} %feats_ref.5) | copy-start | bytes 6291460
  53.8 5.1 %collective-permute-start.4 = (f32[48,128]{1,0:T(8,128)S(1)}, f32[48,128]{1,0:T(8,128)S(1)}, u32[]{:S(2)}, u32[]{:S(2)}) collective-permute-start(f32[48,128]{1,0:T(8,128)S(1)} %get-tuple-element.57), channel_id=1, source_target_pairs={{4,8},{8,4},{12,16},{16,12},{20,24},{24,20},{28,32},{32,28},{36,40... | collective-permute-start | bytes 73736 | tf_op jit(solution)/shard_map/ppermute | solution.py:375
  56.0 3.0 %collective-permute-start.5 = (f32[48,128]{1,0:T(8,128)S(1)}, f32[48,128]{1,0:T(8,128)S(1)}, u32[]{:S(2)}, u32[]{:S(2)}) collective-permute-start(f32[48,128]{1,0:T(8,128)S(1)} %get-tuple-element.56), channel_id=1, source_target_pairs={{0,4},{4,0},{8,12},{12,8},{16,20},{20,16},{24,28},{28,24},{32,36},... | collective-permute-start | bytes 73736 | tf_op jit(solution)/shard_map/ppermute | solution.py:376
  59.0 4.3 %collective-permute-start.6 = (f32[120,128]{1,0:T(8,128)S(1)}, f32[120,128]{1,0:T(8,128)S(1)}, u32[]{:S(2)}, u32[]{:S(2)}) collective-permute-start(f32[120,128]{1,0:T(8,128)S(1)} %get-tuple-element.49), channel_id=1, source_target_pairs={{1,2},{2,1},{5,6},{6,5},{9,10},{10,9},{13,14},{14,13},{17,18},{18,... | collective-permute-start | bytes 184328 | tf_op jit(solution)/shard_map/ppermute | solution.py:375
  59.7 3.6 %collective-permute-start.7 = (f32[120,128]{1,0:T(8,128)S(1)}, f32[120,128]{1,0:T(8,128)S(1)}, u32[]{:S(2)}, u32[]{:S(2)}) collective-permute-start(f32[120,128]{1,0:T(8,128)S(1)} %get-tuple-element.48), channel_id=1, source_target_pairs={{0,1},{1,0},{2,3},{3,2},{4,5},{5,4},{6,7},{7,6},{8,9},{9,8},{10,11... | collective-permute-start | bytes 184328 | tf_op jit(solution)/shard_map/ppermute | solution.py:376
